TPU v7x, 32 devices: a whole 2x2x4 slice. The times are simulated.
32 devices in a mesh: ctx: 8 (over z, x), wt: 4 (over y, core).
Axes of the slice: x: 2, y: 2, z: 4, core: 2. Of those that a mesh axis runs over, the one named last changes fastest.
Arguments:
- tokens: bfloat16 [8, 2048, 768], P('wt', 'ctx'), may hold values from -6 to 6
- documents: int32 [8, 2048], P('wt', 'ctx'), may hold values from 0 to 11, never falling along the last dimension, each value on 1 to 1280 neighbouring positions
- first_gain: bfloat16 [768], P('wt'), may hold values from 0.5 to 1.5
- query_weight: bfloat16 [768, 768], P('wt'), may hold values from -0.4375 to 0.4375
- shared_weight: bfloat16 [768, 128], P('wt'), may hold values from -0.21875 to 0.21875
- mixing_weight: bfloat16 [768, 768], P('wt'), may hold values from -0.875 to 0.875
- second_gain: bfloat16 [768], P('wt'), may hold values from 0.5 to 1.5
- up_weight: bfloat16 [768, 3072], P('wt'), may hold values from -0.21875 to 0.21875
- down_weight: bfloat16 [3072, 768], P('wt'), may hold values from -0.109375 to 0.109375
- cotangent: bfloat16 [8, 2048, 768], P('wt', 'ctx'), may hold values from -6 to 6
Outputs:
- layer_out: bfloat16 [8, 2048, 768], P('wt', 'ctx')
- input_grad: float32 [8, 2048, 768], P('wt', 'ctx')
- first_grad: float32 [768], P('wt')
- query_grad: float32 [768, 768], P('wt')
- shared_grad: float32 [768, 128], P('wt')
- mixing_grad: float32 [768, 768], P('wt')
- second_grad: float32 [768], P('wt')
- up_grad: float32 [768, 3072], P('wt')
- down_grad: float32 [3072, 768], P('wt')
Inputs may be any that keep to these rules, and one draw needn't show every extreme that they name: `documents`: document numbers never fall along a sequence; each document holds 1 to 1280 positions, and one holds exactly 1280.
All inputs are finite; a program needn't handle non-finite values.
Results may differ from a plain program's by a relative error of at most 0.013.
The roundings to bfloat16 on the way count: a program that leaves them out, or rounds other values in their place, can miss the bound.
Values may be sent and summed in bfloat16 or wider, within the bound.
No kernel may reach another device: no remote copies, remote signals or barrier semaphores. Data moves between devices by JAX's collectives and lax.ppermute only.
A program may use at most 128 MiB of HBM per device.

v0:
```python
import jax
import jax.numpy as jnp
from jax import lax
from jax.sharding import PartitionSpec as P

HEADS = 12
HEAD_DIM = 64


EPSILON = 1e-05
NEGATIVE = -1e30


def layer_norm(values):
    center = values - jnp.mean(values, axis=-1, keepdims=True)
    spread = jnp.mean(center * center, axis=-1, keepdims=True)
    return center * lax.rsqrt(spread + EPSILON)


def gelu_tanh(values):
    return jax.nn.gelu(values, approximate=True)


def contract_rows(operand, matrix):
    return lax.dot_general(
        operand, matrix, (((0,), (0,)), ((), ())), preferred_element_type=jnp.float32
    )


def contract_cols(operand, matrix):
    return lax.dot_general(
        operand, matrix, (((1,), (1,)), ((), ())), preferred_element_type=jnp.float32
    )


def block_setup(local_docs, keyvals, all_docs, offset):
    rows_here = local_docs.shape[0]
    block_len = min(512, keyvals.shape[0])
    block_count = keyvals.shape[0] // block_len

    def needed_at(begin_row):
        doc_block = lax.dynamic_slice_in_dim(all_docs, begin_row, block_len, 0)
        return (begin_row <= offset + rows_here - 1) & (doc_block[block_len - 1] >= local_docs[0])

    def scores_at(queries, begin_row):
        key_block = lax.dynamic_slice_in_dim(keyvals, begin_row, block_len, 0)
        doc_block = lax.dynamic_slice_in_dim(all_docs, begin_row, block_len, 0)
        key_part = key_block[:, :HEAD_DIM]
        value_part = key_block[:, HEAD_DIM:]
        scores = jnp.einsum(
            "qhd,kd->qhk", queries, key_part, preferred_element_type=jnp.float32
        ) * (1.0 / HEAD_DIM**0.5)
        row_places = offset + jnp.arange(rows_here, dtype=jnp.int32)
        key_places = begin_row + jnp.arange(block_len, dtype=jnp.int32)
        allowed = (local_docs[:, None, None] == doc_block[None, None, :]) & (
            row_places[:, None, None] >= key_places[None, None, :]
        )
        return (key_part, value_part, scores, allowed)

    return (block_len, block_count, needed_at, scores_at)


def attend_forward(queries, local_docs, keyvals, all_docs, offset):
    rows_here = queries.shape[0]
    block_len, block_count, needed_at, scores_at = block_setup(
        local_docs, keyvals, all_docs, offset
    )

    def stats_step(block_index, current):
        begin_row = block_index * block_len

        def stats_update(carried):
            maxima, totals = carried
            key_part, value_part, scores, allowed = scores_at(queries, begin_row)
            block_max = jnp.max(jnp.where(allowed, scores, NEGATIVE), axis=-1)
            new_max = jnp.maximum(maxima, block_max)
            unnormed = jnp.where(allowed, jnp.exp(scores - new_max[..., None]), 0.0)
            return (new_max, totals * jnp.exp(maxima - new_max) + jnp.sum(unnormed, axis=-1))

        return lax.cond(needed_at(begin_row), stats_update, lambda carried: carried, current)

    start_max = jnp.full((rows_here, HEADS), NEGATIVE, jnp.float32)
    start_tot = jnp.zeros((rows_here, HEADS), jnp.float32)
    maxima, totals = lax.fori_loop(0, block_count, stats_step, (start_max, start_tot))
    log_totals = maxima + jnp.log(totals)

    def output_step(block_index, current):
        begin_row = block_index * block_len

        def output_update(carried):
            rounded_acc, remainder_acc = carried
            key_part, value_part, scores, allowed = scores_at(queries, begin_row)
            chances = jnp.where(allowed, jnp.exp(scores - log_totals[..., None]), 0.0)
            upper_part = chances.astype(jnp.bfloat16)
            lower_part = (chances - upper_part.astype(jnp.float32)).astype(jnp.bfloat16)
            rounded_acc = rounded_acc + jnp.einsum(
                "qhk,kd->qhd", upper_part, value_part, preferred_element_type=jnp.float32
            )
            remainder_acc = remainder_acc + jnp.einsum(
                "qhk,kd->qhd", lower_part, value_part, preferred_element_type=jnp.float32
            )
            return (rounded_acc, remainder_acc)

        return lax.cond(needed_at(begin_row), output_update, lambda carried: carried, current)

    empty_out = jnp.zeros((rows_here, HEADS, HEAD_DIM), jnp.float32)
    rounded_acc, remainder_acc = lax.fori_loop(0, block_count, output_step, (empty_out, empty_out))
    return (rounded_acc, rounded_acc + remainder_acc, log_totals)


def attend_backward(
    queries, local_docs, keyvals, all_docs, log_totals, grad_attended, row_delta, offset
):
    rows_here = queries.shape[0]
    block_len, block_count, needed_at, scores_at = block_setup(
        local_docs, keyvals, all_docs, offset
    )
    inverse_root = 1.0 / HEAD_DIM**0.5

    def grad_step(block_index, current):
        begin_row = block_index * block_len

        def grad_update(carried):
            grad_acc, key_terms = carried
            key_part, value_part, scores, allowed = scores_at(queries, begin_row)
            chances = jnp.where(allowed, jnp.exp(scores - log_totals[..., None]), 0.0)
            grad_probs = jnp.einsum(
                "qhd,kd->qhk", grad_attended, value_part, preferred_element_type=jnp.float32
            )
            grad_scores = (chances * (grad_probs - row_delta[..., None])).astype(jnp.bfloat16)
            grad_acc = (
                grad_acc
                + jnp.einsum(
                    "qhk,kd->qhd", grad_scores, key_part, preferred_element_type=jnp.float32
                )
                * inverse_root
            )
            grad_keys = (
                jnp.einsum("qhk,qhd->kd", grad_scores, queries, preferred_element_type=jnp.float32)
                * inverse_root
            )
            grad_values = jnp.einsum(
                "qhk,qhd->kd",
                chances.astype(jnp.bfloat16),
                grad_attended,
                preferred_element_type=jnp.float32,
            )
            joined = jnp.concatenate([grad_keys, grad_values], axis=-1)
            key_terms = lax.dynamic_update_slice_in_dim(key_terms, joined, begin_row, 0)
            return (grad_acc, key_terms)

        return lax.cond(needed_at(begin_row), grad_update, lambda carried: carried, current)

    empty_grad = jnp.zeros((rows_here, HEADS, HEAD_DIM), jnp.float32)
    empty_terms = jnp.zeros(keyvals.shape, jnp.float32)
    return lax.fori_loop(0, block_count, grad_step, (empty_grad, empty_terms))


def body(
    tokens,
    documents,
    first_gain,
    query_weight,
    shared_weight,
    mixing_weight,
    second_gain,
    up_weight,
    down_weight,
    cotangent,
):
    seqs_here, rows_here, model_width = tokens.shape
    total_rows = seqs_here * rows_here
    inputs = tokens.reshape(total_rows, model_width).astype(jnp.float32)
    normed_one = layer_norm(inputs)
    gain_piece = lax.all_gather(first_gain, "wt", axis=0, tiled=True)
    query_piece = lax.all_gather(query_weight, "wt", axis=0, tiled=True)
    shared_piece = lax.all_gather(shared_weight, "wt", axis=0, tiled=True)
    columns = normed_one
    scaled_part = (columns * gain_piece.astype(jnp.float32)).astype(jnp.bfloat16)
    query_pre = jnp.dot(scaled_part, query_piece, preferred_element_type=jnp.float32)
    shared_pre = jnp.dot(scaled_part, shared_piece, preferred_element_type=jnp.float32)
    query_width = query_pre.shape[1]
    pair_width = shared_pre.shape[1]
    queries = query_pre.astype(jnp.bfloat16).reshape(seqs_here, rows_here, HEADS, HEAD_DIM)
    shared = shared_pre.astype(jnp.bfloat16).reshape(seqs_here, rows_here, pair_width)
    keyvals_all, docs_all = (
        lax.all_gather(shared, "ctx", axis=1, tiled=True),
        lax.all_gather(documents, "ctx", axis=1, tiled=True),
    )
    offset = lax.axis_index("ctx") * rows_here
    rounded_out, exact_out, log_totals = lax.map(
        lambda entries: attend_forward(entries[0], entries[1], entries[2], entries[3], offset),
        (queries, documents, keyvals_all, docs_all),
    )
    attended = rounded_out.astype(jnp.bfloat16).reshape(total_rows, query_width)
    columns = attended
    mixed = jnp.dot(
        columns,
        lax.all_gather(mixing_weight, "wt", axis=0, tiled=True),
        preferred_element_type=jnp.float32,
    )
    hidden = inputs + mixed
    normed_two = layer_norm(hidden)
    gain_piece = lax.all_gather(second_gain, "wt", axis=0, tiled=True)
    up_piece = lax.all_gather(up_weight, "wt", axis=0, tiled=True)
    columns = normed_two
    scaled_part = (columns * gain_piece.astype(jnp.float32)).astype(jnp.bfloat16)
    upper = jnp.dot(scaled_part, up_piece, preferred_element_type=jnp.float32)
    activation = gelu_tanh(upper).astype(jnp.bfloat16)
    columns = activation
    reduced = jnp.dot(
        columns,
        lax.all_gather(down_weight, "wt", axis=0, tiled=True),
        preferred_element_type=jnp.float32,
    )
    layer_out = (hidden + reduced).astype(jnp.bfloat16).reshape(seqs_here, rows_here, model_width)
    first_full, query_full, shared_full, mixing_full, second_full, up_full, down_full = (
        lax.all_gather(first_gain, "wt", axis=0, tiled=True),
        lax.all_gather(query_weight, "wt", axis=0, tiled=True),
        lax.all_gather(shared_weight, "wt", axis=0, tiled=True),
        lax.all_gather(mixing_weight, "wt", axis=0, tiled=True),
        lax.all_gather(second_gain, "wt", axis=0, tiled=True),
        lax.all_gather(up_weight, "wt", axis=0, tiled=True),
        lax.all_gather(down_weight, "wt", axis=0, tiled=True),
    )
    first_float = first_full.astype(jnp.float32)
    second_float = second_full.astype(jnp.float32)
    grad_rows = cotangent.reshape(total_rows, model_width)
    grad_act = contract_cols(grad_rows, down_full)
    down_term = contract_rows(activation, grad_rows)
    unused_gelu, gelu_back = jax.vjp(gelu_tanh, upper)
    grad_upper = gelu_back(grad_act)[0].astype(jnp.bfloat16)
    scaled_two = (normed_two * second_float).astype(jnp.bfloat16)
    up_term = contract_rows(scaled_two, grad_upper)
    grad_scaled_two = contract_cols(grad_upper, up_full)
    second_term = jnp.sum(grad_scaled_two * normed_two, axis=0)
    unused_two, norm_back_two = jax.vjp(layer_norm, hidden)
    grad_hidden = grad_rows.astype(jnp.float32) + norm_back_two(grad_scaled_two * second_float)[0]
    grad_mixed = grad_hidden.astype(jnp.bfloat16)
    mixing_term = contract_rows(attended, grad_mixed)
    grad_attended = (
        contract_cols(grad_mixed, mixing_full)
        .astype(jnp.bfloat16)
        .reshape(seqs_here, rows_here, HEADS, HEAD_DIM)
    )
    row_delta = jnp.sum(grad_attended.astype(jnp.float32) * exact_out, axis=-1)
    grad_queries, key_terms = lax.map(
        lambda entries: attend_backward(
            entries[0],
            entries[1],
            entries[2],
            entries[3],
            entries[4],
            entries[5],
            entries[6],
            offset,
        ),
        (queries, documents, keyvals_all, docs_all, log_totals, grad_attended, row_delta),
    )
    key_sums = lax.psum_scatter(key_terms, "ctx", scatter_dimension=1, tiled=True)
    grad_shared = key_sums.astype(jnp.bfloat16).reshape(total_rows, pair_width)
    grad_query_rows = grad_queries.astype(jnp.bfloat16).reshape(total_rows, query_width)
    scaled_one = (normed_one * first_float).astype(jnp.bfloat16)
    query_term = contract_rows(scaled_one, grad_query_rows)
    shared_term = contract_rows(scaled_one, grad_shared)
    grad_scaled_one = contract_cols(grad_query_rows, query_full) + contract_cols(
        grad_shared, shared_full
    )
    first_term = jnp.sum(grad_scaled_one * normed_one, axis=0)
    unused_one, norm_back_one = jax.vjp(layer_norm, inputs)
    input_grad = grad_hidden + norm_back_one(grad_scaled_one * first_float)[0]
    owned_first, owned_query, owned_shared, owned_mixing, owned_second, owned_up, owned_down = (
        lax.psum_scatter(first_term, "wt", scatter_dimension=0, tiled=True),
        lax.psum_scatter(query_term, "wt", scatter_dimension=0, tiled=True),
        lax.psum_scatter(shared_term, "wt", scatter_dimension=0, tiled=True),
        lax.psum_scatter(mixing_term, "wt", scatter_dimension=0, tiled=True),
        lax.psum_scatter(second_term, "wt", scatter_dimension=0, tiled=True),
        lax.psum_scatter(up_term, "wt", scatter_dimension=0, tiled=True),
        lax.psum_scatter(down_term, "wt", scatter_dimension=0, tiled=True),
    )
    first_grad, query_grad, shared_grad, mixing_grad, second_grad, up_grad, down_grad = lax.psum(
        (owned_first, owned_query, owned_shared, owned_mixing, owned_second, owned_up, owned_down),
        "ctx",
    )
    return (
        layer_out,
        input_grad.reshape(seqs_here, rows_here, model_width),
        first_grad,
        query_grad,
        shared_grad,
        mixing_grad,
        second_grad,
        up_grad,
        down_grad,
    )


def solution(mesh):
    in_specs = (
        P("wt", "ctx", None),
        P("wt", "ctx"),
        P("wt"),
        P("wt", None),
        P("wt", None),
        P("wt", None),
        P("wt"),
        P("wt", None),
        P("wt", None),
        P("wt", "ctx", None),
    )
    out_specs = (
        P("wt", "ctx", None),
        P("wt", "ctx", None),
        P("wt"),
        P("wt", None),
        P("wt", None),
        P("wt", None),
        P("wt"),
        P("wt", None),
        P("wt", None),
    )
    return jax.shard_map(body, mesh=mesh, in_specs=in_specs, out_specs=out_specs, check_vma=False)
```

profile of v0, /device:TPU:0, one launch (start us, length us, event | category | flops | bytes accessed | tf_op | source)
XLA Modules:
  0.0 973.2 jit_solution(3758998610461700746)
XLA Ops:
  11.7 8.3 all-reduce.7
  24.0 6.1 all_gather.36
  34.6 26.2 %all_gather.34 = s32[2,2048]{1,0:T(2,128)S(1)} all-gather(s32[2,256]{1,0:T(2,128)S(1)} %copy-done.28), channel_id=1, replica_groups=mesh['ctx'=8,'wt'=4] {'ctx'}, dimensions={1}, use_global_device_ids=true | all-gather | bytes 18432 | tf_op jit(solution)/shard_map/all_gather | solution.py:188
  64.4 8.3 all-gather.6.cloned.1.call-done
  72.8 107.9 %while.140 = (s32[]{:T(128)}, bf16[2,256,12,64]{1,3,2,0:T(8,128)(2,1)S(1)}, f32[2,256,12,64]{1,0,3,2:T(2,128)}, f32[2,256,12]{1,2,0:T(8,128)S(1)}, s32[2,2048]{1...) while((s32[]{:T(128)}, ...), condition=%wide.region_13.14_spmd, body=%wide.region_2.13_spmd.sunk | while | flops 835004928 | bytes 72426776 | solution.py:191
  75.5 12.6 %while.143 = (s32[]{:T(128)}, f32[256,12]{0,1:T(8,128)S(1)}, f32[256,12]{0,1:T(8,128)S(1)}, s32[]{:T(128)}, s32[2048]{0:T(1024)S(1)}, /*index=5*/s32[256]{0:T(25...) while((s32[]{:T(128)}, f32[256,12]{0,1:T(8,128)S(1)}, ...), condition=%wide.region_8.8_spmd, body=%wide.region_3.7_spmd.sunk | while | flops 212736784 | bytes 13612411 | solution.py:84
  77.9 2.8 conditional.7
  88.3 21.2 %while.144 = (s32[]{:T(128)}, f32[256,12,64]{0,2,1:T(8,128)S(1)}, f32[256,12,64]{0,2,1:T(8,128)S(1)}, s32[]{:T(128)}, s32[2048]{0:T(1024)S(1)}, /*index=5*/s32[2...) while((s32[]{:T(128)}, f32[256,12,64]{0,2,1:T(8,128)S(1)}, ...), condition=%wide.region_12.12_spmd, body=%wide.region_9.11_spmd.sunk | while | flops 622068480 | bytes 48219584 | solution.py:107
  90.8 10.9 %conditional.8 = ((f32[256,12,64]{0,2,1:T(8,128)S(1)}, f32[256,12,64]{0,2,1:T(8,128)S(1)})) conditional(s32[]{:T(128)} %convert_element_type.217, (f32[256,12,64]{0,2,1:T(8,128)S(1)}, f32[256,12,64]{0,2,1:T(8,128)S(1)}) %tuple.244, (s32[256]{0:T(256)S(1)}, s32[]{:T(128)}, s32[2048]{0:T(1024)S(1)}, s32[]{:T(128)}, bf16[2048,128]{0,1:T(8,128)(2,1)S(1)}, ...), branch_computations={%region_10.9_spmd, %region_11.10_spmd} | conditional | flops 622068480 | bytes 48215168 | solution.py:104
  90.8 3.7 fusion.19
  94.8 4.4 fusion.16
  110.4 16.7 %dynamic_update_slice.61 = f32[2,256,12,64]{1,0,3,2:T(2,128)} dynamic-update-slice(f32[2,256,12,64]{1,0,3,2:T(2,128)} %get-tuple-element.2087, f32[1,256,12,64]{1,0,3,2:T(1,128)S(1)} %copy.94, s32[]{:T(128)S(6)} %copy.148, s32[]{:T(128)} %constant.304.clone.1..sunk, s32[]{:T(128)} %constant.304.clone.1..sunk, s32[]{:T(128)} %constant.304.clone.1..sunk) | dynamic-update-slice | bytes 1572868 | tf_op jit(solution)/shard_map/while/body/jit(dynamic_update_index_in_dim)/dynamic_update_slice | solution.py:191
  129.4 12.7 %while.143 = (s32[]{:T(128)}, f32[256,12]{0,1:T(8,128)S(1)}, f32[256,12]{0,1:T(8,128)S(1)}, s32[]{:T(128)}, s32[2048]{0:T(1024)S(1)}, /*index=5*/s32[256]{0:T(25...) while((s32[]{:T(128)}, f32[256,12]{0,1:T(8,128)S(1)}, ...), condition=%wide.region_8.8_spmd, body=%wide.region_3.7_spmd.sunk | while | flops 212736784 | bytes 13612411 | solution.py:84
  131.8 2.8 conditional.7
  142.2 20.7 %while.144 = (s32[]{:T(128)}, f32[256,12,64]{0,2,1:T(8,128)S(1)}, f32[256,12,64]{0,2,1:T(8,128)S(1)}, s32[]{:T(128)}, s32[2048]{0:T(1024)S(1)}, /*index=5*/s32[2...) while((s32[]{:T(128)}, f32[256,12,64]{0,2,1:T(8,128)S(1)}, ...), condition=%wide.region_12.12_spmd, body=%wide.region_9.11_spmd.sunk | while | flops 622068480 | bytes 48219584 | solution.py:107
  144.7 10.5 %conditional.8 = ((f32[256,12,64]{0,2,1:T(8,128)S(1)}, f32[256,12,64]{0,2,1:T(8,128)S(1)})) conditional(s32[]{:T(128)} %convert_element_type.217, (f32[256,12,64]{0,2,1:T(8,128)S(1)}, f32[256,12,64]{0,2,1:T(8,128)S(1)}) %tuple.244, (s32[256]{0:T(256)S(1)}, s32[]{:T(128)}, s32[2048]{0:T(1024)S(1)}, s32[]{:T(128)}, bf16[2048,128]{0,1:T(8,128)(2,1)S(1)}, ...), branch_computations={%region_10.9_spmd, %region_11.10_spmd} | conditional | flops 622068480 | bytes 48215168 | solution.py:104
  144.7 3.7 fusion.19
  148.7 4.4 fusion.16
  163.9 16.7 %dynamic_update_slice.61 = f32[2,256,12,64]{1,0,3,2:T(2,128)} dynamic-update-slice(f32[2,256,12,64]{1,0,3,2:T(2,128)} %get-tuple-element.2087, f32[1,256,12,64]{1,0,3,2:T(1,128)S(1)} %copy.94, s32[]{:T(128)S(6)} %copy.148, s32[]{:T(128)} %constant.304.clone.1..sunk, s32[]{:T(128)} %constant.304.clone.1..sunk, s32[]{:T(128)} %constant.304.clone.1..sunk) | dynamic-update-slice | bytes 1572868 | tf_op jit(solution)/shard_map/while/body/jit(dynamic_update_index_in_dim)/dynamic_update_slice | solution.py:191
  182.5 2.5 fusion.71
  185.4 7.1 fusion.72
  192.4 12.8 %fusion.46 = (bf16[512,3072]{1,0:T(8,128)(2,1)S(1)}, f32[512,3072]{1,0:T(8,128)}) fusion(f32[512,3072]{1,0:T(8,128)} %fusion.72, bf16[768,3072]{1,0:T(8,128)(2,1)} %all-gather.12.cloned.1.call-done, f32[512,768]{1,0:T(8,128)S(1)} %get-tuple-element.1493, f32[768]{0:T(1024)S(1)} %copy-done.22, f32[512]{0:T(512)S(1)} %fusion.61, ...), kind=kOutput, calls=%fused_computation.84 | convolution fusion | flops 2448949248 | bytes 22027264 | tf_op jit(solution)/shard_map/dot_general | solution.py:208
  205.2 3.4 multiply_reduce_fusion
  215.7 54.3 %while.142 = (s32[]{:T(128)}, bf16[2,256,12,64]{1,3,2,0:T(8,128)(2,1)}, f32[2,2048,128]{2,1,0:T(8,128)}, s32[2,2048]{1,0:T(2,128)S(1)}, s32[2,256]{1,0:T(2,128)S...) while((s32[]{:T(128)}, ...), condition=%wide.region_24.25_spmd, body=%wide.region_19.24_spmd.sunk | while | flops 1023247104 | bytes 68378440 | solution.py:247
  218.5 22.4 %while.145 = (s32[]{:T(128)}, f32[256,12,64]{0,2,1:T(8,128)S(1)}, f32[2048,128]{0,1:T(8,128)S(1)}, s32[]{:T(128)}, s32[2048]{0:T(1024)S(1)}, /*index=5*/s32[256]...) while((s32[]{:T(128)}, f32[256,12,64]{0,2,1:T(8,128)S(1)}, ...), condition=%wide.region_23.23_spmd, body=%wide.region_20.22_spmd.sunk | while | flops 1023247104 | bytes 58062308 | solution.py:156
  221.0 12.1 %conditional.6 = ((f32[256,12,64]{0,2,1:T(8,128)S(1)}, f32[2048,128]{0,1:T(8,128)S(1)})) conditional(s32[]{:T(128)} %convert_element_type.215, (f32[256,12,64]{0,2,1:T(8,128)S(1)}, f32[2048,128]{0,1:T(8,128)S(1)}) %tuple.238, (s32[256]{0:T(256)S(1)}, s32[]{:T(128)}, s32[2048]{0:T(1024)S(1)}, s32[]{:T(128)}, bf16[2048,128]{0,1:T(8,128)(2,1)S(1)}, ...), branch_computations={%region_21.20_spmd, %region_22.21_spmd} | conditional | flops 1023247104 | bytes 58057860 | solution.py:152
  221.0 3.7 fusion.35
  225.0 4.9 fusion.25
  245.5 22.4 %while.145 = (s32[]{:T(128)}, f32[256,12,64]{0,2,1:T(8,128)S(1)}, f32[2048,128]{0,1:T(8,128)S(1)}, s32[]{:T(128)}, s32[2048]{0:T(1024)S(1)}, /*index=5*/s32[256]...) while((s32[]{:T(128)}, f32[256,12,64]{0,2,1:T(8,128)S(1)}, ...), condition=%wide.region_23.23_spmd, body=%wide.region_20.22_spmd.sunk | while | flops 1023247104 | bytes 58062308 | solution.py:156
  248.1 12.1 %conditional.6 = ((f32[256,12,64]{0,2,1:T(8,128)S(1)}, f32[2048,128]{0,1:T(8,128)S(1)})) conditional(s32[]{:T(128)} %convert_element_type.215, (f32[256,12,64]{0,2,1:T(8,128)S(1)}, f32[2048,128]{0,1:T(8,128)S(1)}) %tuple.238, (s32[256]{0:T(256)S(1)}, s32[]{:T(128)}, s32[2048]{0:T(1024)S(1)}, s32[]{:T(128)}, bf16[2048,128]{0,1:T(8,128)(2,1)S(1)}, ...), branch_computations={%region_21.20_spmd, %region_22.21_spmd} | conditional | flops 1023247104 | bytes 58057860 | solution.py:152
  248.1 3.7 fusion.35
  252.1 4.9 fusion.25
  272.5 2.2 fusion.74
  274.9 3.3 fusion.75
  278.3 208.7 %reduce-scatter.7.cloned.1.call-done = f32[2,256,128]{2,1,0:T(8,128)} async-done(((f32[2,2048,128]{2,1,0:T(8,128)}), f32[2,256,128]{2,1,0:T(8,128)}) %reduce-scatter.7.cloned.1.call-update) | async-done | bytes 262160 | tf_op jit(solution)/shard_map/reduce_scatter | solution.py:260
  489.2 7.2 fusion.66
  497.6 9.8 %fusion.68 = f32[3072,768]{1,0:T(8,128)} fusion(bf16[512,768]{1,0:T(8,128)(2,1)S(1)} %bitcast.224, f32[512,3072]{1,0:T(8,128)} %get-tuple-element.1495), kind=kOutput, calls=%fused_computation.134 | convolution fusion | flops 2430074880 | bytes 16515072 | tf_op jit(solution)/shard_map/dot_general | solution.py:25
  507.5 14.8 %reduce-scatter.9.cloned.1.call-done = f32[192,768]{1,0:T(8,128)} async-done(((f32[768,768]{1,0:T(8,128)}), f32[192,768]{1,0:T(8,128)}) %reduce-scatter.9.cloned.1.call-update) | async-done | bytes 589840 | tf_op jit(solution)/shard_map/reduce_scatter | solution.py:274
  522.2 36.4 %reduce-scatter.13.cloned.1.call-done = f32[192,768]{1,0:T(8,128)} async-done(((f32[768,768]{1,0:T(8,128)}), f32[192,768]{1,0:T(8,128)}) %reduce-scatter.13.cloned.1.call-update) | async-done | bytes 589840 | tf_op jit(solution)/shard_map/reduce_scatter | solution.py:276
  558.6 24.0 %reduce-scatter.11.cloned.1.call-done = f32[192,128]{1,0:T(8,128)} async-done(((f32[768,128]{1,0:T(8,128)}), f32[192,128]{1,0:T(8,128)}) %reduce-scatter.11.cloned.1.call-update) | async-done | bytes 98320 | tf_op jit(solution)/shard_map/reduce_scatter | solution.py:275
  582.6 80.9 %reduce-scatter.15.cloned.1.call-done = f32[192,3072]{1,0:T(8,128)} async-done(((f32[768,3072]{1,0:T(8,128)}), f32[192,3072]{1,0:T(8,128)}) %reduce-scatter.15.cloned.1.call-update) | async-done | bytes 2359312 | tf_op jit(solution)/shard_map/reduce_scatter | solution.py:278
  663.5 81.0 %reduce-scatter.17.cloned.1.call-done = f32[768,768]{1,0:T(8,128)} async-done(((f32[3072,768]{1,0:T(8,128)}), f32[768,768]{1,0:T(8,128)}) %reduce-scatter.17.cloned.1.call-update) | async-done | bytes 2359312 | tf_op jit(solution)/shard_map/reduce_scatter | solution.py:279
  745.2 8.9 add_convert_fusion
  757.4 6.2 all-reduce.6
  763.7 23.1 %all-reduce.4 = (f32[192]{0:T(256)}, f32[192]{0:T(256)}) all-reduce(f32[192]{0:T(256)S(1)} %dynamic-slice.3, f32[192]{0:T(256)S(1)} %dynamic-slice.5), channel_id=1, replica_groups=mesh['ctx'=8,'wt'=4] {'ctx'}, use_global_device_ids=true, to_apply=%region_30.31 | all-reduce | flops 384 | bytes 3072 | tf_op jit(solution)/shard_map/psum | solution.py:281
  786.8 3.3 add_add_fusion.2
  790.1 166.5 %all-reduce.10.cloned.1.call-done = (f32[192,768]{1,0:T(8,128)}, f32[192,128]{1,0:T(8,128)}, f32[192,768]{1,0:T(8,128)}, f32[192,3072]{1,0:T(8,128)}, f32[768,768]{1,0:T(8,128)}) async-done(((f32[192,768]{1,0:T(8,128)}, f32[192,128]{1,0:T(8,128)}, f32[192,768]{1,0:T(8,128)}, f32[192,3072]{1,0:T(8,128)}, f32[768,768]{1,0:T(8,128)}), (f32[192,768]{1,0:T(8,128)}, f32[192,128]{1,0:T(8,128)}, ...) | async-done | bytes 5996560 | tf_op jit(solution)/shard_map/psum | solution.py:281
  956.6 2.1 copy.172
  (358 shorter events, 104.8 us)
Async XLA Ops:
  7.2 23.0 %copy-start.2 = (bf16[2,256,768]{2,1,0:T(8,128)(2,1)S(1)}, bf16[2,256,768]{2,1,0:T(8,128)(2,1)}, u32[]{:S(2)}) copy-start(bf16[2,256,768]{2,1,0:T(8,128)(2,1)} %param.26) | copy-start | bytes 2359300
  7.2 53.6 %all-gather.8.cloned.1.call-start = ((), (), s32[]{:S(2)}) async-start(), calls=%async_computation.7 | async-start | bytes 1474560 | tf_op jit(solution)/shard_map/all_gather | solution.py:176
  7.9 64.7 %all-gather.6.cloned.1.call-start = ((), (), s32[]{:S(2)}) async-start(), calls=%async_computation.6 | async-start | bytes 1179648 | tf_op jit(solution)/shard_map/all_gather | solution.py:187
  20.0 11.2 %copy-start.24 = (f32[768]{0:T(1024)}, f32[768]{0:T(1024)S(1)}, u32[]{:S(2)}) copy-start(f32[768]{0:T(1024)S(1)} %convert_element_type.113) | copy-start | bytes 9220
  21.3 8.8 copy-start.37
  24.0 7.2 copy-start.33
  24.0 7.2 copy-start.29
  30.9 3.8 copy-start.28
  32.1 150.4 %all-gather.10.cloned.1.call-start = ((), (), s32[]{:S(2)}) async-start(), calls=%async_computation.8 | async-start | bytes 1474560 | tf_op jit(solution)/shard_map/all_gather | solution.py:199
  32.8 152.5 %all-gather.14.cloned.1.call-start = ((), (), s32[]{:S(2)}) async-start(), calls=%async_computation.10 | async-start | bytes 5898240 | tf_op jit(solution)/shard_map/all_gather | solution.py:213
  33.4 159.1 %all-gather.12.cloned.1.call-start = ((), (), s32[]{:S(2)}) async-start(), calls=%async_computation.9 | async-start | bytes 5898240 | tf_op jit(solution)/shard_map/all_gather | solution.py:205
  34.0 453.0 %reduce-scatter.7.cloned.1.call-start = ((), (), s32[]{:S(2)}) async-start(), calls=%async_computation.11 | async-start | bytes 2359296 | tf_op jit(solution)/shard_map/reduce_scatter | solution.py:260
  94.8 5.1 copy-start
  148.7 4.7 copy-start
  180.6 1.9 copy-start.3
  182.5 2.9 copy-start.10
  185.0 23.7 %copy-start.6 = (f32[512,768]{1,0:T(8,128)}, f32[512,768]{1,0:T(8,128)S(1)}, u32[]{:S(2)}) copy-start(f32[512,768]{1,0:T(8,128)S(1)} %get-tuple-element.1493) | copy-start | bytes 4718596
  185.0 23.7 %copy-start.26 = (f32[512]{0:T(512)}, f32[512]{0:T(512)S(1)}, u32[]{:S(2)}) copy-start(f32[512]{0:T(512)S(1)} %broadcast_multiply_fusion) | copy-start | bytes 6148
  185.3 23.3 %copy-start.31 = (f32[512]{0:T(512)}, f32[512]{0:T(512)S(1)}, u32[]{:S(2)}) copy-start(f32[512]{0:T(512)S(1)} %fusion.61) | copy-start | bytes 6148
  185.3 7.1 copy-start.22
  192.4 12.8 %copy-start.43 = (bf16[768,3072]{1,0:T(8,128)(2,1)S(1)}, bf16[768,3072]{1,0:T(8,128)(2,1)}, u32[]{:S(2)}) copy-start(bf16[768,3072]{1,0:T(8,128)(2,1)} %all-gather.12.cloned.1.call-done) | copy-start | bytes 14155780
  205.2 3.4 copy-start.15
  209.3 2.3 copy-start.44
  209.3 3.1 copy-start.35
  212.4 1.5 copy-start.20
  215.7 54.4 %copy-start.25 = (f32[768]{0:T(1024)S(1)}, f32[768]{0:T(1024)}, u32[]{:S(2)}) copy-start(f32[768]{0:T(1024)} %copy-done.24) | copy-start | bytes 9220
  215.7 54.4 %copy-start.38 = (f32[2,256]{1,0:T(2,128)S(1)}, f32[2,256]{1,0:T(2,128)}, u32[]{:S(2)}) copy-start(f32[2,256]{1,0:T(2,128)} %copy-done.37) | copy-start | bytes 6148
  215.7 54.4 %copy-start.41 = (f32[2,256]{1,0:T(2,128)S(1)}, f32[2,256]{1,0:T(2,128)}, u32[]{:S(2)}) copy-start(f32[2,256]{1,0:T(2,128)} %get-tuple-element.1486) | copy-start | bytes 6148
  225.0 5.7 copy-start.1
  252.1 5.6 copy-start.1
  270.1 252.1 %reduce-scatter.9.cloned.1.call-start = ((), (), s32[]{:S(2)}) async-start(), calls=%async_computation.12 | async-start | bytes 2949120 | tf_op jit(solution)/shard_map/reduce_scatter | solution.py:274
  272.5 2.3 copy-start.8
  272.5 2.3 copy-start.13
  274.8 283.8 %reduce-scatter.13.cloned.1.call-start = ((), (), s32[]{:S(2)}) async-start(), calls=%async_computation.14 | async-start | bytes 2949120 | tf_op jit(solution)/shard_map/reduce_scatter | solution.py:276
  278.2 211.0 %copy-start.7 = (f32[512,768]{1,0:T(8,128)S(1)}, f32[512,768]{1,0:T(8,128)}, u32[]{:S(2)}) copy-start(f32[512,768]{1,0:T(8,128)} %copy-done.6) | copy-start | bytes 4718596
  278.2 211.0 %copy-start.23 = (f32[768]{0:T(1024)S(1)}, f32[768]{0:T(1024)}, u32[]{:S(2)}) copy-start(f32[768]{0:T(1024)} %convert_element_type.118) | copy-start | bytes 9220
  278.2 211.0 %copy-start.27 = (f32[512]{0:T(512)S(1)}, f32[512]{0:T(512)}, u32[]{:S(2)}) copy-start(f32[512]{0:T(512)} %copy-done.26) | copy-start | bytes 6148
  278.2 211.0 %copy-start.32 = (f32[512]{0:T(512)S(1)}, f32[512]{0:T(512)}, u32[]{:S(2)}) copy-start(f32[512]{0:T(512)} %copy-done.31) | copy-start | bytes 6148
  278.2 304.4 %reduce-scatter.11.cloned.1.call-start = ((), (), s32[]{:S(2)}) async-start(), calls=%async_computation.13 | async-start | bytes 491520 | tf_op jit(solution)/shard_map/reduce_scatter | solution.py:275
  489.1 174.4 %reduce-scatter.15.cloned.1.call-start = ((), (), s32[]{:S(2)}) async-start(), calls=%async_computation.15 | async-start | bytes 11796480 | tf_op jit(solution)/shard_map/reduce_scatter | solution.py:278
  496.4 248.1 %reduce-scatter.17.cloned.1.call-start = ((), (), s32[]{:S(2)}) async-start(), calls=%async_computation.16 | async-start | bytes 11796480 | tf_op jit(solution)/shard_map/reduce_scatter | solution.py:279
  507.4 449.2 %all-reduce.10.cloned.1.call-start = ((), (), s32[]{:S(2)}) async-start(), calls=%async_computation.17 | async-start | bytes 11993088 | tf_op jit(solution)/shard_map/psum | solution.py:281
  745.1 8.9 copy-start.19
  745.2 9.3 copy-start.21
  745.2 9.3 copy-start.30
  756.5 30.3 %copy-start.36 = (f32[512]{0:T(512)S(1)}, f32[512]{0:T(512)}, u32[]{:S(2)}) copy-start(f32[512]{0:T(512)} %copy-done.35) | copy-start | bytes 6148
  956.6 5.5 copy-start.17
  962.2 2.5 copy-start.16
  (11 other events, 11.6 us)
Sparse Core Ops, SparseCore 0:
  9.6 20.9 all-gather.7
  33.2 39.4 all-gather.5
  74.2 16.3 all-gather.9
  92.1 37.4 all-gather.13
  131.0 37.4 all-gather.11
  270.2 216.6 reduce-scatter.6
  490.0 32.1 reduce-scatter.8
  525.5 33.0 reduce-scatter.12
  561.7 20.8 reduce-scatter.10
  585.0 78.4 reduce-scatter.14
  666.1 78.3 reduce-scatter.16
  749.4 207.1 all-reduce.9
where the time goes:
time: 968 us; the launch traced here: 973 us
  waiting for transfers between devices  623 us (64%)
  matrix products  108 us (11%)
  local copies, waits for them, and re-layouts  106 us (11%)
  blocking collectives  69.9 us (7%)
  loops' own time  32.6 us (3%)
  between operations  16.3 us (2%)
  other arithmetic  15.9 us (2%)
    reduce_scatter x1, waiting for transfers between devices, body(): lax.psum_scatter(key_terms, 'ctx', scatter_dimension=1, tiled=True)  209 us
    psum x1, waiting for transfers between devices, body(): lax.psum((owned_first, owned_query, owned_shared, owned_mixing, owned_sec...  167 us
    reduce_scatter x1, waiting for transfers between devices, body(): lax.psum_scatter(down_term, 'wt', scatter_dimension=0, tiled=True)  81 us
    reduce_scatter x1, waiting for transfers between devices, body(): lax.psum_scatter(up_term, 'wt', scatter_dimension=0, tiled=True)  80.9 us
    dynamic_update_slice x8, local copies, waits for them, and re-layouts, body(): lax.map(lambda entries: attend_forward(entries[0], entries[1], entries[2]...  36.7 us
    reduce_scatter x1, waiting for transfers between devices, body(): lax.psum_scatter(mixing_term, 'wt', scatter_dimension=0, tiled=True)  36.4 us
    all_gather x1, blocking collectives, body(): lax.all_gather(documents, 'ctx', axis=1, tiled=True)  26.2 us
    reduce_scatter x1, waiting for transfers between devices, body(): lax.psum_scatter(shared_term, 'wt', scatter_dimension=0, tiled=True)  24 us
  transfers between devices with their start and end apart: 12, of which 8 were waited for; matrix products, arithmetic and copies ran while one was open for 15% of the time, Pallas kernels for 0%

commit v1 on v0

v1 whole, which is shorter than its diff:
```python
import functools
import math

import jax
import jax.numpy as jnp
from jax import lax
from jax.experimental import pallas as pl
from jax.experimental.pallas import tpu as pltpu
from jax.sharding import PartitionSpec as P

HEADS = 12
HEAD_DIM = 64
PAIRS = HEADS // 2
LANES = 128
EPSILON = 1e-05
BIAS = -1e30
SCALE = math.log2(math.e) / HEAD_DIM**0.5
F32 = jnp.float32
BF16 = jnp.bfloat16
GELU_ROOT = math.sqrt(2.0 / math.pi)
GELU_CUBE = 0.044715


def params(*semantics):
    return pltpu.CompilerParams(
        dimension_semantics=semantics or None, vmem_limit_bytes=56 * 1024 * 1024
    )


def cost(flops, bytes_accessed, transcendentals=0):
    return pl.CostEstimate(
        flops=flops, bytes_accessed=bytes_accessed, transcendentals=transcendentals
    )


def dot_nn(a, b):
    return lax.dot_general(a, b, (((1,), (0,)), ((), ())), preferred_element_type=F32)


def dot_nt(a, b):
    return lax.dot_general(a, b, (((1,), (1,)), ((), ())), preferred_element_type=F32)


def dot_tn(a, b):
    return lax.dot_general(a, b, (((0,), (0,)), ((), ())), preferred_element_type=F32)


def normalize(values):
    center = values - jnp.mean(values, axis=-1, keepdims=True)
    spread = jnp.mean(center * center, axis=-1, keepdims=True)
    inverse = lax.rsqrt(spread + EPSILON)
    return center * inverse, inverse


def norm_back(grad, normed, inverse):
    mean_grad = jnp.mean(grad, axis=-1, keepdims=True)
    mean_both = jnp.mean(grad * normed, axis=-1, keepdims=True)
    return (grad - mean_grad - normed * mean_both) * inverse


def place_rows(spot, pieces, scratch):
    height = scratch.shape[0] // len(pieces)
    for r, piece in enumerate(pieces):
        begin = pl.multiple_of((spot ^ r) * height, height)
        scratch[pl.ds(begin, height), :] = piece[0:height, :]


STEP = 128


def over_rows(rows, run):
    def one(index, carried):
        run(pl.ds(pl.multiple_of(index * STEP, STEP), STEP))
        return carried

    lax.fori_loop(0, rows // STEP, one, 0)


def first_kernel(spot_ref, tokens, gain, *rest, pieces):
    weights = rest[:pieces]
    scaled_out, shared_out, weight = rest[pieces:]
    place_rows(spot_ref[0], weights, weight)

    def run(rows):
        normed, unused = normalize(tokens[rows, :].astype(F32))
        scaled = (normed * gain[...]).astype(BF16)
        scaled_out[rows, :] = scaled
        shared_out[rows, :] = dot_nn(scaled, weight[...]).astype(BF16)

    over_rows(tokens.shape[0], run)


def first_stage(spot, tokens, gain, weights):
    rows, width = tokens.shape
    columns = weights[0].shape[1]
    return pl.pallas_call(
        functools.partial(first_kernel, pieces=len(weights)),
        grid_spec=pltpu.PrefetchScalarGridSpec(
            num_scalar_prefetch=1,
            grid=(),
            in_specs=[pl.BlockSpec(memory_space=pltpu.VMEM)] * (2 + len(weights)),
            out_specs=[pl.BlockSpec(memory_space=pltpu.VMEM)] * 2,
            scratch_shapes=[pltpu.VMEM((width, columns), BF16)],
        ),
        out_shape=[
            jax.ShapeDtypeStruct((rows, width), BF16),
            jax.ShapeDtypeStruct((rows, columns), BF16),
        ],
        compiler_params=params(),
        cost_estimate=cost(2 * rows * width * columns, 4 * rows * width),
        name="first_norm",
    )(spot, tokens, gain, *weights)


def project_kernel(spot_ref, operand, *rest, pieces):
    weights = rest[:pieces]
    out, weight = rest[pieces:]
    place_rows(spot_ref[0], weights, weight)
    out[...] = dot_nn(operand[...], weight[...]).astype(out.dtype)


def project(spot, operand, weights):
    rows, width = operand.shape
    columns = weights[0].shape[1]
    return pl.pallas_call(
        functools.partial(project_kernel, pieces=len(weights)),
        grid_spec=pltpu.PrefetchScalarGridSpec(
            num_scalar_prefetch=1,
            grid=(),
            in_specs=[pl.BlockSpec(memory_space=pltpu.VMEM)] * (1 + len(weights)),
            out_specs=pl.BlockSpec(memory_space=pltpu.VMEM),
            scratch_shapes=[pltpu.VMEM((width, columns), BF16)],
        ),
        out_shape=jax.ShapeDtypeStruct((rows, columns), BF16),
        compiler_params=params(),
        cost_estimate=cost(2 * rows * width * columns, 4 * rows * width),
        name="project",
    )(spot, operand, *weights)


def low_lanes(shape):
    return lax.broadcasted_iota(jnp.int32, shape, len(shape) - 1) < HEAD_DIM


def swap_halves(values):
    return pltpu.roll(values, HEAD_DIM, 1)


def stacked_pairs(ref):
    return jnp.concatenate(
        [ref[0, :, p * LANES : (p + 1) * LANES] for p in range(PAIRS)], axis=0
    )


def tile_bias(starts, key_begin, row_begin, tile_rows, tile_keys):
    key_place = key_begin + lax.broadcasted_iota(jnp.int32, (tile_rows, tile_keys), 1)
    row_place = row_begin + lax.broadcasted_iota(jnp.int32, (tile_rows, tile_keys), 0)
    first = jnp.concatenate([starts] * (tile_keys // LANES), axis=1)
    allowed = (key_place >= first) & (key_place <= row_place)
    bias = jnp.where(allowed, 0.0, BIAS)
    bias = jnp.concatenate([bias, bias], axis=1)
    return jnp.concatenate([bias] * PAIRS, axis=0)


def attend_kernel(
    first_ref, last_ref, queries, starts, *rest, blocks, tile_rows, tile_keys
):
    keyvals = rest[:blocks]
    exact_out, rounded_out, logs_out = rest[blocks : blocks + 3]
    key_even, key_odd, value_even, value_odd, score_scratch, most, total = rest[blocks + 3 :]
    rows = keyvals[0].shape[1]
    seq, tile = pl.program_id(0), pl.program_id(1)

    @pl.when(tile == 0)
    def _():
        low = low_lanes((rows, LANES))
        for j in range(blocks):
            whole = keyvals[j][0].astype(F32)
            turned = swap_halves(whole)
            place = pl.ds(j * rows, rows)
            key_even[place, :] = jnp.where(low, whole, 0.0).astype(BF16)
            key_odd[place, :] = jnp.where(low, 0.0, turned).astype(BF16)
            value_even[place, 0:LANES] = jnp.where(low, turned, 0.0).astype(BF16)
            value_even[place, LANES:] = jnp.where(low, 1.0, 0.0).astype(BF16)
            value_odd[place, 0:LANES] = jnp.where(low, 0.0, whole).astype(BF16)
            value_odd[place, LANES:] = jnp.where(low, 0.0, 1.0).astype(BF16)

    row_begin = (blocks - 1) * rows + tile * tile_rows
    first, last = first_ref[seq, tile], last_ref[seq, tile]
    begin = first // tile_keys
    end = (row_begin + tile_rows - 1) // tile_keys + 1
    stacked = stacked_pairs(queries)
    most[...] = jnp.full_like(most, -3e38)

    def score_step(index, carried):
        key_begin = pl.multiple_of(index * tile_keys, tile_keys)
        place = pl.ds(key_begin, tile_keys)
        both = jnp.concatenate([key_even[place, :], key_odd[place, :]], axis=0)
        scores = dot_nt(stacked, both)
        whole = (key_begin >= last) & (key_begin + tile_keys - 1 <= row_begin)

        def keep(values):
            score_scratch[index - begin] = values
            half = []
            for h in range(2):
                part = values[:, h * tile_keys : h * tile_keys + LANES]
                for q in range(1, tile_keys // LANES):
                    at = h * tile_keys + q * LANES
                    part = jnp.maximum(part, values[:, at : at + LANES])
                half.append(part)
            most[...] = jnp.maximum(most[...], jnp.concatenate(half, axis=1))

        @pl.when(whole)
        def _():
            keep(scores)

        @pl.when(jnp.logical_not(whole))
        def _():
            keep(
                scores
                + tile_bias(starts[0], key_begin, row_begin, tile_rows, tile_keys)
            )

        return carried

    lax.fori_loop(begin, end, score_step, 0)
    stack = PAIRS * tile_rows
    for h in range(2):
        part = jnp.max(most[:, h * LANES : (h + 1) * LANES], axis=1, keepdims=True)
        most[:, h * LANES : (h + 1) * LANES] = jnp.broadcast_to(part, (stack, LANES))
    total[...] = jnp.zeros_like(total)

    def output_step(index, carried):
        place = pl.ds(pl.multiple_of(index * tile_keys, tile_keys), tile_keys)
        both = jnp.concatenate([value_even[place, :], value_odd[place, :]], axis=0)
        shift = jnp.concatenate(
            [most[:, 0:LANES]] * (tile_keys // LANES) + [most[:, LANES:]] * (tile_keys // LANES),
            axis=1,
        )
        powers = jnp.exp2((score_scratch[index - begin] - shift) * SCALE).astype(BF16)
        total[...] += dot_nn(powers, both)
        return carried

    lax.fori_loop(begin, end, output_step, 0)
    low = low_lanes((tile_rows, LANES))
    for p in range(PAIRS):
        at = pl.ds(p * tile_rows, tile_rows)
        lanes = slice(p * LANES, (p + 1) * LANES)
        sums = total[at, LANES:]
        out = total[at, 0:LANES] / sums
        exact_out[0, :, lanes] = out
        rounded_out[0, :, lanes] = out.astype(BF16)
        shift = jnp.where(low, most[at, 0:LANES], most[at, LANES:])
        logs_out[0, :, lanes] = shift * SCALE + jnp.log2(sums)


def attend_back_kernel(
    first_ref, last_ref, queries, starts, exact, logs, grads, *rest, blocks, tile_rows, tile_keys
):
    keyvals = rest[:blocks]
    grad_queries = rest[blocks]
    terms = rest[blocks + 1 : 2 * blocks + 1]
    (
        key_even, key_odd, value_even, value_odd,
        key_total, value_total, query_total,
        log_even, log_odd, delta_even, delta_odd,
    ) = rest[2 * blocks + 1 :]
    rows = keyvals[0].shape[1]
    seq, tile = pl.program_id(0), pl.program_id(1)

    @pl.when(tile == 0)
    def _():
        low = low_lanes((rows, LANES))
        for j in range(blocks):
            whole = keyvals[j][0].astype(F32)
            turned = swap_halves(whole)
            place = pl.ds(j * rows, rows)
            key_even[place, :] = jnp.where(low, whole, 0.0).astype(BF16)
            key_odd[place, :] = jnp.where(low, 0.0, turned).astype(BF16)
            value_even[place, :] = jnp.where(low, turned, 0.0).astype(BF16)
            value_odd[place, :] = jnp.where(low, 0.0, whole).astype(BF16)
        key_total[...] = jnp.zeros_like(key_total)
        value_total[...] = jnp.zeros_like(value_total)

    row_begin = (blocks - 1) * rows + tile * tile_rows
    first, last = first_ref[seq, tile], last_ref[seq, tile]
    begin = first // tile_keys
    end = (row_begin + tile_rows - 1) // tile_keys + 1
    stacked = stacked_pairs(queries)
    grad_stacked = stacked_pairs(grads)
    stacked_turned = stacked.T
    grad_turned = grad_stacked.T
    stack = PAIRS * tile_rows
    low = low_lanes((tile_rows, LANES))
    for p in range(PAIRS):
        at = pl.ds(p * tile_rows, tile_rows)
        lanes = slice(p * LANES, (p + 1) * LANES)
        log = logs[0, :, lanes]
        log_turned = swap_halves(log)
        log_even[at, :] = jnp.where(low, log, log_turned)
        log_odd[at, :] = jnp.where(low, log_turned, log)
        terms_here = exact[0, :, lanes] * grads[0, :, lanes].astype(F32)
        even = jnp.sum(jnp.where(low, terms_here, 0.0), axis=1, keepdims=True)
        odd = jnp.sum(jnp.where(low, 0.0, terms_here), axis=1, keepdims=True)
        delta_even[at, :] = jnp.broadcast_to(even, (tile_rows, LANES))
        delta_odd[at, :] = jnp.broadcast_to(odd, (tile_rows, LANES))
    query_total[...] = jnp.zeros_like(query_total)

    def step(index, carried):
        key_begin = pl.multiple_of(index * tile_keys, tile_keys)
        place = pl.ds(key_begin, tile_keys)
        keys = jnp.concatenate([key_even[place, :], key_odd[place, :]], axis=0)
        values = jnp.concatenate([value_even[place, :], value_odd[place, :]], axis=0)
        scores = dot_nt(stacked, keys)
        copies = tile_keys // LANES
        whole = (key_begin >= last) & (key_begin + tile_keys - 1 <= row_begin)
        log = jnp.concatenate([log_even[...]] * copies + [log_odd[...]] * copies, axis=1)
        delta = jnp.concatenate([delta_even[...]] * copies + [delta_odd[...]] * copies, axis=1)

        def update(scores):
            chances = jnp.exp2(scores * SCALE - log)
            grad_probs = dot_nt(grad_stacked, values)
            grad_scores = (chances * (grad_probs - delta)).astype(BF16)
            query_total[...] += dot_nn(grad_scores, keys)
            key_total[index] += dot_nn(stacked_turned, grad_scores)
            value_total[index] += dot_nn(grad_turned, chances.astype(BF16))

        @pl.when(whole)
        def _():
            update(scores)

        @pl.when(jnp.logical_not(whole))
        def _():
            update(
                scores
                + tile_bias(starts[0], key_begin, row_begin, tile_rows, tile_keys)
            )

        return carried

    lax.fori_loop(begin, end, step, 0)
    root = 1.0 / HEAD_DIM**0.5
    for p in range(PAIRS):
        at = pl.ds(p * tile_rows, tile_rows)
        lanes = slice(p * LANES, (p + 1) * LANES)
        grad_queries[0, :, lanes] = (query_total[at, :] * root).astype(BF16)

    @pl.when(tile == pl.num_programs(1) - 1)
    def _():
        per_block = rows // tile_keys
        for j in range(blocks):
            for i in range(per_block):
                index = j * per_block + i
                key = key_total[index]
                value = value_total[index]
                key = key[0:HEAD_DIM, 0:tile_keys] + key[HEAD_DIM:, tile_keys:]
                value = value[0:HEAD_DIM, 0:tile_keys] + value[HEAD_DIM:, tile_keys:]
                both = jnp.concatenate([key * root, value], axis=0)
                terms[j][0, i * tile_keys : (i + 1) * tile_keys, :] = both.T.astype(BF16)


def attention_sizes(rows, blocks):
    tile_rows = 128 if rows % 128 == 0 else rows
    tile_keys = 256 if rows % 256 == 0 else 128
    return tile_rows, tile_keys, blocks * rows // tile_keys


def attend(firsts, lasts, queries, starts, keyvals):
    seqs, rows, width = queries.shape
    blocks = len(keyvals)
    tile_rows, tile_keys, key_tiles = attention_sizes(rows, blocks)
    stack = PAIRS * tile_rows
    keys = blocks * rows
    row_spec = lambda lanes: pl.BlockSpec((1, tile_rows, lanes), lambda s, t, *_: (s, t, 0))
    key_spec = pl.BlockSpec((1, rows, LANES), lambda s, t, *_: (s, 0, 0))
    return pl.pallas_call(
        functools.partial(
            attend_kernel, blocks=blocks, tile_rows=tile_rows, tile_keys=tile_keys
        ),
        grid_spec=pltpu.PrefetchScalarGridSpec(
            num_scalar_prefetch=2,
            grid=(seqs, rows // tile_rows),
            in_specs=[row_spec(width), row_spec(LANES)] + [key_spec] * blocks,
            out_specs=[row_spec(width)] * 3,
            scratch_shapes=[
                pltpu.VMEM((keys, LANES), BF16),
                pltpu.VMEM((keys, LANES), BF16),
                pltpu.VMEM((keys, 2 * LANES), BF16),
                pltpu.VMEM((keys, 2 * LANES), BF16),
                pltpu.VMEM((key_tiles, stack, 2 * tile_keys), F32),
                pltpu.VMEM((stack, 2 * LANES), F32),
                pltpu.VMEM((stack, 2 * LANES), F32),
            ],
        ),
        out_shape=[
            jax.ShapeDtypeStruct((seqs, rows, width), F32),
            jax.ShapeDtypeStruct((seqs, rows, width), BF16),
            jax.ShapeDtypeStruct((seqs, rows, width), F32),
        ],
        compiler_params=params("arbitrary", "arbitrary"),
        cost_estimate=cost(16 * seqs * rows * keys * width, 12 * seqs * rows * width),
        name="attend",
    )(firsts, lasts, queries, starts, *keyvals)


def attend_back(firsts, lasts, queries, starts, exact, logs, grads, keyvals):
    seqs, rows, width = queries.shape
    blocks = len(keyvals)
    tile_rows, tile_keys, key_tiles = attention_sizes(rows, blocks)
    stack = PAIRS * tile_rows
    keys = blocks * rows
    row_spec = lambda lanes: pl.BlockSpec((1, tile_rows, lanes), lambda s, t, *_: (s, t, 0))
    key_spec = pl.BlockSpec((1, rows, LANES), lambda s, t, *_: (s, 0, 0))
    return pl.pallas_call(
        functools.partial(
            attend_back_kernel, blocks=blocks, tile_rows=tile_rows, tile_keys=tile_keys
        ),
        grid_spec=pltpu.PrefetchScalarGridSpec(
            num_scalar_prefetch=2,
            grid=(seqs, rows // tile_rows),
            in_specs=[row_spec(width), row_spec(LANES)]
            + [row_spec(width)] * 3
            + [key_spec] * blocks,
            out_specs=[row_spec(width)] + [key_spec] * blocks,
            scratch_shapes=[pltpu.VMEM((keys, LANES), BF16)] * 4
            + [pltpu.VMEM((key_tiles, LANES, 2 * tile_keys), F32)] * 2
            + [pltpu.VMEM((stack, LANES), F32)] * 5,
        ),
        out_shape=[jax.ShapeDtypeStruct((seqs, rows, width), BF16)]
        + [jax.ShapeDtypeStruct((seqs, rows, LANES), BF16)] * blocks,
        compiler_params=params("arbitrary", "arbitrary"),
        cost_estimate=cost(40 * seqs * rows * keys * width, 12 * seqs * rows * width),
        name="attend_back",
    )(firsts, lasts, queries, starts, exact, logs, grads, *keyvals)


def mix_kernel(spot_ref, attended, tokens, gain, *rest, pieces):
    weights = rest[:pieces]
    hidden_out, scaled_out, weight = rest[pieces:]
    place_rows(spot_ref[0], weights, weight)

    def run(rows):
        mixed = dot_nn(attended[rows, :], weight[...])
        hidden = tokens[rows, :].astype(F32) + mixed
        hidden_out[rows, :] = hidden
        normed, unused = normalize(hidden)
        scaled_out[rows, :] = (normed * gain[...]).astype(BF16)

    over_rows(tokens.shape[0], run)


def mix_stage(spot, attended, tokens, gain, weights):
    rows, width = tokens.shape
    return pl.pallas_call(
        functools.partial(mix_kernel, pieces=len(weights)),
        grid_spec=pltpu.PrefetchScalarGridSpec(
            num_scalar_prefetch=1,
            grid=(),
            in_specs=[pl.BlockSpec(memory_space=pltpu.VMEM)] * (3 + len(weights)),
            out_specs=[pl.BlockSpec(memory_space=pltpu.VMEM)] * 2,
            scratch_shapes=[pltpu.VMEM(attended.shape[1:] + (width,), BF16)],
        ),
        out_shape=[
            jax.ShapeDtypeStruct((rows, width), F32),
            jax.ShapeDtypeStruct((rows, width), BF16),
        ],
        compiler_params=params(),
        cost_estimate=cost(2 * rows * width * width, 8 * rows * width),
        name="mix",
    )(spot, attended, tokens, gain, *weights)


TILE = 256


def feed_kernel(spot_ref, scaled, cotangent, *rest, pieces, chunk, chunks):
    ups, downs = rest[:pieces], rest[pieces : 2 * pieces]
    rest = rest[2 * pieces :]
    if chunk:
        reduced_in, grads_in = rest[:2]
        rest = rest[2:]
    reduced_out, grads_out = rest[:2]
    keep_out, send_out = rest[2:4]
    up_tile, down_tile, up_sems, down_sems, up_term = rest[4:]
    spot = spot_ref[0]
    step = pl.program_id(0)
    width = scaled.shape[1]
    height = width // pieces
    groups = width // TILE

    def up_copy(s, r):
        column = pl.multiple_of(((spot ^ s) * chunks + chunk) * TILE, TILE)
        row = pl.multiple_of((spot ^ r) * height, height)
        return pltpu.make_async_copy(
            ups[r].at[:, pl.ds(column, TILE)],
            up_tile.at[s, pl.ds(row, height), :],
            up_sems.at[s, r],
        )

    def down_copy(s):
        return pltpu.make_async_copy(
            downs[s].at[pl.ds(chunk * TILE, TILE), :], down_tile.at[s], down_sems.at[s]
        )

    @pl.when(step == 0)
    def _():
        for s in range(pieces):
            for r in range(pieces):
                up_copy(s, r).start()
            down_copy(s).start()
        if chunk:
            reduced_out[...] = reduced_in[...]
            grads_out[...] = grads_in[...]
        else:
            reduced_out[...] = jnp.zeros_like(reduced_out)
            grads_out[...] = jnp.zeros_like(grads_out)

    for s in range(pieces):

        @pl.when(step == s)
        def _():
            for r in range(pieces):
                up_copy(s, r).wait()
            down_copy(s).wait()

    up = up_tile[step]
    down = down_tile[step]
    upper = dot_nn(scaled[...], up)
    grad_act = dot_nt(cotangent[...], down)
    square = upper * upper
    inner = jnp.tanh(GELU_ROOT * (upper + GELU_CUBE * upper * square))
    half = 0.5 * (1.0 + inner)
    slope = half + 0.5 * upper * (1.0 - inner * inner) * (
        GELU_ROOT * (1.0 + 3.0 * GELU_CUBE * square)
    )
    active = (upper * half).astype(BF16)
    grad_upper = (grad_act * slope).astype(BF16)
    reduced_out[...] += dot_nn(active, down)
    grads_out[...] += dot_nt(grad_upper, up)
    down_term = dot_tn(active, cotangent[...]).astype(BF16)
    up_term[...] = dot_tn(scaled[...], grad_upper)

    def place(s):
        return (keep_out if (s & 1) == 0 else send_out), s >> 1

    for s in range(pieces):

        @pl.when(step == s)
        def _():
            out, at = place(s)
            for g in range(groups):
                out[at, g * TILE : (g + 1) * TILE, :] = down_term[
                    :, g * TILE : (g + 1) * TILE
                ]

    row = pl.multiple_of(groups * TILE + (spot ^ step) * height, height)
    for s in range(pieces):
        out, at = place(s)
        begin = pl.multiple_of((spot ^ s) * height, height)
        out[at, pl.ds(row, height), :] = up_term[pl.ds(begin, height), :].astype(BF16)


def feed_stage(spot, scaled, cotangent, ups, downs, totals, chunk, chunks):
    rows, width = scaled.shape
    pieces = len(ups)
    height = width // pieces
    tall = width + pieces * height
    whole = pl.BlockSpec((rows, width), lambda i, *_: (0, 0))
    message = pl.BlockSpec((pieces // 2, tall, TILE), lambda i, *_: (0, 0, 0))
    message_shape = jax.ShapeDtypeStruct((pieces // 2, tall, TILE), BF16)
    count = 3 + 2 * pieces
    return pl.pallas_call(
        functools.partial(feed_kernel, pieces=pieces, chunk=chunk, chunks=chunks),
        grid_spec=pltpu.PrefetchScalarGridSpec(
            num_scalar_prefetch=1,
            grid=(pieces,),
            in_specs=[whole] * 2
            + [pl.BlockSpec(memory_space=pl.ANY)] * (2 * pieces)
            + [whole] * len(totals),
            out_specs=[whole] * 2 + [message] * 2,
            scratch_shapes=[
                pltpu.VMEM((pieces, width, TILE), BF16),
                pltpu.VMEM((pieces, TILE, width), BF16),
                pltpu.SemaphoreType.DMA((pieces, pieces)),
                pltpu.SemaphoreType.DMA((pieces,)),
                pltpu.VMEM((width, TILE), F32),
            ],
        ),
        out_shape=[jax.ShapeDtypeStruct((rows, width), F32)] * 2 + [message_shape] * 2,
        input_output_aliases={count: 0, count + 1: 1} if totals else {},
        compiler_params=params("arbitrary"),
        cost_estimate=cost(
            12 * rows * width * TILE * pieces, 12 * rows * width + 8 * tall * TILE * pieces
        ),
        name="feed",
    )(spot, scaled, cotangent, *ups, *downs, *totals)


def split_out(spot, pieces, source, keep_out, send_out, lanes):
    height = source.shape[0] // pieces
    for s in range(pieces):
        out = keep_out if (s & 1) == 0 else send_out
        begin = pl.multiple_of((spot ^ s) * height, height)
        out[s >> 1, :, lanes] = source[pl.ds(begin, height), :].astype(BF16)


def put_vector(pieces, vector, keep_out, send_out, begin):
    height = keep_out.shape[1]
    count = vector.shape[1] // LANES
    row = lax.broadcasted_iota(jnp.int32, (height, LANES), 0)
    block = jnp.zeros((height, LANES), F32)
    for i in range(count):
        block = jnp.where(row == i, vector[:, i * LANES : (i + 1) * LANES], block)
    for s in range(pieces):
        out = keep_out if (s & 1) == 0 else send_out
        out[s >> 1, :, begin : begin + LANES] = block.astype(BF16)


def after_kernel(spot_ref, hidden, reduced, grads, gain, cotangent, attended, *rest, pieces):
    weights = rest[:pieces]
    layer_out, grad_hidden_out, grad_attended_out, keep_out, send_out = rest[pieces : pieces + 5]
    weight, grad_mixed, sums, term = rest[pieces + 5 :]
    spot = spot_ref[0]
    width = hidden.shape[1]
    place_rows(spot, weights, weight)
    sums[...] = jnp.zeros_like(sums)

    def run(rows):
        values = hidden[rows, :]
        layer_out[rows, :] = (values + reduced[rows, :]).astype(BF16)
        normed, inverse = normalize(values)
        grad = grads[rows, :]
        sums[...] += jnp.sum((grad * normed).reshape(STEP // 8, 8, width), axis=0)
        grad_hidden = cotangent[rows, :].astype(F32) + norm_back(
            grad * gain[...], normed, inverse
        )
        grad_hidden_out[rows, :] = grad_hidden
        rounded = grad_hidden.astype(BF16)
        grad_mixed[rows, :] = rounded
        grad_attended_out[rows, :] = dot_nt(rounded, weight[...]).astype(BF16)

    over_rows(hidden.shape[0], run)
    term[...] = dot_tn(attended[...], grad_mixed[...])
    split_out(spot, pieces, term, keep_out, send_out, slice(0, width))
    put_vector(
        pieces, jnp.sum(sums[...], axis=0, keepdims=True), keep_out, send_out, width
    )


def after_stage(spot, hidden, reduced, grads, gain, cotangent, attended, weights):
    rows, width = hidden.shape
    pieces = len(weights)
    message = jax.ShapeDtypeStruct((pieces // 2, width // pieces, width + LANES), BF16)
    return pl.pallas_call(
        functools.partial(after_kernel, pieces=pieces),
        grid_spec=pltpu.PrefetchScalarGridSpec(
            num_scalar_prefetch=1,
            grid=(),
            in_specs=[pl.BlockSpec(memory_space=pltpu.VMEM)] * (6 + pieces),
            out_specs=[pl.BlockSpec(memory_space=pltpu.VMEM)] * 5,
            scratch_shapes=[
                pltpu.VMEM((width, width), BF16),
                pltpu.VMEM((rows, width), BF16),
                pltpu.VMEM((8, width), F32),
                pltpu.VMEM((width, width), F32),
            ],
        ),
        out_shape=[
            jax.ShapeDtypeStruct((rows, width), BF16),
            jax.ShapeDtypeStruct((rows, width), F32),
            jax.ShapeDtypeStruct((rows, width), BF16),
            message,
            message,
        ],
        compiler_params=params(),
        cost_estimate=cost(4 * rows * width * width, 24 * rows * width),
        name="after",
    )(spot, hidden, reduced, grads, gain, cotangent, attended, *weights)


def query_kernel(spot_ref, scaled, grad_queries, *rest, pieces):
    weights = rest[:pieces]
    grad_out, keep_out, send_out, weight, term = rest[pieces:]
    spot = spot_ref[0]
    width = scaled.shape[1]
    term[...] = dot_tn(scaled[...], grad_queries[...])
    split_out(spot, pieces, term, keep_out, send_out, slice(0, width))
    place_rows(spot, weights, weight)
    grad_out[...] = dot_nt(grad_queries[...], weight[...])


def query_stage(spot, scaled, grad_queries, weights):
    rows, width = scaled.shape
    pieces = len(weights)
    message = jax.ShapeDtypeStruct((pieces // 2, width // pieces, width), BF16)
    return pl.pallas_call(
        functools.partial(query_kernel, pieces=pieces),
        grid_spec=pltpu.PrefetchScalarGridSpec(
            num_scalar_prefetch=1,
            grid=(),
            in_specs=[pl.BlockSpec(memory_space=pltpu.VMEM)] * (2 + pieces),
            out_specs=[pl.BlockSpec(memory_space=pltpu.VMEM)] * 3,
            scratch_shapes=[
                pltpu.VMEM((width, width), BF16),
                pltpu.VMEM((width, width), F32),
            ],
        ),
        out_shape=[jax.ShapeDtypeStruct((rows, width), F32), message, message],
        compiler_params=params(),
        cost_estimate=cost(4 * rows * width * width, 12 * rows * width),
        name="query_grad",
    )(spot, scaled, grad_queries, *weights)


def last_kernel(spot_ref, tokens, gain, scaled, grad_shared, grad_scaled, grad_hidden, *rest, pieces):
    weights = rest[:pieces]
    input_grad, keep_out, send_out, weight, sums, term = rest[pieces:]
    spot = spot_ref[0]
    width = tokens.shape[1]
    place_rows(spot, weights, weight)
    sums[...] = jnp.zeros_like(sums)
    term[...] = dot_tn(scaled[...], grad_shared[...])
    split_out(spot, pieces, term, keep_out, send_out, slice(0, LANES))

    def run(rows):
        normed, inverse = normalize(tokens[rows, :].astype(F32))
        grad = grad_scaled[rows, :] + dot_nt(grad_shared[rows, :], weight[...])
        sums[...] += jnp.sum((grad * normed).reshape(STEP // 8, 8, width), axis=0)
        input_grad[rows, :] = grad_hidden[rows, :] + norm_back(
            grad * gain[...], normed, inverse
        )

    over_rows(tokens.shape[0], run)
    put_vector(
        pieces, jnp.sum(sums[...], axis=0, keepdims=True), keep_out, send_out, LANES
    )


def last_stage(spot, tokens, gain, scaled, grad_shared, grad_scaled, grad_hidden, weights):
    rows, width = tokens.shape
    pieces = len(weights)
    message = jax.ShapeDtypeStruct((pieces // 2, width // pieces, 2 * LANES), BF16)
    return pl.pallas_call(
        functools.partial(last_kernel, pieces=pieces),
        grid_spec=pltpu.PrefetchScalarGridSpec(
            num_scalar_prefetch=1,
            grid=(),
            in_specs=[pl.BlockSpec(memory_space=pltpu.VMEM)] * (6 + pieces),
            out_specs=[pl.BlockSpec(memory_space=pltpu.VMEM)] * 3,
            scratch_shapes=[
                pltpu.VMEM((width, LANES), BF16),
                pltpu.VMEM((8, width), F32),
                pltpu.VMEM((width, LANES), F32),
            ],
        ),
        out_shape=[jax.ShapeDtypeStruct((rows, width), F32), message, message],
        compiler_params=params(),
        cost_estimate=cost(4 * rows * width * LANES, 20 * rows * width),
        name="last",
    )(spot, tokens, gain, scaled, grad_shared, grad_scaled, grad_hidden, *weights)


def swap(values, axis, size, mask):
    return lax.ppermute(values, axis, [(i, i ^ mask) for i in range(size)])


def gather_pieces(piece, size):
    found = [piece]
    order = [0]
    mask = size // 2
    while mask:
        found = found + [swap(one, "wt", size, mask) for one in found]
        order = order + [r ^ mask for r in order]
        mask //= 2
    placed = [None] * size
    for r, one in zip(order, found):
        placed[r] = one
    return placed


def own_order(values, spot, size):
    mask = 1
    while mask < size:
        split = values.reshape((size // (2 * mask), 2, mask) + values.shape[1:])
        split = jnp.where((spot & mask) != 0, split[:, ::-1], split)
        values = split.reshape(values.shape)
        mask *= 2
    return values


def reduce_all(keep, send, place, sizes):
    wt_size, ctx_size = sizes
    half = swap(send, "wt", wt_size, 1)
    mask = wt_size // 2
    total = keep.astype(F32) + half.astype(F32)
    while mask > 1:
        count = total.shape[0] // 2
        sent = swap(total[count:].astype(BF16), "wt", wt_size, mask)
        total = total[:count] + sent.astype(F32)
        mask //= 2
    total = total[0]
    rows, lanes = total.shape
    total = total.reshape(2, rows // 2, lanes)
    low = place & 1
    sent = swap(
        lax.dynamic_index_in_dim(total, 1 - low, 0, False).astype(BF16), "ctx", ctx_size, 1
    )
    total = lax.dynamic_index_in_dim(total, low, 0, False) + sent.astype(F32)
    groups = ctx_size // 2
    high = place >> 1
    total = total.reshape(groups, rows // ctx_size, lanes)
    rounded = total.astype(BF16)
    result = lax.dynamic_index_in_dim(total, high, 0, False)
    for k in range(1, groups):
        sent = swap(
            lax.dynamic_index_in_dim(rounded, high ^ k, 0, False), "ctx", ctx_size, 2 * k
        )
        result = result + sent.astype(F32)
    result = result.astype(BF16)
    whole = jnp.zeros((groups,) + result.shape, BF16)
    whole = lax.dynamic_update_index_in_dim(whole, result, high, 0)
    for k in range(1, groups):
        whole = lax.dynamic_update_index_in_dim(
            whole, swap(result, "ctx", ctx_size, 2 * k), high ^ k, 0
        )
    other = swap(whole, "ctx", ctx_size, 1)
    both = jnp.where(low == 0, jnp.stack([whole, other]), jnp.stack([other, whole]))
    return both.reshape(rows, lanes).astype(F32)


def shift(values, size, k):
    pairs = [(i, i + k) for i in range(size - k)] if k > 0 else [(i, i + k) for i in range(-k, size)]
    return lax.ppermute(values, "ctx", pairs)


def body(
    tokens,
    documents,
    first_gain,
    query_weight,
    shared_weight,
    mixing_weight,
    second_gain,
    up_weight,
    down_weight,
    cotangent,
    *,
    wt_size,
    ctx_size,
):
    sizes = (wt_size, ctx_size)
    seqs, rows, width = tokens.shape
    count = seqs * rows
    spot_index = lax.axis_index("wt")
    place = lax.axis_index("ctx")
    spot = spot_index.astype(jnp.int32).reshape(1)
    length = ctx_size * rows
    doc_most = length * 5 // 8
    before = min(ctx_size - 1, -(-(doc_most - 1) // rows))
    blocks = before + 1
    height = width // wt_size

    gain_rows = -(-height // LANES)
    pad = lambda gain: jnp.pad(gain, (0, gain_rows * LANES - height)).reshape(gain_rows, LANES)
    small = jnp.concatenate([shared_weight, pad(first_gain), pad(second_gain)], axis=0)
    small = jnp.pad(small, ((0, -small.shape[0] % 16), (0, 0)))
    small_pieces = gather_pieces(small, wt_size)
    query_pieces = gather_pieces(query_weight, wt_size)
    mixing_pieces = gather_pieces(mixing_weight, wt_size)
    up_pieces = gather_pieces(up_weight, wt_size)
    down_pieces = gather_pieces(down_weight, wt_size)

    gains = jnp.stack([one[height : height + 2 * gain_rows] for one in small_pieces])
    gains = gains.reshape(wt_size, 2, gain_rows * LANES)[:, :, :height].astype(F32)
    gains = own_order(gains, spot_index, wt_size)
    gain_one = gains[:, 0].reshape(1, width)
    gain_two = gains[:, 1].reshape(1, width)

    window = [
        jnp.where(place >= k, shift(documents, ctx_size, k), -1) if k else documents
        for k in range(before, -1, -1)
    ]
    window = jnp.concatenate(window, axis=1)
    starts = jnp.sum(
        (window[:, None, :] < documents[:, :, None]).astype(jnp.int32), axis=-1
    )
    tile_rows = attention_sizes(rows, blocks)[0]
    firsts = starts[:, ::tile_rows]
    lasts = starts[:, tile_rows - 1 :: tile_rows]
    starts = jnp.broadcast_to(starts[:, :, None], (seqs, rows, LANES))

    inputs = tokens.reshape(count, width)
    scaled_one, shared = first_stage(spot, inputs, gain_one, small_pieces)
    shared = shared.reshape(seqs, rows, 2 * HEAD_DIM)
    keyvals = [shift(shared, ctx_size, k) for k in range(before, 0, -1)] + [shared]
    queries = project(spot, scaled_one, query_pieces).reshape(seqs, rows, width)

    exact, attended, logs = attend(firsts, lasts, queries, starts, keyvals)
    attended = attended.reshape(count, width)
    hidden, scaled_two = mix_stage(spot, attended, inputs, gain_two, mixing_pieces)

    grads_in = cotangent.reshape(count, width)
    chunks = up_weight.shape[1] // wt_size // TILE
    totals = ()
    messages = []
    for chunk in range(chunks):
        reduced, grads, keep, send = feed_stage(
            spot, scaled_two, grads_in, up_pieces, down_pieces, totals, chunk, chunks
        )
        totals = (reduced, grads)
        messages.append((keep, send))
    layer_out, grad_hidden, grad_attended, keep, send = after_stage(
        spot, hidden, reduced, grads, gain_two, grads_in, attended, mixing_pieces
    )
    feed_sums = [reduce_all(*message, place, sizes) for message in messages]
    mixing_sum = reduce_all(keep, send, place, sizes)

    grad_queries, *terms = attend_back(
        firsts,
        lasts,
        queries,
        starts,
        exact,
        logs,
        grad_attended.reshape(seqs, rows, width),
        keyvals,
    )
    grad_shared = terms[-1].astype(F32)
    for k in range(1, before + 1):
        grad_shared = grad_shared + shift(terms[before - k], ctx_size, -k).astype(F32)
    grad_shared = grad_shared.astype(BF16).reshape(count, 2 * HEAD_DIM)
    grad_scaled, keep, send = query_stage(
        spot, scaled_one, grad_queries.reshape(count, width), query_pieces
    )
    query_sum = reduce_all(keep, send, place, sizes)
    input_grad, keep, send = last_stage(
        spot, inputs, gain_one, scaled_one, grad_shared, grad_scaled, grad_hidden, small_pieces
    )
    shared_sum = reduce_all(keep, send, place, sizes)

    def own_gain(columns):
        vector = columns[: width // LANES].reshape(width)
        return lax.dynamic_slice_in_dim(vector, spot_index * height, height, 0)

    down_grad = jnp.stack(
        [one[:width].reshape(width // TILE, TILE, TILE).transpose(1, 0, 2) for one in feed_sums]
    ).reshape(chunks * TILE, width)
    up_grad = jnp.stack(
        [one[width:].reshape(wt_size, height, TILE).transpose(1, 0, 2) for one in feed_sums], axis=2
    ).reshape(height, wt_size * chunks * TILE)
    return (
        layer_out.reshape(seqs, rows, width),
        input_grad.reshape(seqs, rows, width),
        own_gain(shared_sum[:, LANES:]),
        query_sum,
        shared_sum[:, :LANES],
        mixing_sum[:, :width],
        own_gain(mixing_sum[:, width:]),
        up_grad,
        down_grad,
    )


def solution(mesh):
    in_specs = (
        P("wt", "ctx", None),
        P("wt", "ctx"),
        P("wt"),
        P("wt", None),
        P("wt", None),
        P("wt", None),
        P("wt"),
        P("wt", None),
        P("wt", None),
        P("wt", "ctx", None),
    )
    out_specs = (
        P("wt", "ctx", None),
        P("wt", "ctx", None),
        P("wt"),
        P("wt", None),
        P("wt", None),
        P("wt", None),
        P("wt"),
        P("wt", None),
        P("wt", None),
    )
    run = functools.partial(body, wt_size=mesh.shape["wt"], ctx_size=mesh.shape["ctx"])
    return jax.shard_map(run, mesh=mesh, in_specs=in_specs, out_specs=out_specs, check_vma=False)
```

time: 968 us -> 438 us (0.45)
  waiting for transfers between devices: 623 us -> 193 us
  starting transfers between devices: 0.74 us -> 122 us
  matrix products: 108 us -> 0 us
  Pallas kernels: 0 us -> 92.3 us
  local copies, waits for them, and re-layouts: 106 us -> 19.6 us
  blocking collectives: 69.9 us -> 0 us
  loops' own time: 32.6 us -> 0 us
  between operations: 16.3 us -> 1.89 us
    reduce_scatter x6 -> x0, waiting for transfers between devices: 446 us -> none  [the longest x1 209 us: body(): lax.psum_scatter(key_terms, 'ctx', scatter_dimension=1, tiled=True)]
    ppermute x0 -> x90, waiting for transfers between devices: none -> 193 us  [the longest x75 146 us: swap(): return lax.ppermute(values, axis, [(i, i ^ mask) for i in range(size)])]
    psum x1 -> x0, waiting for transfers between devices: 167 us -> none  [body(): lax.psum((owned_first, owned_query, owned_shared, owned_mixing, owned_sec...]
    ppermute x0 -> x90, starting transfers between devices: none -> 122 us  [the longest x75 84.7 us: swap(): return lax.ppermute(values, axis, [(i, i ^ mask) for i in range(size)])]
    dot_general x33 -> x0, matrix products: 108 us -> none  [the longest x5 23.7 us: contract_rows(): lax.dot_general(operand, matrix, (((0,), (0,)), ((), ())), preferred_elem...]
    pallas_call x0 -> x11, Pallas kernels: none -> 92.3 us  [the longest x3 40.2 us: feed_stage(): pl.pallas_call(functools.partial(feed_kernel, pieces=pieces, chunk=chunk,...]
    dynamic_update_slice x12 -> x18, local copies, waits for them, and re-layouts: 39.5 us -> 0.16 us  [reduce_all(): lax.dynamic_update_index_in_dim(whole, swap(result, 'ctx', ctx_size, 2 *...]
    another operation x32 -> x0, loops' own time: 32.6 us -> none  [the longest x2 10.5 us: attend_forward(): lax.fori_loop(0, block_count, output_step, (empty_out, empty_out))]
  transfers between devices with their start and end apart: 12 -> 90, of which waited for: 8 -> 43; matrix products, arithmetic and copies ran while one was open for 15% -> 3% of each run, Pallas kernels for 0% -> 6%
where the time goes in v1:
time: 438 us; the launch traced here: 436 us
  waiting for transfers between devices  193 us (44%)
  starting transfers between devices  122 us (28%)
  Pallas kernels  92.3 us (21%)
  local copies, waits for them, and re-layouts  19.6 us (4%)
  other arithmetic  8.17 us (2%)
    ppermute x75, waiting for transfers between devices, swap(): return lax.ppermute(values, axis, [(i, i ^ mask) for i in range(size)])  146 us
    ppermute x75, starting transfers between devices, swap(): return lax.ppermute(values, axis, [(i, i ^ mask) for i in range(size)])  84.7 us
    ppermute x15, waiting for transfers between devices, shift(): return lax.ppermute(values, 'ctx', pairs)  46.1 us
    pallas_call x3, Pallas kernels, feed_stage(): pl.pallas_call(functools.partial(feed_kernel, pieces=pieces, chunk=chunk,...  40.2 us
    ppermute x15, starting transfers between devices, shift(): return lax.ppermute(values, 'ctx', pairs)  37 us
    pallas_call x1, Pallas kernels, attend_back(): pl.pallas_call(functools.partial(attend_back_kernel, blocks=blocks, tile_...  12.1 us
    pallas_call x1, Pallas kernels, attend(): pl.pallas_call(functools.partial(attend_kernel, blocks=blocks, tile_rows=...  9.37 us
  transfers between devices with their start and end apart: 90, of which 43 were waited for; matrix products, arithmetic and copies ran while one was open for 3% of the time, Pallas kernels for 6%

profile of v1, /device:TPU:0, one launch (start us, length us, event | category | flops | bytes accessed | tf_op | source)
XLA Modules:
  0.0 436.2 jit_solution(11379092512060433547)
XLA Ops:
  2.1 3.0 collective-permute-start.6
  5.2 5.4 %collective-permute-start = (s32[2,256]{1,0:T(2,128)}, s32[2,256]{1,0:T(2,128)S(1)}, u32[]{:S(2)}, u32[]{:S(2)}) collective-permute-start(s32[2,256]{1,0:T(2,128)} %param.11), channel_id=1, source_target_pairs={{0,20},{4,24},{8,28},{1,21},{5,25},{9,29},{2,22},{6,26},{10,30},{3... | collective-permute-start | bytes 6152 | tf_op jit(solution)/shard_map/ppermute | solution.py:833
  11.9 3.5 collective-permute-start.2
  18.6 3.6 first_norm.1
  23.6 3.1 collective-permute-start.4
  28.9 3.2 collective-permute-start.12
  35.4 7.2 %collective-permute-start.14 = (bf16[2,256,128]{2,1,0:T(8,128)(2,1)}, bf16[2,256,128]{2,1,0:T(8,128)(2,1)S(1)}, u32[]{:S(2)}, u32[]{:S(2)}) collective-permute-start(bf16[2,256,128]{2,1,0:T(8,128)(2,1)} %bitcast.316), channel_id=1, source_target_pairs={{0,8},{4,12},{8,16},{12,20},{16,24},{20,28},{1,9},{5,13},{9,17},{1... | collective-permute-start | bytes 393224 | tf_op jit(solution)/shard_map/ppermute | solution.py:833
  42.6 2.8 collective-permute-start.15
  49.2 27.0 %collective-permute-done.9.rest_2_ = bf16[192,768]{1,0:T(8,128)(2,1)S(1)} collective-permute-done((bf16[192,768]{1,0:T(8,128)(2,1)}, bf16[192,768]{1,0:T(8,128)(2,1)S(1)}, u32[]{:S(2)}, u32[]{:S(2)}) %collective-permute-start.9) | collective-permute-done | bytes 294944 | tf_op jit(solution)/shard_map/ppermute | solution.py:764
  76.8 5.3 %collective-permute-done.17.rest_2_ = bf16[192,768]{1,0:T(8,128)(2,1)S(1)} collective-permute-done((bf16[192,768]{1,0:T(8,128)(2,1)}, bf16[192,768]{1,0:T(8,128)(2,1)S(1)}, u32[]{:S(2)}, u32[]{:S(2)}) %collective-permute-start.17) | collective-permute-done | bytes 294944 | tf_op jit(solution)/shard_map/ppermute | solution.py:764
  87.0 3.2 project.1
  91.1 9.4 %attend.1 = (f32[2,256,768]{2,1,0:T(8,128)}, bf16[2,256,768]{2,1,0:T(8,128)(2,1)}, f32[2,256,768]{2,1,0:T(8,128)}) custom-call(s32[2,2]{1,0:T(2,128)} %slice.109.first_ref, s32[2,2]{1,0:T(2,128)} %slice.110.last_ref, bf16[2,256,768]{2,1,0:T(8,128)(2,1)} %bitcast.292, s32[2,256,128]{2,1,0:T(8,128)} %broadcast_in_dim.102.starts, ...), custom_call_target="tpu_custom_call" | custom-call | flops 9663676416 | bytes 4718592 | tf_op jit(solution)/shard_map/attend/pallas_call | solution.py:376
  101.3 5.1 %mix.1 = (f32[512,768]{1,0:T(8,128)}, bf16[512,768]{1,0:T(8,128)(2,1)}) custom-call(s32[1]{0:T(128)} %bitcast.spot_ref, bf16[512,768]{1,0:T(8,128)(2,1)} %bitcast.271, bf16[512,768]{1,0:T(8,128)(2,1)} %bitcast.257, f32[1,768]{1,0:T(1,128)} %reshape_squeeze.25.gain, bf16[192,768]{1,0:T(8,128)(2,1)} %rest_0_.12, bf16[192,768]{1,0:T(8,128)(2,1)} %copy-done.4, ...), custom_call_target="tpu_custom_call" | custom-call | flops 603979776 | bytes 3145728 | tf_op jit(solution)/shard_map/mix/pallas_call | solution.py:454
  106.4 12.7 %feed.3 = (f32[512,768]{1,0:T(8,128)}, f32[512,768]{1,0:T(8,128)}, bf16[2,1536,256]{2,1,0:T(8,128)(2,1)}, bf16[2,1536,256]{2,1,0:T(8,128)(2,1)}) custom-call(s32[1]{0:T(128)} %bitcast.spot_ref, bf16[512,768]{1,0:T(8,128)(2,1)} %get-tuple-element.50.scaled, bf16[512,768]{1,0:T(8,128)(2,1)} %bitcast.288, bf16[192,3072]{1,0:T(8,128)(2,1)} %rest_0_.11, ...), custom_call_target="tpu_custom_call" | custom-call | flops 4831838208 | bytes 17301504 | tf_op jit(solution)/shard_map/feed/pallas_call | solution.py:572
  119.1 13.7 %feed.4 = (f32[512,768]{1,0:T(8,128)}, f32[512,768]{1,0:T(8,128)}, bf16[2,1536,256]{2,1,0:T(8,128)(2,1)}, bf16[2,1536,256]{2,1,0:T(8,128)(2,1)}) custom-call(s32[1]{0:T(128)} %bitcast.spot_ref, bf16[512,768]{1,0:T(8,128)(2,1)} %get-tuple-element.50.scaled, bf16[512,768]{1,0:T(8,128)(2,1)} %bitcast.289, ...), custom_call_target="tpu_custom_call", output_to_operand_aliasing={{0}: (11, {}), {1}: (12, {})} | custom-call | flops 4831838208 | bytes 17301504 | tf_op jit(solution)/shard_map/feed/pallas_call | solution.py:572
  132.9 13.8 %feed.5 = (f32[512,768]{1,0:T(8,128)}, f32[512,768]{1,0:T(8,128)}, bf16[2,1536,256]{2,1,0:T(8,128)(2,1)}, bf16[2,1536,256]{2,1,0:T(8,128)(2,1)}) custom-call(s32[1]{0:T(128)} %bitcast.spot_ref, bf16[512,768]{1,0:T(8,128)(2,1)} %get-tuple-element.50.scaled, bf16[512,768]{1,0:T(8,128)(2,1)} %bitcast.290, ...), custom_call_target="tpu_custom_call", output_to_operand_aliasing={{0}: (11, {}), {1}: (12, {})} | custom-call | flops 4831838208 | bytes 17301504 | tf_op jit(solution)/shard_map/feed/pallas_call | solution.py:572
  146.6 8.5 %after.1 = (bf16[512,768]{1,0:T(8,128)(2,1)}, f32[512,768]{1,0:T(8,128)}, bf16[512,768]{1,0:T(8,128)(2,1)}, bf16[2,192,896]{2,1,0:T(8,128)(2,1)}, bf16[2,192,896]{2,1,0:T(8,128)(2,1)}) custom-call(s32[1]{0:T(128)} %bitcast.spot_ref, f32[512,768]{1,0:T(8,128)} %get-tuple-element.49.hidden, f32[512,768]{1,0:T(8,128)} %get-tuple-element.55.reduced, ...), custom_call_target="tpu_custom_call" | custom-call | flops 1207959552 | bytes 9437184 | tf_op jit(solution)/shard_map/after/pallas_call | solution.py:654
  155.1 12.1 %attend_back.1 = (bf16[2,256,768]{2,1,0:T(8,128)(2,1)}, bf16[2,256,128]{2,1,0:T(8,128)(2,1)}, bf16[2,256,128]{2,1,0:T(8,128)(2,1)}, bf16[2,256,128]{2,1,0:T(8,12...) custom-call(s32[2,2]{1,0:T(2,128)} %slice.109.first_ref, ...), custom_call_target="tpu_custom_call" | custom-call | flops 24159191040 | bytes 4718592 | tf_op jit(solution)/shard_map/attend_back/pallas_call | solution.py:414
  173.8 4.4 %query_grad.1 = (f32[512,768]{1,0:T(8,128)}, bf16[2,192,768]{2,1,0:T(8,128)(2,1)}, bf16[2,192,768]{2,1,0:T(8,128)(2,1)}) custom-call(s32[1]{0:T(128)} %bitcast.spot_ref, bf16[512,768]{1,0:T(8,128)(2,1)} %get-tuple-element.46.operand.scaled, bf16[512,768]{1,0:T(8,128)(2,1)} %bitcast.320, bf16[192,768]{1,0:T(8,128)(2,1)} %rest_0_.13, ...), custom_call_target="tpu_custom_call" | custom-call | flops 1207959552 | bytes 4718592 | tf_op jit(solution)/shard_map/query_grad/pallas_call | solution.py:696
  180.6 6.3 %collective-permute-done.26 = bf16[2,256,128]{2,1,0:T(8,128)(2,1)S(1)} collective-permute-done((bf16[2,256,128]{2,1,0:T(8,128)(2,1)}, bf16[2,256,128]{2,1,0:T(8,128)(2,1)S(1)}, u32[]{:S(2)}, u32[]{:S(2)}) %collective-permute-start.26) | collective-permute-done | bytes 131104 | tf_op jit(solution)/shard_map/ppermute | solution.py:833
  186.9 11.3 %collective-permute-done.27 = bf16[2,256,128]{2,1,0:T(8,128)(2,1)S(1)} collective-permute-done((bf16[2,256,128]{2,1,0:T(8,128)(2,1)}, bf16[2,256,128]{2,1,0:T(8,128)(2,1)S(1)}, u32[]{:S(2)}, u32[]{:S(2)}) %collective-permute-start.27) | collective-permute-done | bytes 131104 | tf_op jit(solution)/shard_map/ppermute | solution.py:833
  198.2 13.7 %collective-permute-done.28 = bf16[2,256,128]{2,1,0:T(8,128)(2,1)S(1)} collective-permute-done((bf16[2,256,128]{2,1,0:T(8,128)(2,1)}, bf16[2,256,128]{2,1,0:T(8,128)(2,1)S(1)}, u32[]{:S(2)}, u32[]{:S(2)}) %collective-permute-start.28) | collective-permute-done | bytes 131104 | tf_op jit(solution)/shard_map/ppermute | solution.py:833
  211.9 7.8 %collective-permute-done.29 = bf16[2,256,128]{2,1,0:T(8,128)(2,1)S(1)} collective-permute-done((bf16[2,256,128]{2,1,0:T(8,128)(2,1)}, bf16[2,256,128]{2,1,0:T(8,128)(2,1)S(1)}, u32[]{:S(2)}, u32[]{:S(2)}) %collective-permute-start.29) | collective-permute-done | bytes 131104 | tf_op jit(solution)/shard_map/ppermute | solution.py:833
  220.4 5.8 %last.1 = (f32[512,768]{1,0:T(8,128)}, bf16[2,192,256]{2,1,0:T(8,128)(2,1)}, bf16[2,192,256]{2,1,0:T(8,128)(2,1)}) custom-call(s32[1]{0:T(128)} %bitcast.spot_ref, bf16[512,768]{1,0:T(8,128)(2,1)} %bitcast.258, f32[1,768]{1,0:T(1,128)} %reshape_squeeze.24.gain, bf16[512,768]{1,0:T(8,128)(2,1)} %get-tuple-element.46.operand.scaled, ...), custom_call_target="tpu_custom_call" | custom-call | flops 201326592 | bytes 7864320 | tf_op jit(solution)/shard_map/last/pallas_call | solution.py:743
  229.0 4.8 %collective-permute-done.31 = bf16[1,192,256]{2,1,0:T(8,128)(2,1)S(1)} collective-permute-done((bf16[1,192,256]{2,1,0:T(8,128)(2,1)S(1)}, bf16[1,192,256]{2,1,0:T(8,128)(2,1)S(1)}, u32[]{:S(2)}, u32[]{:S(2)}) %collective-permute-start.31) | collective-permute-done | bytes 98336 | tf_op jit(solution)/shard_map/ppermute | solution.py:764
  234.0 4.1 collective-permute-done.32
  238.2 4.3 collective-permute-start.35
  244.9 3.8 collective-permute-start.37
  250.3 3.8 collective-permute-done.38
  254.8 3.5 collective-permute-done.39
  260.1 5.2 %collective-permute-done.41 = bf16[1,192,768]{2,1,0:T(8,128)(2,1)S(1)} collective-permute-done((bf16[1,192,768]{2,1,0:T(8,128)(2,1)S(1)}, bf16[1,192,768]{2,1,0:T(8,128)(2,1)S(1)}, u32[]{:S(2)}, u32[]{:S(2)}) %collective-permute-start.41) | collective-permute-done | bytes 294944 | tf_op jit(solution)/shard_map/ppermute | solution.py:764
  267.1 3.6 collective-permute-done.42
  271.8 2.8 collective-permute-done.51
  275.8 4.7 %collective-permute-done.45 = bf16[24,768]{1,0:T(8,128)(2,1)S(1)} collective-permute-done((bf16[24,768]{1,0:T(8,128)(2,1)S(1)}, bf16[24,768]{1,0:T(8,128)(2,1)S(1)}, u32[]{:S(2)}, u32[]{:S(2)}) %collective-permute-start.45) | collective-permute-done | bytes 36896 | tf_op jit(solution)/shard_map/ppermute | solution.py:764
  308.4 3.5 collective-permute-done.59
  318.3 16.2 %collective-permute-done.61 = bf16[1,1536,256]{2,1,0:T(8,128)(2,1)S(1)} collective-permute-done((bf16[1,1536,256]{2,1,0:T(8,128)(2,1)S(1)}, bf16[1,1536,256]{2,1,0:T(8,128)(2,1)S(1)}, u32[]{:S(2)}, u32[]{:S(2)}) %collective-permute-start.61) | collective-permute-done | bytes 786464 | tf_op jit(solution)/shard_map/ppermute | solution.py:764
  335.8 15.5 %collective-permute-done.71 = bf16[1,1536,256]{2,1,0:T(8,128)(2,1)S(1)} collective-permute-done((bf16[1,1536,256]{2,1,0:T(8,128)(2,1)S(1)}, bf16[1,1536,256]{2,1,0:T(8,128)(2,1)S(1)}, u32[]{:S(2)}, u32[]{:S(2)}) %collective-permute-start.71) | collective-permute-done | bytes 786464 | tf_op jit(solution)/shard_map/ppermute | solution.py:764
  352.7 9.0 %collective-permute-done.81 = bf16[1,1536,256]{2,1,0:T(8,128)(2,1)S(1)} collective-permute-done((bf16[1,1536,256]{2,1,0:T(8,128)(2,1)S(1)}, bf16[1,1536,256]{2,1,0:T(8,128)(2,1)S(1)}, u32[]{:S(2)}, u32[]{:S(2)}) %collective-permute-start.81) | collective-permute-done | bytes 786464 | tf_op jit(solution)/shard_map/ppermute | solution.py:764
  374.5 6.9 %collective-permute-start.84 = (bf16[192,256]{1,0:T(8,128)(2,1)S(1)}, bf16[192,256]{1,0:T(8,128)(2,1)S(1)}, u32[]{:S(2)}, u32[]{:S(2)}) collective-permute-start(bf16[192,256]{1,0:T(8,128)(2,1)S(1)} %get-tuple-element.111), channel_id=1, source_target_pairs={{0,16},{4,20},{8,24},{12,28},{16,0},{20,4},{24,8},{28,12},{1,17},{... | collective-permute-start | bytes 294920 | tf_op jit(solution)/shard_map/ppermute | solution.py:764
  383.9 4.6 %collective-permute-start.67 = (bf16[192,256]{1,0:T(8,128)(2,1)S(1)}, bf16[192,256]{1,0:T(8,128)(2,1)S(1)}, u32[]{:S(2)}, u32[]{:S(2)}) collective-permute-start(bf16[192,256]{1,0:T(8,128)(2,1)S(1)} %get-tuple-element.86), channel_id=1, source_target_pairs={{0,16},{4,20},{8,24},{12,28},{16,0},{20,4},{24,8},{28,12},{1,17},{... | collective-permute-start | bytes 294920 | tf_op jit(solution)/shard_map/ppermute | solution.py:764
  388.6 3.7 collective-permute-start.68
  392.3 5.3 %collective-permute-start.77 = (bf16[192,256]{1,0:T(8,128)(2,1)S(1)}, bf16[192,256]{1,0:T(8,128)(2,1)S(1)}, u32[]{:S(2)}, u32[]{:S(2)}) collective-permute-start(bf16[192,256]{1,0:T(8,128)(2,1)S(1)} %get-tuple-element.88), channel_id=1, source_target_pairs={{0,16},{4,20},{8,24},{12,28},{16,0},{20,4},{24,8},{28,12},{1,17},{... | collective-permute-start | bytes 294920 | tf_op jit(solution)/shard_map/ppermute | solution.py:764
  397.8 3.0 collective-permute-start.78
  400.9 5.9 %collective-permute-start.87 = (bf16[192,256]{1,0:T(8,128)(2,1)S(1)}, bf16[192,256]{1,0:T(8,128)(2,1)S(1)}, u32[]{:S(2)}, u32[]{:S(2)}) collective-permute-start(bf16[192,256]{1,0:T(8,128)(2,1)S(1)} %get-tuple-element.90), channel_id=1, source_target_pairs={{0,16},{4,20},{8,24},{12,28},{16,0},{20,4},{24,8},{28,12},{1,17},{... | collective-permute-start | bytes 294920 | tf_op jit(solution)/shard_map/ppermute | solution.py:764
  415.5 3.4 collective-permute-done.69
  419.1 4.0 collective-permute-done.79
  423.3 4.0 collective-permute-done.89
  433.3 2.9 reshape.210
  (317 shorter events, 114.3 us)
Async XLA Ops:
  2.1 13.2 %collective-permute-start.6 = (bf16[208,128]{1,0:T(8,128)(2,1)S(1)}, bf16[208,128]{1,0:T(8,128)(2,1)S(1)}, u32[]{:S(2)}, u32[]{:S(2)}) collective-permute-start(bf16[208,128]{1,0:T(8,128)(2,1)S(1)} %fusion.27.rest_0_), channel_id=1, source_target_pairs={{0,2},{1,3},{2,0},{3,1},{4,6},{5,7},{6,4},{7,5},{8,10},{9,11},{10,... | collective-permute-start | bytes 159752 | tf_op jit(solution)/shard_map/ppermute | solution.py:764
  5.2 10.4 %collective-permute-start.5 = (bf16[208,128]{1,0:T(8,128)(2,1)S(1)}, bf16[208,128]{1,0:T(8,128)(2,1)S(1)}, u32[]{:S(2)}, u32[]{:S(2)}) collective-permute-start(bf16[208,128]{1,0:T(8,128)(2,1)S(1)} %fusion.27.rest_0_), channel_id=1, source_target_pairs={{0,1},{1,0},{2,3},{3,2},{4,5},{5,4},{6,7},{7,6},{8,9},{9,8},{10,11... | collective-permute-start | bytes 159752 | tf_op jit(solution)/shard_map/ppermute | solution.py:764
  5.2 17.0 %collective-permute-start = (s32[2,256]{1,0:T(2,128)}, s32[2,256]{1,0:T(2,128)S(1)}, u32[]{:S(2)}, u32[]{:S(2)}) collective-permute-start(s32[2,256]{1,0:T(2,128)} %param.11), channel_id=1, source_target_pairs={{0,20},{4,24},{8,28},{1,21},{5,25},{9,29},{2,22},{6,26},{10,30},{3... | collective-permute-start | bytes 6152 | tf_op jit(solution)/shard_map/ppermute | solution.py:833
  10.6 13.0 %collective-permute-start.1 = (s32[2,256]{1,0:T(2,128)}, s32[2,256]{1,0:T(2,128)S(1)}, u32[]{:S(2)}, u32[]{:S(2)}) collective-permute-start(s32[2,256]{1,0:T(2,128)} %param.11), channel_id=1, source_target_pairs={{0,16},{4,20},{8,24},{12,28},{1,17},{5,21},{9,25},{13,29},{2,18},{... | collective-permute-start | bytes 6152 | tf_op jit(solution)/shard_map/ppermute | solution.py:833
  11.9 14.8 %collective-permute-start.2 = (s32[2,256]{1,0:T(2,128)}, s32[2,256]{1,0:T(2,128)S(1)}, u32[]{:S(2)}, u32[]{:S(2)}) collective-permute-start(s32[2,256]{1,0:T(2,128)} %param.11), channel_id=1, source_target_pairs={{0,12},{4,16},{8,20},{12,24},{16,28},{1,13},{5,17},{9,21},{13,25},... | collective-permute-start | bytes 6152 | tf_op jit(solution)/shard_map/ppermute | solution.py:833
  15.6 67.1 %collective-permute-start.20 = (bf16[192,3072]{1,0:T(8,128)(2,1)}, bf16[192,3072]{1,0:T(8,128)(2,1)S(1)}, u32[]{:S(2)}, u32[]{:S(2)}) collective-permute-start(bf16[192,3072]{1,0:T(8,128)(2,1)} %rest_0_.11), channel_id=1, source_target_pairs={{0,2},{1,3},{2,0},{3,1},{4,6},{5,7},{6,4},{7,5},{8,10},{9,11},{10,... | collective-permute-start | bytes 3538952 | tf_op jit(solution)/shard_map/ppermute | solution.py:764
  16.7 66.0 %collective-permute-start.23 = (bf16[768,768]{1,0:T(8,128)(2,1)}, bf16[768,768]{1,0:T(8,128)(2,1)}, u32[]{:S(2)}, u32[]{:S(2)}) collective-permute-start(bf16[768,768]{1,0:T(8,128)(2,1)} %rest_4_.5), channel_id=1, source_target_pairs={{0,2},{1,3},{2,0},{3,1},{4,6},{5,7},{6,4},{7,5},{8,10},{9,11},{10,... | collective-permute-start | bytes 3538952 | tf_op jit(solution)/shard_map/ppermute | solution.py:764
  28.1 48.2 %collective-permute-start.9 = (bf16[192,768]{1,0:T(8,128)(2,1)}, bf16[192,768]{1,0:T(8,128)(2,1)S(1)}, u32[]{:S(2)}, u32[]{:S(2)}) collective-permute-start(bf16[192,768]{1,0:T(8,128)(2,1)} %rest_0_.13), channel_id=1, source_target_pairs={{0,2},{1,3},{2,0},{3,1},{4,6},{5,7},{6,4},{7,5},{8,10},{9,11},{10,... | collective-permute-start | bytes 884744 | tf_op jit(solution)/shard_map/ppermute | solution.py:764
  32.1 10.4 %collective-permute-start.13 = (bf16[2,256,128]{2,1,0:T(8,128)(2,1)}, bf16[2,256,128]{2,1,0:T(8,128)(2,1)S(1)}, u32[]{:S(2)}, u32[]{:S(2)}) collective-permute-start(bf16[2,256,128]{2,1,0:T(8,128)(2,1)} %bitcast.315), channel_id=1, source_target_pairs={{0,12},{4,16},{8,20},{12,24},{16,28},{1,13},{5,17},{9,21},{13,25},... | collective-permute-start | bytes 393224 | tf_op jit(solution)/shard_map/ppermute | solution.py:833
  45.4 30.8 %collective-permute-start.8 = (bf16[192,768]{1,0:T(8,128)(2,1)}, bf16[192,768]{1,0:T(8,128)(2,1)S(1)}, u32[]{:S(2)}, u32[]{:S(2)}) collective-permute-start(bf16[192,768]{1,0:T(8,128)(2,1)} %rest_0_.13), channel_id=1, source_target_pairs={{0,1},{1,0},{2,3},{3,2},{4,5},{5,4},{6,7},{7,6},{8,9},{9,8},{10,11... | collective-permute-start | bytes 884744 | tf_op jit(solution)/shard_map/ppermute | solution.py:764
  48.2 33.9 %collective-permute-start.17 = (bf16[192,768]{1,0:T(8,128)(2,1)}, bf16[192,768]{1,0:T(8,128)(2,1)S(1)}, u32[]{:S(2)}, u32[]{:S(2)}) collective-permute-start(bf16[192,768]{1,0:T(8,128)(2,1)} %rest_0_.12), channel_id=1, source_target_pairs={{0,2},{1,3},{2,0},{3,1},{4,6},{5,7},{6,4},{7,5},{8,10},{9,11},{10,... | collective-permute-start | bytes 884744 | tf_op jit(solution)/shard_map/ppermute | solution.py:764
  76.3 13.9 %collective-permute-start.16 = (bf16[192,768]{1,0:T(8,128)(2,1)}, bf16[192,768]{1,0:T(8,128)(2,1)S(1)}, u32[]{:S(2)}, u32[]{:S(2)}) collective-permute-start(bf16[192,768]{1,0:T(8,128)(2,1)} %rest_0_.12), channel_id=1, source_target_pairs={{0,1},{1,0},{2,3},{3,2},{4,5},{5,4},{6,7},{7,6},{8,9},{9,8},{10,11... | collective-permute-start | bytes 884744 | tf_op jit(solution)/shard_map/ppermute | solution.py:764
  82.1 24.3 %collective-permute-start.19 = (bf16[192,3072]{1,0:T(8,128)(2,1)}, bf16[192,3072]{1,0:T(8,128)(2,1)}, u32[]{:S(2)}, u32[]{:S(2)}) collective-permute-start(bf16[192,3072]{1,0:T(8,128)(2,1)} %rest_0_.11), channel_id=1, source_target_pairs={{0,1},{1,0},{2,3},{3,2},{4,5},{5,4},{6,7},{7,6},{8,9},{9,8},{10,11... | collective-permute-start | bytes 3538952 | tf_op jit(solution)/shard_map/ppermute | solution.py:764
  82.1 24.2 %collective-permute-start.22 = (bf16[768,768]{1,0:T(8,128)(2,1)}, bf16[768,768]{1,0:T(8,128)(2,1)}, u32[]{:S(2)}, u32[]{:S(2)}) collective-permute-start(bf16[768,768]{1,0:T(8,128)(2,1)} %rest_4_.5), channel_id=1, source_target_pairs={{0,1},{1,0},{2,3},{3,2},{4,5},{5,4},{6,7},{7,6},{8,9},{9,8},{10,11... | collective-permute-start | bytes 3538952 | tf_op jit(solution)/shard_map/ppermute | solution.py:764
  82.6 23.7 %collective-permute-start.21 = (bf16[192,3072]{1,0:T(8,128)(2,1)S(1)}, bf16[192,3072]{1,0:T(8,128)(2,1)}, u32[]{:S(2)}, u32[]{:S(2)}) collective-permute-start(bf16[192,3072]{1,0:T(8,128)(2,1)S(1)} %collective-permute-done.20.rest_2_), channel_id=1, source_target_pairs={{0,1},{1,0},{2,3},{3,2},{4,5},{5,4},{6,7},{7,6},{8,9},{9,8},{10,11... | collective-permute-start | bytes 3538952 | tf_op jit(solution)/shard_map/ppermute | solution.py:764
  82.7 23.7 %collective-permute-start.24 = (bf16[768,768]{1,0:T(8,128)(2,1)}, bf16[768,768]{1,0:T(8,128)(2,1)}, u32[]{:S(2)}, u32[]{:S(2)}) collective-permute-start(bf16[768,768]{1,0:T(8,128)(2,1)} %collective-permute-done.23.rest_6_), channel_id=1, source_target_pairs={{0,1},{1,0},{2,3},{3,2},{4,5},{5,4},{6,7},{7,6},{8,9},{9,8},{10,11... | collective-permute-start | bytes 3538952 | tf_op jit(solution)/shard_map/ppermute | solution.py:764
  90.2 10.4 %collective-permute-start.18 = (bf16[192,768]{1,0:T(8,128)(2,1)S(1)}, bf16[192,768]{1,0:T(8,128)(2,1)S(1)}, u32[]{:S(2)}, u32[]{:S(2)}) collective-permute-start(bf16[192,768]{1,0:T(8,128)(2,1)S(1)} %collective-permute-done.17.rest_2_), channel_id=1, source_target_pairs={{0,1},{1,0},{2,3},{3,2},{4,5},{5,4},{6,7},{7,6},{8,9},{9,8},{10,11... | collective-permute-start | bytes 884744 | tf_op jit(solution)/shard_map/ppermute | solution.py:764
  167.3 13.3 %collective-permute-start.25 = (bf16[2,256,128]{2,1,0:T(8,128)(2,1)}, bf16[2,256,128]{2,1,0:T(8,128)(2,1)S(1)}, u32[]{:S(2)}, u32[]{:S(2)}) collective-permute-start(bf16[2,256,128]{2,1,0:T(8,128)(2,1)} %get-tuple-element.62), channel_id=1, source_target_pairs={{4,0},{8,4},{12,8},{16,12},{20,16},{24,20},{28,24},{5,1},{9,5},{13... | collective-permute-start | bytes 393224 | tf_op jit(solution)/shard_map/ppermute | solution.py:833
  168.6 18.4 %collective-permute-start.26 = (bf16[2,256,128]{2,1,0:T(8,128)(2,1)}, bf16[2,256,128]{2,1,0:T(8,128)(2,1)S(1)}, u32[]{:S(2)}, u32[]{:S(2)}) collective-permute-start(bf16[2,256,128]{2,1,0:T(8,128)(2,1)} %get-tuple-element.63), channel_id=1, source_target_pairs={{8,0},{12,4},{16,8},{20,12},{24,16},{28,20},{9,1},{13,5},{17,9},{2... | collective-permute-start | bytes 393224 | tf_op jit(solution)/shard_map/ppermute | solution.py:833
  169.9 28.3 %collective-permute-start.27 = (bf16[2,256,128]{2,1,0:T(8,128)(2,1)}, bf16[2,256,128]{2,1,0:T(8,128)(2,1)S(1)}, u32[]{:S(2)}, u32[]{:S(2)}) collective-permute-start(bf16[2,256,128]{2,1,0:T(8,128)(2,1)} %get-tuple-element.64), channel_id=1, source_target_pairs={{12,0},{16,4},{20,8},{24,12},{28,16},{13,1},{17,5},{21,9},{25,13},... | collective-permute-start | bytes 393224 | tf_op jit(solution)/shard_map/ppermute | solution.py:833
  171.2 40.7 %collective-permute-start.28 = (bf16[2,256,128]{2,1,0:T(8,128)(2,1)}, bf16[2,256,128]{2,1,0:T(8,128)(2,1)S(1)}, u32[]{:S(2)}, u32[]{:S(2)}) collective-permute-start(bf16[2,256,128]{2,1,0:T(8,128)(2,1)} %get-tuple-element.65), channel_id=1, source_target_pairs={{16,0},{20,4},{24,8},{28,12},{17,1},{21,5},{25,9},{29,13},{18,2},{... | collective-permute-start | bytes 393224 | tf_op jit(solution)/shard_map/ppermute | solution.py:833
  172.5 47.2 %collective-permute-start.29 = (bf16[2,256,128]{2,1,0:T(8,128)(2,1)}, bf16[2,256,128]{2,1,0:T(8,128)(2,1)S(1)}, u32[]{:S(2)}, u32[]{:S(2)}) collective-permute-start(bf16[2,256,128]{2,1,0:T(8,128)(2,1)} %get-tuple-element.66), channel_id=1, source_target_pairs={{20,0},{24,4},{28,8},{21,1},{25,5},{29,9},{22,2},{26,6},{30,10},{2... | collective-permute-start | bytes 393224 | tf_op jit(solution)/shard_map/ppermute | solution.py:833
  244.9 13.4 %collective-permute-start.40 = (bf16[2,192,768]{2,1,0:T(8,128)(2,1)}, bf16[2,192,768]{2,1,0:T(8,128)(2,1)S(1)}, u32[]{:S(2)}, u32[]{:S(2)}) collective-permute-start(bf16[2,192,768]{2,1,0:T(8,128)(2,1)} %get-tuple-element.74), channel_id=1, source_target_pairs={{0,1},{1,0},{2,3},{3,2},{4,5},{5,4},{6,7},{7,6},{8,9},{9,8},{10,11... | collective-permute-start | bytes 1769480 | tf_op jit(solution)/shard_map/ppermute | solution.py:764
  254.2 59.3 %collective-permute-start.60 = (bf16[2,1536,256]{2,1,0:T(8,128)(2,1)}, bf16[2,1536,256]{2,1,0:T(8,128)(2,1)S(1)}, u32[]{:S(2)}, u32[]{:S(2)}) collective-permute-start(bf16[2,1536,256]{2,1,0:T(8,128)(2,1)} %get-tuple-element.78), channel_id=1, source_target_pairs={{0,1},{1,0},{2,3},{3,2},{4,5},{5,4},{6,7},{7,6},{8,9},{9,8},{10,11... | collective-permute-start | bytes 4718600 | tf_op jit(solution)/shard_map/ppermute | solution.py:764
  254.2 60.1 %collective-permute-start.70 = (bf16[2,1536,256]{2,1,0:T(8,128)(2,1)S(1)}, bf16[2,1536,256]{2,1,0:T(8,128)(2,1)S(1)}, u32[]{:S(2)}, u32[]{:S(2)}) collective-permute-start(bf16[2,1536,256]{2,1,0:T(8,128)(2,1)S(1)} %copy-done.17), channel_id=1, source_target_pairs={{0,1},{1,0},{2,3},{3,2},{4,5},{5,4},{6,7},{7,6},{8,9},{9,8},{10,11... | collective-permute-start | bytes 4718600 | tf_op jit(solution)/shard_map/ppermute | solution.py:764
  254.7 11.9 %collective-permute-start.50 = (bf16[2,192,896]{2,1,0:T(8,128)(2,1)S(1)}, bf16[2,192,896]{2,1,0:T(8,128)(2,1)S(1)}, u32[]{:S(2)}, u32[]{:S(2)}) collective-permute-start(bf16[2,192,896]{2,1,0:T(8,128)(2,1)S(1)} %copy-done.19), channel_id=1, source_target_pairs={{0,1},{1,0},{2,3},{3,2},{4,5},{5,4},{6,7},{7,6},{8,9},{9,8},{10,11... | collective-permute-start | bytes 2064392 | tf_op jit(solution)/shard_map/ppermute | solution.py:764
  291.2 25.3 %collective-permute-start.80 = (bf16[2,1536,256]{2,1,0:T(8,128)(2,1)S(1)}, bf16[2,1536,256]{2,1,0:T(8,128)(2,1)S(1)}, u32[]{:S(2)}, u32[]{:S(2)}) collective-permute-start(bf16[2,1536,256]{2,1,0:T(8,128)(2,1)S(1)} %copy-done.16), channel_id=1, source_target_pairs={{0,1},{1,0},{2,3},{3,2},{4,5},{5,4},{6,7},{7,6},{8,9},{9,8},{10,11... | collective-permute-start | bytes 4718600 | tf_op jit(solution)/shard_map/ppermute | solution.py:764
  313.9 20.5 %collective-permute-start.61 = (bf16[1,1536,256]{2,1,0:T(8,128)(2,1)S(1)}, bf16[1,1536,256]{2,1,0:T(8,128)(2,1)S(1)}, u32[]{:S(2)}, u32[]{:S(2)}) collective-permute-start(bf16[1,1536,256]{2,1,0:T(8,128)(2,1)S(1)} %slice.187), channel_id=1, source_target_pairs={{0,2},{1,3},{2,0},{3,1},{4,6},{5,7},{6,4},{7,5},{8,10},{9,11},{10,... | collective-permute-start | bytes 2359304 | tf_op jit(solution)/shard_map/ppermute | solution.py:764
  315.7 35.6 %collective-permute-start.71 = (bf16[1,1536,256]{2,1,0:T(8,128)(2,1)S(1)}, bf16[1,1536,256]{2,1,0:T(8,128)(2,1)S(1)}, u32[]{:S(2)}, u32[]{:S(2)}) collective-permute-start(bf16[1,1536,256]{2,1,0:T(8,128)(2,1)S(1)} %slice.186), channel_id=1, source_target_pairs={{0,2},{1,3},{2,0},{3,1},{4,6},{5,7},{6,4},{7,5},{8,10},{9,11},{10,... | collective-permute-start | bytes 2359304 | tf_op jit(solution)/shard_map/ppermute | solution.py:764
  317.4 44.2 %collective-permute-start.81 = (bf16[1,1536,256]{2,1,0:T(8,128)(2,1)S(1)}, bf16[1,1536,256]{2,1,0:T(8,128)(2,1)S(1)}, u32[]{:S(2)}, u32[]{:S(2)}) collective-permute-start(bf16[1,1536,256]{2,1,0:T(8,128)(2,1)S(1)} %slice.185), channel_id=1, source_target_pairs={{0,2},{1,3},{2,0},{3,1},{4,6},{5,7},{6,4},{7,5},{8,10},{9,11},{10,... | collective-permute-start | bytes 2359304 | tf_op jit(solution)/shard_map/ppermute | solution.py:764
  334.7 27.7 %collective-permute-start.62 = (bf16[768,256]{1,0:T(8,128)(2,1)S(1)}, bf16[768,256]{1,0:T(8,128)(2,1)S(1)}, u32[]{:S(2)}, u32[]{:S(2)}) collective-permute-start(bf16[768,256]{1,0:T(8,128)(2,1)S(1)} %fusion.3), channel_id=1, source_target_pairs={{0,4},{4,0},{8,12},{12,8},{16,20},{20,16},{24,28},{28,24},{1,5},{5... | collective-permute-start | bytes 1179656 | tf_op jit(solution)/shard_map/ppermute | solution.py:764
  351.5 15.5 %collective-permute-start.72 = (bf16[768,256]{1,0:T(8,128)(2,1)S(1)}, bf16[768,256]{1,0:T(8,128)(2,1)S(1)}, u32[]{:S(2)}, u32[]{:S(2)}) collective-permute-start(bf16[768,256]{1,0:T(8,128)(2,1)S(1)} %fusion.4), channel_id=1, source_target_pairs={{0,4},{4,0},{8,12},{12,8},{16,20},{20,16},{24,28},{28,24},{1,5},{5... | collective-permute-start | bytes 1179656 | tf_op jit(solution)/shard_map/ppermute | solution.py:764
  367.2 14.3 %collective-permute-start.73 = (bf16[192,256]{1,0:T(8,128)(2,1)S(1)}, bf16[192,256]{1,0:T(8,128)(2,1)S(1)}, u32[]{:S(2)}, u32[]{:S(2)}) collective-permute-start(bf16[192,256]{1,0:T(8,128)(2,1)S(1)} %get-tuple-element.106), channel_id=1, source_target_pairs={{0,8},{4,12},{8,0},{12,4},{16,24},{20,28},{24,16},{28,20},{1,9},{5... | collective-permute-start | bytes 294920 | tf_op jit(solution)/shard_map/ppermute | solution.py:764
  369.7 14.2 %collective-permute-start.74 = (bf16[192,256]{1,0:T(8,128)(2,1)S(1)}, bf16[192,256]{1,0:T(8,128)(2,1)S(1)}, u32[]{:S(2)}, u32[]{:S(2)}) collective-permute-start(bf16[192,256]{1,0:T(8,128)(2,1)S(1)} %get-tuple-element.108), channel_id=1, source_target_pairs={{0,16},{4,20},{8,24},{12,28},{16,0},{20,4},{24,8},{28,12},{1,17},{... | collective-permute-start | bytes 294920 | tf_op jit(solution)/shard_map/ppermute | solution.py:764
  371.3 12.6 %collective-permute-start.75 = (bf16[192,256]{1,0:T(8,128)(2,1)S(1)}, bf16[192,256]{1,0:T(8,128)(2,1)S(1)}, u32[]{:S(2)}, u32[]{:S(2)}) collective-permute-start(bf16[192,256]{1,0:T(8,128)(2,1)S(1)} %get-tuple-element.107), channel_id=1, source_target_pairs={{0,24},{4,28},{8,16},{12,20},{16,8},{20,12},{24,0},{28,4},{1,25},{... | collective-permute-start | bytes 294920 | tf_op jit(solution)/shard_map/ppermute | solution.py:764
  374.5 14.1 %collective-permute-start.83 = (bf16[192,256]{1,0:T(8,128)(2,1)S(1)}, bf16[192,256]{1,0:T(8,128)(2,1)S(1)}, u32[]{:S(2)}, u32[]{:S(2)}) collective-permute-start(bf16[192,256]{1,0:T(8,128)(2,1)S(1)} %get-tuple-element.109), channel_id=1, source_target_pairs={{0,8},{4,12},{8,0},{12,4},{16,24},{20,28},{24,16},{28,20},{1,9},{5... | collective-permute-start | bytes 294920 | tf_op jit(solution)/shard_map/ppermute | solution.py:764
  374.5 17.8 %collective-permute-start.84 = (bf16[192,256]{1,0:T(8,128)(2,1)S(1)}, bf16[192,256]{1,0:T(8,128)(2,1)S(1)}, u32[]{:S(2)}, u32[]{:S(2)}) collective-permute-start(bf16[192,256]{1,0:T(8,128)(2,1)S(1)} %get-tuple-element.111), channel_id=1, source_target_pairs={{0,16},{4,20},{8,24},{12,28},{16,0},{20,4},{24,8},{28,12},{1,17},{... | collective-permute-start | bytes 294920 | tf_op jit(solution)/shard_map/ppermute | solution.py:764
  381.5 10.9 %collective-permute-start.85 = (bf16[192,256]{1,0:T(8,128)(2,1)S(1)}, bf16[192,256]{1,0:T(8,128)(2,1)S(1)}, u32[]{:S(2)}, u32[]{:S(2)}) collective-permute-start(bf16[192,256]{1,0:T(8,128)(2,1)S(1)} %get-tuple-element.110), channel_id=1, source_target_pairs={{0,24},{4,28},{8,16},{12,20},{16,8},{20,12},{24,0},{28,4},{1,25},{... | collective-permute-start | bytes 294920 | tf_op jit(solution)/shard_map/ppermute | solution.py:764
  383.9 13.9 %collective-permute-start.66 = (bf16[192,256]{1,0:T(8,128)(2,1)S(1)}, bf16[192,256]{1,0:T(8,128)(2,1)S(1)}, u32[]{:S(2)}, u32[]{:S(2)}) collective-permute-start(bf16[192,256]{1,0:T(8,128)(2,1)S(1)} %get-tuple-element.86), channel_id=1, source_target_pairs={{0,8},{4,12},{8,0},{12,4},{16,24},{20,28},{24,16},{28,20},{1,9},{5... | collective-permute-start | bytes 294920 | tf_op jit(solution)/shard_map/ppermute | solution.py:764
  383.9 16.9 %collective-permute-start.67 = (bf16[192,256]{1,0:T(8,128)(2,1)S(1)}, bf16[192,256]{1,0:T(8,128)(2,1)S(1)}, u32[]{:S(2)}, u32[]{:S(2)}) collective-permute-start(bf16[192,256]{1,0:T(8,128)(2,1)S(1)} %get-tuple-element.86), channel_id=1, source_target_pairs={{0,16},{4,20},{8,24},{12,28},{16,0},{20,4},{24,8},{28,12},{1,17},{... | collective-permute-start | bytes 294920 | tf_op jit(solution)/shard_map/ppermute | solution.py:764
  388.6 12.3 %collective-permute-start.68 = (bf16[192,256]{1,0:T(8,128)(2,1)S(1)}, bf16[192,256]{1,0:T(8,128)(2,1)S(1)}, u32[]{:S(2)}, u32[]{:S(2)}) collective-permute-start(bf16[192,256]{1,0:T(8,128)(2,1)S(1)} %get-tuple-element.86), channel_id=1, source_target_pairs={{0,24},{4,28},{8,16},{12,20},{16,8},{20,12},{24,0},{28,4},{1,25},{... | collective-permute-start | bytes 294920 | tf_op jit(solution)/shard_map/ppermute | solution.py:764
  392.3 14.4 %collective-permute-start.76 = (bf16[192,256]{1,0:T(8,128)(2,1)S(1)}, bf16[192,256]{1,0:T(8,128)(2,1)S(1)}, u32[]{:S(2)}, u32[]{:S(2)}) collective-permute-start(bf16[192,256]{1,0:T(8,128)(2,1)S(1)} %get-tuple-element.88), channel_id=1, source_target_pairs={{0,8},{4,12},{8,0},{12,4},{16,24},{20,28},{24,16},{28,20},{1,9},{5... | collective-permute-start | bytes 294920 | tf_op jit(solution)/shard_map/ppermute | solution.py:764
  392.3 16.8 %collective-permute-start.77 = (bf16[192,256]{1,0:T(8,128)(2,1)S(1)}, bf16[192,256]{1,0:T(8,128)(2,1)S(1)}, u32[]{:S(2)}, u32[]{:S(2)}) collective-permute-start(bf16[192,256]{1,0:T(8,128)(2,1)S(1)} %get-tuple-element.88), channel_id=1, source_target_pairs={{0,16},{4,20},{8,24},{12,28},{16,0},{20,4},{24,8},{28,12},{1,17},{... | collective-permute-start | bytes 294920 | tf_op jit(solution)/shard_map/ppermute | solution.py:764
  397.8 13.6 %collective-permute-start.78 = (bf16[192,256]{1,0:T(8,128)(2,1)S(1)}, bf16[192,256]{1,0:T(8,128)(2,1)S(1)}, u32[]{:S(2)}, u32[]{:S(2)}) collective-permute-start(bf16[192,256]{1,0:T(8,128)(2,1)S(1)} %get-tuple-element.88), channel_id=1, source_target_pairs={{0,24},{4,28},{8,16},{12,20},{16,8},{20,12},{24,0},{28,4},{1,25},{... | collective-permute-start | bytes 294920 | tf_op jit(solution)/shard_map/ppermute | solution.py:764
  400.8 10.7 %collective-permute-start.86 = (bf16[192,256]{1,0:T(8,128)(2,1)S(1)}, bf16[192,256]{1,0:T(8,128)(2,1)S(1)}, u32[]{:S(2)}, u32[]{:S(2)}) collective-permute-start(bf16[192,256]{1,0:T(8,128)(2,1)S(1)} %get-tuple-element.90), channel_id=1, source_target_pairs={{0,8},{4,12},{8,0},{12,4},{16,24},{20,28},{24,16},{28,20},{1,9},{5... | collective-permute-start | bytes 294920 | tf_op jit(solution)/shard_map/ppermute | solution.py:764
  400.9 11.0 %collective-permute-start.87 = (bf16[192,256]{1,0:T(8,128)(2,1)S(1)}, bf16[192,256]{1,0:T(8,128)(2,1)S(1)}, u32[]{:S(2)}, u32[]{:S(2)}) collective-permute-start(bf16[192,256]{1,0:T(8,128)(2,1)S(1)} %get-tuple-element.90), channel_id=1, source_target_pairs={{0,16},{4,20},{8,24},{12,28},{16,0},{20,4},{24,8},{28,12},{1,17},{... | collective-permute-start | bytes 294920 | tf_op jit(solution)/shard_map/ppermute | solution.py:764
  411.4 11.6 %collective-permute-start.79 = (bf16[4,192,256]{2,1,0:T(8,128)(2,1)S(1)}, bf16[4,192,256]{2,1,0:T(8,128)(2,1)S(1)}, u32[]{:S(2)}, u32[]{:S(2)}) collective-permute-start(bf16[4,192,256]{2,1,0:T(8,128)(2,1)S(1)} %bitcast_dynamic-update-slice_fusion.4), channel_id=1, source_target_pairs={{0,4},{4,0},{8,12},{12,8},{16,20},{20,16},{24,28},{28,24},{1,5},{5... | collective-permute-start | bytes 1179656 | tf_op jit(solution)/shard_map/ppermute | solution.py:764
  413.4 13.9 %collective-permute-start.89 = (bf16[4,192,256]{2,1,0:T(8,128)(2,1)S(1)}, bf16[4,192,256]{2,1,0:T(8,128)(2,1)S(1)}, u32[]{:S(2)}, u32[]{:S(2)}) collective-permute-start(bf16[4,192,256]{2,1,0:T(8,128)(2,1)S(1)} %bitcast_dynamic-update-slice_fusion), channel_id=1, source_target_pairs={{0,4},{4,0},{8,12},{12,8},{16,20},{20,16},{24,28},{28,24},{1,5},{5... | collective-permute-start | bytes 1179656 | tf_op jit(solution)/shard_map/ppermute | solution.py:764
  (67 other events, 763.5 us)

commit v2 on v1

v2 whole, which is shorter than its diff:
```python
import functools
import math

import jax
import jax.numpy as jnp
from jax import lax
from jax.experimental import pallas as pl
from jax.experimental.pallas import tpu as pltpu
from jax.sharding import PartitionSpec as P

HEADS = 12
HEAD_DIM = 64
PAIRS = HEADS // 2
LANES = 128
EPSILON = 1e-05
BIAS = -1e30
SCALE = math.log2(math.e) / HEAD_DIM**0.5
F32 = jnp.float32
BF16 = jnp.bfloat16
GELU_ROOT = math.sqrt(2.0 / math.pi)
GELU_CUBE = 0.044715


def params(*semantics):
    return pltpu.CompilerParams(
        dimension_semantics=semantics or None, vmem_limit_bytes=56 * 1024 * 1024
    )


def weight():
    return pl.CostEstimate(flops=1, bytes_accessed=1, transcendentals=0)


def dot_nn(a, b):
    return lax.dot_general(a, b, (((1,), (0,)), ((), ())), preferred_element_type=F32)


def dot_nt(a, b):
    return lax.dot_general(a, b, (((1,), (1,)), ((), ())), preferred_element_type=F32)


def dot_tn(a, b):
    return lax.dot_general(a, b, (((0,), (0,)), ((), ())), preferred_element_type=F32)


def normalize(values):
    center = values - jnp.mean(values, axis=-1, keepdims=True)
    spread = jnp.mean(center * center, axis=-1, keepdims=True)
    inverse = lax.rsqrt(spread + EPSILON)
    return center * inverse, inverse


def norm_back(grad, normed, inverse):
    mean_grad = jnp.mean(grad, axis=-1, keepdims=True)
    mean_both = jnp.mean(grad * normed, axis=-1, keepdims=True)
    return (grad - mean_grad - normed * mean_both) * inverse


def place_rows(spot, pieces, scratch):
    height = scratch.shape[0] // len(pieces)
    for r, piece in enumerate(pieces):
        begin = pl.multiple_of((spot ^ r) * height, height)
        scratch[pl.ds(begin, height), :] = piece[0:height, :]


STEP = 128


def over_rows(rows, run):
    def one(index, carried):
        run(pl.ds(pl.multiple_of(index * STEP, STEP), STEP))
        return carried

    lax.fori_loop(0, rows // STEP, one, 0)


def first_kernel(spot_ref, tokens, gain, *rest, pieces):
    weights = rest[:pieces]
    scaled_out, shared_out, weight = rest[pieces:]
    place_rows(spot_ref[0], weights, weight)

    def run(rows):
        normed, unused = normalize(tokens[rows, :].astype(F32))
        scaled = (normed * gain[...]).astype(BF16)
        scaled_out[rows, :] = scaled
        shared_out[rows, :] = dot_nn(scaled, weight[...]).astype(BF16)

    over_rows(tokens.shape[0], run)


def first_stage(spot, tokens, gain, weights):
    rows, width = tokens.shape
    columns = weights[0].shape[1]
    return pl.pallas_call(
        functools.partial(first_kernel, pieces=len(weights)),
        grid_spec=pltpu.PrefetchScalarGridSpec(
            num_scalar_prefetch=1,
            grid=(),
            in_specs=[pl.BlockSpec(memory_space=pltpu.VMEM)] * (2 + len(weights)),
            out_specs=[pl.BlockSpec(memory_space=pltpu.VMEM)] * 2,
            scratch_shapes=[pltpu.VMEM((width, columns), BF16)],
        ),
        out_shape=[
            jax.ShapeDtypeStruct((rows, width), BF16),
            jax.ShapeDtypeStruct((rows, columns), BF16),
        ],
        compiler_params=params(),
        cost_estimate=weight(),
        name="first_norm",
    )(spot, tokens, gain, *weights)


def project_kernel(spot_ref, operand, *rest, pieces):
    weights = rest[:pieces]
    out, weight = rest[pieces:]
    place_rows(spot_ref[0], weights, weight)
    out[...] = dot_nn(operand[...], weight[...]).astype(out.dtype)


def project(spot, operand, weights):
    rows, width = operand.shape
    columns = weights[0].shape[1]
    return pl.pallas_call(
        functools.partial(project_kernel, pieces=len(weights)),
        grid_spec=pltpu.PrefetchScalarGridSpec(
            num_scalar_prefetch=1,
            grid=(),
            in_specs=[pl.BlockSpec(memory_space=pltpu.VMEM)] * (1 + len(weights)),
            out_specs=pl.BlockSpec(memory_space=pltpu.VMEM),
            scratch_shapes=[pltpu.VMEM((width, columns), BF16)],
        ),
        out_shape=jax.ShapeDtypeStruct((rows, columns), BF16),
        compiler_params=params(),
        cost_estimate=weight(),
        name="project",
    )(spot, operand, *weights)


def low_lanes(shape):
    return lax.broadcasted_iota(jnp.int32, shape, len(shape) - 1) < HEAD_DIM


def swap_halves(values):
    return pltpu.roll(values, HEAD_DIM, 1)


def stacked_pairs(ref):
    return jnp.concatenate(
        [ref[0, :, p * LANES : (p + 1) * LANES] for p in range(PAIRS)], axis=0
    )


def tile_bias(starts, key_begin, row_begin, tile_rows, tile_keys):
    key_place = key_begin + lax.broadcasted_iota(jnp.int32, (tile_rows, tile_keys), 1)
    row_place = row_begin + lax.broadcasted_iota(jnp.int32, (tile_rows, tile_keys), 0)
    first = jnp.concatenate([starts] * (tile_keys // LANES), axis=1)
    allowed = (key_place >= first) & (key_place <= row_place)
    bias = jnp.where(allowed, 0.0, BIAS)
    bias = jnp.concatenate([bias, bias], axis=1)
    return jnp.concatenate([bias] * PAIRS, axis=0)


def block_at(place_ref, j, blocks):
    return jnp.maximum(place_ref[0] - (blocks - 1) + j, 0)


def attend_kernel(
    first_ref, place_ref, queries, starts, keyvals, exact_out, rounded_out, logs_out,
    key_even, key_odd, value_even, value_odd, score_scratch, most, total,
    *, blocks, tile_rows, tile_keys
):
    rows = keyvals.shape[2]
    seq, tile = pl.program_id(0), pl.program_id(1)

    @pl.when(tile == 0)
    def _():
        low = low_lanes((rows, LANES))
        for j in range(blocks):
            whole = keyvals[block_at(place_ref, j, blocks), 0].astype(F32)
            turned = swap_halves(whole)
            place = pl.ds(j * rows, rows)
            key_even[place, :] = jnp.where(low, whole, 0.0).astype(BF16)
            key_odd[place, :] = jnp.where(low, 0.0, turned).astype(BF16)
            value_even[place, 0:LANES] = jnp.where(low, turned, 0.0).astype(BF16)
            value_even[place, LANES:] = jnp.where(low, 1.0, 0.0).astype(BF16)
            value_odd[place, 0:LANES] = jnp.where(low, 0.0, whole).astype(BF16)
            value_odd[place, LANES:] = jnp.where(low, 0.0, 1.0).astype(BF16)

    row_begin = (blocks - 1) * rows + tile * tile_rows
    begin = first_ref[seq, tile] // tile_keys
    end = (row_begin + tile_rows - 1) // tile_keys + 1
    stacked = stacked_pairs(queries)
    most[...] = jnp.full_like(most, -3e38)
    copies = tile_keys // LANES

    def score(index):
        key_begin = pl.multiple_of(index * tile_keys, tile_keys)
        place = pl.ds(key_begin, tile_keys)
        both = jnp.concatenate([key_even[place, :], key_odd[place, :]], axis=0)
        values = dot_nt(stacked, both) + tile_bias(
            starts[0], key_begin, row_begin, tile_rows, tile_keys
        )
        score_scratch[index - begin] = values
        half = []
        for h in range(2):
            part = values[:, h * tile_keys : h * tile_keys + LANES]
            for q in range(1, copies):
                at = h * tile_keys + q * LANES
                part = jnp.maximum(part, values[:, at : at + LANES])
            half.append(part)
        return jnp.concatenate(half, axis=1)

    def output(index):
        place = pl.ds(pl.multiple_of(index * tile_keys, tile_keys), tile_keys)
        both = jnp.concatenate([value_even[place, :], value_odd[place, :]], axis=0)
        shift = jnp.concatenate([most[:, 0:LANES]] * copies + [most[:, LANES:]] * copies, axis=1)
        powers = jnp.exp2((score_scratch[index - begin] - shift) * SCALE).astype(BF16)
        return dot_nn(powers, both)

    def in_pairs(one, join, total):
        def two(index, carried):
            at = begin + 2 * index
            total[...] = join(total[...], join(one(at), one(at + 1)))
            return carried

        count = end - begin
        lax.fori_loop(0, count // 2, two, 0)

        @pl.when(count % 2 == 1)
        def _():
            total[...] = join(total[...], one(end - 1))

    in_pairs(score, jnp.maximum, most)
    stack = PAIRS * tile_rows
    for h in range(2):
        part = jnp.max(most[:, h * LANES : (h + 1) * LANES], axis=1, keepdims=True)
        most[:, h * LANES : (h + 1) * LANES] = jnp.broadcast_to(part, (stack, LANES))
    total[...] = jnp.zeros_like(total)
    in_pairs(output, jnp.add, total)
    low = low_lanes((tile_rows, LANES))
    for p in range(PAIRS):
        at = pl.ds(p * tile_rows, tile_rows)
        lanes = slice(p * LANES, (p + 1) * LANES)
        sums = total[at, LANES:]
        out = total[at, 0:LANES] / sums
        exact_out[0, :, lanes] = out
        rounded_out[0, :, lanes] = out.astype(BF16)
        shift = jnp.where(low, most[at, 0:LANES], most[at, LANES:])
        logs_out[0, :, lanes] = shift * SCALE + jnp.log2(sums)


def attend_back_kernel(
    first_ref, place_ref, queries, starts, exact, logs, grads, keyvals, grad_queries, terms,
    *rest, seq, blocks, tile_rows, tile_keys
):
    (
        key_even, key_odd, value_even, value_odd,
        key_total, value_total, query_total,
        log_even, log_odd, delta_even, delta_odd,
    ) = rest
    rows = keyvals.shape[2]
    tile = pl.program_id(0)

    @pl.when(tile == 0)
    def _():
        low = low_lanes((rows, LANES))
        for j in range(blocks):
            whole = keyvals[block_at(place_ref, j, blocks), 0].astype(F32)
            turned = swap_halves(whole)
            place = pl.ds(j * rows, rows)
            key_even[place, :] = jnp.where(low, whole, 0.0).astype(BF16)
            key_odd[place, :] = jnp.where(low, 0.0, turned).astype(BF16)
            value_even[place, :] = jnp.where(low, turned, 0.0).astype(BF16)
            value_odd[place, :] = jnp.where(low, 0.0, whole).astype(BF16)
        key_total[...] = jnp.zeros_like(key_total)
        value_total[...] = jnp.zeros_like(value_total)

    row_begin = (blocks - 1) * rows + tile * tile_rows
    begin = first_ref[seq, tile] // tile_keys
    end = (row_begin + tile_rows - 1) // tile_keys + 1
    stacked = stacked_pairs(queries)
    grad_stacked = stacked_pairs(grads)
    stacked_turned = stacked.T
    grad_turned = grad_stacked.T
    stack = PAIRS * tile_rows
    low = low_lanes((tile_rows, LANES))
    for p in range(PAIRS):
        at = pl.ds(p * tile_rows, tile_rows)
        lanes = slice(p * LANES, (p + 1) * LANES)
        log = logs[0, :, lanes]
        log_turned = swap_halves(log)
        log_even[at, :] = jnp.where(low, log, log_turned)
        log_odd[at, :] = jnp.where(low, log_turned, log)
        terms_here = exact[0, :, lanes] * grads[0, :, lanes].astype(F32)
        even = jnp.sum(jnp.where(low, terms_here, 0.0), axis=1, keepdims=True)
        odd = jnp.sum(jnp.where(low, 0.0, terms_here), axis=1, keepdims=True)
        delta_even[at, :] = jnp.broadcast_to(even, (tile_rows, LANES))
        delta_odd[at, :] = jnp.broadcast_to(odd, (tile_rows, LANES))
    query_total[...] = jnp.zeros_like(query_total)

    def step(index, carried):
        key_begin = pl.multiple_of(index * tile_keys, tile_keys)
        place = pl.ds(key_begin, tile_keys)
        keys = jnp.concatenate([key_even[place, :], key_odd[place, :]], axis=0)
        values = jnp.concatenate([value_even[place, :], value_odd[place, :]], axis=0)
        copies = tile_keys // LANES
        log = jnp.concatenate([log_even[...]] * copies + [log_odd[...]] * copies, axis=1)
        delta = jnp.concatenate([delta_even[...]] * copies + [delta_odd[...]] * copies, axis=1)
        scores = dot_nt(stacked, keys) + tile_bias(
            starts[0], key_begin, row_begin, tile_rows, tile_keys
        )
        chances = jnp.exp2(scores * SCALE - log)
        grad_probs = dot_nt(grad_stacked, values)
        grad_scores = (chances * (grad_probs - delta)).astype(BF16)
        query_total[...] += dot_nn(grad_scores, keys)
        key_total[index] += dot_nn(stacked_turned, grad_scores)
        value_total[index] += dot_nn(grad_turned, chances.astype(BF16))
        return carried

    lax.fori_loop(begin, end, step, 0)
    root = 1.0 / HEAD_DIM**0.5
    for p in range(PAIRS):
        at = pl.ds(p * tile_rows, tile_rows)
        lanes = slice(p * LANES, (p + 1) * LANES)
        grad_queries[0, :, lanes] = (query_total[at, :] * root).astype(BF16)

    @pl.when(tile == pl.num_programs(0) - 1)
    def _():
        per_block = rows // tile_keys
        terms[...] = jnp.zeros_like(terms)

        def block_terms(j, carried):
            for i in range(per_block):
                index = j * per_block + i
                key = key_total[index]
                value = value_total[index]
                key = key[0:HEAD_DIM, 0:tile_keys] + key[HEAD_DIM:, tile_keys:]
                value = value[0:HEAD_DIM, 0:tile_keys] + value[HEAD_DIM:, tile_keys:]
                both = jnp.concatenate([key * root, value], axis=0)
                owner = block_at(place_ref, j, blocks)
                terms[owner, i * tile_keys : (i + 1) * tile_keys, :] = both.T.astype(BF16)
            return carried

        missing = jnp.maximum(blocks - 1 - place_ref[0], 0)
        lax.fori_loop(missing, blocks, block_terms, 0)


def attention_sizes(rows, blocks):
    tile_rows = 128 if rows % 128 == 0 else rows
    tile_keys = 256 if rows % 256 == 0 else 128
    return tile_rows, tile_keys, blocks * rows // tile_keys


def attend(firsts, place, queries, starts, keyvals, blocks):
    seqs, rows, width = queries.shape
    tile_rows, tile_keys, key_tiles = attention_sizes(rows, blocks)
    stack = PAIRS * tile_rows
    keys = blocks * rows
    row_spec = lambda lanes: pl.BlockSpec((1, tile_rows, lanes), lambda s, t, *_: (s, t, 0))
    return pl.pallas_call(
        functools.partial(
            attend_kernel, blocks=blocks, tile_rows=tile_rows, tile_keys=tile_keys
        ),
        grid_spec=pltpu.PrefetchScalarGridSpec(
            num_scalar_prefetch=2,
            grid=(seqs, rows // tile_rows),
            in_specs=[
                row_spec(width),
                row_spec(LANES),
                pl.BlockSpec((keyvals.shape[0], 1, rows, LANES), lambda s, t, *_: (0, s, 0, 0)),
            ],
            out_specs=[row_spec(width)] * 3,
            scratch_shapes=[
                pltpu.VMEM((keys, LANES), BF16),
                pltpu.VMEM((keys, LANES), BF16),
                pltpu.VMEM((keys, 2 * LANES), BF16),
                pltpu.VMEM((keys, 2 * LANES), BF16),
                pltpu.VMEM((key_tiles, stack, 2 * tile_keys), F32),
                pltpu.VMEM((stack, 2 * LANES), F32),
                pltpu.VMEM((stack, 2 * LANES), F32),
            ],
        ),
        out_shape=[
            jax.ShapeDtypeStruct((seqs, rows, width), F32),
            jax.ShapeDtypeStruct((seqs, rows, width), BF16),
            jax.ShapeDtypeStruct((seqs, rows, width), F32),
        ],
        compiler_params=params("arbitrary", "arbitrary"),
        cost_estimate=weight(),
        name="attend",
    )(firsts, place, queries, starts, keyvals)


def attend_back(
    seq, firsts, place, queries, starts, exact, logs, grads, keyvals, blocks
):
    seqs, rows, width = queries.shape
    ctx_size = keyvals.shape[0]
    tile_rows, tile_keys, key_tiles = attention_sizes(rows, blocks)
    stack = PAIRS * tile_rows
    keys = blocks * rows
    row_spec = lambda lanes: pl.BlockSpec((1, tile_rows, lanes), lambda t, *_: (seq, t, 0))
    return pl.pallas_call(
        functools.partial(
            attend_back_kernel, seq=seq, blocks=blocks, tile_rows=tile_rows, tile_keys=tile_keys
        ),
        grid_spec=pltpu.PrefetchScalarGridSpec(
            num_scalar_prefetch=2,
            grid=(rows // tile_rows,),
            in_specs=[row_spec(width), row_spec(LANES)]
            + [row_spec(width)] * 3
            + [pl.BlockSpec((ctx_size, 1, rows, LANES), lambda t, *_: (0, seq, 0, 0))],
            out_specs=[
                pl.BlockSpec((1, tile_rows, width), lambda t, *_: (0, t, 0)),
                pl.BlockSpec((ctx_size, rows, LANES), lambda t, *_: (0, 0, 0)),
            ],
            scratch_shapes=[pltpu.VMEM((keys, LANES), BF16)] * 4
            + [pltpu.VMEM((key_tiles, LANES, 2 * tile_keys), F32)] * 2
            + [pltpu.VMEM((stack, LANES), F32)] * 5,
        ),
        out_shape=[
            jax.ShapeDtypeStruct((1, rows, width), BF16),
            jax.ShapeDtypeStruct((ctx_size, rows, LANES), BF16),
        ],
        compiler_params=params("arbitrary"),
        cost_estimate=weight(),
        name="attend_back",
    )(firsts, place, queries, starts, exact, logs, grads, keyvals)


TILE = 256


def round_up(count, unit):
    return -(-count // unit) * unit


def mixing_rows(width, pieces, ctx_size):
    unit = 8 * ctx_size
    tall = 2 * width + width // pieces * (width // TILE)
    return round_up(tall + width // LANES, unit) - 2 * width


def message_of(keep, send, s):
    return (keep if (s & 1) == 0 else send), s >> 1


def split_out(spot, pieces, source, keep_out, send_out, first_row=0):
    height, lanes = source.shape[0] // pieces, keep_out.shape[2]
    across = min(lanes, source.shape[1])
    for s in range(pieces):
        out, at = message_of(keep_out, send_out, s)
        begin = pl.multiple_of((spot ^ s) * height, height)
        for g in range(source.shape[1] // across):
            row = first_row + g * height
            out[at, row : row + height, 0:across] = source[
                pl.ds(begin, height), g * lanes : g * lanes + across
            ].astype(BF16)


def put_vector(pieces, vector, keep_out, send_out, first_row, begin):
    height, lanes = keep_out.shape[1] - first_row, keep_out.shape[2]
    count = vector.shape[1] // LANES
    row = lax.broadcasted_iota(jnp.int32, (height, LANES), 0)
    block = jnp.zeros((height, LANES), F32)
    for i in range(count):
        block = jnp.where(row == i, vector[:, i * LANES : (i + 1) * LANES], block)
    for s in range(pieces):
        out, at = message_of(keep_out, send_out, s)
        out[at, first_row:, begin : begin + LANES] = block.astype(BF16)
        if begin == 0:
            out[at, first_row:, LANES:] = jnp.zeros((height, lanes - LANES), BF16)


def feed_kernel(spot_ref, *refs, pieces, chunk, chunks, names):
    use = dict(zip(names, refs))
    spot = spot_ref[0]
    step = pl.program_id(0)
    last_step = pl.num_programs(0) - 1
    first, last = chunk == 0, chunk == chunks - 1
    group = lambda key: [use[f"{key}{r}"] for r in range(pieces)]
    ups, downs, mixings = group("up"), group("down"), group("mixing") if first or last else None
    cotangent, keep_out, send_out = use["cotangent"], use["keep"], use["send"]
    reduced, grads, scaled, hidden = use["reduced"], use["grads"], use["scaled"], use["hidden"]
    up_tile, down_tile, up_sems, down_sems = (
        use["up_tile"], use["down_tile"], use["up_sems"], use["down_sems"]
    )
    rows, width = cotangent.shape
    height = width // pieces
    groups = width // TILE
    both = 2 * TILE

    def copies(at):
        for h in range(2):
            s = 2 * at + h
            column = pl.multiple_of(((spot ^ s) * chunks + chunk) * TILE, TILE)
            for r in range(pieces):
                row = pl.multiple_of((spot ^ r) * height, height)
                yield pltpu.make_async_copy(
                    ups[r].at[:, pl.ds(column, TILE)],
                    up_tile.at[at, pl.ds(row, height), pl.ds(h * TILE, TILE)],
                    up_sems.at[s, r],
                )
            yield pltpu.make_async_copy(
                downs[s].at[pl.ds(chunk * TILE, TILE), :],
                down_tile.at[at, pl.ds(h * TILE, TILE), :],
                down_sems.at[s],
            )

    @pl.when(step == 0)
    def _():
        for at in range(pieces // 2):
            for one in copies(at):
                one.start()
        if first or last:
            place_rows(spot, mixings, use["mixing_all"])
        if first:

            def begin(here):
                mixed = dot_nn(use["attended"][here, :], use["mixing_all"][...])
                values = use["tokens"][here, :].astype(F32) + mixed
                hidden[here, :] = values
                normed, unused = normalize(values)
                scaled[here, :] = (normed * use["gain"][...]).astype(BF16)

            over_rows(rows, begin)

    for at in range(pieces // 2):

        @pl.when(step == at)
        def _():
            for one in copies(at):
                one.wait()

    up = up_tile[step]
    down = down_tile[step]
    upper = dot_nn(scaled[...], up)
    grad_act = dot_nt(cotangent[...], down)
    square = upper * upper
    inner = jnp.tanh(GELU_ROOT * (upper + GELU_CUBE * upper * square))
    half = 0.5 * (1.0 + inner)
    slope = half + 0.5 * upper * (1.0 - inner * inner) * (
        GELU_ROOT * (1.0 + 3.0 * GELU_CUBE * square)
    )
    active = (upper * half).astype(BF16)
    grad_upper = (grad_act * slope).astype(BF16)
    reduced_here = dot_nn(active, down)
    grads_here = dot_nt(grad_upper, up)

    @pl.when(step == 0)
    def _():
        if first:
            reduced[...] = reduced_here
            grads[...] = grads_here
        else:
            reduced[...] = use["reduced_in"][...] + reduced_here
            grads[...] = use["grads_in"][...] + grads_here

    @pl.when(step > 0)
    def _():
        reduced[...] += reduced_here
        grads[...] += grads_here

    down_term = dot_tn(active, cotangent[...]).astype(BF16)
    for g in range(groups):
        column = slice(g * TILE, (g + 1) * TILE)
        keep_out[step, column, :] = down_term[0:TILE, column]
        send_out[step, column, :] = down_term[TILE:, column]
    up_term = use["up_term"]
    up_term[...] = dot_tn(scaled[...], grad_upper)
    for s in range(pieces):
        out, at = message_of(keep_out, send_out, s)
        begin = pl.multiple_of((spot ^ s) * height, height)
        for h in range(2):
            row = pl.multiple_of(groups * TILE + (spot ^ (2 * step + h)) * height, height)
            out[at, pl.ds(row, height), :] = up_term[
                pl.ds(begin, height), h * TILE : (h + 1) * TILE
            ].astype(BF16)

    if last:

        @pl.when(step == last_step)
        def _():
            sums, grad_mixed, term = use["sums"], use["grad_mixed"], use["term"]
            sums[...] = jnp.zeros_like(sums)

            def end(here):
                values = hidden[here, :]
                use["layer_out"][here, :] = (values + reduced[here, :]).astype(BF16)
                normed, inverse = normalize(values)
                grad = grads[here, :]
                sums[...] += jnp.sum((grad * normed).reshape(STEP // 8, 8, width), axis=0)
                grad_hidden = cotangent[here, :].astype(F32) + norm_back(
                    grad * use["gain"][...], normed, inverse
                )
                use["grad_hidden"][here, :] = grad_hidden
                rounded = grad_hidden.astype(BF16)
                grad_mixed[here, :] = rounded
                use["grad_attended"][here, :] = dot_nt(rounded, use["mixing_all"][...]).astype(
                    BF16
                )

            over_rows(rows, end)
            term[...] = dot_tn(use["attended"][...], grad_mixed[...])
            tall = 2 * width
            split_out(spot, pieces, term, keep_out, send_out, tall)
            put_vector(
                pieces,
                jnp.sum(sums[...], axis=0, keepdims=True),
                keep_out,
                send_out,
                tall + height * groups,
                0,
            )


def feed_stage(spot, arrays, ups, downs, mixings, chunk, chunks, ctx_size):
    first, last = chunk == 0, chunk == chunks - 1
    rows, width = arrays["cotangent"].shape
    pieces = len(ups)
    tall = 2 * width + (mixing_rows(width, pieces, ctx_size) if last else 0)
    wide = jax.ShapeDtypeStruct((rows, width), F32)
    narrow = jax.ShapeDtypeStruct((rows, width), BF16)
    message = jax.ShapeDtypeStruct((pieces // 2, tall, TILE), BF16)
    inputs, scratch = {}, {}
    inputs["cotangent"] = arrays["cotangent"]
    for r in range(pieces):
        inputs[f"up{r}"], inputs[f"down{r}"] = ups[r], downs[r]
    outputs = {"keep": message, "send": message}
    if first:
        for name in ("attended", "tokens", "gain"):
            inputs[name] = arrays[name]
        outputs.update(hidden=wide, scaled=narrow, reduced=wide, grads=wide)
    else:
        inputs["scaled"], inputs["hidden"] = arrays["scaled"], arrays["hidden"]
        inputs["reduced_in"], inputs["grads_in"] = arrays["reduced"], arrays["grads"]
        if not last:
            outputs.update(reduced=wide, grads=wide)
    if last:
        for name in ("attended", "gain"):
            inputs[name] = arrays[name]
        outputs.update(layer_out=narrow, grad_hidden=wide, grad_attended=narrow)
        scratch.update(
            reduced=pltpu.VMEM((rows, width), F32),
            grads=pltpu.VMEM((rows, width), F32),
            sums=pltpu.VMEM((8, width), F32),
            grad_mixed=pltpu.VMEM((rows, width), BF16),
            term=pltpu.VMEM((width, width), F32),
        )
    if first or last:
        for r in range(pieces):
            inputs[f"mixing{r}"] = mixings[r]
        scratch["mixing_all"] = pltpu.VMEM((width, width), BF16)
    scratch.update(
        up_tile=pltpu.VMEM((pieces // 2, width, 2 * TILE), BF16),
        down_tile=pltpu.VMEM((pieces // 2, 2 * TILE, width), BF16),
        up_sems=pltpu.SemaphoreType.DMA((pieces, pieces)),
        down_sems=pltpu.SemaphoreType.DMA((pieces,)),
        up_term=pltpu.VMEM((width, 2 * TILE), F32),
    )

    def spec(name, array):
        if name[:2] == "up" or name[:4] == "down" or (name == "hidden" and not (first or last)):
            return pl.BlockSpec(memory_space=pl.ANY)
        rank = len(array.shape)
        return pl.BlockSpec(
            array.shape, lambda i, *_: (0,) * rank, pipeline_mode=pl.Buffered(1)
        )

    results = pl.pallas_call(
        functools.partial(
            feed_kernel,
            pieces=pieces,
            chunk=chunk,
            chunks=chunks,
            names=(*inputs, *outputs, *scratch),
        ),
        grid_spec=pltpu.PrefetchScalarGridSpec(
            num_scalar_prefetch=1,
            grid=(pieces // 2,),
            in_specs=[spec(*one) for one in inputs.items()],
            out_specs=[spec(*one) for one in outputs.items()],
            scratch_shapes=list(scratch.values()),
        ),
        out_shape=list(outputs.values()),
        compiler_params=params("arbitrary"),
        cost_estimate=weight(),
        name=f"feed{chunk}",
    )(spot, *inputs.values())
    return {**arrays, **dict(zip(outputs, results))}


def query_kernel(spot_ref, scaled, *rest, pieces, seqs):
    grad_queries, weights = rest[:seqs], rest[seqs : seqs + pieces]
    grad_out, keep_out, send_out, weight, term = rest[seqs + pieces :]
    spot = spot_ref[0]
    rows = scaled.shape[0] // seqs
    place_rows(spot, weights, weight)
    for i, one in enumerate(grad_queries):
        here = slice(i * rows, (i + 1) * rows)
        part = dot_tn(scaled[here, :], one[...])
        term[...] = part if i == 0 else term[...] + part
        grad_out[here, :] = dot_nt(one[...], weight[...])
    split_out(spot, pieces, term, keep_out, send_out)


def query_stage(spot, scaled, grad_queries, weights, ctx_size):
    rows, width = scaled.shape
    pieces = len(weights)
    tall = round_up(width // pieces * (width // TILE), 8 * ctx_size)
    message = jax.ShapeDtypeStruct((pieces // 2, tall, TILE), BF16)
    return pl.pallas_call(
        functools.partial(query_kernel, pieces=pieces, seqs=len(grad_queries)),
        grid_spec=pltpu.PrefetchScalarGridSpec(
            num_scalar_prefetch=1,
            grid=(),
            in_specs=[pl.BlockSpec(memory_space=pltpu.VMEM)] * (1 + len(grad_queries) + pieces),
            out_specs=[pl.BlockSpec(memory_space=pltpu.VMEM)] * 3,
            scratch_shapes=[
                pltpu.VMEM((width, width), BF16),
                pltpu.VMEM((width, width), F32),
            ],
        ),
        out_shape=[jax.ShapeDtypeStruct((rows, width), F32), message, message],
        compiler_params=params(),
        cost_estimate=weight(),
        name="query_grad",
    )(spot, scaled, *grad_queries, *weights)


def last_kernel(spot_ref, tokens, gain, scaled, arrived, grad_scaled, grad_hidden, *rest, pieces):
    weights = rest[:pieces]
    input_grad, keep_out, send_out, weight, sums, term, grad_shared = rest[pieces:]
    spot = spot_ref[0]
    width = tokens.shape[1]
    place_rows(spot, weights, weight)
    sums[...] = jnp.zeros_like(sums)
    places, seqs, here, unused = arrived.shape
    for i in range(seqs):
        total = arrived[0, i].astype(F32)
        for j in range(1, places):
            total = total + arrived[j, i].astype(F32)
        grad_shared[i * here : (i + 1) * here, :] = total.astype(BF16)
    term[...] = dot_tn(scaled[...], grad_shared[...])
    split_out(spot, pieces, term, keep_out, send_out)

    def run(rows):
        normed, inverse = normalize(tokens[rows, :].astype(F32))
        grad = grad_scaled[rows, :] + dot_nt(grad_shared[rows, :], weight[...])
        sums[...] += jnp.sum((grad * normed).reshape(STEP // 8, 8, width), axis=0)
        input_grad[rows, :] = grad_hidden[rows, :] + norm_back(
            grad * gain[...], normed, inverse
        )

    over_rows(tokens.shape[0], run)
    put_vector(
        pieces, jnp.sum(sums[...], axis=0, keepdims=True), keep_out, send_out, 0, LANES
    )


def last_stage(spot, tokens, gain, scaled, arrived, grad_scaled, grad_hidden, weights):
    rows, width = tokens.shape
    pieces = len(weights)
    message = jax.ShapeDtypeStruct((pieces // 2, width // pieces, 2 * LANES), BF16)
    return pl.pallas_call(
        functools.partial(last_kernel, pieces=pieces),
        grid_spec=pltpu.PrefetchScalarGridSpec(
            num_scalar_prefetch=1,
            grid=(),
            in_specs=[pl.BlockSpec(memory_space=pltpu.VMEM)] * (6 + pieces),
            out_specs=[pl.BlockSpec(memory_space=pltpu.VMEM)] * 3,
            scratch_shapes=[
                pltpu.VMEM((width, LANES), BF16),
                pltpu.VMEM((8, width), F32),
                pltpu.VMEM((width, LANES), F32),
                pltpu.VMEM((rows, LANES), BF16),
            ],
        ),
        out_shape=[jax.ShapeDtypeStruct((rows, width), F32), message, message],
        compiler_params=params(),
        cost_estimate=weight(),
        name="last",
    )(spot, tokens, gain, scaled, arrived, grad_scaled, grad_hidden, *weights)


def final_kernel(place_ref, *refs, count, chunks, pieces, width):
    messages, refs = refs[:count], refs[count:]
    shared_sum, down_out, up_out, mixing_out, query_out, shared_out, first_out, second_out, whole = refs
    height = width // pieces
    groups = width // TILE
    low, high = place_ref[0] & 1, place_ref[0] >> 1

    def load(halves):
        deep, rows, unused = halves[0].shape
        for half, x in zip(halves, (low, 1 - low)):
            for k in range(deep):
                begin = pl.multiple_of((2 * (high ^ k) + x) * rows, 8)
                whole[pl.ds(begin, rows), :] = half[k].astype(F32)

    def columns(out, first_row, rows, out_row, step, across):
        for g in range(across):
            row = first_row + g * rows
            out[out_row : out_row + rows, g * step : g * step + TILE] = whole[row : row + rows, :]

    for chunk in range(chunks):
        load(messages[2 * chunk : 2 * chunk + 2])
        columns(down_out, 0, TILE, chunk * TILE, TILE, groups)
        for j in range(pieces):
            row = width + j * height
            column = (j * chunks + chunk) * TILE
            up_out[:, column : column + TILE] = whole[row : row + height, :]
    columns(mixing_out, 2 * width, height, 0, TILE, groups)
    row = 2 * width + groups * height
    second_out[...] = whole[row : row + second_out.shape[0], 0:LANES]
    load(messages[-2:])
    columns(query_out, 0, height, 0, TILE, groups)
    shared_out[...] = shared_sum[:, 0:LANES]
    first_out[...] = shared_sum[0 : first_out.shape[0], LANES:]


def final_stage(place, messages, shared_sum, chunks, pieces, width):
    height = width // pieces
    tallest = max(2 * one.shape[0] * one.shape[1] for one in messages)
    shape = lambda *dims: jax.ShapeDtypeStruct(dims, F32)
    vector = round_up(width // LANES, 8)
    return pl.pallas_call(
        functools.partial(
            final_kernel, count=len(messages), chunks=chunks, pieces=pieces, width=width
        ),
        grid_spec=pltpu.PrefetchScalarGridSpec(
            num_scalar_prefetch=1,
            grid=(),
            in_specs=[pl.BlockSpec(memory_space=pltpu.VMEM)] * (len(messages) + 1),
            out_specs=[pl.BlockSpec(memory_space=pltpu.VMEM)] * 7,
            scratch_shapes=[pltpu.VMEM((tallest, TILE), F32)],
        ),
        out_shape=[
            shape(chunks * TILE, width),
            shape(height, pieces * chunks * TILE),
            shape(height, width),
            shape(height, width),
            shape(height, LANES),
            shape(vector, LANES),
            shape(vector, LANES),
        ],
        compiler_params=params(),
        cost_estimate=weight(),
        name="final",
    )(place, *messages, shared_sum.reshape(height, 2 * LANES))


def swap(values, axis, size, mask):
    return lax.ppermute(values, axis, [(i, i ^ mask) for i in range(size)])


class Gather:
    def __init__(self, piece, size):
        self.size, self.own = size, piece
        self.far = swap(piece, "wt", size, 2)
        self.near = swap(piece, "wt", size, 1)

    def finish(self):
        return [self.own, self.near, self.far, swap(self.far, "wt", self.size, 1)]


def own_order(values, spot, size):
    mask = 1
    while mask < size:
        split = values.reshape((size // (2 * mask), 2, mask) + values.shape[1:])
        split = jnp.where((spot & mask) != 0, split[:, ::-1], split)
        values = split.reshape(values.shape)
        mask *= 2
    return values


class Reduction:
    def __init__(self, keep, send, place, sizes):
        self.wt_size, self.ctx_size = sizes
        self.groups = self.ctx_size // 2
        self.low, self.high = place & 1, place >> 1
        self.owners, self.rows, self.lanes = keep.shape
        split = (self.owners, self.groups, 2, self.rows // self.ctx_size, self.lanes)
        self.held = keep.reshape(split)
        self.sent = [send.reshape(split)]
        self.routes = [("wt", self.wt_size, 1)]
        self.coming = None

    def launch(self):
        if self.sent:
            self.coming = [swap(one, *route) for one, route in zip(self.sent, self.routes)]
            self.sent = []

    def add(self, pick):
        return pick(self.held).astype(F32) + pick(self.coming[0]).astype(F32)

    def y(self):
        self.held, self.sent = self.add(lambda v: v[0]), [self.add(lambda v: v[1]).astype(BF16)]
        self.routes = [("wt", self.wt_size, 2)]

    def x(self):
        low, axis = self.low, self.held.ndim - 3
        mine = lambda v: lax.dynamic_index_in_dim(v, low, axis, False)
        other = lambda v: lax.dynamic_index_in_dim(v, 1 - low, axis, False)
        self.held, self.sent = self.add(mine), [self.add(other).astype(BF16)]
        self.routes = [("ctx", self.ctx_size, 1)]

    def far(self):
        return [("ctx", self.ctx_size, 2 * k) for k in range(1, self.groups)]

    def z(self):
        pick = lambda k: lambda v: lax.dynamic_index_in_dim(v, self.high ^ k, 0, False)
        self.sent = [self.add(pick(k)).astype(BF16) for k in range(1, self.groups)]
        self.held = self.add(pick(0))
        self.routes = self.far()

    def total(self):
        parts = [self.held.astype(F32)] + [one.astype(F32) for one in self.coming]
        while len(parts) > 1:
            parts = [parts[i] + parts[i + 1] for i in range(0, len(parts), 2)]
        return parts[0]

    def z_back(self):
        self.held = self.total().astype(BF16)
        self.sent = [self.held] * (self.groups - 1)

    def x_back(self):
        self.held = jnp.stack([self.held] + self.coming)
        self.sent = [self.held]
        self.routes = [("ctx", self.ctx_size, 1)]

    def x_all(self):
        self.held = self.add(lambda v: v).astype(BF16)
        self.sent = [self.held]
        self.routes = [("ctx", self.ctx_size, 1)]

    def z_all(self):
        self.held = self.add(lambda v: v).astype(BF16)
        self.sent = [self.held] * (self.groups - 1)
        self.routes = self.far()


def tie(main, *reductions):
    state = [(one.held, one.sent) for one in reductions]
    main, state = lax.optimization_barrier((main, state))
    for one, (held, sent) in zip(reductions, state):
        one.held, one.sent = held, sent
        one.launch()
    return main


def shift(values, size, k):
    pairs = [(i, i + k) for i in range(size) if 0 <= i + k < size]
    return lax.ppermute(values, "ctx", pairs)


def body(
    tokens,
    documents,
    first_gain,
    query_weight,
    shared_weight,
    mixing_weight,
    second_gain,
    up_weight,
    down_weight,
    cotangent,
    *,
    wt_size,
    ctx_size,
):
    sizes = (wt_size, ctx_size)
    seqs, rows, width = tokens.shape
    count = seqs * rows
    spot_index = lax.axis_index("wt")
    place = lax.axis_index("ctx")
    spot = spot_index.astype(jnp.int32).reshape(1)
    length = ctx_size * rows
    doc_most = length * 5 // 8
    before = min(ctx_size - 1, -(-(doc_most - 1) // rows))
    blocks = before + 1
    height = width // wt_size
    chunks = up_weight.shape[1] // wt_size // TILE

    gain_rows = -(-height // LANES)
    pad = lambda gain: jnp.pad(gain, (0, gain_rows * LANES - height)).reshape(gain_rows, LANES)
    small = jnp.concatenate([shared_weight, pad(first_gain), pad(second_gain)], axis=0)
    small = jnp.pad(small, ((0, -small.shape[0] % 16), (0, 0)))
    small_pieces = Gather(small, wt_size).finish()
    query_gather = Gather(query_weight, wt_size)
    mixing_weight, small_pieces[2] = lax.optimization_barrier((mixing_weight, small_pieces[2]))
    mixing_gather = Gather(mixing_weight, wt_size)

    gains = jnp.stack([one[height : height + 2 * gain_rows] for one in small_pieces])
    gains = gains.reshape(wt_size, 2, gain_rows * LANES)[:, :, :height].astype(F32)
    gains = own_order(gains, spot_index, wt_size)
    gain_one = gains[:, 0].reshape(1, width)
    gain_two = gains[:, 1].reshape(1, width)

    inputs = tokens.reshape(count, width)
    scaled_one, shared = first_stage(spot, inputs, gain_one, small_pieces)
    keyvals = jnp.broadcast_to(
        shared.reshape(seqs, rows, 2 * HEAD_DIM), (ctx_size, seqs, rows, 2 * HEAD_DIM)
    )
    keyvals, documents = lax.optimization_barrier((keyvals, documents))
    keyvals = lax.all_to_all(keyvals, "ctx", 0, 0)
    scaled_late, up_weight, down_weight, query_gather.far, mixing_gather.far = (
        lax.optimization_barrier(
            (scaled_one, up_weight, down_weight, query_gather.far, mixing_gather.far)
        )
    )
    up_gather = Gather(up_weight, wt_size)
    down_gather = Gather(down_weight, wt_size)

    everywhere = jnp.broadcast_to(documents, (ctx_size, seqs, rows))
    everywhere = lax.all_to_all(everywhere, "ctx", 0, 0)
    starts = jnp.sum(
        (everywhere[:, :, None, :] < documents[None, :, :, None]).astype(jnp.int32), axis=(0, 3)
    )
    starts = starts - (place - before).astype(jnp.int32) * rows
    tile_rows = attention_sizes(rows, blocks)[0]
    firsts = starts[:, ::tile_rows]
    starts = jnp.broadcast_to(starts[:, :, None], (seqs, rows, LANES))

    query_pieces = query_gather.finish()
    queries = project(spot, scaled_one, query_pieces).reshape(seqs, rows, width)
    queries, mixing_gather.far = lax.optimization_barrier((queries, mixing_gather.far))
    mixing_pieces = mixing_gather.finish()
    place_one = place.astype(jnp.int32).reshape(1)

    exact, attended, logs = attend(firsts, place_one, queries, starts, keyvals, blocks)
    attended, up_gather.far, down_gather.far = lax.optimization_barrier(
        (attended, up_gather.far, down_gather.far)
    )
    up_pieces = up_gather.finish()
    down_pieces = down_gather.finish()

    arrays = {
        "attended": attended.reshape(count, width),
        "tokens": inputs,
        "gain": gain_two,
        "cotangent": cotangent.reshape(count, width),
    }
    feed = lambda chunk, arrays: feed_stage(
        spot, arrays, up_pieces, down_pieces, mixing_pieces, chunk, chunks, ctx_size
    )
    feeds = []
    for chunk in range(chunks):
        arrays = feed(chunk, arrays)
        feeds.append(Reduction(arrays["keep"], arrays["send"], place, sizes))
        if chunk == 0:
            arrays["scaled"] = tie(arrays["scaled"], *feeds)
        elif chunk < chunks - 1:
            arrays["scaled"] = tie(arrays["scaled"], *feeds)
            feeds[-2].y()
            arrays["scaled"] = tie(arrays["scaled"], *feeds)
    grad_attended = tie(arrays["grad_attended"], *feeds)
    feeds[0].x()
    feeds[1].y()
    grad_attended = tie(grad_attended, *feeds)
    grad_attended = grad_attended.reshape(seqs, rows, width)

    backs = []
    for seq in range(seqs):
        back = attend_back(
            seq, firsts, place_one, queries, starts, exact, logs, grad_attended, keyvals, blocks
        )
        back, grad_attended = tie((back, grad_attended), *feeds)
        backs.append(back)
        if seq == 0:
            feeds[0].z()
            feeds[1].x()
            feeds[2].y()
            grad_attended = tie(grad_attended, *feeds)
    grad_queries = [one[0][0] for one in backs]
    arriving = jnp.stack([one[1] for one in backs], axis=1)
    arriving, *grad_queries = tie((arriving, *grad_queries))
    arriving = lax.all_to_all(arriving, "ctx", 0, 0)
    feeds[0].z_back()
    feeds[1].z()
    grad_queries = tie(grad_queries, *feeds)
    grad_scaled, keep, send = query_stage(spot, scaled_late, grad_queries, query_pieces, ctx_size)
    query = Reduction(keep, send, place, sizes)
    grad_scaled = tie(grad_scaled, *feeds, query)
    feeds[2].x()
    query.y()
    grad_scaled = tie(grad_scaled, *feeds, query)
    input_grad, keep, send = last_stage(
        spot, inputs, gain_one, scaled_late, arriving, grad_scaled, arrays["grad_hidden"], small_pieces
    )
    shared = Reduction(keep, send, place, sizes)
    input_grad = tie(input_grad, *feeds, query, shared)
    feeds[2].z()
    shared.y()
    input_grad = tie(input_grad, *feeds, query, shared)
    feeds[1].z_back()
    query.x()
    shared.x_all()
    input_grad = tie(input_grad, *feeds, query, shared)
    feeds[2].z_back()
    query.z()
    input_grad = tie(input_grad, *feeds, query, shared)
    shared.z_all()
    feeds[0].x_back()
    feeds[1].x_back()
    input_grad = tie(input_grad, *feeds, query, shared)
    query.z_back()
    feeds[2].x_back()
    input_grad = tie(input_grad, *feeds, query, shared)
    query.x_back()
    query.launch()
    messages = []
    for one in (*feeds, query):
        messages += [one.held, one.coming[0]]
    down_grad, up_grad, mixing_grad, query_grad, shared_grad, first_grad, second_grad = final_stage(
        place_one, messages, shared.total(), chunks, wt_size, width
    )

    def own_gain(lines):
        vector = lines[: width // LANES].reshape(width)
        return lax.dynamic_slice_in_dim(vector, spot_index * height, height, 0)

    return (
        arrays["layer_out"].reshape(seqs, rows, width),
        input_grad.reshape(seqs, rows, width),
        own_gain(first_grad),
        query_grad,
        shared_grad,
        mixing_grad,
        own_gain(second_grad),
        up_grad,
        down_grad,
    )


def solution(mesh):
    in_specs = (
        P("wt", "ctx", None),
        P("wt", "ctx"),
        P("wt"),
        P("wt", None),
        P("wt", None),
        P("wt", None),
        P("wt"),
        P("wt", None),
        P("wt", None),
        P("wt", "ctx", None),
    )
    out_specs = (
        P("wt", "ctx", None),
        P("wt", "ctx", None),
        P("wt"),
        P("wt", None),
        P("wt", None),
        P("wt", None),
        P("wt"),
        P("wt", None),
        P("wt", None),
    )
    run = functools.partial(body, wt_size=mesh.shape["wt"], ctx_size=mesh.shape["ctx"])
    return jax.shard_map(run, mesh=mesh, in_specs=in_specs, out_specs=out_specs, check_vma=False)
```

time: 438 us -> 368 us (0.84)
  waiting for transfers between devices: 193 us -> 128 us
  starting transfers between devices: 122 us -> 90.3 us
  other arithmetic: 8.17 us -> 23.7 us
  blocking collectives: 0 us -> 12.7 us
    ppermute x15 -> x0, waiting for transfers between devices: 46.1 us -> none  [shift(): return lax.ppermute(values, 'ctx', pairs)]
    ppermute x15 -> x0, starting transfers between devices: 37 us -> none  [shift(): return lax.ppermute(values, 'ctx', pairs)]
    ppermute x75 -> x61, waiting for transfers between devices: 146 us -> 123 us  [swap(): return lax.ppermute(values, axis, [(i, i ^ mask) for i in range(size)])]
    convert_element_type x13 -> x19, other arithmetic: 2.33 us -> 19.2 us  [the longest x5 8.67 us: y(): self.add(lambda v: v[1]).astype(BF16)]
    all_to_all x0 -> x1, blocking collectives: none -> 12.7 us  [body(): everywhere = lax.all_to_all(everywhere, 'ctx', 0, 0)]
    pallas_call x3, Pallas kernels: 40.2 us -> 48.2 us  [feed_stage(): pl.pallas_call(functools.partial(feed_kernel, pieces=pieces, chunk=chunk,...]
    all_to_all x0 -> x2, starting transfers between devices: none -> 7.8 us  [the longest x1 4.25 us: body(): arriving = lax.all_to_all(arriving, 'ctx', 0, 0)]
    optimization_barrier x0 -> x4, local copies, waits for them, and re-layouts: none -> 7.45 us  [tie(): main, state = lax.optimization_barrier((main, state))]
  transfers between devices with their start and end apart: 90 -> 63, of which waited for: 43 -> 33; matrix products, arithmetic and copies ran while one was open for 3% -> 8% of each run, Pallas kernels for 6% -> 19%
where the time goes in v2:
time: 368 us; the launch traced here: 367 us
  waiting for transfers between devices  128 us (35%)
  Pallas kernels  93.5 us (25%)
  starting transfers between devices  90.3 us (25%)
  other arithmetic  23.7 us (6%)
  local copies, waits for them, and re-layouts  17.9 us (5%)
  blocking collectives  12.7 us (3%)
    ppermute x61, waiting for transfers between devices, swap(): return lax.ppermute(values, axis, [(i, i ^ mask) for i in range(size)])  123 us
    ppermute x61, starting transfers between devices, swap(): return lax.ppermute(values, axis, [(i, i ^ mask) for i in range(size)])  82.5 us
    pallas_call x3, Pallas kernels, feed_stage(): pl.pallas_call(functools.partial(feed_kernel, pieces=pieces, chunk=chunk,...  48.2 us
    pallas_call x2, Pallas kernels, attend_back(): pl.pallas_call(functools.partial(attend_back_kernel, seq=seq, blocks=bloc...  14.1 us
    all_to_all x1, blocking collectives, body(): everywhere = lax.all_to_all(everywhere, 'ctx', 0, 0)  12.7 us
    convert_element_type x5, other arithmetic, y(): self.add(lambda v: v[1]).astype(BF16)  8.67 us
    pallas_call x1, Pallas kernels, attend(): pl.pallas_call(functools.partial(attend_kernel, blocks=blocks, tile_rows=...  8.66 us
    optimization_barrier x4, local copies, waits for them, and re-layouts, tie(): main, state = lax.optimization_barrier((main, state))  7.45 us
  transfers between devices with their start and end apart: 63, of which 33 were waited for; matrix products, arithmetic and copies ran while one was open for 8% of the time, Pallas kernels for 19%

profile of v2, /device:TPU:0, one launch (start us, length us, event | category | flops | bytes accessed | tf_op | source)
XLA Modules:
  0.0 367.3 jit_solution(23849018464005630)
XLA Ops:
  2.1 3.0 collective-permute-start.1
  9.3 3.5 first_norm.1
  12.8 2.2 broadcast_in_dim.6
  15.1 12.7 %all_to_all.15 = s32[8,2,256]{2,1,0:T(2,128)S(1)} all-to-all(s32[8,2,256]{2,1,0:T(2,128)S(1)} %broadcast_in_dim.7), channel_id=1, replica_groups=mesh['ctx'=8,'wt'=4] {'ctx'}, dimensions={0} | all-to-all | bytes 32768 | tf_op jit(solution)/shard_map/all_to_all | solution.py:1015
  27.7 3.6 all-to-all-start.1
  33.4 8.1 %collective-permute-done.3.rest_2_.rest_4_ = bf16[192,768]{1,0:T(8,128)(2,1)S(1)} collective-permute-done((bf16[192,768]{1,0:T(8,128)(2,1)}, bf16[192,768]{1,0:T(8,128)(2,1)S(1)}, u32[]{:S(2)}, u32[]{:S(2)}) %collective-permute-start.3) | collective-permute-done | bytes 294944 | tf_op jit(solution)/shard_map/ppermute | solution.py:853
  41.5 4.1 %collective-permute-done.4.refs_14_.refs_17_ = bf16[192,768]{1,0:T(8,128)(2,1)} collective-permute-done((bf16[192,768]{1,0:T(8,128)(2,1)}, bf16[192,768]{1,0:T(8,128)(2,1)}, u32[]{:S(2)}, u32[]{:S(2)}) %collective-permute-start.4) | collective-permute-done | bytes 294944 | tf_op jit(solution)/shard_map/ppermute | solution.py:853
  50.0 3.2 project.1
  53.3 3.1 all-to-all-done.1.keyvals
  57.4 8.7 %attend.1 = (f32[2,256,768]{2,1,0:T(8,128)}, bf16[2,256,768]{2,1,0:T(8,128)(2,1)}, f32[2,256,768]{2,1,0:T(8,128)}) custom-call(s32[2,2]{1,0:T(2,128)} %slice.95.first_ref, s32[1]{0:T(128)} %bitcast.9.place_ref, bf16[2,256,768]{2,1,0:T(8,128)(2,1)} %bitcast.122, s32[2,256,128]{2,1,0:T(8,128)} %broadcast_in_dim.16.starts, bf16[8,2,256,128]{3,2,1,0:T(8,128)(2,1)} %copy-done), custom_call_target="tpu_custom_call" | custom-call | flops 1 | bytes 1 | tf_op jit(solution)/shard_map/attend/pallas_call | solution.py:360
  66.1 8.6 %collective-permute-done.10.refs_6_ = bf16[768,768]{1,0:T(8,128)(2,1)} collective-permute-done((bf16[768,768]{1,0:T(8,128)(2,1)S(1)}, bf16[768,768]{1,0:T(8,128)(2,1)}, u32[]{:S(2)}, u32[]{:S(2)}) %collective-permute-start.10) | collective-permute-done | bytes 1179680 | tf_op jit(solution)/shard_map/ppermute | solution.py:853
  74.7 22.1 %collective-permute-done.9.refs_5_ = bf16[192,3072]{1,0:T(8,128)(2,1)} collective-permute-done((bf16[192,3072]{1,0:T(8,128)(2,1)S(1)}, bf16[192,3072]{1,0:T(8,128)(2,1)}, u32[]{:S(2)}, u32[]{:S(2)}) %collective-permute-start.9) | collective-permute-done | bytes 1179680 | tf_op jit(solution)/shard_map/ppermute | solution.py:853
  97.2 3.2 collective-permute-done.13.refs_13_.refs_16_
  103.0 14.5 %feed0.1 = (bf16[2,1536,256]{2,1,0:T(8,128)(2,1)}, bf16[2,1536,256]{2,1,0:T(8,128)(2,1)}, f32[512,768]{1,0:T(8,128)}, bf16[512,768]{1,0:T(8,128)(2,1)}, f32[512,768]{1,0:T(8,128)}, /*index=5*/f32[512,768]{1,0:T(8,128)}) custom-call(s32[1]{0:T(128)} %bitcast.spot_ref, bf16[512,768]{1,0:T(8,128)(2,1)} %bitcast.125, bf16[192,3072]{1,0:T(8,128)(2,1)} %refs_1_.2, ...), custom_call_target="tpu_custom_call" | custom-call | flops 1 | bytes 1 | tf_op jit(solution)/shard_map/feed0/pallas_call | solution.py:670
  119.3 14.0 %feed1.1 = (bf16[2,1536,256]{2,1,0:T(8,128)(2,1)}, bf16[2,1536,256]{2,1,0:T(8,128)(2,1)}, f32[512,768]{1,0:T(8,128)}, f32[512,768]{1,0:T(8,128)}) custom-call(s32[1]{0:T(128)} %bitcast.spot_ref, bf16[512,768]{1,0:T(8,128)(2,1)} %bitcast.126, bf16[192,3072]{1,0:T(8,128)(2,1)} %refs_1_.2, bf16[768,768]{1,0:T(8,128)(2,1)} %refs_2_.2, ...), custom_call_target="tpu_custom_call" | custom-call | flops 1 | bytes 1 | tf_op jit(solution)/shard_map/feed1/pallas_call | solution.py:670
  136.6 19.7 %feed2.1 = (bf16[2,2176,256]{2,1,0:T(8,128)(2,1)}, bf16[2,2176,256]{2,1,0:T(8,128)(2,1)}, bf16[512,768]{1,0:T(8,128)(2,1)}, f32[512,768]{1,0:T(8,128)}, bf16[512,768]{1,0:T(8,128)(2,1)}) custom-call(s32[1]{0:T(128)} %bitcast.spot_ref, bf16[512,768]{1,0:T(8,128)(2,1)} %bitcast.127, bf16[192,3072]{1,0:T(8,128)(2,1)} %refs_1_.2, bf16[768,768]{1,0:T(8,128)(2,1)} %refs_2_.2, ...), custom_call_target="tpu_custom_call" | custom-call | flops 1 | bytes 1 | tf_op jit(solution)/shard_map/feed2/pallas_call | solution.py:670
  156.3 3.1 copy.41
  161.2 3.1 fusion.2
  164.3 15.4 %collective-permute-done.16 = bf16[4,2,192,256]{3,2,0,1:T(8,128)(2,1)} collective-permute-done((bf16[4,2,192,256]{3,2,0,1:T(8,128)(2,1)}, bf16[4,2,192,256]{3,2,0,1:T(8,128)(2,1)}, u32[]{:S(2)}, u32[]{:S(2)}) %collective-permute-start.16) | collective-permute-done | bytes 786464 | tf_op jit(solution)/shard_map/ppermute | solution.py:853
  184.7 7.1 %attend_back.2 = (bf16[1,256,768]{2,1,0:T(8,128)(2,1)}, bf16[8,256,128]{2,1,0:T(8,128)(2,1)}) custom-call(s32[2,2]{1,0:T(2,128)} %slice.95.first_ref, s32[1]{0:T(128)} %bitcast.9.place_ref, bf16[2,256,768]{2,1,0:T(8,128)(2,1)} %bitcast.123, s32[2,256,128]{2,1,0:T(8,128)} %broadcast_in_dim.16.starts, f32[2,256,768]{2,1,0:T(8,128)} %get-tuple-element.225.exact, ...), custom_call_target="tpu_custom_call" | custom-call | flops 1 | bytes 1 | tf_op jit(solution)/shard_map/attend_back/pallas_call | solution.py:403
  193.6 7.4 %collective-permute-done.19 = bf16[4,2,192,256]{3,2,0,1:T(8,128)(2,1)} collective-permute-done((bf16[4,2,192,256]{3,2,0,1:T(8,128)(2,1)}, bf16[4,2,192,256]{3,2,0,1:T(8,128)(2,1)}, u32[]{:S(2)}, u32[]{:S(2)}) %collective-permute-start.19) | collective-permute-done | bytes 786464 | tf_op jit(solution)/shard_map/ppermute | solution.py:853
  203.2 3.2 fusion
  207.6 7.0 %attend_back.3 = (bf16[1,256,768]{2,1,0:T(8,128)(2,1)}, bf16[8,256,128]{2,1,0:T(8,128)(2,1)}) custom-call(s32[2,2]{1,0:T(2,128)} %slice.95.first_ref, s32[1]{0:T(128)} %bitcast.9.place_ref, bf16[2,256,768]{2,1,0:T(8,128)(2,1)} %bitcast.124, s32[2,256,128]{2,1,0:T(8,128)} %broadcast_in_dim.16.starts, f32[2,256,768]{2,1,0:T(8,128)} %get-tuple-element.225.exact, ...), custom_call_target="tpu_custom_call" | custom-call | flops 1 | bytes 1 | tf_op jit(solution)/shard_map/attend_back/pallas_call | solution.py:403
  214.6 3.7 %collective-permute-start.21 = (bf16[192,256]{1,0:T(8,128)(2,1)S(1)}, bf16[192,256]{1,0:T(8,128)(2,1)}, u32[]{:S(2)}, u32[]{:S(2)}) collective-permute-start(bf16[192,256]{1,0:T(8,128)(2,1)S(1)} %get-tuple-element.265), channel_id=1, source_target_pairs={{0,8},{4,12},{8,0},{12,4},{16,24},{20,28},{24,16},{28,20},{1,9},{5... | collective-permute-start | bytes 294920 | tf_op jit(solution)/shard_map/ppermute | solution.py:853
  218.3 5.7 %collective-permute-start.22 = (bf16[192,256]{1,0:T(8,128)(2,1)S(1)}, bf16[192,256]{1,0:T(8,128)(2,1)}, u32[]{:S(2)}, u32[]{:S(2)}) collective-permute-start(bf16[192,256]{1,0:T(8,128)(2,1)S(1)} %get-tuple-element.266), channel_id=1, source_target_pairs={{0,16},{4,20},{8,24},{12,28},{16,0},{20,4},{24,8},{28,12},{1,17},{... | collective-permute-start | bytes 294920 | tf_op jit(solution)/shard_map/ppermute | solution.py:853
  227.1 3.5 collective-permute-start.25
  230.6 4.2 %all-to-all-start.2 = ((bf16[8,2,256,128]{3,2,1,0:T(8,128)(2,1)}), bf16[8,2,256,128]{3,2,1,0:T(8,128)(2,1)}, u32[]{:S(2)}, u32[]{:S(2)}) async-start(bf16[8,2,256,128]{3,2,1,0:T(8,128)(2,1)} %pad_maximum_fusion), calls=%async_computation.2 | async-start | bytes 2097152 | tf_op jit(solution)/shard_map/all_to_all | solution.py:1077
  238.3 4.6 %query_grad.1 = (f32[512,768]{1,0:T(8,128)}, bf16[2,576,256]{2,1,0:T(8,128)(2,1)}, bf16[2,576,256]{2,1,0:T(8,128)(2,1)}) custom-call(s32[1]{0:T(128)} %bitcast.spot_ref, bf16[512,768]{1,0:T(8,128)(2,1)} %get-tuple-element.224.operand.scaled, bf16[256,768]{1,0:T(8,128)(2,1)} %bitcast.149, bf16[256,768]{1,0:T(8,128)(2,1)} %bitcast.150, ...), custom_call_target="tpu_custom_call" | custom-call | flops 1 | bytes 1 | tf_op jit(solution)/shard_map/query_grad/pallas_call | solution.py:712
  247.3 8.5 %collective-permute-done.25 = bf16[4,2,272,256]{3,2,0,1:T(8,128)(2,1)} collective-permute-done((bf16[4,2,272,256]{3,2,0,1:T(8,128)(2,1)}, bf16[4,2,272,256]{3,2,0,1:T(8,128)(2,1)}, u32[]{:S(2)}, u32[]{:S(2)}) %collective-permute-start.25) | collective-permute-done | bytes 1114144 | tf_op jit(solution)/shard_map/ppermute | solution.py:853
  255.7 2.3 fusion.3
  260.0 6.2 %last.1 = (f32[512,768]{1,0:T(8,128)}, bf16[2,192,256]{2,1,0:T(8,128)(2,1)}, bf16[2,192,256]{2,1,0:T(8,128)(2,1)}) custom-call(s32[1]{0:T(128)} %bitcast.spot_ref, bf16[512,768]{1,0:T(8,128)(2,1)} %bitcast.130, f32[1,768]{1,0:T(1,128)} %reshape_squeeze.6.gain, bf16[512,768]{1,0:T(8,128)(2,1)} %get-tuple-element.224.operand.scaled, ...), custom_call_target="tpu_custom_call" | custom-call | flops 1 | bytes 1 | tf_op jit(solution)/shard_map/last/pallas_call | solution.py:765
  267.8 2.9 collective-permute-start.31
  273.1 3.4 collective-permute-start.39
  278.8 3.3 collective-permute-start.34
  282.1 3.4 collective-permute-start.35
  287.3 2.3 collective-permute-start.37
  289.6 5.0 %collective-permute-done.35 = bf16[272,256]{1,0:T(8,128)(2,1)S(1)} collective-permute-done((bf16[272,256]{1,0:T(8,128)(2,1)S(1)}, bf16[272,256]{1,0:T(8,128)(2,1)S(1)}, u32[]{:S(2)}, u32[]{:S(2)}) %collective-permute-start.35) | collective-permute-done | bytes 139296 | tf_op jit(solution)/shard_map/ppermute | solution.py:853
  303.2 4.0 %collective-permute-done.42 = bf16[192,256]{1,0:T(8,128)(2,1)S(1)} collective-permute-done((bf16[192,256]{1,0:T(8,128)(2,1)S(1)}, bf16[192,256]{1,0:T(8,128)(2,1)S(1)}, u32[]{:S(2)}, u32[]{:S(2)}) %collective-permute-start.42) | collective-permute-done | bytes 98336 | tf_op jit(solution)/shard_map/ppermute | solution.py:853
  307.3 4.2 %collective-permute-start.49 = (bf16[72,256]{1,0:T(8,128)(2,1)S(1)}, bf16[72,256]{1,0:T(8,128)(2,1)S(1)}, u32[]{:S(2)}, u32[]{:S(2)}) collective-permute-start(bf16[72,256]{1,0:T(8,128)(2,1)S(1)} %get-tuple-element.346), channel_id=1, source_target_pairs={{0,16},{4,20},{8,24},{12,28},{16,0},{20,4},{24,8},{28,12},{1,17},{... | collective-permute-start | bytes 110600 | tf_op jit(solution)/shard_map/ppermute | solution.py:853
  313.8 2.5 collective-permute-start.46
  318.1 3.6 collective-permute-done.45
  321.7 3.2 collective-permute-done.46
  325.0 2.5 collective-permute-start.53
  332.1 2.3 collective-permute-start.55
  337.0 2.5 collective-permute-start.59
  340.2 2.3 collective-permute-start.60
  347.4 11.2 %collective-permute-done.57.refs_7_ = bf16[4,72,256]{2,1,0:T(8,128)(2,1)S(1)} collective-permute-done((bf16[4,72,256]{2,1,0:T(8,128)(2,1)S(1)}, bf16[4,72,256]{2,1,0:T(8,128)(2,1)S(1)}, u32[]{:S(2)}, u32[]{:S(2)}) %collective-permute-start.57) | collective-permute-done | bytes 147488 | tf_op jit(solution)/shard_map/ppermute | solution.py:853
  359.7 5.0 %final.1 = (f32[768,768]{1,0:T(8,128)}, f32[192,3072]{1,0:T(8,128)}, f32[192,768]{1,0:T(8,128)}, f32[192,768]{1,0:T(8,128)}, f32[192,128]{1,0:T(8,128)}, /*index=5*/f32[8,128]{1,0:T(8,128)}, f32[8,128]{1,0:T(8,128)}) custom-call(s32[1]{0:T(128)} %bitcast.9.place_ref, bf16[4,192,256]{2,1,0:T(8,128)(2,1)} %copy-done.9, bf16[4,192,256]{2,1,0:T(8,128)(2,1)} %copy-done.20, ...), custom_call_target="tpu_custom_call" | custom-call | flops 1 | bytes 1 | tf_op jit(solution)/shard_map/final/pallas_call | solution.py:826
  (210 shorter events, 83.2 us)
Async XLA Ops:
  27.7 28.6 %all-to-all-start.1 = ((bf16[8,2,256,128]{3,2,1,0:T(8,128)(2,1)}), bf16[8,2,256,128]{3,2,1,0:T(8,128)(2,1)S(1)}, u32[]{:S(2)}, u32[]{:S(2)}) async-start(bf16[8,2,256,128]{3,2,1,0:T(8,128)(2,1)} %broadcast_in_dim.6), calls=%async_computation.1 | async-start | bytes 2097152 | tf_op jit(solution)/shard_map/all_to_all | solution.py:1005
  31.3 10.2 %collective-permute-start.3 = (bf16[192,768]{1,0:T(8,128)(2,1)}, bf16[192,768]{1,0:T(8,128)(2,1)S(1)}, u32[]{:S(2)}, u32[]{:S(2)}) collective-permute-start(bf16[192,768]{1,0:T(8,128)(2,1)} %rest_2_.1), channel_id=1, source_target_pairs={{0,2},{1,3},{2,0},{3,1},{4,6},{5,7},{6,4},{7,5},{8,10},{9,11},{10,... | collective-permute-start | bytes 884744 | tf_op jit(solution)/shard_map/ppermute | solution.py:853
  32.9 12.8 %collective-permute-start.4 = (bf16[192,768]{1,0:T(8,128)(2,1)}, bf16[192,768]{1,0:T(8,128)(2,1)}, u32[]{:S(2)}, u32[]{:S(2)}) collective-permute-start(bf16[192,768]{1,0:T(8,128)(2,1)} %refs_15_), channel_id=1, source_target_pairs={{0,2},{1,3},{2,0},{3,1},{4,6},{5,7},{6,4},{7,5},{8,10},{9,11},{10,... | collective-permute-start | bytes 884744 | tf_op jit(solution)/shard_map/ppermute | solution.py:853
  45.7 29.0 %collective-permute-start.10 = (bf16[768,768]{1,0:T(8,128)(2,1)S(1)}, bf16[768,768]{1,0:T(8,128)(2,1)}, u32[]{:S(2)}, u32[]{:S(2)}) collective-permute-start(bf16[768,768]{1,0:T(8,128)(2,1)S(1)} %copy-done.2), channel_id=1, source_target_pairs={{0,2},{1,3},{2,0},{3,1},{4,6},{5,7},{6,4},{7,5},{8,10},{9,11},{10,... | collective-permute-start | bytes 3538952 | tf_op jit(solution)/shard_map/ppermute | solution.py:853
  47.2 49.5 %collective-permute-start.9 = (bf16[192,3072]{1,0:T(8,128)(2,1)S(1)}, bf16[192,3072]{1,0:T(8,128)(2,1)}, u32[]{:S(2)}, u32[]{:S(2)}) collective-permute-start(bf16[192,3072]{1,0:T(8,128)(2,1)S(1)} %copy-done.1), channel_id=1, source_target_pairs={{0,2},{1,3},{2,0},{3,1},{4,6},{5,7},{6,4},{7,5},{8,10},{9,11},{10,... | collective-permute-start | bytes 3538952 | tf_op jit(solution)/shard_map/ppermute | solution.py:853
  49.5 52.9 %collective-permute-start.5 = (bf16[192,3072]{1,0:T(8,128)(2,1)S(1)}, bf16[192,3072]{1,0:T(8,128)(2,1)}, u32[]{:S(2)}, u32[]{:S(2)}) collective-permute-start(bf16[192,3072]{1,0:T(8,128)(2,1)S(1)} %copy-done.1), channel_id=1, source_target_pairs={{0,1},{1,0},{2,3},{3,2},{4,5},{5,4},{6,7},{7,6},{8,9},{9,8},{10,11... | collective-permute-start | bytes 3538952 | tf_op jit(solution)/shard_map/ppermute | solution.py:853
  49.6 52.7 %collective-permute-start.6 = (bf16[768,768]{1,0:T(8,128)(2,1)S(1)}, bf16[768,768]{1,0:T(8,128)(2,1)}, u32[]{:S(2)}, u32[]{:S(2)}) collective-permute-start(bf16[768,768]{1,0:T(8,128)(2,1)S(1)} %copy-done.2), channel_id=1, source_target_pairs={{0,1},{1,0},{2,3},{3,2},{4,5},{5,4},{6,7},{7,6},{8,9},{9,8},{10,11... | collective-permute-start | bytes 3538952 | tf_op jit(solution)/shard_map/ppermute | solution.py:853
  119.1 16.2 %collective-permute-start.15 = (bf16[2,4,2,192,256]{4,3,1,2,0:T(8,128)(2,1)S(1)}, bf16[2,4,2,192,256]{4,3,1,2,0:T(8,128)(2,1)S(1)}, u32[]{:S(2)}, u32[]{:S(2)}) collective-permute-start(bf16[2,4,2,192,256]{4,3,1,2,0:T(8,128)(2,1)S(1)} %copy.35), channel_id=1, source_target_pairs={{0,1},{1,0},{2,3},{3,2},{4,5},{5,4},{6,7},{7,6},{8,9},{9,8},{10,11... | collective-permute-start | bytes 4718600 | tf_op jit(solution)/shard_map/ppermute | solution.py:853
  135.0 26.2 %collective-permute-start.17 = (bf16[2,4,2,192,256]{4,3,1,2,0:T(8,128)(2,1)S(1)}, bf16[2,4,2,192,256]{4,3,1,2,0:T(8,128)(2,1)}, u32[]{:S(2)}, u32[]{:S(2)}) collective-permute-start(bf16[2,4,2,192,256]{4,3,1,2,0:T(8,128)(2,1)S(1)} %copy.38), channel_id=1, source_target_pairs={{0,1},{1,0},{2,3},{3,2},{4,5},{5,4},{6,7},{7,6},{8,9},{9,8},{10,11... | collective-permute-start | bytes 4718600 | tf_op jit(solution)/shard_map/ppermute | solution.py:853
  159.4 43.8 %collective-permute-start.20 = (bf16[2,4,2,272,256]{4,3,1,2,0:T(8,128)(2,1)}, bf16[2,4,2,272,256]{4,3,1,2,0:T(8,128)(2,1)}, u32[]{:S(2)}, u32[]{:S(2)}) collective-permute-start(bf16[2,4,2,272,256]{4,3,1,2,0:T(8,128)(2,1)} %copy.41), channel_id=1, source_target_pairs={{0,1},{1,0},{2,3},{3,2},{4,5},{5,4},{6,7},{7,6},{8,9},{9,8},{10,11... | collective-permute-start | bytes 6684680 | tf_op jit(solution)/shard_map/ppermute | solution.py:853
  159.6 20.0 %collective-permute-start.16 = (bf16[4,2,192,256]{3,2,0,1:T(8,128)(2,1)}, bf16[4,2,192,256]{3,2,0,1:T(8,128)(2,1)}, u32[]{:S(2)}, u32[]{:S(2)}) collective-permute-start(bf16[4,2,192,256]{3,2,0,1:T(8,128)(2,1)} %get-tuple-element.234), channel_id=1, source_target_pairs={{0,2},{1,3},{2,0},{3,1},{4,6},{5,7},{6,4},{7,5},{8,10},{9,11},{10,... | collective-permute-start | bytes 2359304 | tf_op jit(solution)/shard_map/ppermute | solution.py:853
  181.8 19.2 %collective-permute-start.19 = (bf16[4,2,192,256]{3,2,0,1:T(8,128)(2,1)}, bf16[4,2,192,256]{3,2,0,1:T(8,128)(2,1)}, u32[]{:S(2)}, u32[]{:S(2)}) collective-permute-start(bf16[4,2,192,256]{3,2,0,1:T(8,128)(2,1)} %get-tuple-element.249), channel_id=1, source_target_pairs={{0,2},{1,3},{2,0},{3,1},{4,6},{5,7},{6,4},{7,5},{8,10},{9,11},{10,... | collective-permute-start | bytes 2359304 | tf_op jit(solution)/shard_map/ppermute | solution.py:853
  183.4 10.2 %collective-permute-start.18 = (bf16[4,192,256]{2,1,0:T(8,128)(2,1)S(1)}, bf16[4,192,256]{2,1,0:T(8,128)(2,1)S(1)}, u32[]{:S(2)}, u32[]{:S(2)}) collective-permute-start(bf16[4,192,256]{2,1,0:T(8,128)(2,1)S(1)} %get-tuple-element.247), channel_id=1, source_target_pairs={{0,4},{4,0},{8,12},{12,8},{16,20},{20,16},{24,28},{28,24},{1,5},{5... | collective-permute-start | bytes 1179656 | tf_op jit(solution)/shard_map/ppermute | solution.py:853
  206.3 30.2 %collective-permute-start.24 = (bf16[4,192,256]{2,1,0:T(8,128)(2,1)}, bf16[4,192,256]{2,1,0:T(8,128)(2,1)}, u32[]{:S(2)}, u32[]{:S(2)}) collective-permute-start(bf16[4,192,256]{2,1,0:T(8,128)(2,1)} %get-tuple-element.269), channel_id=1, source_target_pairs={{0,4},{4,0},{8,12},{12,8},{16,20},{20,16},{24,28},{28,24},{1,5},{5... | collective-permute-start | bytes 1179656 | tf_op jit(solution)/shard_map/ppermute | solution.py:853
  214.6 20.2 %collective-permute-start.21 = (bf16[192,256]{1,0:T(8,128)(2,1)S(1)}, bf16[192,256]{1,0:T(8,128)(2,1)}, u32[]{:S(2)}, u32[]{:S(2)}) collective-permute-start(bf16[192,256]{1,0:T(8,128)(2,1)S(1)} %get-tuple-element.265), channel_id=1, source_target_pairs={{0,8},{4,12},{8,0},{12,4},{16,24},{20,28},{24,16},{28,20},{1,9},{5... | collective-permute-start | bytes 294920 | tf_op jit(solution)/shard_map/ppermute | solution.py:853
  218.3 16.5 %collective-permute-start.22 = (bf16[192,256]{1,0:T(8,128)(2,1)S(1)}, bf16[192,256]{1,0:T(8,128)(2,1)}, u32[]{:S(2)}, u32[]{:S(2)}) collective-permute-start(bf16[192,256]{1,0:T(8,128)(2,1)S(1)} %get-tuple-element.266), channel_id=1, source_target_pairs={{0,16},{4,20},{8,24},{12,28},{16,0},{20,4},{24,8},{28,12},{1,17},{... | collective-permute-start | bytes 294920 | tf_op jit(solution)/shard_map/ppermute | solution.py:853
  224.1 10.8 %collective-permute-start.23 = (bf16[192,256]{1,0:T(8,128)(2,1)S(1)}, bf16[192,256]{1,0:T(8,128)(2,1)}, u32[]{:S(2)}, u32[]{:S(2)}) collective-permute-start(bf16[192,256]{1,0:T(8,128)(2,1)S(1)} %get-tuple-element.267), channel_id=1, source_target_pairs={{0,24},{4,28},{8,16},{12,20},{16,8},{20,12},{24,0},{28,4},{1,25},{... | collective-permute-start | bytes 294920 | tf_op jit(solution)/shard_map/ppermute | solution.py:853
  227.1 28.6 %collective-permute-start.25 = (bf16[4,2,272,256]{3,2,0,1:T(8,128)(2,1)}, bf16[4,2,272,256]{3,2,0,1:T(8,128)(2,1)}, u32[]{:S(2)}, u32[]{:S(2)}) collective-permute-start(bf16[4,2,272,256]{3,2,0,1:T(8,128)(2,1)} %get-tuple-element.283), channel_id=1, source_target_pairs={{0,2},{1,3},{2,0},{3,1},{4,6},{5,7},{6,4},{7,5},{8,10},{9,11},{10,... | collective-permute-start | bytes 3342344 | tf_op jit(solution)/shard_map/ppermute | solution.py:853
  230.6 29.4 %all-to-all-start.2 = ((bf16[8,2,256,128]{3,2,1,0:T(8,128)(2,1)}), bf16[8,2,256,128]{3,2,1,0:T(8,128)(2,1)}, u32[]{:S(2)}, u32[]{:S(2)}) async-start(bf16[8,2,256,128]{3,2,1,0:T(8,128)(2,1)} %pad_maximum_fusion), calls=%async_computation.2 | async-start | bytes 2097152 | tf_op jit(solution)/shard_map/all_to_all | solution.py:1077
  258.0 14.3 %collective-permute-start.27 = (bf16[4,272,256]{2,1,0:T(8,128)(2,1)}, bf16[4,272,256]{2,1,0:T(8,128)(2,1)S(1)}, u32[]{:S(2)}, u32[]{:S(2)}) collective-permute-start(bf16[4,272,256]{2,1,0:T(8,128)(2,1)} %get-tuple-element.299), channel_id=1, source_target_pairs={{0,4},{4,0},{8,12},{12,8},{16,20},{20,16},{24,28},{28,24},{1,5},{5... | collective-permute-start | bytes 1671176 | tf_op jit(solution)/shard_map/ppermute | solution.py:853
  266.2 6.8 %collective-permute-start.28 = (bf16[2,4,2,24,256]{4,3,2,1,0:T(8,128)(2,1)}, bf16[2,4,2,24,256]{4,3,2,1,0:T(8,128)(2,1)S(1)}, u32[]{:S(2)}, u32[]{:S(2)}) collective-permute-start(bf16[2,4,2,24,256]{4,3,2,1,0:T(8,128)(2,1)} %bitcast.170), channel_id=1, source_target_pairs={{0,1},{1,0},{2,3},{3,2},{4,5},{5,4},{6,7},{7,6},{8,9},{9,8},{10,11... | collective-permute-start | bytes 589832 | tf_op jit(solution)/shard_map/ppermute | solution.py:853
  266.3 6.9 %collective-permute-start.29 = (bf16[192,256]{1,0:T(8,128)(2,1)S(1)}, bf16[192,256]{1,0:T(8,128)(2,1)S(1)}, u32[]{:S(2)}, u32[]{:S(2)}) collective-permute-start(bf16[192,256]{1,0:T(8,128)(2,1)S(1)} %copy-done.30), channel_id=1, source_target_pairs={{0,8},{4,12},{8,0},{12,4},{16,24},{20,28},{24,16},{28,20},{1,9},{5... | collective-permute-start | bytes 294920 | tf_op jit(solution)/shard_map/ppermute | solution.py:853
  266.4 11.5 %collective-permute-start.30 = (bf16[192,256]{1,0:T(8,128)(2,1)S(1)}, bf16[192,256]{1,0:T(8,128)(2,1)S(1)}, u32[]{:S(2)}, u32[]{:S(2)}) collective-permute-start(bf16[192,256]{1,0:T(8,128)(2,1)S(1)} %copy-done.29), channel_id=1, source_target_pairs={{0,16},{4,20},{8,24},{12,28},{16,0},{20,4},{24,8},{28,12},{1,17},{... | collective-permute-start | bytes 294920 | tf_op jit(solution)/shard_map/ppermute | solution.py:853
  267.8 10.9 %collective-permute-start.31 = (bf16[192,256]{1,0:T(8,128)(2,1)S(1)}, bf16[192,256]{1,0:T(8,128)(2,1)S(1)}, u32[]{:S(2)}, u32[]{:S(2)}) collective-permute-start(bf16[192,256]{1,0:T(8,128)(2,1)S(1)} %copy-done.28), channel_id=1, source_target_pairs={{0,24},{4,28},{8,16},{12,20},{16,8},{20,12},{24,0},{28,4},{1,25},{... | collective-permute-start | bytes 294920 | tf_op jit(solution)/shard_map/ppermute | solution.py:853
  272.3 39.4 %collective-permute-start.38 = (bf16[192,256]{1,0:T(8,128)(2,1)S(1)}, bf16[192,256]{1,0:T(8,128)(2,1)S(1)}, u32[]{:S(2)}, u32[]{:S(2)}) collective-permute-start(bf16[192,256]{1,0:T(8,128)(2,1)S(1)} %copy-done.19), channel_id=1, source_target_pairs={{0,8},{4,12},{8,0},{12,4},{16,24},{20,28},{24,16},{28,20},{1,9},{5... | collective-permute-start | bytes 294920 | tf_op jit(solution)/shard_map/ppermute | solution.py:853
  273.0 9.1 %collective-permute-start.32 = (bf16[4,2,72,256]{3,2,0,1:T(8,128)(2,1)S(1)}, bf16[4,2,72,256]{3,2,0,1:T(8,128)(2,1)S(1)}, u32[]{:S(2)}, u32[]{:S(2)}) collective-permute-start(bf16[4,2,72,256]{3,2,0,1:T(8,128)(2,1)S(1)} %copy-done.22), channel_id=1, source_target_pairs={{0,2},{1,3},{2,0},{3,1},{4,6},{5,7},{6,4},{7,5},{8,10},{9,11},{10,... | collective-permute-start | bytes 884744 | tf_op jit(solution)/shard_map/ppermute | solution.py:853
  273.1 40.3 %collective-permute-start.39 = (bf16[192,256]{1,0:T(8,128)(2,1)S(1)}, bf16[192,256]{1,0:T(8,128)(2,1)S(1)}, u32[]{:S(2)}, u32[]{:S(2)}) collective-permute-start(bf16[192,256]{1,0:T(8,128)(2,1)S(1)} %copy-done.19), channel_id=1, source_target_pairs={{0,16},{4,20},{8,24},{12,28},{16,0},{20,4},{24,8},{28,12},{1,17},{... | collective-permute-start | bytes 294920 | tf_op jit(solution)/shard_map/ppermute | solution.py:853
  277.8 7.7 %collective-permute-start.33 = (bf16[4,2,24,256]{3,2,1,0:T(8,128)(2,1)S(1)}, bf16[4,2,24,256]{3,2,1,0:T(8,128)(2,1)S(1)}, u32[]{:S(2)}, u32[]{:S(2)}) collective-permute-start(bf16[4,2,24,256]{3,2,1,0:T(8,128)(2,1)S(1)} %get-tuple-element.313), channel_id=1, source_target_pairs={{0,2},{1,3},{2,0},{3,1},{4,6},{5,7},{6,4},{7,5},{8,10},{9,11},{10,... | collective-permute-start | bytes 294920 | tf_op jit(solution)/shard_map/ppermute | solution.py:853
  278.8 8.6 %collective-permute-start.34 = (bf16[272,256]{1,0:T(8,128)(2,1)S(1)}, bf16[272,256]{1,0:T(8,128)(2,1)S(1)}, u32[]{:S(2)}, u32[]{:S(2)}) collective-permute-start(bf16[272,256]{1,0:T(8,128)(2,1)S(1)} %get-tuple-element.318), channel_id=1, source_target_pairs={{0,8},{4,12},{8,0},{12,4},{16,24},{20,28},{24,16},{28,20},{1,9},{5... | collective-permute-start | bytes 417800 | tf_op jit(solution)/shard_map/ppermute | solution.py:853
  282.1 12.5 %collective-permute-start.35 = (bf16[272,256]{1,0:T(8,128)(2,1)S(1)}, bf16[272,256]{1,0:T(8,128)(2,1)S(1)}, u32[]{:S(2)}, u32[]{:S(2)}) collective-permute-start(bf16[272,256]{1,0:T(8,128)(2,1)S(1)} %get-tuple-element.319), channel_id=1, source_target_pairs={{0,16},{4,20},{8,24},{12,28},{16,0},{20,4},{24,8},{28,12},{1,17},{... | collective-permute-start | bytes 417800 | tf_op jit(solution)/shard_map/ppermute | solution.py:853
  285.6 9.8 %collective-permute-start.36 = (bf16[272,256]{1,0:T(8,128)(2,1)S(1)}, bf16[272,256]{1,0:T(8,128)(2,1)S(1)}, u32[]{:S(2)}, u32[]{:S(2)}) collective-permute-start(bf16[272,256]{1,0:T(8,128)(2,1)S(1)} %get-tuple-element.320), channel_id=1, source_target_pairs={{0,24},{4,28},{8,16},{12,20},{16,8},{20,12},{24,0},{28,4},{1,25},{... | collective-permute-start | bytes 417800 | tf_op jit(solution)/shard_map/ppermute | solution.py:853
  287.3 9.6 %collective-permute-start.37 = (bf16[4,72,256]{2,1,0:T(8,128)(2,1)S(1)}, bf16[4,72,256]{2,1,0:T(8,128)(2,1)S(1)}, u32[]{:S(2)}, u32[]{:S(2)}) collective-permute-start(bf16[4,72,256]{2,1,0:T(8,128)(2,1)S(1)} %get-tuple-element.322), channel_id=1, source_target_pairs={{0,4},{4,0},{8,12},{12,8},{16,20},{20,16},{24,28},{28,24},{1,5},{5... | collective-permute-start | bytes 442376 | tf_op jit(solution)/shard_map/ppermute | solution.py:853
  295.4 6.9 %collective-permute-start.41 = (bf16[192,256]{1,0:T(8,128)(2,1)S(1)}, bf16[192,256]{1,0:T(8,128)(2,1)S(1)}, u32[]{:S(2)}, u32[]{:S(2)}) collective-permute-start(bf16[192,256]{1,0:T(8,128)(2,1)S(1)} %add_convert_fusion.14), channel_id=1, source_target_pairs={{0,8},{4,12},{8,0},{12,4},{16,24},{20,28},{24,16},{28,20},{1,9},{5... | collective-permute-start | bytes 294920 | tf_op jit(solution)/shard_map/ppermute | solution.py:853
  297.0 10.2 %collective-permute-start.42 = (bf16[192,256]{1,0:T(8,128)(2,1)S(1)}, bf16[192,256]{1,0:T(8,128)(2,1)S(1)}, u32[]{:S(2)}, u32[]{:S(2)}) collective-permute-start(bf16[192,256]{1,0:T(8,128)(2,1)S(1)} %add_convert_fusion.14), channel_id=1, source_target_pairs={{0,16},{4,20},{8,24},{12,28},{16,0},{20,4},{24,8},{28,12},{1,17},{... | collective-permute-start | bytes 294920 | tf_op jit(solution)/shard_map/ppermute | solution.py:853
  299.2 8.1 %collective-permute-start.43 = (bf16[192,256]{1,0:T(8,128)(2,1)S(1)}, bf16[192,256]{1,0:T(8,128)(2,1)S(1)}, u32[]{:S(2)}, u32[]{:S(2)}) collective-permute-start(bf16[192,256]{1,0:T(8,128)(2,1)S(1)} %add_convert_fusion.14), channel_id=1, source_target_pairs={{0,24},{4,28},{8,16},{12,20},{16,8},{20,12},{24,0},{28,4},{1,25},{... | collective-permute-start | bytes 294920 | tf_op jit(solution)/shard_map/ppermute | solution.py:853
  302.3 11.1 %collective-permute-start.40 = (bf16[192,256]{1,0:T(8,128)(2,1)S(1)}, bf16[192,256]{1,0:T(8,128)(2,1)S(1)}, u32[]{:S(2)}, u32[]{:S(2)}) collective-permute-start(bf16[192,256]{1,0:T(8,128)(2,1)S(1)} %copy-done.19), channel_id=1, source_target_pairs={{0,24},{4,28},{8,16},{12,20},{16,8},{20,12},{24,0},{28,4},{1,25},{... | collective-permute-start | bytes 294920 | tf_op jit(solution)/shard_map/ppermute | solution.py:853
  307.2 9.0 %collective-permute-start.48 = (bf16[72,256]{1,0:T(8,128)(2,1)S(1)}, bf16[72,256]{1,0:T(8,128)(2,1)S(1)}, u32[]{:S(2)}, u32[]{:S(2)}) collective-permute-start(bf16[72,256]{1,0:T(8,128)(2,1)S(1)} %get-tuple-element.345), channel_id=1, source_target_pairs={{0,8},{4,12},{8,0},{12,4},{16,24},{20,28},{24,16},{28,20},{1,9},{5... | collective-permute-start | bytes 110600 | tf_op jit(solution)/shard_map/ppermute | solution.py:853
  307.3 10.6 %collective-permute-start.49 = (bf16[72,256]{1,0:T(8,128)(2,1)S(1)}, bf16[72,256]{1,0:T(8,128)(2,1)S(1)}, u32[]{:S(2)}, u32[]{:S(2)}) collective-permute-start(bf16[72,256]{1,0:T(8,128)(2,1)S(1)} %get-tuple-element.346), channel_id=1, source_target_pairs={{0,16},{4,20},{8,24},{12,28},{16,0},{20,4},{24,8},{28,12},{1,17},{... | collective-permute-start | bytes 110600 | tf_op jit(solution)/shard_map/ppermute | solution.py:853
  311.6 6.4 %collective-permute-start.50 = (bf16[72,256]{1,0:T(8,128)(2,1)S(1)}, bf16[72,256]{1,0:T(8,128)(2,1)S(1)}, u32[]{:S(2)}, u32[]{:S(2)}) collective-permute-start(bf16[72,256]{1,0:T(8,128)(2,1)S(1)} %get-tuple-element.347), channel_id=1, source_target_pairs={{0,24},{4,28},{8,16},{12,20},{16,8},{20,12},{24,0},{28,4},{1,25},{... | collective-permute-start | bytes 110600 | tf_op jit(solution)/shard_map/ppermute | solution.py:853
  313.5 8.2 %collective-permute-start.45 = (bf16[272,256]{1,0:T(8,128)(2,1)S(1)}, bf16[272,256]{1,0:T(8,128)(2,1)S(1)}, u32[]{:S(2)}, u32[]{:S(2)}) collective-permute-start(bf16[272,256]{1,0:T(8,128)(2,1)S(1)} %add_convert_fusion.8), channel_id=1, source_target_pairs={{0,8},{4,12},{8,0},{12,4},{16,24},{20,28},{24,16},{28,20},{1,9},{5... | collective-permute-start | bytes 417800 | tf_op jit(solution)/shard_map/ppermute | solution.py:853
  313.8 11.1 %collective-permute-start.46 = (bf16[272,256]{1,0:T(8,128)(2,1)S(1)}, bf16[272,256]{1,0:T(8,128)(2,1)S(1)}, u32[]{:S(2)}, u32[]{:S(2)}) collective-permute-start(bf16[272,256]{1,0:T(8,128)(2,1)S(1)} %add_convert_fusion.8), channel_id=1, source_target_pairs={{0,16},{4,20},{8,24},{12,28},{16,0},{20,4},{24,8},{28,12},{1,17},{... | collective-permute-start | bytes 417800 | tf_op jit(solution)/shard_map/ppermute | solution.py:853
  316.2 8.6 %collective-permute-start.47 = (bf16[272,256]{1,0:T(8,128)(2,1)S(1)}, bf16[272,256]{1,0:T(8,128)(2,1)S(1)}, u32[]{:S(2)}, u32[]{:S(2)}) collective-permute-start(bf16[272,256]{1,0:T(8,128)(2,1)S(1)} %add_convert_fusion.8), channel_id=1, source_target_pairs={{0,24},{4,28},{8,16},{12,20},{16,8},{20,12},{24,0},{28,4},{1,25},{... | collective-permute-start | bytes 417800 | tf_op jit(solution)/shard_map/ppermute | solution.py:853
  325.0 33.7 %collective-permute-start.53 = (bf16[4,272,256]{2,1,0:T(8,128)(2,1)S(1)}, bf16[4,272,256]{2,1,0:T(8,128)(2,1)S(1)}, u32[]{:S(2)}, u32[]{:S(2)}) collective-permute-start(bf16[4,272,256]{2,1,0:T(8,128)(2,1)S(1)} %pad_maximum_fusion.1.refs_4_), channel_id=1, source_target_pairs={{0,4},{4,0},{8,12},{12,8},{16,20},{20,16},{24,28},{28,24},{1,5},{5... | collective-permute-start | bytes 1671176 | tf_op jit(solution)/shard_map/ppermute | solution.py:853
  329.6 29.1 %collective-permute-start.51 = (bf16[4,192,256]{2,1,0:T(8,128)(2,1)S(1)}, bf16[4,192,256]{2,1,0:T(8,128)(2,1)S(1)}, u32[]{:S(2)}, u32[]{:S(2)}) collective-permute-start(bf16[4,192,256]{2,1,0:T(8,128)(2,1)S(1)} %pad_maximum_fusion.2.refs_0_), channel_id=1, source_target_pairs={{0,4},{4,0},{8,12},{12,8},{16,20},{20,16},{24,28},{28,24},{1,5},{5... | collective-permute-start | bytes 1179656 | tf_op jit(solution)/shard_map/ppermute | solution.py:853
  330.1 28.5 %collective-permute-start.52 = (bf16[4,192,256]{2,1,0:T(8,128)(2,1)S(1)}, bf16[4,192,256]{2,1,0:T(8,128)(2,1)S(1)}, u32[]{:S(2)}, u32[]{:S(2)}) collective-permute-start(bf16[4,192,256]{2,1,0:T(8,128)(2,1)S(1)} %pad_maximum_fusion.3.refs_2_), channel_id=1, source_target_pairs={{0,4},{4,0},{8,12},{12,8},{16,20},{20,16},{24,28},{28,24},{1,5},{5... | collective-permute-start | bytes 1179656 | tf_op jit(solution)/shard_map/ppermute | solution.py:853
  337.0 7.6 %collective-permute-start.59 = (bf16[4,2,24,256]{3,2,1,0:T(8,128)(2,1)S(1)}, bf16[4,2,24,256]{3,2,1,0:T(8,128)(2,1)S(1)}, u32[]{:S(2)}, u32[]{:S(2)}) collective-permute-start(bf16[4,2,24,256]{3,2,1,0:T(8,128)(2,1)S(1)} %add_convert_fusion.12), channel_id=1, source_target_pairs={{0,16},{4,20},{8,24},{12,28},{16,0},{20,4},{24,8},{28,12},{1,17},{... | collective-permute-start | bytes 294920 | tf_op jit(solution)/shard_map/ppermute | solution.py:853
  340.2 6.4 %collective-permute-start.60 = (bf16[4,2,24,256]{3,2,1,0:T(8,128)(2,1)S(1)}, bf16[4,2,24,256]{3,2,1,0:T(8,128)(2,1)S(1)}, u32[]{:S(2)}, u32[]{:S(2)}) collective-permute-start(bf16[4,2,24,256]{3,2,1,0:T(8,128)(2,1)S(1)} %add_convert_fusion.12), channel_id=1, source_target_pairs={{0,24},{4,28},{8,16},{12,20},{16,8},{20,12},{24,0},{28,4},{1,25},{... | collective-permute-start | bytes 294920 | tf_op jit(solution)/shard_map/ppermute | solution.py:853
  344.6 14.1 %collective-permute-start.57 = (bf16[4,72,256]{2,1,0:T(8,128)(2,1)S(1)}, bf16[4,72,256]{2,1,0:T(8,128)(2,1)S(1)}, u32[]{:S(2)}, u32[]{:S(2)}) collective-permute-start(bf16[4,72,256]{2,1,0:T(8,128)(2,1)S(1)} %pad_maximum_fusion.4.refs_6_), channel_id=1, source_target_pairs={{0,4},{4,0},{8,12},{12,8},{16,20},{20,16},{24,28},{28,24},{1,5},{5... | collective-permute-start | bytes 442376 | tf_op jit(solution)/shard_map/ppermute | solution.py:853
  (47 other events, 451.9 us)

commit v3 on v2

v3 whole, which is shorter than its diff:
```python
import functools
import math

import jax
import jax.numpy as jnp
from jax import lax
from jax.experimental import pallas as pl
from jax.experimental.pallas import tpu as pltpu
from jax.sharding import PartitionSpec as P

HEADS = 12
HEAD_DIM = 64
PAIRS = HEADS // 2
LANES = 128
EPSILON = 1e-05
BIAS = -1e30
SCALE = math.log2(math.e) / HEAD_DIM**0.5
F32 = jnp.float32
BF16 = jnp.bfloat16
GELU_ROOT = math.sqrt(2.0 / math.pi)
GELU_CUBE = 0.044715


def params(*semantics):
    return pltpu.CompilerParams(
        dimension_semantics=semantics or None, vmem_limit_bytes=56 * 1024 * 1024
    )


def weight():
    return pl.CostEstimate(flops=1, bytes_accessed=1, transcendentals=0)


def dot_nn(a, b):
    return lax.dot_general(a, b, (((1,), (0,)), ((), ())), preferred_element_type=F32)


def dot_nt(a, b):
    return lax.dot_general(a, b, (((1,), (1,)), ((), ())), preferred_element_type=F32)


def dot_tn(a, b):
    return lax.dot_general(a, b, (((0,), (0,)), ((), ())), preferred_element_type=F32)


def normalize(values):
    center = values - jnp.mean(values, axis=-1, keepdims=True)
    spread = jnp.mean(center * center, axis=-1, keepdims=True)
    inverse = lax.rsqrt(spread + EPSILON)
    return center * inverse, inverse


def norm_back(grad, normed, inverse):
    mean_grad = jnp.mean(grad, axis=-1, keepdims=True)
    mean_both = jnp.mean(grad * normed, axis=-1, keepdims=True)
    return (grad - mean_grad - normed * mean_both) * inverse


def place_rows(spot, pieces, scratch):
    height = scratch.shape[0] // len(pieces)
    for r, piece in enumerate(pieces):
        begin = pl.multiple_of((spot ^ r) * height, height)
        scratch[pl.ds(begin, height), :] = piece[0:height, :]


STEP = 128


def over_rows(rows, run):
    def one(index, carried):
        run(pl.ds(pl.multiple_of(index * STEP, STEP), STEP))
        return carried

    lax.fori_loop(0, rows // STEP, one, 0)


TILE = 256


def pack_kernel(up, down, *outs, chunks, pieces):
    width = down.shape[1]
    height = up.shape[0]
    for chunk, out in enumerate(outs):
        for g in range(width // TILE):
            out[g * TILE : (g + 1) * TILE, :] = down[
                chunk * TILE : (chunk + 1) * TILE, g * TILE : (g + 1) * TILE
            ]
        for j in range(pieces):
            row, column = width + j * height, (j * chunks + chunk) * TILE
            out[row : row + height, :] = up[:, column : column + TILE]


def pack_stage(up, down, chunks, pieces):
    width = down.shape[1]
    return pl.pallas_call(
        functools.partial(pack_kernel, chunks=chunks, pieces=pieces),
        in_specs=[pl.BlockSpec(memory_space=pltpu.VMEM)] * 2,
        out_specs=[pl.BlockSpec(memory_space=pltpu.VMEM)] * chunks,
        out_shape=[jax.ShapeDtypeStruct((2 * width, TILE), BF16)] * chunks,
        compiler_params=params(),
        cost_estimate=weight(),
        name="pack",
    )(up, down)


DOC_ROWS = 16


def first_kernel(spot_ref, tokens, gain, documents, *rest, pieces):
    weights = rest[:pieces]
    scaled_out, shared_out, weight = rest[pieces:]
    place_rows(spot_ref[0], weights, weight)
    seqs, doc_lines, unused = documents.shape
    places, tall, unused = shared_out.shape
    tall = tall // seqs
    rows = tall - DOC_ROWS
    per_seq = rows // STEP

    def run(index, carried):
        here = pl.ds(pl.multiple_of(index * STEP, STEP), STEP)
        seq = index // per_seq
        there = pl.multiple_of(seq * tall + (index - seq * per_seq) * STEP, DOC_ROWS)
        normed, unused = normalize(tokens[here, :].astype(F32))
        scaled = (normed * gain[...]).astype(BF16)
        scaled_out[here, :] = scaled
        shared = dot_nn(scaled, weight[...]).astype(BF16)

        def put(c, carried):
            shared_out[c, pl.ds(there, STEP), :] = shared
            return carried

        return lax.fori_loop(0, places, put, carried)

    lax.fori_loop(0, seqs * per_seq, run, 0)

    def put(c, carried):
        for seq in range(seqs):
            begin = seq * tall + rows
            shared_out[c, begin : begin + DOC_ROWS, :] = jnp.zeros((DOC_ROWS, LANES), BF16)
            shared_out[c, begin : begin + doc_lines, :] = documents[seq]
        return carried

    lax.fori_loop(0, places, put, 0)


def first_stage(spot, tokens, gain, documents, weights, places):
    count, width = tokens.shape
    columns = weights[0].shape[1]
    seqs, doc_lines, unused = documents.shape
    return pl.pallas_call(
        functools.partial(first_kernel, pieces=len(weights)),
        grid_spec=pltpu.PrefetchScalarGridSpec(
            num_scalar_prefetch=1,
            grid=(),
            in_specs=[pl.BlockSpec(memory_space=pltpu.VMEM)] * (3 + len(weights)),
            out_specs=[pl.BlockSpec(memory_space=pltpu.VMEM)] * 2,
            scratch_shapes=[pltpu.VMEM((width, columns), BF16)],
        ),
        out_shape=[
            jax.ShapeDtypeStruct((count, width), BF16),
            jax.ShapeDtypeStruct((places, count + seqs * DOC_ROWS, columns), BF16),
        ],
        compiler_params=params(),
        cost_estimate=weight(),
        name="first_norm",
    )(spot, tokens, gain, documents, *weights)


def low_lanes(shape):
    return lax.broadcasted_iota(jnp.int32, shape, len(shape) - 1) < HEAD_DIM


def swap_halves(values):
    return pltpu.roll(values, HEAD_DIM, 1)


def stacked_pairs(ref):
    return jnp.concatenate(
        [ref[0, :, p * LANES : (p + 1) * LANES] for p in range(PAIRS)], axis=0
    )


def tile_bias(starts, key_begin, row_begin, tile_rows, tile_keys):
    key_place = key_begin + lax.broadcasted_iota(jnp.int32, (tile_rows, tile_keys), 1)
    row_place = row_begin + lax.broadcasted_iota(jnp.int32, (tile_rows, tile_keys), 0)
    first = jnp.concatenate([starts] * (tile_keys // LANES), axis=1)
    allowed = (key_place >= first) & (key_place <= row_place)
    bias = jnp.where(allowed, 0.0, BIAS)
    bias = jnp.concatenate([bias, bias], axis=1)
    return jnp.concatenate([bias] * PAIRS, axis=0)


def block_at(place_ref, j, blocks):
    return jnp.maximum(place_ref[0] - (blocks - 1) + j, 0)


def attend_kernel(
    spot_ref, place_ref, scaled, marks, keyvals, *rest, blocks, tile_rows, tile_keys, pieces
):
    weights, rest = rest[:pieces], rest[pieces:]
    queries, starts_out, exact_out, rounded_out, logs_out = rest[:5]
    (
        key_even, key_odd, value_even, value_odd, score_scratch, most, total, weight_all, projected,
    ) = rest[5:]
    rows = keyvals.shape[2] - DOC_ROWS
    seq, tile = pl.program_id(0), pl.program_id(1)

    @pl.when((seq == 0) & (tile == 0))
    def _():
        place_rows(spot_ref[0], weights, weight_all)

    @pl.when(tile == 0)
    def _():
        projected[...] = dot_nn(scaled[...], weight_all[...]).astype(BF16)
        low = low_lanes((rows, LANES))
        for j in range(blocks):
            whole = keyvals[block_at(place_ref, j, blocks), 0, 0:rows, :].astype(F32)
            turned = swap_halves(whole)
            place = pl.ds(j * rows, rows)
            key_even[place, :] = jnp.where(low, whole, 0.0).astype(BF16)
            key_odd[place, :] = jnp.where(low, 0.0, turned).astype(BF16)
            value_even[place, 0:LANES] = jnp.where(low, turned, 0.0).astype(BF16)
            value_even[place, LANES:] = jnp.where(low, 1.0, 0.0).astype(BF16)
            value_odd[place, 0:LANES] = jnp.where(low, 0.0, whole).astype(BF16)
            value_odd[place, LANES:] = jnp.where(low, 0.0, 1.0).astype(BF16)

    queries[0] = projected[pl.ds(pl.multiple_of(tile * tile_rows, tile_rows), tile_rows), :]

    def smaller(j, count):
        lines = keyvals[block_at(place_ref, j, blocks), 0, rows:, :].astype(F32)
        missing = place_ref[0] - (blocks - 1) + j < 0
        for h in range(rows // LANES):
            line = jnp.where(missing, -1.0, lines[h : h + 1, :])
            count = count + jnp.where(line < marks[0], 1.0, 0.0)
        return count

    count = lax.fori_loop(0, blocks, smaller, jnp.zeros((tile_rows, LANES), F32))
    count = jnp.sum(count, axis=1, keepdims=True).astype(jnp.int32)
    starts = starts_out
    starts[0] = jnp.broadcast_to(count, (tile_rows, LANES))
    row_begin = (blocks - 1) * rows + tile * tile_rows
    begin = jnp.min(starts[0]) // tile_keys
    end = (row_begin + tile_rows - 1) // tile_keys + 1
    stacked = stacked_pairs(queries)
    most[...] = jnp.full_like(most, -3e38)
    copies = tile_keys // LANES

    def score(index):
        key_begin = pl.multiple_of(index * tile_keys, tile_keys)
        place = pl.ds(key_begin, tile_keys)
        both = jnp.concatenate([key_even[place, :], key_odd[place, :]], axis=0)
        values = dot_nt(stacked, both) + tile_bias(
            starts[0], key_begin, row_begin, tile_rows, tile_keys
        )
        score_scratch[index - begin] = values
        half = []
        for h in range(2):
            part = values[:, h * tile_keys : h * tile_keys + LANES]
            for q in range(1, copies):
                at = h * tile_keys + q * LANES
                part = jnp.maximum(part, values[:, at : at + LANES])
            half.append(part)
        return jnp.concatenate(half, axis=1)

    def output(index):
        place = pl.ds(pl.multiple_of(index * tile_keys, tile_keys), tile_keys)
        both = jnp.concatenate([value_even[place, :], value_odd[place, :]], axis=0)
        shift = jnp.concatenate([most[:, 0:LANES]] * copies + [most[:, LANES:]] * copies, axis=1)
        powers = jnp.exp2((score_scratch[index - begin] - shift) * SCALE).astype(BF16)
        return dot_nn(powers, both)

    def in_pairs(one, join, total):
        def two(index, carried):
            at = begin + 2 * index
            total[...] = join(total[...], join(one(at), one(at + 1)))
            return carried

        count = end - begin
        lax.fori_loop(0, count // 2, two, 0)

        @pl.when(count % 2 == 1)
        def _():
            total[...] = join(total[...], one(end - 1))

    in_pairs(score, jnp.maximum, most)
    stack = PAIRS * tile_rows
    for h in range(2):
        part = jnp.max(most[:, h * LANES : (h + 1) * LANES], axis=1, keepdims=True)
        most[:, h * LANES : (h + 1) * LANES] = jnp.broadcast_to(part, (stack, LANES))
    total[...] = jnp.zeros_like(total)
    in_pairs(output, jnp.add, total)
    low = low_lanes((tile_rows, LANES))
    for p in range(PAIRS):
        at = pl.ds(p * tile_rows, tile_rows)
        lanes = slice(p * LANES, (p + 1) * LANES)
        sums = total[at, LANES:]
        out = total[at, 0:LANES] / sums
        exact_out[0, :, lanes] = out
        rounded_out[0, :, lanes] = out.astype(BF16)
        shift = jnp.where(low, most[at, 0:LANES], most[at, LANES:])
        logs_out[0, :, lanes] = shift * SCALE + jnp.log2(sums)


def attend_back_kernel(
    place_ref, queries, starts, exact, logs, grads, keyvals, *rest,
    seq, blocks, tile_rows, tile_keys
):
    grad_queries, terms, *rest = rest[1:] if seq else rest
    (
        key_even, key_odd, value_even, value_odd,
        key_total, value_total, query_total,
        log_even, log_odd, delta_even, delta_odd,
    ) = rest
    rows = keyvals.shape[2] - DOC_ROWS
    tile = pl.program_id(0)

    @pl.when(tile == 0)
    def _():
        low = low_lanes((rows, LANES))
        for j in range(blocks):
            whole = keyvals[block_at(place_ref, j, blocks), 0, 0:rows, :].astype(F32)
            turned = swap_halves(whole)
            place = pl.ds(j * rows, rows)
            key_even[place, :] = jnp.where(low, whole, 0.0).astype(BF16)
            key_odd[place, :] = jnp.where(low, 0.0, turned).astype(BF16)
            value_even[place, :] = jnp.where(low, turned, 0.0).astype(BF16)
            value_odd[place, :] = jnp.where(low, 0.0, whole).astype(BF16)
        key_total[...] = jnp.zeros_like(key_total)
        value_total[...] = jnp.zeros_like(value_total)

    row_begin = (blocks - 1) * rows + tile * tile_rows
    begin = jnp.min(starts[0]) // tile_keys
    end = (row_begin + tile_rows - 1) // tile_keys + 1
    stacked = stacked_pairs(queries)
    grad_stacked = stacked_pairs(grads)
    stacked_turned = stacked.T
    grad_turned = grad_stacked.T
    stack = PAIRS * tile_rows
    low = low_lanes((tile_rows, LANES))
    for p in range(PAIRS):
        at = pl.ds(p * tile_rows, tile_rows)
        lanes = slice(p * LANES, (p + 1) * LANES)
        log = logs[0, :, lanes]
        log_turned = swap_halves(log)
        log_even[at, :] = jnp.where(low, log, log_turned)
        log_odd[at, :] = jnp.where(low, log_turned, log)
        terms_here = exact[0, :, lanes] * grads[0, :, lanes].astype(F32)
        even = jnp.sum(jnp.where(low, terms_here, 0.0), axis=1, keepdims=True)
        odd = jnp.sum(jnp.where(low, 0.0, terms_here), axis=1, keepdims=True)
        delta_even[at, :] = jnp.broadcast_to(even, (tile_rows, LANES))
        delta_odd[at, :] = jnp.broadcast_to(odd, (tile_rows, LANES))
    query_total[...] = jnp.zeros_like(query_total)

    def step(index, carried):
        key_begin = pl.multiple_of(index * tile_keys, tile_keys)
        place = pl.ds(key_begin, tile_keys)
        keys = jnp.concatenate([key_even[place, :], key_odd[place, :]], axis=0)
        values = jnp.concatenate([value_even[place, :], value_odd[place, :]], axis=0)
        copies = tile_keys // LANES
        log = jnp.concatenate([log_even[...]] * copies + [log_odd[...]] * copies, axis=1)
        delta = jnp.concatenate([delta_even[...]] * copies + [delta_odd[...]] * copies, axis=1)
        scores = dot_nt(stacked, keys) + tile_bias(
            starts[0], key_begin, row_begin, tile_rows, tile_keys
        )
        chances = jnp.exp2(scores * SCALE - log)
        grad_probs = dot_nt(grad_stacked, values)
        grad_scores = (chances * (grad_probs - delta)).astype(BF16)
        query_total[...] += dot_nn(grad_scores, keys)
        key_total[index] += dot_nn(stacked_turned, grad_scores)
        value_total[index] += dot_nn(grad_turned, chances.astype(BF16))
        return carried

    lax.fori_loop(begin, end, step, 0)
    root = 1.0 / HEAD_DIM**0.5
    for p in range(PAIRS):
        at = pl.ds(p * tile_rows, tile_rows)
        lanes = slice(p * LANES, (p + 1) * LANES)
        grad_queries[0, :, lanes] = (query_total[at, :] * root).astype(BF16)

    @pl.when(tile == pl.num_programs(0) - 1)
    def _():
        per_block = rows // tile_keys
        terms[...] = jnp.zeros_like(terms)

        def block_terms(j, carried):
            for i in range(per_block):
                index = j * per_block + i
                key = key_total[index]
                value = value_total[index]
                key = key[0:HEAD_DIM, 0:tile_keys] + key[HEAD_DIM:, tile_keys:]
                value = value[0:HEAD_DIM, 0:tile_keys] + value[HEAD_DIM:, tile_keys:]
                both = jnp.concatenate([key * root, value], axis=0)
                owner = block_at(place_ref, j, blocks)
                terms[owner, 0, i * tile_keys : (i + 1) * tile_keys, :] = both.T.astype(BF16)
            return carried

        missing = jnp.maximum(blocks - 1 - place_ref[0], 0)
        lax.fori_loop(missing, blocks, block_terms, 0)


def attention_sizes(rows, blocks):
    tile_rows = 128 if rows % 128 == 0 else rows
    tile_keys = 256 if rows % 256 == 0 else 128
    return tile_rows, tile_keys, blocks * rows // tile_keys


def attend(spot, place, scaled, marks, keyvals, weights, blocks):
    unused, seqs, tall, unused = keyvals.shape
    rows = tall - DOC_ROWS
    width = scaled.shape[1]
    tile_rows, tile_keys, key_tiles = attention_sizes(rows, blocks)
    stack = PAIRS * tile_rows
    keys = blocks * rows
    row_spec = lambda lanes: pl.BlockSpec((1, tile_rows, lanes), lambda s, t, *_: (s, t, 0))
    wide = lambda dtype: jax.ShapeDtypeStruct((seqs, rows, width), dtype)
    return pl.pallas_call(
        functools.partial(
            attend_kernel,
            blocks=blocks,
            tile_rows=tile_rows,
            tile_keys=tile_keys,
            pieces=len(weights),
        ),
        grid_spec=pltpu.PrefetchScalarGridSpec(
            num_scalar_prefetch=2,
            grid=(seqs, rows // tile_rows),
            in_specs=[
                pl.BlockSpec((rows, width), lambda s, t, *_: (s, 0)),
                row_spec(LANES),
                pl.BlockSpec((keyvals.shape[0], 1, tall, LANES), lambda s, t, *_: (0, s, 0, 0)),
            ]
            + [
                pl.BlockSpec(
                    (one.shape[0], width), lambda s, t, *_: (0, 0), pipeline_mode=pl.Buffered(1)
                )
                for one in weights
            ],
            out_specs=[row_spec(width), row_spec(LANES)] + [row_spec(width)] * 3,
            scratch_shapes=[
                pltpu.VMEM((keys, LANES), BF16),
                pltpu.VMEM((keys, LANES), BF16),
                pltpu.VMEM((keys, 2 * LANES), BF16),
                pltpu.VMEM((keys, 2 * LANES), BF16),
                pltpu.VMEM((key_tiles, stack, 2 * tile_keys), F32),
                pltpu.VMEM((stack, 2 * LANES), F32),
                pltpu.VMEM((stack, 2 * LANES), F32),
                pltpu.VMEM((width, width), BF16),
                pltpu.VMEM((rows, width), BF16),
            ],
        ),
        out_shape=[
            wide(BF16),
            jax.ShapeDtypeStruct((seqs, rows, LANES), jnp.int32),
            wide(F32),
            wide(BF16),
            wide(F32),
        ],
        compiler_params=params("arbitrary", "arbitrary"),
        cost_estimate=weight(),
        name="attend",
    )(spot, place, scaled, marks, keyvals, *weights)


def attend_back(
    seq, place, queries, starts, exact, logs, grads, keyvals, terms, blocks
):
    seqs, rows, width = queries.shape
    ctx_size = keyvals.shape[0]
    tile_rows, tile_keys, key_tiles = attention_sizes(rows, blocks)
    stack = PAIRS * tile_rows
    keys = blocks * rows
    row_spec = lambda lanes: pl.BlockSpec((1, tile_rows, lanes), lambda t, *_: (seq, t, 0))
    return pl.pallas_call(
        functools.partial(
            attend_back_kernel, seq=seq, blocks=blocks, tile_rows=tile_rows, tile_keys=tile_keys
        ),
        grid_spec=pltpu.PrefetchScalarGridSpec(
            num_scalar_prefetch=1,
            grid=(rows // tile_rows,),
            in_specs=[row_spec(width), row_spec(LANES)]
            + [row_spec(width)] * 3
            + [pl.BlockSpec((ctx_size, 1, keyvals.shape[2], LANES), lambda t, *_: (0, seq, 0, 0))]
            + [pl.BlockSpec(memory_space=pl.ANY)] * len(terms),
            out_specs=[
                pl.BlockSpec((1, tile_rows, width), lambda t, *_: (0, t, 0)),
                pl.BlockSpec((ctx_size, 1, rows, LANES), lambda t, *_: (0, seq, 0, 0)),
            ],
            scratch_shapes=[pltpu.VMEM((keys, LANES), BF16)] * 4
            + [pltpu.VMEM((key_tiles, LANES, 2 * tile_keys), F32)] * 2
            + [pltpu.VMEM((stack, LANES), F32)] * 5,
        ),
        out_shape=[
            jax.ShapeDtypeStruct((1, rows, width), BF16),
            jax.ShapeDtypeStruct((ctx_size, seqs, rows, LANES), BF16),
        ],
        input_output_aliases={7: 1} if terms else {},
        compiler_params=params("arbitrary"),
        cost_estimate=weight(),
        name="attend_back",
    )(place, queries, starts, exact, logs, grads, keyvals, *terms)


def round_up(count, unit):
    return -(-count // unit) * unit


def mixing_rows(width, pieces, ctx_size):
    unit = 8 * ctx_size
    tall = 2 * width + width // pieces * (width // TILE)
    return round_up(tall + width // LANES, unit) - 2 * width


def message_of(messages, s):
    return messages[s & 1], s >> 1


def split_out(spot, pieces, source, messages, first_row=0):
    height, lanes = source.shape[0] // pieces, messages[0].shape[2]
    across = min(lanes, source.shape[1])
    for s in range(pieces):
        out, at = message_of(messages, s)
        begin = pl.multiple_of((spot ^ s) * height, height)
        for g in range(source.shape[1] // across):
            row = first_row + g * height
            out[at, row : row + height, 0:across] = source[
                pl.ds(begin, height), g * lanes : g * lanes + across
            ].astype(BF16)


def put_vector(pieces, vector, messages, first_row, begin):
    height, lanes = messages[0].shape[1] - first_row, messages[0].shape[2]
    count = vector.shape[1] // LANES
    row = lax.broadcasted_iota(jnp.int32, (height, LANES), 0)
    block = jnp.zeros((height, LANES), F32)
    for i in range(count):
        block = jnp.where(row == i, vector[:, i * LANES : (i + 1) * LANES], block)
    for s in range(pieces):
        out, at = message_of(messages, s)
        out[at, first_row:, begin : begin + LANES] = block.astype(BF16)
        if begin == 0:
            out[at, first_row:, LANES:] = jnp.zeros((height, lanes - LANES), BF16)


def feed_kernel(spot_ref, *refs, pieces, part, first, last, names):
    use = dict(zip(names, refs))
    spot = spot_ref[0]
    step = pl.program_id(0)
    steps = len(part) * (pieces // 2)
    cotangent = use["cotangent"]
    reduced, grads, scaled, hidden = use["reduced"], use["grads"], use["scaled"], use["hidden"]
    up_tile, down_tile, up_sems, down_sems = (
        use["up_tile"], use["down_tile"], use["up_sems"], use["down_sems"]
    )
    rows, width = cotangent.shape
    height = width // pieces
    groups = width // TILE

    def messages_of(chunk):
        return use[f"keep{chunk}"], use[f"send{chunk}"]

    def owners(n):
        chunk, at = divmod(n, pieces // 2)
        return part[chunk], (2 * at, 2 * at + 1)

    def copies(n):
        chunk, pair = owners(n)
        for h, s in enumerate(pair):
            source = pl.multiple_of(width + (spot ^ s) * height, height)
            for r in range(pieces):
                row = pl.multiple_of((spot ^ r) * height, height)
                yield pltpu.make_async_copy(
                    use[f"message{chunk}_{r}"].at[pl.ds(source, height), :],
                    up_tile.at[n, pl.ds(row, height), pl.ds(h * TILE, TILE)],
                    up_sems.at[n, h, r],
                )
            for g in range(groups):
                yield pltpu.make_async_copy(
                    use[f"message{chunk}_{s}"].at[pl.ds(g * TILE, TILE), :],
                    down_tile.at[n, pl.ds(h * TILE, TILE), pl.ds(g * TILE, TILE)],
                    down_sems.at[n, h, g],
                )

    @pl.when(step == 0)
    def _():
        for n in range(steps):
            for one in copies(n):
                one.start()
        if first:

            def begin(here):
                mixed = dot_nn(use["attended"][here, :], use["mixing_all"][...])
                values = use["tokens"][here, :].astype(F32) + mixed
                hidden[here, :] = values
                normed, unused = normalize(values)
                scaled[here, :] = (normed * use["gain"][...]).astype(BF16)

            place_rows(spot, [use[f"mixing{r}"] for r in range(pieces)], use["mixing_all"])
            over_rows(rows, begin)

    for n in range(steps):

        @pl.when(step == n)
        def _():
            for one in copies(n):
                one.wait()

    up = up_tile[step]
    down = down_tile[step]
    upper = dot_nn(scaled[...], up)
    grad_act = dot_nt(cotangent[...], down)
    square = upper * upper
    inner = jnp.tanh(GELU_ROOT * (upper + GELU_CUBE * upper * square))
    half = 0.5 * (1.0 + inner)
    slope = half + 0.5 * upper * (1.0 - inner * inner) * (
        GELU_ROOT * (1.0 + 3.0 * GELU_CUBE * square)
    )
    active = (upper * half).astype(BF16)
    grad_upper = (grad_act * slope).astype(BF16)
    reduced_here = dot_nn(active, down)
    grads_here = dot_nt(grad_upper, up)

    @pl.when(step == 0)
    def _():
        if first:
            reduced[...] = reduced_here
            grads[...] = grads_here
        else:
            reduced[...] = use["reduced_in"][...] + reduced_here
            grads[...] = use["grads_in"][...] + grads_here

    @pl.when(step > 0)
    def _():
        reduced[...] += reduced_here
        grads[...] += grads_here

    down_term = dot_tn(active, cotangent[...]).astype(BF16)
    up_term = use["up_term"]
    up_term[...] = dot_tn(scaled[...], grad_upper)
    for n in range(steps):

        @pl.when(step == n)
        def _():
            chunk, pair = owners(n)
            messages = messages_of(chunk)
            for h, s in enumerate(pair):
                out, at = message_of(messages, s)
                for g in range(groups):
                    column = slice(g * TILE, (g + 1) * TILE)
                    out[at, column, :] = down_term[h * TILE : (h + 1) * TILE, column]
            for s in range(pieces):
                out, at = message_of(messages, s)
                begin = pl.multiple_of((spot ^ s) * height, height)
                for h, t in enumerate(pair):
                    row = pl.multiple_of(width + (spot ^ t) * height, height)
                    out[at, pl.ds(row, height), :] = up_term[
                        pl.ds(begin, height), h * TILE : (h + 1) * TILE
                    ].astype(BF16)

    if last:

        @pl.when(step == steps - 1)
        def _():
            sums, grad_mixed, term = use["sums"], use["grad_mixed"], use["term"]
            sums[...] = jnp.zeros_like(sums)
            place_rows(spot, [use[f"mixing{r}"] for r in range(pieces)], use["mixing_all"])

            def end(here):
                values = hidden[here, :]
                use["layer_out"][here, :] = (values + reduced[here, :]).astype(BF16)
                normed, inverse = normalize(values)
                grad = grads[here, :]
                sums[...] += jnp.sum((grad * normed).reshape(STEP // 8, 8, width), axis=0)
                grad_hidden = cotangent[here, :].astype(F32) + norm_back(
                    grad * use["gain"][...], normed, inverse
                )
                use["grad_hidden"][here, :] = grad_hidden
                rounded = grad_hidden.astype(BF16)
                grad_mixed[here, :] = rounded
                use["grad_attended"][here, :] = dot_nt(rounded, use["mixing_all"][...]).astype(
                    BF16
                )

            over_rows(rows, end)
            term[...] = dot_tn(use["attended"][...], grad_mixed[...])
            tall = 2 * width
            messages = messages_of(part[-1])
            split_out(spot, pieces, term, messages, tall)
            put_vector(
                pieces,
                jnp.sum(sums[...], axis=0, keepdims=True),
                messages,
                tall + height * groups,
                0,
            )


def feed_stage(spot, arrays, gathered, mixing_pieces, part, chunks, ctx_size):
    first, last = part[0] == 0, part[-1] == chunks - 1
    rows, width = arrays["cotangent"].shape
    pieces = len(gathered[part[0]])
    wide = jax.ShapeDtypeStruct((rows, width), F32)
    narrow = jax.ShapeDtypeStruct((rows, width), BF16)
    inputs, outputs, scratch = {}, {}, {}
    for chunk in part:
        more = mixing_rows(width, pieces, ctx_size) if chunk == chunks - 1 else 0
        message = jax.ShapeDtypeStruct((pieces // 2, 2 * width + more, TILE), BF16)
        outputs[f"keep{chunk}"] = outputs[f"send{chunk}"] = message
    inputs["cotangent"] = arrays["cotangent"]
    for chunk in part:
        for r in range(pieces):
            inputs[f"message{chunk}_{r}"] = gathered[chunk][r]
    for r in range(pieces):
        inputs[f"mixing{r}"] = mixing_pieces[r]
    scratch["mixing_all"] = pltpu.VMEM((width, width), BF16)
    if first:
        for name in ("attended", "tokens", "gain"):
            inputs[name] = arrays[name]
        outputs.update(hidden=wide, scaled=narrow, reduced=wide, grads=wide)
    if last:
        for name in ("attended", "gain", "scaled", "hidden"):
            inputs[name] = arrays[name]
        inputs["reduced_in"], inputs["grads_in"] = arrays["reduced"], arrays["grads"]
        outputs.update(layer_out=narrow, grad_hidden=wide, grad_attended=narrow)
        scratch.update(
            reduced=pltpu.VMEM((rows, width), F32),
            grads=pltpu.VMEM((rows, width), F32),
            sums=pltpu.VMEM((8, width), F32),
            grad_mixed=pltpu.VMEM((rows, width), BF16),
            term=pltpu.VMEM((width, width), F32),
        )
    steps = len(part) * (pieces // 2)
    scratch.update(
        up_tile=pltpu.VMEM((steps, width, 2 * TILE), BF16),
        down_tile=pltpu.VMEM((steps, 2 * TILE, width), BF16),
        up_sems=pltpu.SemaphoreType.DMA((steps, 2, pieces)),
        down_sems=pltpu.SemaphoreType.DMA((steps, 2, width // TILE)),
        up_term=pltpu.VMEM((width, 2 * TILE), F32),
    )

    def spec(name, array):
        if name[:7] == "message":
            return pl.BlockSpec(memory_space=pl.ANY)
        once = pl.Buffered(1)
        rank = len(array.shape)
        return pl.BlockSpec(array.shape, lambda i, *_: (0,) * rank, pipeline_mode=once)

    results = pl.pallas_call(
        functools.partial(
            feed_kernel,
            pieces=pieces,
            part=part,
            first=first,
            last=last,
            names=(*inputs, *outputs, *scratch),
        ),
        grid_spec=pltpu.PrefetchScalarGridSpec(
            num_scalar_prefetch=1,
            grid=(steps,),
            in_specs=[spec(*one) for one in inputs.items()],
            out_specs=[spec(*one) for one in outputs.items()],
            scratch_shapes=list(scratch.values()),
        ),
        out_shape=list(outputs.values()),
        compiler_params=params("arbitrary"),
        cost_estimate=weight(),
        name=f"feed{part[0]}",
    )(spot, *inputs.values())
    return {**arrays, **dict(zip(outputs, results))}


def query_kernel(spot_ref, scaled, *rest, pieces, seqs):
    grad_queries, weights = rest[:seqs], rest[seqs : seqs + pieces]
    grad_out, keep_out, send_out, weight, term = rest[seqs + pieces :]
    spot = spot_ref[0]
    rows = scaled.shape[0] // seqs
    place_rows(spot, weights, weight)
    for i, one in enumerate(grad_queries):
        here = slice(i * rows, (i + 1) * rows)
        part = dot_tn(scaled[here, :], one[...])
        term[...] = part if i == 0 else term[...] + part
        grad_out[here, :] = dot_nt(one[...], weight[...])
    split_out(spot, pieces, term, (keep_out, send_out))


def query_stage(spot, scaled, grad_queries, weights, ctx_size):
    rows, width = scaled.shape
    pieces = len(weights)
    tall = round_up(width // pieces * (width // TILE), 8 * ctx_size)
    message = jax.ShapeDtypeStruct((pieces // 2, tall, TILE), BF16)
    outs = [jax.ShapeDtypeStruct((rows, width), F32), message, message]
    whole = lambda one: pl.BlockSpec(one.shape, lambda i, *_: (0,) * len(one.shape))
    return pl.pallas_call(
        functools.partial(query_kernel, pieces=pieces, seqs=len(grad_queries)),
        grid_spec=pltpu.PrefetchScalarGridSpec(
            num_scalar_prefetch=1,
            grid=(1,),
            in_specs=[whole(scaled)]
            + [whole(one) for one in grad_queries]
            + [pl.BlockSpec((width // pieces, width), lambda i, *_: (0, 0))] * pieces,
            out_specs=[whole(one) for one in outs],
            scratch_shapes=[
                pltpu.VMEM((width, width), BF16),
                pltpu.VMEM((width, width), F32),
            ],
        ),
        out_shape=outs,
        compiler_params=params(),
        cost_estimate=weight(),
        name="query_grad",
    )(spot, scaled, *grad_queries, *weights)


def last_kernel(spot_ref, tokens, gain, scaled, arrived, grad_scaled, grad_hidden, *rest, pieces):
    weights = rest[:pieces]
    input_grad, keep_out, send_out, weight, sums, term, grad_shared = rest[pieces:]
    spot = spot_ref[0]
    width = tokens.shape[1]
    place_rows(spot, weights, weight)
    sums[...] = jnp.zeros_like(sums)
    places, seqs, here, unused = arrived.shape
    for i in range(seqs):
        total = arrived[0, i].astype(F32)
        for j in range(1, places):
            total = total + arrived[j, i].astype(F32)
        grad_shared[i * here : (i + 1) * here, :] = total.astype(BF16)
    term[...] = dot_tn(scaled[...], grad_shared[...])
    split_out(spot, pieces, term, (keep_out, send_out))

    def run(rows):
        normed, inverse = normalize(tokens[rows, :].astype(F32))
        grad = grad_scaled[rows, :] + dot_nt(grad_shared[rows, :], weight[...])
        sums[...] += jnp.sum((grad * normed).reshape(STEP // 8, 8, width), axis=0)
        input_grad[rows, :] = grad_hidden[rows, :] + norm_back(
            grad * gain[...], normed, inverse
        )

    over_rows(tokens.shape[0], run)
    put_vector(
        pieces, jnp.sum(sums[...], axis=0, keepdims=True), (keep_out, send_out), 0, LANES
    )


def last_stage(spot, tokens, gain, scaled, arrived, grad_scaled, grad_hidden, weights):
    rows, width = tokens.shape
    pieces, places = len(weights), arrived.shape[0]
    message = jax.ShapeDtypeStruct(
        (pieces // 2, round_up(width // pieces, 8 * places), 2 * LANES), BF16
    )
    return pl.pallas_call(
        functools.partial(last_kernel, pieces=pieces),
        grid_spec=pltpu.PrefetchScalarGridSpec(
            num_scalar_prefetch=1,
            grid=(),
            in_specs=[pl.BlockSpec(memory_space=pltpu.VMEM)] * (6 + pieces),
            out_specs=[pl.BlockSpec(memory_space=pltpu.VMEM)] * 3,
            scratch_shapes=[
                pltpu.VMEM((width, LANES), BF16),
                pltpu.VMEM((8, width), F32),
                pltpu.VMEM((width, LANES), F32),
                pltpu.VMEM((rows, LANES), BF16),
            ],
        ),
        out_shape=[jax.ShapeDtypeStruct((rows, width), F32), message, message],
        compiler_params=params(),
        cost_estimate=weight(),
        name="last",
    )(spot, tokens, gain, scaled, arrived, grad_scaled, grad_hidden, *weights)


def final_kernel(
    place_ref, early_own, early_other, last_own, last_other, late,
    down_out, up_out, mixing_out, query_out, shared_out, first_out, second_out, whole,
    *, chunks, pieces, width, query_rows,
):
    height = width // pieces
    groups = width // TILE
    places, deep = late.shape[0], last_own.shape[0]
    low, high = place_ref[0] & 1, place_ref[0] >> 1

    def columns(out, first_row, rows, out_row, across):
        for g in range(across):
            row = first_row + g * rows
            out[out_row : out_row + rows, g * TILE : (g + 1) * TILE] = whole[row : row + rows, :]

    def put_chunk(chunk):
        columns(down_out, 0, TILE, chunk * TILE, groups)
        for j in range(pieces):
            row = width + j * height
            column = (j * chunks + chunk) * TILE
            up_out[:, column : column + TILE] = whole[row : row + height, :]

    def load(source, begin, rows):
        for c in range(places):
            at = ((c & 1) * deep + (c >> 1)) * rows
            whole[at : at + rows, :] = source[c, begin : begin + rows, :].astype(F32)

    def load_halves(own, other, at):
        rows = own.shape[2]
        for half, x in ((own, low), (other, 1 - low)):
            for k in range(deep):
                begin = pl.multiple_of((x * deep + (high ^ k)) * rows, 8)
                whole[pl.ds(begin, rows), :] = half[k, at].astype(F32)

    for chunk in range(chunks - 1):
        load_halves(early_own, early_other, chunk)
        put_chunk(chunk)
    load_halves(last_own, last_other, 0)
    put_chunk(chunks - 1)
    columns(mixing_out, 2 * width, height, 0, groups)
    row = 2 * width + groups * height
    second_out[...] = whole[row : row + second_out.shape[0], 0:LANES]
    load(late, 0, query_rows)
    columns(query_out, 0, height, 0, groups)
    load(late, query_rows, late.shape[1] - query_rows)
    shared_out[...] = whole[0:height, 0:LANES]
    first_out[...] = whole[0 : first_out.shape[0], LANES:]


def final_stage(place, halves, late, query_rows, chunks, pieces, width):
    height = width // pieces
    shape = lambda *dims: jax.ShapeDtypeStruct(dims, F32)
    vector = round_up(width // LANES, 8)
    tallest = max(2 * one.shape[0] * one.shape[2] for one in halves)
    tallest = max(tallest, late.shape[0] * late.shape[1])
    return pl.pallas_call(
        functools.partial(
            final_kernel, chunks=chunks, pieces=pieces, width=width, query_rows=query_rows
        ),
        grid_spec=pltpu.PrefetchScalarGridSpec(
            num_scalar_prefetch=1,
            grid=(),
            in_specs=[pl.BlockSpec(memory_space=pltpu.VMEM)] * 5,
            out_specs=[pl.BlockSpec(memory_space=pltpu.VMEM)] * 7,
            scratch_shapes=[pltpu.VMEM((tallest, TILE), F32)],
        ),
        out_shape=[
            shape(chunks * TILE, width),
            shape(height, pieces * chunks * TILE),
            shape(height, width),
            shape(height, width),
            shape(height, LANES),
            shape(vector, LANES),
            shape(vector, LANES),
        ],
        compiler_params=params(),
        cost_estimate=weight(),
        name="final",
    )(place, *halves, late)


def swap(values, axis, size, mask):
    return lax.ppermute(values, axis, [(i, i ^ mask) for i in range(size)])


class Gather:
    def __init__(self, piece, size):
        self.size, self.own = size, piece
        self.far = swap(piece, "wt", size, 2)
        self.near = swap(piece, "wt", size, 1)

    def finish(self):
        return [self.own, self.near, self.far, swap(self.far, "wt", self.size, 1)]


def own_order(values, spot, size):
    mask = 1
    while mask < size:
        split = values.reshape((size // (2 * mask), 2, mask) + values.shape[1:])
        split = jnp.where((spot & mask) != 0, split[:, ::-1], split)
        values = split.reshape(values.shape)
        mask *= 2
    return values


class Reduction:
    def __init__(self, keep, send, place, sizes):
        self.wt_size, self.ctx_size = sizes
        self.groups = self.ctx_size // 2
        self.low, self.high = place & 1, place >> 1
        self.owners, self.rows, self.lanes = keep.shape
        split = (self.owners, 2, self.groups, self.rows // self.ctx_size, self.lanes)
        self.held = keep.reshape(split)
        self.sent = [send.reshape(split)]
        self.routes = [("wt", self.wt_size, 1)]
        self.coming = []

    def launch(self):
        if self.sent:
            self.coming = [swap(one, *route) for one, route in zip(self.sent, self.routes)]
            self.sent = []

    def add(self, pick):
        return pick(self.held).astype(F32) + pick(self.coming[0]).astype(F32)

    def y(self, cuts=()):
        edges = (0, *cuts, self.rows // self.ctx_size)
        self.later = [
            self.add(lambda v: v[1][..., begin:end, :]).astype(BF16)
            for begin, end in zip(edges, edges[1:])
        ]
        self.held = self.add(lambda v: v[0])
        self.sent = [self.later.pop(0)]
        self.routes = [("wt", self.wt_size, 2)]

    def y_more(self):
        self.before, self.sent = self.coming, [self.later.pop(0)]

    def y_joined(self):
        self.coming = [jnp.concatenate(self.before + self.coming, axis=-2)]

    def x(self):
        low, axis = self.low, self.held.ndim - 4
        half = lambda x: self.add(lambda v: lax.dynamic_index_in_dim(v, x, axis, False))
        self.held, self.sent = half(low), [half(1 - low).astype(BF16)]
        self.routes = [("ctx", self.ctx_size, 1)]

    def far(self):
        return [("ctx", self.ctx_size, 2 * k) for k in range(1, self.groups)]

    def z(self, *others):
        def part(k):
            pick = lambda v: lax.dynamic_index_in_dim(v, self.high ^ k, 0, False)
            return jnp.stack([one.add(pick) for one in (self, *others)])

        self.sent = [part(k).astype(BF16) for k in range(1, self.groups)]
        self.held = part(0)
        self.routes = self.far()

    def total(self):
        parts = [self.held.astype(F32)] + [one.astype(F32) for one in self.coming]
        while len(parts) > 1:
            parts = [parts[i] + parts[i + 1] for i in range(0, len(parts), 2)]
        return parts[0].astype(BF16)

    def z_back(self):
        self.held = self.total()
        self.sent = [self.held] * (self.groups - 1)

    def x_back(self):
        self.held = jnp.stack([self.held] + self.coming)
        self.sent = [self.held]
        self.routes = [("ctx", self.ctx_size, 1)]

    def everywhere(self):
        return self.add(lambda v: v).astype(BF16).swapaxes(0, 1).reshape(
            self.ctx_size, self.rows // self.ctx_size, self.lanes
        )


def tie(main, *reductions, came=()):
    state = [(one.held, one.sent) for one in reductions]
    main, state, coming = lax.optimization_barrier((main, state, [one.coming for one in came]))
    for one, (held, sent) in zip(reductions, state):
        one.held, one.sent = held, sent
    for one, values in zip(came, coming):
        one.coming = values
    for one in reductions:
        one.launch()
    return main


def body(
    tokens,
    documents,
    first_gain,
    query_weight,
    shared_weight,
    mixing_weight,
    second_gain,
    up_weight,
    down_weight,
    cotangent,
    *,
    wt_size,
    ctx_size,
):
    sizes = (wt_size, ctx_size)
    seqs, rows, width = tokens.shape
    count = seqs * rows
    spot_index = lax.axis_index("wt")
    place = lax.axis_index("ctx")
    spot = spot_index.astype(jnp.int32).reshape(1)
    length = ctx_size * rows
    doc_most = length * 5 // 8
    before = min(ctx_size - 1, -(-(doc_most - 1) // rows))
    blocks = before + 1
    height = width // wt_size
    chunks = up_weight.shape[1] // wt_size // TILE

    gain_rows = -(-height // LANES)
    pad = lambda gain: jnp.pad(gain, (0, gain_rows * LANES - height)).reshape(gain_rows, LANES)
    small = jnp.concatenate([shared_weight, pad(first_gain), pad(second_gain)], axis=0)
    small = jnp.pad(small, ((0, -small.shape[0] % 16), (0, 0)))
    small_pieces = Gather(small, wt_size).finish()
    query_gather = Gather(query_weight, wt_size)

    gains = jnp.stack([one[height : height + 2 * gain_rows] for one in small_pieces])
    gains = gains.reshape(wt_size, 2, gain_rows * LANES)[:, :, :height].astype(F32)
    gains = own_order(gains, spot_index, wt_size)
    gain_one = gains[:, 0].reshape(1, width)
    gain_two = gains[:, 1].reshape(1, width)

    inputs = tokens.reshape(count, width)
    doc_lines = documents.astype(BF16).reshape(seqs, rows // LANES, LANES)
    scaled_one, shared = first_stage(spot, inputs, gain_one, doc_lines, small_pieces, ctx_size)
    shared, query_gather.far, mixing_weight, *packed = lax.optimization_barrier(
        (shared, query_gather.far, mixing_weight, up_weight, down_weight)
    )
    keyvals = lax.all_to_all(shared, "ctx", 0, 0).reshape(ctx_size, seqs, rows + DOC_ROWS, LANES)
    packed = list(pack_stage(*packed, chunks, wt_size))
    gathers = [Gather(packed[0], wt_size)]
    mixing_gather = Gather(mixing_weight, wt_size)
    marks = jnp.broadcast_to(documents.astype(F32)[:, :, None], (seqs, rows, LANES))
    query_pieces = query_gather.finish()
    place_one = place.astype(jnp.int32).reshape(1)

    keyvals, gathers[0].far, mixing_gather.far, query_pieces[3], marks, packed[1:] = (
        lax.optimization_barrier(
            (keyvals, gathers[0].far, mixing_gather.far, query_pieces[3], marks, packed[1:])
        )
    )
    gathered = [gathers[0].finish()]
    mixing_pieces = mixing_gather.finish()
    gathers.append(Gather(packed[1], wt_size))
    queries, starts, exact, attended, logs = attend(
        spot, place_one, scaled_one, marks, keyvals, query_pieces, blocks
    )
    attended, gathers[1].far, packed[2:] = lax.optimization_barrier(
        (attended, gathers[1].far, packed[2:])
    )
    gathered.append(gathers[1].finish())
    gathers += [Gather(one, wt_size) for one in packed[2:]]

    arrays = {
        "attended": attended.reshape(count, width),
        "tokens": inputs,
        "gain": gain_two,
        "cotangent": cotangent.reshape(count, width),
    }
    feed = lambda arrays, part: feed_stage(
        spot, arrays, gathered, mixing_pieces, part, chunks, ctx_size
    )
    arrays = feed(arrays, (0, 1))
    zero, one = (
        Reduction(arrays[f"keep{chunk}"], arrays[f"send{chunk}"], place, sizes) for chunk in (0, 1)
    )
    arrays, gathers[-1].far = tie((arrays, gathers[-1].far), zero, one)
    gathered.append(gathers[-1].finish())
    arrays = tie(arrays, zero, one, came=[zero])
    zero.y()
    arrays = tie(arrays, zero, one, came=[one])
    one.x()
    arrays = tie(arrays, zero, one)
    arrays = feed(arrays, (2,))
    two = Reduction(arrays["keep2"], arrays["send2"], place, sizes)
    grad_attended = tie(arrays["grad_attended"], zero, one, two, came=[zero, one])
    zero.x()
    one.y()
    grad_attended = tie(grad_attended, zero, one, two, came=[two])
    two.y([round_up(two.rows // ctx_size * 2 // 5, 8)])
    grad_attended = tie(grad_attended, zero, one, two).reshape(seqs, rows, width)
    grad_queries, terms = [], []
    for seq in range(seqs):
        part, *terms = attend_back(
            seq, place_one, queries, starts, exact, logs, grad_attended, keyvals, terms, blocks
        )
        came = [zero, one, two] if seq == 0 else [zero, two]
        part, grad_attended, terms = tie((part, grad_attended, terms), *came, came=came)
        grad_queries.append(part[0])
        if seq == 0:
            zero.z(one)
            two.y_more()
            grad_attended = tie(grad_attended, zero, two)
    two.y_joined()
    two.x()
    grad_queries, terms = tie((grad_queries, terms), zero, two)
    arriving = lax.all_to_all(terms[0], "ctx", 0, 0)
    zero.z_back()
    grad_scaled, keep, send = query_stage(spot, scaled_one, grad_queries, query_pieces, ctx_size)
    query = Reduction(keep, send, place, sizes)
    grad_scaled = tie(grad_scaled, zero, two, query)
    query.y()
    grad_scaled, arriving = tie((grad_scaled, arriving), zero, query)
    input_grad, keep, send = last_stage(
        spot, inputs, gain_one, scaled_one, arriving, grad_scaled, arrays["grad_hidden"], small_pieces
    )
    shared = Reduction(keep, send, place, sizes)
    input_grad = tie(input_grad, zero, two, shared, query, came=[two, zero])
    two.z()
    zero.x_back()
    input_grad = tie(input_grad, zero, two)
    input_grad = tie(input_grad, shared, query, came=[shared])
    shared.y()
    input_grad = tie(input_grad, shared)
    input_grad = tie(input_grad, shared, query, came=[shared, query])
    late = jnp.concatenate([query.everywhere(), shared.everywhere()], axis=1)
    late = lax.all_to_all(late, "ctx", 0, 0)
    two.z_back()
    input_grad = tie(input_grad, two)
    two.x_back()
    input_grad = tie(input_grad, two)
    late = jnp.sum(late.astype(F32), axis=0).astype(BF16)
    late = lax.all_to_all(jnp.broadcast_to(late, (ctx_size,) + late.shape), "ctx", 0, 0)
    down_grad, up_grad, mixing_grad, query_grad, shared_grad, first_grad, second_grad = final_stage(
        place_one,
        [zero.held, zero.coming[0], two.held, two.coming[0]],
        late,
        query.rows // ctx_size,
        chunks,
        wt_size,
        width,
    )

    def own_gain(lines):
        vector = lines[: width // LANES].reshape(width)
        return lax.dynamic_slice_in_dim(vector, spot_index * height, height, 0)

    return (
        arrays["layer_out"].reshape(seqs, rows, width),
        input_grad.reshape(seqs, rows, width),
        own_gain(first_grad),
        query_grad,
        shared_grad,
        mixing_grad,
        own_gain(second_grad),
        up_grad,
        down_grad,
    )


def solution(mesh):
    in_specs = (
        P("wt", "ctx", None),
        P("wt", "ctx"),
        P("wt"),
        P("wt", None),
        P("wt", None),
        P("wt", None),
        P("wt"),
        P("wt", None),
        P("wt", None),
        P("wt", "ctx", None),
    )
    out_specs = (
        P("wt", "ctx", None),
        P("wt", "ctx", None),
        P("wt"),
        P("wt", None),
        P("wt", None),
        P("wt", None),
        P("wt"),
        P("wt", None),
        P("wt", None),
    )
    run = functools.partial(body, wt_size=mesh.shape["wt"], ctx_size=mesh.shape["ctx"])
    return jax.shard_map(run, mesh=mesh, in_specs=in_specs, out_specs=out_specs, check_vma=False)
```

time: 368 us -> 328 us (0.89)
  starting transfers between devices: 90.3 us -> 72.4 us
  blocking collectives: 12.7 us -> 0 us
  other arithmetic: 23.7 us -> 19 us
    ppermute x61 -> x46, starting transfers between devices: 82.5 us -> 50.1 us  [swap(): return lax.ppermute(values, axis, [(i, i ^ mask) for i in range(size)])]
    ppermute x61 -> x46, waiting for transfers between devices: 123 us -> 106 us  [swap(): return lax.ppermute(values, axis, [(i, i ^ mask) for i in range(size)])]
    all_to_all x2 -> x4, waiting for transfers between devices: 5.13 us -> 20.9 us  [the longest x1 20.9 us: body(): arriving = lax.all_to_all(terms[0], 'ctx', 0, 0)]
    all_to_all x2 -> x4, starting transfers between devices: 7.8 us -> 22.3 us  [the longest x1 9.6 us: body(): arriving = lax.all_to_all(terms[0], 'ctx', 0, 0)]
    all_to_all x1 -> x0, blocking collectives: 12.7 us -> none  [body(): everywhere = lax.all_to_all(everywhere, 'ctx', 0, 0)]
    convert_element_type x19 -> x15, other arithmetic: 19.2 us -> 12.9 us  [the longest x6 5.75 us: y(): self.add(lambda v: v[1][..., begin:end, :]).astype(BF16)]
    unnamed x64 -> x85, local copies, waits for them, and re-layouts: 2.02 us -> 7.69 us
    optimization_barrier x4 -> x3, local copies, waits for them, and re-layouts: 7.45 us -> 2.67 us  [tie(): lax.optimization_barrier((main, state, [one.coming for one in came]))]
  transfers between devices with their start and end apart: 63 -> 50, of which waited for: 33 -> 20; matrix products, arithmetic and copies ran while one was open for 8% -> 5% of each run, Pallas kernels for 19% -> 26%
where the time goes in v3:
time: 328 us; the launch traced here: 329 us
  waiting for transfers between devices  127 us (39%)
  Pallas kernels  90.9 us (28%)
  starting transfers between devices  72.4 us (22%)
  other arithmetic  19 us (6%)
  local copies, waits for them, and re-layouts  17.7 us (5%)
    ppermute x46, waiting for transfers between devices, swap(): return lax.ppermute(values, axis, [(i, i ^ mask) for i in range(size)])  106 us
    ppermute x46, starting transfers between devices, swap(): return lax.ppermute(values, axis, [(i, i ^ mask) for i in range(size)])  50.1 us
    pallas_call x2, Pallas kernels, feed_stage(): pl.pallas_call(functools.partial(feed_kernel, pieces=pieces, part=part, f...  44 us
    all_to_all x1, waiting for transfers between devices, body(): arriving = lax.all_to_all(terms[0], 'ctx', 0, 0)  20.9 us
    pallas_call x2, Pallas kernels, attend_back(): pl.pallas_call(functools.partial(attend_back_kernel, seq=seq, blocks=bloc...  13.1 us
    pallas_call x1, Pallas kernels, attend(): pl.pallas_call(functools.partial(attend_kernel, blocks=blocks, tile_rows=...  10.5 us
    all_to_all x1, starting transfers between devices, body(): arriving = lax.all_to_all(terms[0], 'ctx', 0, 0)  9.6 us
    unnamed x85, local copies, waits for them, and re-layouts  7.69 us
  transfers between devices with their start and end apart: 50, of which 20 were waited for; matrix products, arithmetic and copies ran while one was open for 5% of the time, Pallas kernels for 26%

profile of v3, /device:TPU:0, one launch (start us, length us, event | category | flops | bytes accessed | tf_op | source)
XLA Modules:
  0.0 328.6 jit_solution(3249065998476399909)
XLA Ops:
  2.1 3.0 collective-permute-start.1
  9.4 4.3 %first_norm.1 = (bf16[512,768]{1,0:T(8,128)(2,1)}, bf16[8,544,128]{2,1,0:T(8,128)(2,1)}) custom-call(s32[1]{0:T(128)} %bitcast.spot_ref, bf16[512,768]{1,0:T(8,128)(2,1)} %bitcast.85, f32[1,768]{1,0:T(1,128)} %reshape_squeeze.6.gain, bf16[2,2,128]{2,1,0:T(2,128)(2,1)} %reshape.172.documents, bf16[208,128]{1,0:T(8,128)(2,1)} %copy-done.27, ...), custom_call_target="tpu_custom_call" | custom-call | flops 1 | bytes 1 | tf_op jit(solution)/shard_map/first_norm/pallas_call | solution.py:150
  14.8 5.8 %all-to-all-start = ((bf16[8,544,128]{2,1,0:T(8,128)(2,1)}), bf16[8,544,128]{2,1,0:T(8,128)(2,1)S(1)}, u32[]{:S(2)}, u32[]{:S(2)}) async-start(bf16[8,544,128]{2,1,0:T(8,128)(2,1)} %get-tuple-element.208), calls=%async_computation | async-start | bytes 2228224 | tf_op jit(solution)/shard_map/all_to_all | solution.py:1109
  20.6 3.1 pack.1
  25.8 23.4 %collective-permute-done.5.refs_11_.refs_7_ = bf16[192,768]{1,0:T(8,128)(2,1)S(1)} collective-permute-done((bf16[192,768]{1,0:T(8,128)(2,1)S(1)}, bf16[192,768]{1,0:T(8,128)(2,1)S(1)}, u32[]{:S(2)}, u32[]{:S(2)}) %collective-permute-start.5) | collective-permute-done | bytes 294944 | tf_op jit(solution)/shard_map/ppermute | solution.py:952
  50.2 1.6 collective-permute-start.8
  54.1 10.5 %attend.1 = (bf16[2,256,768]{2,1,0:T(8,128)(2,1)}, s32[2,256,128]{2,1,0:T(8,128)}, f32[2,256,768]{2,1,0:T(8,128)}, bf16[2,256,768]{2,1,0:T(8,128)(2,1)}, f32[2,256,768]{2,1,0:T(8,128)}) custom-call(s32[1]{0:T(128)} %bitcast.spot_ref, s32[1]{0:T(128)} %bitcast.1.place_ref, bf16[512,768]{1,0:T(8,128)(2,1)} %get-tuple-element.206.scaled, ...), custom_call_target="tpu_custom_call" | custom-call | flops 1 | bytes 1 | tf_op jit(solution)/shard_map/attend/pallas_call | solution.py:416
  64.6 4.2 %collective-permute-done.8.refs_7_ = bf16[1536,256]{1,0:T(8,128)(2,1)} collective-permute-done((bf16[1536,256]{1,0:T(8,128)(2,1)}, bf16[1536,256]{1,0:T(8,128)(2,1)}, u32[]{:S(2)}, u32[]{:S(2)}) %collective-permute-start.8) | collective-permute-done | bytes 786464 | tf_op jit(solution)/shard_map/ppermute | solution.py:952
  68.8 1.8 collective-permute-start.15
  73.3 23.9 %feed0.1 = (bf16[2,1536,256]{2,1,0:T(8,128)(2,1)}, bf16[2,1536,256]{2,1,0:T(8,128)(2,1)}, bf16[2,1536,256]{2,1,0:T(8,128)(2,1)}, bf16[2,1536,256]{2,1,0:T(8,128)...) custom-call(s32[1]{0:T(128)} %bitcast.spot_ref, ...), custom_call_target="tpu_custom_call" | custom-call | flops 1 | bytes 1 | tf_op jit(solution)/shard_map/feed0/pallas_call | solution.py:747
  97.4 1.6 copy.22
  101.0 2.6 fusion
  103.6 1.7 collective-permute-done.17
  105.3 1.8 fusion.1
  107.0 1.5 collective-permute-start.21
  109.6 20.1 %feed2.1 = (bf16[2,2176,256]{2,1,0:T(8,128)(2,1)}, bf16[2,2176,256]{2,1,0:T(8,128)(2,1)}, bf16[512,768]{1,0:T(8,128)(2,1)}, f32[512,768]{1,0:T(8,128)}, bf16[512,768]{1,0:T(8,128)(2,1)}) custom-call(s32[1]{0:T(128)} %bitcast.spot_ref, bf16[512,768]{1,0:T(8,128)(2,1)} %bitcast.89, bf16[1536,256]{1,0:T(8,128)(2,1)} %get-tuple-element.234.refs_1_, ...), custom_call_target="tpu_custom_call" | custom-call | flops 1 | bytes 1 | tf_op jit(solution)/shard_map/feed2/pallas_call | solution.py:747
  132.2 2.2 collective-permute-done.22
  139.1 6.6 %attend_back.2 = (bf16[1,256,768]{2,1,0:T(8,128)(2,1)}, bf16[8,2,256,128]{3,2,1,0:T(8,128)(2,1)}) custom-call(s32[1]{0:T(128)} %bitcast.1.place_ref, bf16[2,256,768]{2,1,0:T(8,128)(2,1)} %get-tuple-element.275.queries, s32[2,256,128]{2,1,0:T(8,128)} %get-tuple-element.276.starts, f32[2,256,768]{2,1,0:T(8,128)} %get-tuple-element.277.exact, ...), custom_call_target="tpu_custom_call" | custom-call | flops 1 | bytes 1 | tf_op jit(solution)/shard_map/attend_back/pallas_call | solution.py:473
  145.8 2.8 collective-permute-done.23
  148.6 9.1 %collective-permute-done.24 = bf16[4,192,256]{2,1,0:T(8,128)(2,1)} collective-permute-done((bf16[4,192,256]{2,1,0:T(8,128)(2,1)}, bf16[4,192,256]{2,1,0:T(8,128)(2,1)}, u32[]{:S(2)}, u32[]{:S(2)}) %collective-permute-start.24) | collective-permute-done | bytes 393248 | tf_op jit(solution)/shard_map/ppermute | solution.py:952
  161.9 1.5 collective-permute-start.26
  163.3 8.4 %collective-permute-start.27 = (bf16[2,192,256]{2,1,0:T(8,128)(2,1)S(1)}, bf16[2,192,256]{2,1,0:T(8,128)(2,1)S(1)}, u32[]{:S(2)}, u32[]{:S(2)}) collective-permute-start(bf16[2,192,256]{2,1,0:T(8,128)(2,1)S(1)} %pad_maximum_fusion.5), channel_id=1, source_target_pairs={{0,16},{4,20},{8,24},{12,28},{16,0},{20,4},{24,8},{28,12},{1,17},{... | collective-permute-start | bytes 589832 | tf_op jit(solution)/shard_map/ppermute | solution.py:952
  171.8 6.5 %attend_back.3 = (bf16[1,256,768]{2,1,0:T(8,128)(2,1)}, bf16[8,2,256,128]{3,2,1,0:T(8,128)(2,1)}) custom-call(s32[1]{0:T(128)} %bitcast.1.place_ref, bf16[2,256,768]{2,1,0:T(8,128)(2,1)} %get-tuple-element.275.queries, s32[2,256,128]{2,1,0:T(8,128)} %get-tuple-element.276.starts, ...), custom_call_target="tpu_custom_call", output_to_operand_aliasing={{1}: (7, {})} | custom-call | flops 1 | bytes 1 | tf_op jit(solution)/shard_map/attend_back/pallas_call | solution.py:473
  179.3 6.7 %collective-permute-done.27 = bf16[2,192,256]{2,1,0:T(8,128)(2,1)S(1)} collective-permute-done((bf16[2,192,256]{2,1,0:T(8,128)(2,1)S(1)}, bf16[2,192,256]{2,1,0:T(8,128)(2,1)S(1)}, u32[]{:S(2)}, u32[]{:S(2)}) %collective-permute-start.27) | collective-permute-done | bytes 196640 | tf_op jit(solution)/shard_map/ppermute | solution.py:952
  187.9 9.6 %all-to-all-start.1 = ((bf16[8,2,256,128]{3,2,1,0:T(8,128)(2,1)}), bf16[8,2,256,128]{3,2,1,0:T(8,128)(2,1)S(1)}, u32[]{:S(2)}, u32[]{:S(2)}) async-start(bf16[8,2,256,128]{3,2,1,0:T(8,128)(2,1)} %get-tuple-element.341), calls=%async_computation.1 | async-start | bytes 2097152 | tf_op jit(solution)/shard_map/all_to_all | solution.py:1177
  197.5 4.7 %query_grad.1 = (f32[512,768]{1,0:T(8,128)}, bf16[2,576,256]{2,1,0:T(8,128)(2,1)}, bf16[2,576,256]{2,1,0:T(8,128)(2,1)}) custom-call(s32[1]{0:T(128)} %bitcast.spot_ref, bf16[512,768]{1,0:T(8,128)(2,1)} %get-tuple-element.206.scaled, bf16[256,768]{1,0:T(8,128)(2,1)} %bitcast.105, bf16[256,768]{1,0:T(8,128)(2,1)} %bitcast.106, bf16[192,768]{1,0:T(8,128)(2,1)} %rest_2_.1, ...), custom_call_target="tpu_custom_call" | custom-call | flops 1 | bytes 1 | tf_op jit(solution)/shard_map/query_grad/pallas_call | solution.py:792
  203.4 2.1 collective-permute-start.31
  205.5 1.5 collective-permute-start.32
  206.9 2.4 collective-permute-start.33
  210.7 20.9 %all-to-all-done.1.arrived = bf16[8,2,256,128]{3,2,1,0:T(8,128)(2,1)S(1)} async-done(((bf16[8,2,256,128]{3,2,1,0:T(8,128)(2,1)}), bf16[8,2,256,128]{3,2,1,0:T(8,128)(2,1)S(1)}, u32[]{:S(2)}, u32[]{:S(2)}) %all-to-all-start.1) | async-done | bytes 1048608 | tf_op jit(solution)/shard_map/all_to_all | solution.py:1177
  232.5 6.1 %last.1 = (f32[512,768]{1,0:T(8,128)}, bf16[2,192,256]{2,1,0:T(8,128)(2,1)}, bf16[2,192,256]{2,1,0:T(8,128)(2,1)}) custom-call(s32[1]{0:T(128)} %bitcast.spot_ref, bf16[512,768]{1,0:T(8,128)(2,1)} %bitcast.87, f32[1,768]{1,0:T(1,128)} %reshape_squeeze.6.gain, bf16[512,768]{1,0:T(8,128)(2,1)} %get-tuple-element.206.scaled, ...), custom_call_target="tpu_custom_call" | custom-call | flops 1 | bytes 1 | tf_op jit(solution)/shard_map/last/pallas_call | solution.py:849
  239.8 2.0 add_convert_fusion.11
  243.1 2.1 collective-permute-start.36
  245.2 9.3 %collective-permute-done.36 = bf16[2,4,24,256]{3,2,0,1:T(8,128)(2,1)S(1)} collective-permute-done((bf16[2,4,24,256]{3,2,0,1:T(8,128)(2,1)S(1)}, bf16[2,4,24,256]{3,2,0,1:T(8,128)(2,1)S(1)}, u32[]{:S(2)}, u32[]{:S(2)}) %collective-permute-start.36) | collective-permute-done | bytes 98336 | tf_op jit(solution)/shard_map/ppermute | solution.py:952
  255.3 3.5 %all-to-all-start.2 = ((bf16[8,96,256]{2,1,0:T(8,128)(2,1)}), bf16[8,96,256]{2,1,0:T(8,128)(2,1)S(1)}, u32[]{:S(2)}, u32[]{:S(2)}) async-start(bf16[8,96,256]{2,1,0:T(8,128)(2,1)} %pad_maximum_fusion.3), calls=%async_computation.2 | async-start | bytes 786432 | tf_op jit(solution)/shard_map/all_to_all | solution.py:1197
  258.8 1.9 collective-permute-start.38
  260.7 2.4 collective-permute-start.39
  263.3 7.4 %collective-permute-done.38 = bf16[1,272,256]{2,1,0:T(8,128)(2,1)S(1)} collective-permute-done((bf16[1,272,256]{2,1,0:T(8,128)(2,1)S(1)}, bf16[1,272,256]{2,1,0:T(8,128)(2,1)S(1)}, u32[]{:S(2)}, u32[]{:S(2)}) %collective-permute-start.38) | collective-permute-done | bytes 139296 | tf_op jit(solution)/shard_map/ppermute | solution.py:952
  270.6 10.2 %collective-permute-done.39 = bf16[1,272,256]{2,1,0:T(8,128)(2,1)S(1)} collective-permute-done((bf16[1,272,256]{2,1,0:T(8,128)(2,1)S(1)}, bf16[1,272,256]{2,1,0:T(8,128)(2,1)S(1)}, u32[]{:S(2)}, u32[]{:S(2)}) %collective-permute-start.39) | collective-permute-done | bytes 139296 | tf_op jit(solution)/shard_map/ppermute | solution.py:952
  280.9 2.2 collective-permute-start.41
  283.1 2.4 collective-permute-start.43
  285.6 1.5 collective-permute-start.44
  287.9 3.5 %all-to-all-start.3 = ((bf16[8,96,256]{2,1,0:T(8,128)(2,1)}), bf16[8,96,256]{2,1,0:T(8,128)(2,1)S(1)}, u32[]{:S(2)}, u32[]{:S(2)}) async-start(bf16[8,96,256]{2,1,0:T(8,128)(2,1)} %broadcast_in_dim.10), calls=%async_computation.3 | async-start | bytes 786432 | tf_op jit(solution)/shard_map/all_to_all | solution.py:1203
  291.3 7.0 %collective-permute-done.42 = bf16[1,272,256]{2,1,0:T(8,128)(2,1)S(1)} collective-permute-done((bf16[1,272,256]{2,1,0:T(8,128)(2,1)S(1)}, bf16[1,272,256]{2,1,0:T(8,128)(2,1)S(1)}, u32[]{:S(2)}, u32[]{:S(2)}) %collective-permute-start.42) | collective-permute-done | bytes 139296 | tf_op jit(solution)/shard_map/ppermute | solution.py:952
  298.4 3.6 %collective-permute-start.45 = (bf16[4,1,272,256]{3,2,1,0:T(8,128)(2,1)S(1)}, bf16[4,1,272,256]{3,2,1,0:T(8,128)(2,1)S(1)}, u32[]{:S(2)}, u32[]{:S(2)}) collective-permute-start(bf16[4,1,272,256]{3,2,1,0:T(8,128)(2,1)S(1)} %pad_maximum_fusion.1.last_own), channel_id=1, source_target_pairs={{0,4},{4,0},{8,12},{12,8},{16,20},{20,16},{24,28},{28,24},{1,5},{5... | collective-permute-start | bytes 1671176 | tf_op jit(solution)/shard_map/ppermute | solution.py:952
  302.0 7.2 %collective-permute-done.44.early_other = bf16[4,2,192,256]{3,2,1,0:T(8,128)(2,1)S(1)} collective-permute-done((bf16[4,2,192,256]{3,2,1,0:T(8,128)(2,1)S(1)}, bf16[4,2,192,256]{3,2,1,0:T(8,128)(2,1)S(1)}, u32[]{:S(2)}, u32[]{:S(2)}) %collective-permute-start.44) | collective-permute-done | bytes 786464 | tf_op jit(solution)/shard_map/ppermute | solution.py:952
  309.2 10.2 %collective-permute-done.45.last_other = bf16[4,1,272,256]{3,2,1,0:T(8,128)(2,1)S(1)} collective-permute-done((bf16[4,1,272,256]{3,2,1,0:T(8,128)(2,1)S(1)}, bf16[4,1,272,256]{3,2,1,0:T(8,128)(2,1)S(1)}, u32[]{:S(2)}, u32[]{:S(2)}) %collective-permute-start.45) | collective-permute-done | bytes 557088 | tf_op jit(solution)/shard_map/ppermute | solution.py:952
  320.9 5.0 %final.1 = (f32[768,768]{1,0:T(8,128)}, f32[192,3072]{1,0:T(8,128)}, f32[192,768]{1,0:T(8,128)}, f32[192,768]{1,0:T(8,128)}, f32[192,128]{1,0:T(8,128)}, /*index=5*/f32[8,128]{1,0:T(8,128)}, f32[8,128]{1,0:T(8,128)}) custom-call(s32[1]{0:T(128)} %bitcast.1.place_ref, bf16[4,2,192,256]{3,2,1,0:T(8,128)(2,1)} %copy-done.5, ...), custom_call_target="tpu_custom_call" | custom-call | flops 1 | bytes 1 | tf_op jit(solution)/shard_map/final/pallas_call | solution.py:925
  (203 shorter events, 44.3 us)
Async XLA Ops:
  2.1 5.2 %collective-permute-start.1 = (bf16[208,128]{1,0:T(8,128)(2,1)S(1)}, bf16[208,128]{1,0:T(8,128)(2,1)S(1)}, u32[]{:S(2)}, u32[]{:S(2)}) collective-permute-start(bf16[208,128]{1,0:T(8,128)(2,1)S(1)} %fusion.11.rest_0_), channel_id=1, source_target_pairs={{0,2},{1,3},{2,0},{3,1},{4,6},{5,7},{6,4},{7,5},{8,10},{9,11},{10,... | collective-permute-start | bytes 159752 | tf_op jit(solution)/shard_map/ppermute | solution.py:952
  5.2 2.8 collective-permute-start
  5.2 9.6 %collective-permute-start.3 = (bf16[192,768]{1,0:T(8,128)(2,1)}, bf16[192,768]{1,0:T(8,128)(2,1)S(1)}, u32[]{:S(2)}, u32[]{:S(2)}) collective-permute-start(bf16[192,768]{1,0:T(8,128)(2,1)} %rest_2_.1), channel_id=1, source_target_pairs={{0,2},{1,3},{2,0},{3,1},{4,6},{5,7},{6,4},{7,5},{8,10},{9,11},{10,... | collective-permute-start | bytes 884744 | tf_op jit(solution)/shard_map/ppermute | solution.py:952
  14.8 34.4 %all-to-all-start = ((bf16[8,544,128]{2,1,0:T(8,128)(2,1)}), bf16[8,544,128]{2,1,0:T(8,128)(2,1)S(1)}, u32[]{:S(2)}, u32[]{:S(2)}) async-start(bf16[8,544,128]{2,1,0:T(8,128)(2,1)} %get-tuple-element.208), calls=%async_computation | async-start | bytes 2228224 | tf_op jit(solution)/shard_map/all_to_all | solution.py:1109
  23.8 25.4 %collective-permute-start.4 = (bf16[1536,256]{1,0:T(8,128)(2,1)}, bf16[1536,256]{1,0:T(8,128)(2,1)S(1)}, u32[]{:S(2)}, u32[]{:S(2)}) collective-permute-start(bf16[1536,256]{1,0:T(8,128)(2,1)} %get-tuple-element.211.refs_1_), channel_id=1, source_target_pairs={{0,2},{1,3},{2,0},{3,1},{4,6},{5,7},{6,4},{7,5},{8,10},{9,11},{10,... | collective-permute-start | bytes 2359304 | tf_op jit(solution)/shard_map/ppermute | solution.py:952
  24.9 24.3 %collective-permute-start.5 = (bf16[192,768]{1,0:T(8,128)(2,1)S(1)}, bf16[192,768]{1,0:T(8,128)(2,1)S(1)}, u32[]{:S(2)}, u32[]{:S(2)}) collective-permute-start(bf16[192,768]{1,0:T(8,128)(2,1)S(1)} %copy-done.13), channel_id=1, source_target_pairs={{0,2},{1,3},{2,0},{3,1},{4,6},{5,7},{6,4},{7,5},{8,10},{9,11},{10,... | collective-permute-start | bytes 884744 | tf_op jit(solution)/shard_map/ppermute | solution.py:952
  25.8 23.4 %collective-permute-start.6 = (bf16[192,768]{1,0:T(8,128)(2,1)S(1)}, bf16[192,768]{1,0:T(8,128)(2,1)S(1)}, u32[]{:S(2)}, u32[]{:S(2)}) collective-permute-start(bf16[192,768]{1,0:T(8,128)(2,1)S(1)} %collective-permute-done.3.rest_2_.rest_4_), channel_id=1, source_target_pairs={{0,1},{1,0},{2,3},{3,2},{4,5},{5,4},{6,7},{7,6},{8,9},{9,8},{10,11... | collective-permute-start | bytes 884744 | tf_op jit(solution)/shard_map/ppermute | solution.py:952
  50.2 18.6 %collective-permute-start.8 = (bf16[1536,256]{1,0:T(8,128)(2,1)}, bf16[1536,256]{1,0:T(8,128)(2,1)}, u32[]{:S(2)}, u32[]{:S(2)}) collective-permute-start(bf16[1536,256]{1,0:T(8,128)(2,1)} %get-tuple-element.220.refs_5_), channel_id=1, source_target_pairs={{0,2},{1,3},{2,0},{3,1},{4,6},{5,7},{6,4},{7,5},{8,10},{9,11},{10,... | collective-permute-start | bytes 2359304 | tf_op jit(solution)/shard_map/ppermute | solution.py:952
  51.8 18.8 %collective-permute-start.9 = (bf16[1536,256]{1,0:T(8,128)(2,1)}, bf16[1536,256]{1,0:T(8,128)(2,1)}, u32[]{:S(2)}, u32[]{:S(2)}) collective-permute-start(bf16[1536,256]{1,0:T(8,128)(2,1)} %get-tuple-element.211.refs_1_), channel_id=1, source_target_pairs={{0,1},{1,0},{2,3},{3,2},{4,5},{5,4},{6,7},{7,6},{8,9},{9,8},{10,11... | collective-permute-start | bytes 2359304 | tf_op jit(solution)/shard_map/ppermute | solution.py:952
  52.3 16.5 %collective-permute-start.13 = (bf16[192,768]{1,0:T(8,128)(2,1)S(1)}, bf16[192,768]{1,0:T(8,128)(2,1)S(1)}, u32[]{:S(2)}, u32[]{:S(2)}) collective-permute-start(bf16[192,768]{1,0:T(8,128)(2,1)S(1)} %copy-done.13), channel_id=1, source_target_pairs={{0,1},{1,0},{2,3},{3,2},{4,5},{5,4},{6,7},{7,6},{8,9},{9,8},{10,11... | collective-permute-start | bytes 884744 | tf_op jit(solution)/shard_map/ppermute | solution.py:952
  52.4 19.9 %collective-permute-start.11 = (bf16[1536,256]{1,0:T(8,128)(2,1)}, bf16[1536,256]{1,0:T(8,128)(2,1)}, u32[]{:S(2)}, u32[]{:S(2)}) collective-permute-start(bf16[1536,256]{1,0:T(8,128)(2,1)} %get-tuple-element.220.refs_5_), channel_id=1, source_target_pairs={{0,1},{1,0},{2,3},{3,2},{4,5},{5,4},{6,7},{7,6},{8,9},{9,8},{10,11... | collective-permute-start | bytes 2359304 | tf_op jit(solution)/shard_map/ppermute | solution.py:952
  53.4 18.9 %collective-permute-start.10 = (bf16[1536,256]{1,0:T(8,128)(2,1)}, bf16[1536,256]{1,0:T(8,128)(2,1)}, u32[]{:S(2)}, u32[]{:S(2)}) collective-permute-start(bf16[1536,256]{1,0:T(8,128)(2,1)} %copy-done.21), channel_id=1, source_target_pairs={{0,1},{1,0},{2,3},{3,2},{4,5},{5,4},{6,7},{7,6},{8,9},{9,8},{10,11... | collective-permute-start | bytes 2359304 | tf_op jit(solution)/shard_map/ppermute | solution.py:952
  68.8 3.4 %collective-permute-start.12 = (bf16[1536,256]{1,0:T(8,128)(2,1)}, bf16[1536,256]{1,0:T(8,128)(2,1)S(1)}, u32[]{:S(2)}, u32[]{:S(2)}) collective-permute-start(bf16[1536,256]{1,0:T(8,128)(2,1)} %collective-permute-done.8.refs_7_), channel_id=1, source_target_pairs={{0,1},{1,0},{2,3},{3,2},{4,5},{5,4},{6,7},{7,6},{8,9},{9,8},{10,11... | collective-permute-start | bytes 2359304 | tf_op jit(solution)/shard_map/ppermute | solution.py:952
  68.8 28.3 %collective-permute-start.15 = (bf16[1536,256]{1,0:T(8,128)(2,1)}, bf16[1536,256]{1,0:T(8,128)(2,1)}, u32[]{:S(2)}, u32[]{:S(2)}) collective-permute-start(bf16[1536,256]{1,0:T(8,128)(2,1)} %get-tuple-element.234.refs_1_), channel_id=1, source_target_pairs={{0,2},{1,3},{2,0},{3,1},{4,6},{5,7},{6,4},{7,5},{8,10},{9,11},{10,... | collective-permute-start | bytes 2359304 | tf_op jit(solution)/shard_map/ppermute | solution.py:952
  70.7 1.6 collective-permute-start.14
  97.2 3.8 %collective-permute-start.16 = (bf16[2,2,4,192,256]{4,3,2,1,0:T(8,128)(2,1)}, bf16[2,2,4,192,256]{4,3,2,1,0:T(8,128)(2,1)}, u32[]{:S(2)}, u32[]{:S(2)}) collective-permute-start(bf16[2,2,4,192,256]{4,3,2,1,0:T(8,128)(2,1)} %bitcast.118), channel_id=1, source_target_pairs={{0,1},{1,0},{2,3},{3,2},{4,5},{5,4},{6,7},{7,6},{8,9},{9,8},{10,11... | collective-permute-start | bytes 4718600 | tf_op jit(solution)/shard_map/ppermute | solution.py:952
  99.0 6.2 %collective-permute-start.17 = (bf16[2,2,4,192,256]{4,3,2,0,1:T(8,128)(2,1)S(1)}, bf16[2,2,4,192,256]{4,3,2,0,1:T(8,128)(2,1)}, u32[]{:S(2)}, u32[]{:S(2)}) collective-permute-start(bf16[2,2,4,192,256]{4,3,2,0,1:T(8,128)(2,1)S(1)} %copy.22), channel_id=1, source_target_pairs={{0,1},{1,0},{2,3},{3,2},{4,5},{5,4},{6,7},{7,6},{8,9},{9,8},{10,11... | collective-permute-start | bytes 4718600 | tf_op jit(solution)/shard_map/ppermute | solution.py:952
  99.4 10.2 %collective-permute-start.18 = (bf16[1536,256]{1,0:T(8,128)(2,1)}, bf16[1536,256]{1,0:T(8,128)(2,1)}, u32[]{:S(2)}, u32[]{:S(2)}) collective-permute-start(bf16[1536,256]{1,0:T(8,128)(2,1)} %get-tuple-element.234.refs_1_), channel_id=1, source_target_pairs={{0,1},{1,0},{2,3},{3,2},{4,5},{5,4},{6,7},{7,6},{8,9},{9,8},{10,11... | collective-permute-start | bytes 2359304 | tf_op jit(solution)/shard_map/ppermute | solution.py:952
  99.6 10.0 %collective-permute-start.19 = (bf16[1536,256]{1,0:T(8,128)(2,1)}, bf16[1536,256]{1,0:T(8,128)(2,1)}, u32[]{:S(2)}, u32[]{:S(2)}) collective-permute-start(bf16[1536,256]{1,0:T(8,128)(2,1)} %collective-permute-done.15.refs_3_), channel_id=1, source_target_pairs={{0,1},{1,0},{2,3},{3,2},{4,5},{5,4},{6,7},{7,6},{8,9},{9,8},{10,11... | collective-permute-start | bytes 2359304 | tf_op jit(solution)/shard_map/ppermute | solution.py:952
  107.0 22.7 %collective-permute-start.21 = (bf16[2,4,192,256]{3,2,1,0:T(8,128)(2,1)S(1)}, bf16[2,4,192,256]{3,2,1,0:T(8,128)(2,1)S(1)}, u32[]{:S(2)}, u32[]{:S(2)}) collective-permute-start(bf16[2,4,192,256]{3,2,1,0:T(8,128)(2,1)S(1)} %get-tuple-element.285), channel_id=1, source_target_pairs={{0,4},{4,0},{8,12},{12,8},{16,20},{20,16},{24,28},{28,24},{1,5},{5... | collective-permute-start | bytes 2359304 | tf_op jit(solution)/shard_map/ppermute | solution.py:952
  108.5 21.2 %collective-permute-start.20 = (bf16[2,4,192,256]{3,2,1,0:T(8,128)(2,1)}, bf16[2,4,192,256]{3,2,1,0:T(8,128)(2,1)S(1)}, u32[]{:S(2)}, u32[]{:S(2)}) collective-permute-start(bf16[2,4,192,256]{3,2,1,0:T(8,128)(2,1)} %get-tuple-element.284), channel_id=1, source_target_pairs={{0,2},{1,3},{2,0},{3,1},{4,6},{5,7},{6,4},{7,5},{8,10},{9,11},{10,... | collective-permute-start | bytes 2359304 | tf_op jit(solution)/shard_map/ppermute | solution.py:952
  129.7 4.6 %collective-permute-start.22 = (bf16[2,2,4,272,256]{4,3,2,1,0:T(8,128)(2,1)}, bf16[2,2,4,272,256]{4,3,2,1,0:T(8,128)(2,1)S(1)}, u32[]{:S(2)}, u32[]{:S(2)}) collective-permute-start(bf16[2,2,4,272,256]{4,3,2,1,0:T(8,128)(2,1)} %bitcast.116), channel_id=1, source_target_pairs={{0,1},{1,0},{2,3},{3,2},{4,5},{5,4},{6,7},{7,6},{8,9},{9,8},{10,11... | collective-permute-start | bytes 6684680 | tf_op jit(solution)/shard_map/ppermute | solution.py:952
  136.4 21.3 %collective-permute-start.25 = (bf16[2,4,112,256]{3,2,1,0:T(8,128)(2,1)}, bf16[2,4,112,256]{3,2,1,0:T(8,128)(2,1)}, u32[]{:S(2)}, u32[]{:S(2)}) collective-permute-start(bf16[2,4,112,256]{3,2,1,0:T(8,128)(2,1)} %add_convert_fusion.4), channel_id=1, source_target_pairs={{0,2},{1,3},{2,0},{3,1},{4,6},{5,7},{6,4},{7,5},{8,10},{9,11},{10,... | collective-permute-start | bytes 1376264 | tf_op jit(solution)/shard_map/ppermute | solution.py:952
  137.4 11.2 %collective-permute-start.23 = (bf16[4,192,256]{2,1,0:T(8,128)(2,1)}, bf16[4,192,256]{2,1,0:T(8,128)(2,1)}, u32[]{:S(2)}, u32[]{:S(2)}) collective-permute-start(bf16[4,192,256]{2,1,0:T(8,128)(2,1)} %get-tuple-element.304), channel_id=1, source_target_pairs={{0,4},{4,0},{8,12},{12,8},{16,20},{20,16},{24,28},{28,24},{1,5},{5... | collective-permute-start | bytes 1179656 | tf_op jit(solution)/shard_map/ppermute | solution.py:952
  138.0 19.7 %collective-permute-start.24 = (bf16[4,192,256]{2,1,0:T(8,128)(2,1)}, bf16[4,192,256]{2,1,0:T(8,128)(2,1)}, u32[]{:S(2)}, u32[]{:S(2)}) collective-permute-start(bf16[4,192,256]{2,1,0:T(8,128)(2,1)} %get-tuple-element.305), channel_id=1, source_target_pairs={{0,2},{1,3},{2,0},{3,1},{4,6},{5,7},{6,4},{7,5},{8,10},{9,11},{10,... | collective-permute-start | bytes 1179656 | tf_op jit(solution)/shard_map/ppermute | solution.py:952
  160.9 25.1 %collective-permute-start.29 = (bf16[2,4,160,256]{3,2,1,0:T(8,128)(2,1)S(1)}, bf16[2,4,160,256]{3,2,1,0:T(8,128)(2,1)S(1)}, u32[]{:S(2)}, u32[]{:S(2)}) collective-permute-start(bf16[2,4,160,256]{3,2,1,0:T(8,128)(2,1)S(1)} %add_convert_fusion.2), channel_id=1, source_target_pairs={{0,2},{1,3},{2,0},{3,1},{4,6},{5,7},{6,4},{7,5},{8,10},{9,11},{10,... | collective-permute-start | bytes 1966088 | tf_op jit(solution)/shard_map/ppermute | solution.py:952
  161.9 17.5 %collective-permute-start.26 = (bf16[2,192,256]{2,1,0:T(8,128)(2,1)S(1)}, bf16[2,192,256]{2,1,0:T(8,128)(2,1)S(1)}, u32[]{:S(2)}, u32[]{:S(2)}) collective-permute-start(bf16[2,192,256]{2,1,0:T(8,128)(2,1)S(1)} %pad_maximum_fusion.4), channel_id=1, source_target_pairs={{0,8},{4,12},{8,0},{12,4},{16,24},{20,28},{24,16},{28,20},{1,9},{5... | collective-permute-start | bytes 589832 | tf_op jit(solution)/shard_map/ppermute | solution.py:952
  163.3 22.7 %collective-permute-start.27 = (bf16[2,192,256]{2,1,0:T(8,128)(2,1)S(1)}, bf16[2,192,256]{2,1,0:T(8,128)(2,1)S(1)}, u32[]{:S(2)}, u32[]{:S(2)}) collective-permute-start(bf16[2,192,256]{2,1,0:T(8,128)(2,1)S(1)} %pad_maximum_fusion.5), channel_id=1, source_target_pairs={{0,16},{4,20},{8,24},{12,28},{16,0},{20,4},{24,8},{28,12},{1,17},{... | collective-permute-start | bytes 589832 | tf_op jit(solution)/shard_map/ppermute | solution.py:952
  171.8 14.2 %collective-permute-start.28 = (bf16[2,192,256]{2,1,0:T(8,128)(2,1)S(1)}, bf16[2,192,256]{2,1,0:T(8,128)(2,1)S(1)}, u32[]{:S(2)}, u32[]{:S(2)}) collective-permute-start(bf16[2,192,256]{2,1,0:T(8,128)(2,1)S(1)} %pad_maximum_fusion.6), channel_id=1, source_target_pairs={{0,24},{4,28},{8,16},{12,20},{16,8},{20,12},{24,0},{28,4},{1,25},{... | collective-permute-start | bytes 589832 | tf_op jit(solution)/shard_map/ppermute | solution.py:952
  187.9 43.7 %all-to-all-start.1 = ((bf16[8,2,256,128]{3,2,1,0:T(8,128)(2,1)}), bf16[8,2,256,128]{3,2,1,0:T(8,128)(2,1)S(1)}, u32[]{:S(2)}, u32[]{:S(2)}) async-start(bf16[8,2,256,128]{3,2,1,0:T(8,128)(2,1)} %get-tuple-element.341), calls=%async_computation.1 | async-start | bytes 2097152 | tf_op jit(solution)/shard_map/all_to_all | solution.py:1177
  203.3 6.5 %collective-permute-start.30 = (bf16[2,2,4,72,256]{4,3,1,2,0:T(8,128)(2,1)S(1)}, bf16[2,2,4,72,256]{4,3,1,2,0:T(8,128)(2,1)S(1)}, u32[]{:S(2)}, u32[]{:S(2)}) collective-permute-start(bf16[2,2,4,72,256]{4,3,1,2,0:T(8,128)(2,1)S(1)} %copy.26), channel_id=1, source_target_pairs={{0,1},{1,0},{2,3},{3,2},{4,5},{5,4},{6,7},{7,6},{8,9},{9,8},{10,11... | collective-permute-start | bytes 1769480 | tf_op jit(solution)/shard_map/ppermute | solution.py:952
  203.4 35.3 %collective-permute-start.31 = (bf16[4,272,256]{2,1,0:T(8,128)(2,1)}, bf16[4,272,256]{2,1,0:T(8,128)(2,1)}, u32[]{:S(2)}, u32[]{:S(2)}) collective-permute-start(bf16[4,272,256]{2,1,0:T(8,128)(2,1)} %get-tuple-element.354), channel_id=1, source_target_pairs={{0,4},{4,0},{8,12},{12,8},{16,20},{20,16},{24,28},{28,24},{1,5},{5... | collective-permute-start | bytes 1671176 | tf_op jit(solution)/shard_map/ppermute | solution.py:952
  205.5 33.2 %collective-permute-start.32 = (bf16[2,192,256]{2,1,0:T(8,128)(2,1)S(1)}, bf16[2,192,256]{2,1,0:T(8,128)(2,1)S(1)}, u32[]{:S(2)}, u32[]{:S(2)}) collective-permute-start(bf16[2,192,256]{2,1,0:T(8,128)(2,1)S(1)} %add_convert_fusion.9), channel_id=1, source_target_pairs={{0,8},{4,12},{8,0},{12,4},{16,24},{20,28},{24,16},{28,20},{1,9},{5... | collective-permute-start | bytes 589832 | tf_op jit(solution)/shard_map/ppermute | solution.py:952
  206.9 31.7 %collective-permute-start.33 = (bf16[2,192,256]{2,1,0:T(8,128)(2,1)S(1)}, bf16[2,192,256]{2,1,0:T(8,128)(2,1)S(1)}, u32[]{:S(2)}, u32[]{:S(2)}) collective-permute-start(bf16[2,192,256]{2,1,0:T(8,128)(2,1)S(1)} %add_convert_fusion.9), channel_id=1, source_target_pairs={{0,16},{4,20},{8,24},{12,28},{16,0},{20,4},{24,8},{28,12},{1,17},{... | collective-permute-start | bytes 589832 | tf_op jit(solution)/shard_map/ppermute | solution.py:952
  209.3 29.4 %collective-permute-start.34 = (bf16[2,192,256]{2,1,0:T(8,128)(2,1)S(1)}, bf16[2,192,256]{2,1,0:T(8,128)(2,1)}, u32[]{:S(2)}, u32[]{:S(2)}) collective-permute-start(bf16[2,192,256]{2,1,0:T(8,128)(2,1)S(1)} %add_convert_fusion.9), channel_id=1, source_target_pairs={{0,24},{4,28},{8,16},{12,20},{16,8},{20,12},{24,0},{28,4},{1,25},{... | collective-permute-start | bytes 589832 | tf_op jit(solution)/shard_map/ppermute | solution.py:952
  239.7 3.3 collective-permute-start.35
  242.9 11.5 %collective-permute-start.37 = (bf16[2,4,72,256]{3,2,0,1:T(8,128)(2,1)S(1)}, bf16[2,4,72,256]{3,2,0,1:T(8,128)(2,1)S(1)}, u32[]{:S(2)}, u32[]{:S(2)}) collective-permute-start(bf16[2,4,72,256]{3,2,0,1:T(8,128)(2,1)S(1)} %copy-done.28), channel_id=1, source_target_pairs={{0,2},{1,3},{2,0},{3,1},{4,6},{5,7},{6,4},{7,5},{8,10},{9,11},{10,... | collective-permute-start | bytes 884744 | tf_op jit(solution)/shard_map/ppermute | solution.py:952
  243.1 11.3 %collective-permute-start.36 = (bf16[2,4,24,256]{3,2,0,1:T(8,128)(2,1)S(1)}, bf16[2,4,24,256]{3,2,0,1:T(8,128)(2,1)S(1)}, u32[]{:S(2)}, u32[]{:S(2)}) collective-permute-start(bf16[2,4,24,256]{3,2,0,1:T(8,128)(2,1)S(1)} %get-tuple-element.375), channel_id=1, source_target_pairs={{0,2},{1,3},{2,0},{3,1},{4,6},{5,7},{6,4},{7,5},{8,10},{9,11},{10,... | collective-permute-start | bytes 294920 | tf_op jit(solution)/shard_map/ppermute | solution.py:952
  255.3 31.7 %all-to-all-start.2 = ((bf16[8,96,256]{2,1,0:T(8,128)(2,1)}), bf16[8,96,256]{2,1,0:T(8,128)(2,1)S(1)}, u32[]{:S(2)}, u32[]{:S(2)}) async-start(bf16[8,96,256]{2,1,0:T(8,128)(2,1)} %pad_maximum_fusion.3), calls=%async_computation.2 | async-start | bytes 786432 | tf_op jit(solution)/shard_map/all_to_all | solution.py:1197
  258.8 11.8 %collective-permute-start.38 = (bf16[1,272,256]{2,1,0:T(8,128)(2,1)S(1)}, bf16[1,272,256]{2,1,0:T(8,128)(2,1)S(1)}, u32[]{:S(2)}, u32[]{:S(2)}) collective-permute-start(bf16[1,272,256]{2,1,0:T(8,128)(2,1)S(1)} %copy-done.41), channel_id=1, source_target_pairs={{0,8},{4,12},{8,0},{12,4},{16,24},{20,28},{24,16},{28,20},{1,9},{5... | collective-permute-start | bytes 417800 | tf_op jit(solution)/shard_map/ppermute | solution.py:952
  260.7 20.1 %collective-permute-start.39 = (bf16[1,272,256]{2,1,0:T(8,128)(2,1)S(1)}, bf16[1,272,256]{2,1,0:T(8,128)(2,1)S(1)}, u32[]{:S(2)}, u32[]{:S(2)}) collective-permute-start(bf16[1,272,256]{2,1,0:T(8,128)(2,1)S(1)} %copy-done.40), channel_id=1, source_target_pairs={{0,16},{4,20},{8,24},{12,28},{16,0},{20,4},{24,8},{28,12},{1,17},{... | collective-permute-start | bytes 417800 | tf_op jit(solution)/shard_map/ppermute | solution.py:952
  263.1 17.7 %collective-permute-start.40 = (bf16[1,272,256]{2,1,0:T(8,128)(2,1)S(1)}, bf16[1,272,256]{2,1,0:T(8,128)(2,1)S(1)}, u32[]{:S(2)}, u32[]{:S(2)}) collective-permute-start(bf16[1,272,256]{2,1,0:T(8,128)(2,1)S(1)} %copy-done.39), channel_id=1, source_target_pairs={{0,24},{4,28},{8,16},{12,20},{16,8},{20,12},{24,0},{28,4},{1,25},{... | collective-permute-start | bytes 417800 | tf_op jit(solution)/shard_map/ppermute | solution.py:952
  280.9 10.5 %collective-permute-start.41 = (bf16[1,272,256]{2,1,0:T(8,128)(2,1)S(1)}, bf16[1,272,256]{2,1,0:T(8,128)(2,1)S(1)}, u32[]{:S(2)}, u32[]{:S(2)}) collective-permute-start(bf16[1,272,256]{2,1,0:T(8,128)(2,1)S(1)} %add_convert_fusion.10), channel_id=1, source_target_pairs={{0,8},{4,12},{8,0},{12,4},{16,24},{20,28},{24,16},{28,20},{1,9},{5... | collective-permute-start | bytes 417800 | tf_op jit(solution)/shard_map/ppermute | solution.py:952
  283.1 15.2 %collective-permute-start.42 = (bf16[1,272,256]{2,1,0:T(8,128)(2,1)S(1)}, bf16[1,272,256]{2,1,0:T(8,128)(2,1)S(1)}, u32[]{:S(2)}, u32[]{:S(2)}) collective-permute-start(bf16[1,272,256]{2,1,0:T(8,128)(2,1)S(1)} %add_convert_fusion.10), channel_id=1, source_target_pairs={{0,16},{4,20},{8,24},{12,28},{16,0},{20,4},{24,8},{28,12},{1,17},{... | collective-permute-start | bytes 417800 | tf_op jit(solution)/shard_map/ppermute | solution.py:952
  283.1 15.2 %collective-permute-start.43 = (bf16[1,272,256]{2,1,0:T(8,128)(2,1)S(1)}, bf16[1,272,256]{2,1,0:T(8,128)(2,1)S(1)}, u32[]{:S(2)}, u32[]{:S(2)}) collective-permute-start(bf16[1,272,256]{2,1,0:T(8,128)(2,1)S(1)} %add_convert_fusion.10), channel_id=1, source_target_pairs={{0,24},{4,28},{8,16},{12,20},{16,8},{20,12},{24,0},{28,4},{1,25},{... | collective-permute-start | bytes 417800 | tf_op jit(solution)/shard_map/ppermute | solution.py:952
  285.6 23.6 %collective-permute-start.44 = (bf16[4,2,192,256]{3,2,1,0:T(8,128)(2,1)S(1)}, bf16[4,2,192,256]{3,2,1,0:T(8,128)(2,1)S(1)}, u32[]{:S(2)}, u32[]{:S(2)}) collective-permute-start(bf16[4,2,192,256]{3,2,1,0:T(8,128)(2,1)S(1)} %pad_maximum_fusion.early_own), channel_id=1, source_target_pairs={{0,4},{4,0},{8,12},{12,8},{16,20},{20,16},{24,28},{28,24},{1,5},{5... | collective-permute-start | bytes 2359304 | tf_op jit(solution)/shard_map/ppermute | solution.py:952
  287.9 31.5 %all-to-all-start.3 = ((bf16[8,96,256]{2,1,0:T(8,128)(2,1)}), bf16[8,96,256]{2,1,0:T(8,128)(2,1)S(1)}, u32[]{:S(2)}, u32[]{:S(2)}) async-start(bf16[8,96,256]{2,1,0:T(8,128)(2,1)} %broadcast_in_dim.10), calls=%async_computation.3 | async-start | bytes 786432 | tf_op jit(solution)/shard_map/all_to_all | solution.py:1203
  298.4 21.0 %collective-permute-start.45 = (bf16[4,1,272,256]{3,2,1,0:T(8,128)(2,1)S(1)}, bf16[4,1,272,256]{3,2,1,0:T(8,128)(2,1)S(1)}, u32[]{:S(2)}, u32[]{:S(2)}) collective-permute-start(bf16[4,1,272,256]{3,2,1,0:T(8,128)(2,1)S(1)} %pad_maximum_fusion.1.last_own), channel_id=1, source_target_pairs={{0,4},{4,0},{8,12},{12,8},{16,20},{20,16},{24,28},{28,24},{1,5},{5... | collective-permute-start | bytes 1671176 | tf_op jit(solution)/shard_map/ppermute | solution.py:952
  (44 other events, 309.5 us)

commit v4 on v3

--- a/solution.py
+++ b/solution.py
@@ -166,6 +166,32 @@
     )(spot, tokens, gain, documents, *weights)
 
 
+def project_kernel(spot_ref, operand, *rest, pieces):
+    weights = rest[:pieces]
+    out, weight_all = rest[pieces:]
+    place_rows(spot_ref[0], weights, weight_all)
+    out[...] = dot_nn(operand[...], weight_all[...]).astype(out.dtype)
+
+
+def project(spot, operand, weights):
+    rows, width = operand.shape
+    columns = weights[0].shape[1]
+    return pl.pallas_call(
+        functools.partial(project_kernel, pieces=len(weights)),
+        grid_spec=pltpu.PrefetchScalarGridSpec(
+            num_scalar_prefetch=1,
+            grid=(),
+            in_specs=[pl.BlockSpec(memory_space=pltpu.VMEM)] * (1 + len(weights)),
+            out_specs=pl.BlockSpec(memory_space=pltpu.VMEM),
+            scratch_shapes=[pltpu.VMEM((width, columns), BF16)],
+        ),
+        out_shape=jax.ShapeDtypeStruct((rows, columns), BF16),
+        compiler_params=params(),
+        cost_estimate=weight(),
+        name="project",
+    )(spot, operand, *weights)
+
+
 def low_lanes(shape):
     return lax.broadcasted_iota(jnp.int32, shape, len(shape) - 1) < HEAD_DIM
 
@@ -195,23 +221,15 @@
 
 
 def attend_kernel(
-    spot_ref, place_ref, scaled, marks, keyvals, *rest, blocks, tile_rows, tile_keys, pieces
+    place_ref, queries, marks, keyvals, starts_out, exact_out, rounded_out, logs_out, *rest,
+    blocks, tile_rows, tile_keys
 ):
-    weights, rest = rest[:pieces], rest[pieces:]
-    queries, starts_out, exact_out, rounded_out, logs_out = rest[:5]
-    (
-        key_even, key_odd, value_even, value_odd, score_scratch, most, total, weight_all, projected,
-    ) = rest[5:]
+    key_even, key_odd, value_even, value_odd, score_scratch, most, total = rest
     rows = keyvals.shape[2] - DOC_ROWS
-    seq, tile = pl.program_id(0), pl.program_id(1)
-
-    @pl.when((seq == 0) & (tile == 0))
-    def _():
-        place_rows(spot_ref[0], weights, weight_all)
+    tile = pl.program_id(1)
 
     @pl.when(tile == 0)
     def _():
-        projected[...] = dot_nn(scaled[...], weight_all[...]).astype(BF16)
         low = low_lanes((rows, LANES))
         for j in range(blocks):
             whole = keyvals[block_at(place_ref, j, blocks), 0, 0:rows, :].astype(F32)
@@ -223,8 +241,6 @@
             value_even[place, LANES:] = jnp.where(low, 1.0, 0.0).astype(BF16)
             value_odd[place, 0:LANES] = jnp.where(low, 0.0, whole).astype(BF16)
             value_odd[place, LANES:] = jnp.where(low, 0.0, 1.0).astype(BF16)
-
-    queries[0] = projected[pl.ds(pl.multiple_of(tile * tile_rows, tile_rows), tile_rows), :]
 
     def smaller(j, count):
         lines = keyvals[block_at(place_ref, j, blocks), 0, rows:, :].astype(F32)
@@ -305,7 +321,7 @@
     place_ref, queries, starts, exact, logs, grads, keyvals, *rest,
     seq, blocks, tile_rows, tile_keys
 ):
-    grad_queries, terms, *rest = rest[1:] if seq else rest
+    grad_queries, keep, send, *rest = rest
     (
         key_even, key_odd, value_even, value_odd,
         key_total, value_total, query_total,
@@ -380,7 +396,8 @@
     @pl.when(tile == pl.num_programs(0) - 1)
     def _():
         per_block = rows // tile_keys
-        terms[...] = jnp.zeros_like(terms)
+        keep[...] = jnp.zeros_like(keep)
+        send[...] = jnp.zeros_like(send)
 
         def block_terms(j, carried):
             for i in range(per_block):
@@ -390,8 +407,19 @@
                 key = key[0:HEAD_DIM, 0:tile_keys] + key[HEAD_DIM:, tile_keys:]
                 value = value[0:HEAD_DIM, 0:tile_keys] + value[HEAD_DIM:, tile_keys:]
                 both = jnp.concatenate([key * root, value], axis=0)
+                both = both.T.astype(BF16)
                 owner = block_at(place_ref, j, blocks)
-                terms[owner, 0, i * tile_keys : (i + 1) * tile_keys, :] = both.T.astype(BF16)
+                here = slice(i * tile_keys, (i + 1) * tile_keys)
+                same = (owner & 1) == (place_ref[0] & 1)
+
+                @pl.when(same)
+                def _():
+                    keep[owner >> 1, here, :] = both
+
+                @pl.when(jnp.logical_not(same))
+                def _():
+                    send[owner >> 1, here, :] = both
+
             return carried
 
         missing = jnp.maximum(blocks - 1 - place_ref[0], 0)
@@ -404,10 +432,10 @@
     return tile_rows, tile_keys, blocks * rows // tile_keys
 
 
-def attend(spot, place, scaled, marks, keyvals, weights, blocks):
+def attend(place, queries, marks, keyvals, blocks):
     unused, seqs, tall, unused = keyvals.shape
     rows = tall - DOC_ROWS
-    width = scaled.shape[1]
+    width = queries.shape[2]
     tile_rows, tile_keys, key_tiles = attention_sizes(rows, blocks)
     stack = PAIRS * tile_rows
     keys = blocks * rows
@@ -415,27 +443,17 @@
     wide = lambda dtype: jax.ShapeDtypeStruct((seqs, rows, width), dtype)
     return pl.pallas_call(
         functools.partial(
-            attend_kernel,
-            blocks=blocks,
-            tile_rows=tile_rows,
-            tile_keys=tile_keys,
-            pieces=len(weights),
+            attend_kernel, blocks=blocks, tile_rows=tile_rows, tile_keys=tile_keys
         ),
         grid_spec=pltpu.PrefetchScalarGridSpec(
-            num_scalar_prefetch=2,
+            num_scalar_prefetch=1,
             grid=(seqs, rows // tile_rows),
             in_specs=[
-                pl.BlockSpec((rows, width), lambda s, t, *_: (s, 0)),
+                row_spec(width),
                 row_spec(LANES),
                 pl.BlockSpec((keyvals.shape[0], 1, tall, LANES), lambda s, t, *_: (0, s, 0, 0)),
-            ]
-            + [
-                pl.BlockSpec(
-                    (one.shape[0], width), lambda s, t, *_: (0, 0), pipeline_mode=pl.Buffered(1)
-                )
-                for one in weights
             ],
-            out_specs=[row_spec(width), row_spec(LANES)] + [row_spec(width)] * 3,
+            out_specs=[row_spec(LANES)] + [row_spec(width)] * 3,
             scratch_shapes=[
                 pltpu.VMEM((keys, LANES), BF16),
                 pltpu.VMEM((keys, LANES), BF16),
@@ -444,12 +462,9 @@
                 pltpu.VMEM((key_tiles, stack, 2 * tile_keys), F32),
                 pltpu.VMEM((stack, 2 * LANES), F32),
                 pltpu.VMEM((stack, 2 * LANES), F32),
-                pltpu.VMEM((width, width), BF16),
-                pltpu.VMEM((rows, width), BF16),
             ],
         ),
         out_shape=[
-            wide(BF16),
             jax.ShapeDtypeStruct((seqs, rows, LANES), jnp.int32),
             wide(F32),
             wide(BF16),
@@ -458,11 +473,11 @@
         compiler_params=params("arbitrary", "arbitrary"),
         cost_estimate=weight(),
         name="attend",
-    )(spot, place, scaled, marks, keyvals, *weights)
+    )(place, queries, marks, keyvals)
 
 
 def attend_back(
-    seq, place, queries, starts, exact, logs, grads, keyvals, terms, blocks
+    seq, place, queries, starts, exact, logs, grads, keyvals, blocks
 ):
     seqs, rows, width = queries.shape
     ctx_size = keyvals.shape[0]
@@ -479,25 +494,23 @@
             grid=(rows // tile_rows,),
             in_specs=[row_spec(width), row_spec(LANES)]
             + [row_spec(width)] * 3
-            + [pl.BlockSpec((ctx_size, 1, keyvals.shape[2], LANES), lambda t, *_: (0, seq, 0, 0))]
-            + [pl.BlockSpec(memory_space=pl.ANY)] * len(terms),
+            + [pl.BlockSpec((ctx_size, 1, keyvals.shape[2], LANES), lambda t, *_: (0, seq, 0, 0))],
             out_specs=[
                 pl.BlockSpec((1, tile_rows, width), lambda t, *_: (0, t, 0)),
-                pl.BlockSpec((ctx_size, 1, rows, LANES), lambda t, *_: (0, seq, 0, 0)),
-            ],
+            ]
+            + [pl.BlockSpec((ctx_size // 2, rows, LANES), lambda t, *_: (0, 0, 0))] * 2,
             scratch_shapes=[pltpu.VMEM((keys, LANES), BF16)] * 4
             + [pltpu.VMEM((key_tiles, LANES, 2 * tile_keys), F32)] * 2
             + [pltpu.VMEM((stack, LANES), F32)] * 5,
         ),
         out_shape=[
             jax.ShapeDtypeStruct((1, rows, width), BF16),
-            jax.ShapeDtypeStruct((ctx_size, seqs, rows, LANES), BF16),
-        ],
-        input_output_aliases={7: 1} if terms else {},
+        ]
+        + [jax.ShapeDtypeStruct((ctx_size // 2, rows, LANES), BF16)] * 2,
         compiler_params=params("arbitrary"),
         cost_estimate=weight(),
         name="attend_back",
-    )(place, queries, starts, exact, logs, grads, keyvals, *terms)
+    )(place, queries, starts, exact, logs, grads, keyvals)
 
 
 def round_up(count, unit):
@@ -646,15 +659,23 @@
                 out, at = message_of(messages, s)
                 for g in range(groups):
                     column = slice(g * TILE, (g + 1) * TILE)
-                    out[at, column, :] = down_term[h * TILE : (h + 1) * TILE, column]
+                    part_here = down_term[h * TILE : (h + 1) * TILE, column]
+                    if chunk == 1:
+                        out[0, at, column, :] = part_here
+                    else:
+                        out[at, column, :] = part_here
             for s in range(pieces):
                 out, at = message_of(messages, s)
                 begin = pl.multiple_of((spot ^ s) * height, height)
                 for h, t in enumerate(pair):
-                    row = pl.multiple_of(width + (spot ^ t) * height, height)
-                    out[at, pl.ds(row, height), :] = up_term[
+                    part_here = up_term[
                         pl.ds(begin, height), h * TILE : (h + 1) * TILE
                     ].astype(BF16)
+                    row = pl.multiple_of((spot ^ t) * height, height)
+                    if chunk == 1:
+                        out[1, at, pl.ds(row, height), :] = part_here
+                    else:
+                        out[at, pl.ds(width + row, height), :] = part_here
 
     if last:
 
@@ -704,6 +725,8 @@
     for chunk in part:
         more = mixing_rows(width, pieces, ctx_size) if chunk == chunks - 1 else 0
         message = jax.ShapeDtypeStruct((pieces // 2, 2 * width + more, TILE), BF16)
+        if chunk == 1:
+            message = jax.ShapeDtypeStruct((2, pieces // 2, width, TILE), BF16)
         outputs[f"keep{chunk}"] = outputs[f"send{chunk}"] = message
     inputs["cotangent"] = arrays["cotangent"]
     for chunk in part:
@@ -840,9 +863,9 @@
     )
 
 
-def last_stage(spot, tokens, gain, scaled, arrived, grad_scaled, grad_hidden, weights):
+def last_stage(spot, tokens, gain, scaled, arrived, grad_scaled, grad_hidden, weights, places):
     rows, width = tokens.shape
-    pieces, places = len(weights), arrived.shape[0]
+    pieces = len(weights)
     message = jax.ShapeDtypeStruct(
         (pieces // 2, round_up(width // pieces, 8 * places), 2 * LANES), BF16
     )
@@ -891,8 +914,7 @@
 
     def load(source, begin, rows):
         for c in range(places):
-            at = ((c & 1) * deep + (c >> 1)) * rows
-            whole[at : at + rows, :] = source[c, begin : begin + rows, :].astype(F32)
+            whole[c * rows : (c + 1) * rows, :] = source[c, begin : begin + rows, :].astype(F32)
 
     def load_halves(own, other, at):
         rows = own.shape[2]
@@ -972,25 +994,31 @@
     return values
 
 
-class Reduction:
+class Transfer:
+    def __init__(self, held, sent, routes):
+        self.held, self.sent, self.routes, self.coming = held, sent, routes, []
+
+    def launch(self):
+        if self.sent:
+            self.coming = [swap(one, *route) for one, route in zip(self.sent, self.routes)]
+            self.sent = []
+
+    def add(self, pick):
+        return pick(self.held).astype(F32) + pick(self.coming[0]).astype(F32)
+
+
+class Reduction(Transfer):
     def __init__(self, keep, send, place, sizes):
         self.wt_size, self.ctx_size = sizes
         self.groups = self.ctx_size // 2
         self.low, self.high = place & 1, place >> 1
-        self.owners, self.rows, self.lanes = keep.shape
-        split = (self.owners, 2, self.groups, self.rows // self.ctx_size, self.lanes)
-        self.held = keep.reshape(split)
-        self.sent = [send.reshape(split)]
-        self.routes = [("wt", self.wt_size, 1)]
-        self.coming = []
-
-    def launch(self):
-        if self.sent:
-            self.coming = [swap(one, *route) for one, route in zip(self.sent, self.routes)]
-            self.sent = []
-
-    def add(self, pick):
-        return pick(self.held).astype(F32) + pick(self.coming[0]).astype(F32)
+        *outer, rows, self.lanes = keep.shape
+        self.rows = rows if len(outer) == 1 else 2 * rows
+        inner = (self.groups, self.rows // self.ctx_size, self.lanes)
+        split = (*outer, *inner) if len(outer) == 2 else (*outer, 2, *inner)
+        super().__init__(
+            keep.reshape(split), [send.reshape(split)], [("wt", self.wt_size, 1)]
+        )
 
     def y(self, cuts=()):
         edges = (0, *cuts, self.rows // self.ctx_size)
@@ -1009,9 +1037,8 @@
         self.coming = [jnp.concatenate(self.before + self.coming, axis=-2)]
 
     def x(self):
-        low, axis = self.low, self.held.ndim - 4
-        half = lambda x: self.add(lambda v: lax.dynamic_index_in_dim(v, x, axis, False))
-        self.held, self.sent = half(low), [half(1 - low).astype(BF16)]
+        half = lambda x: self.add(lambda v: lax.dynamic_index_in_dim(v, x, 0, False))
+        self.held, self.sent = half(self.low), [half(1 - self.low).astype(BF16)]
         self.routes = [("ctx", self.ctx_size, 1)]
 
     def far(self):
@@ -1042,7 +1069,7 @@
         self.routes = [("ctx", self.ctx_size, 1)]
 
     def everywhere(self):
-        return self.add(lambda v: v).astype(BF16).swapaxes(0, 1).reshape(
+        return self.add(lambda v: v).astype(BF16).reshape(
             self.ctx_size, self.rows // self.ctx_size, self.lanes
         )
 
@@ -1114,17 +1141,16 @@
     query_pieces = query_gather.finish()
     place_one = place.astype(jnp.int32).reshape(1)
 
-    keyvals, gathers[0].far, mixing_gather.far, query_pieces[3], marks, packed[1:] = (
+    queries = project(spot, scaled_one, query_pieces).reshape(seqs, rows, width)
+    keyvals, gathers[0].far, mixing_gather.far, queries, marks, packed[1:] = (
         lax.optimization_barrier(
-            (keyvals, gathers[0].far, mixing_gather.far, query_pieces[3], marks, packed[1:])
+            (keyvals, gathers[0].far, mixing_gather.far, queries, marks, packed[1:])
         )
     )
     gathered = [gathers[0].finish()]
     mixing_pieces = mixing_gather.finish()
     gathers.append(Gather(packed[1], wt_size))
-    queries, starts, exact, attended, logs = attend(
-        spot, place_one, scaled_one, marks, keyvals, query_pieces, blocks
-    )
+    starts, exact, attended, logs = attend(place_one, queries, marks, keyvals, blocks)
     attended, gathers[1].far, packed[2:] = lax.optimization_barrier(
         (attended, gathers[1].far, packed[2:])
     )
@@ -1161,42 +1187,54 @@
     grad_attended = tie(grad_attended, zero, one, two).reshape(seqs, rows, width)
     grad_queries, terms = [], []
     for seq in range(seqs):
-        part, *terms = attend_back(
-            seq, place_one, queries, starts, exact, logs, grad_attended, keyvals, terms, blocks
+        part, keep, send = attend_back(
+            seq, place_one, queries, starts, exact, logs, grad_attended, keyvals, blocks
         )
         came = [zero, one, two] if seq == 0 else [zero, two]
-        part, grad_attended, terms = tie((part, grad_attended, terms), *came, came=came)
+        term = Transfer(keep, [send], [("ctx", ctx_size, 1)])
+        part, grad_attended = tie((part, grad_attended), *came, term, *terms, came=came + terms)
         grad_queries.append(part[0])
+        terms.append(term)
         if seq == 0:
             zero.z(one)
             two.y_more()
             grad_attended = tie(grad_attended, zero, two)
     two.y_joined()
     two.x()
-    grad_queries, terms = tie((grad_queries, terms), zero, two)
-    arriving = lax.all_to_all(terms[0], "ctx", 0, 0)
     zero.z_back()
+    grad_queries = tie(grad_queries, zero, two)
     grad_scaled, keep, send = query_stage(spot, scaled_one, grad_queries, query_pieces, ctx_size)
     query = Reduction(keep, send, place, sizes)
-    grad_scaled = tie(grad_scaled, zero, two, query)
+    grad_scaled = tie(grad_scaled, zero, query, *terms, came=terms[1:])
+    arriving = jnp.stack([one.add(lambda v: v).astype(BF16) for one in terms], axis=1)
+    arriving, grad_scaled = tie((arriving, grad_scaled), query)
+    arriving = lax.all_to_all(
+        arriving,
+        "ctx",
+        0,
+        0,
+        axis_index_groups=[list(range(x, ctx_size, 2)) for x in range(2)],
+    )
     query.y()
-    grad_scaled, arriving = tie((grad_scaled, arriving), zero, query)
+    grad_scaled = tie(grad_scaled, query)
+    grad_scaled = tie(grad_scaled, two, came=[two])
+    two.z()
+    grad_scaled, arriving = tie((grad_scaled, arriving), two)
     input_grad, keep, send = last_stage(
-        spot, inputs, gain_one, scaled_one, arriving, grad_scaled, arrays["grad_hidden"], small_pieces
+        spot, inputs, gain_one, scaled_one, arriving, grad_scaled, arrays["grad_hidden"], small_pieces, ctx_size
     )
     shared = Reduction(keep, send, place, sizes)
-    input_grad = tie(input_grad, zero, two, shared, query, came=[two, zero])
-    two.z()
+    input_grad = tie(input_grad, zero, two, shared, query, came=[two, query])
+    two.z_back()
+    input_grad = tie(input_grad, two)
     zero.x_back()
-    input_grad = tie(input_grad, zero, two)
+    input_grad = tie(input_grad, zero)
     input_grad = tie(input_grad, shared, query, came=[shared])
     shared.y()
     input_grad = tie(input_grad, shared)
-    input_grad = tie(input_grad, shared, query, came=[shared, query])
+    input_grad = tie(input_grad, shared, query, came=[shared])
     late = jnp.concatenate([query.everywhere(), shared.everywhere()], axis=1)
     late = lax.all_to_all(late, "ctx", 0, 0)
-    two.z_back()
-    input_grad = tie(input_grad, two)
     two.x_back()
     input_grad = tie(input_grad, two)
     late = jnp.sum(late.astype(F32), axis=0).astype(BF16)

time: 328 us -> 305 us (0.930)
  waiting for transfers between devices: 127 us -> 105 us
  local copies, waits for them, and re-layouts: 17.7 us -> 13.3 us
    all_to_all x1, waiting for transfers between devices: 20.9 us -> 0.01 us  [body(): lax.all_to_all(arriving, 'ctx', 0, 0, axis_index_groups=[list(range(x, ct...]
    ppermute x46 -> x48, waiting for transfers between devices: 106 us -> 96.1 us  [swap(): return lax.ppermute(values, axis, [(i, i ^ mask) for i in range(size)])]
    all_to_all x1, waiting for transfers between devices: 0.01 us -> 8.95 us  [body(): late = lax.all_to_all(late, 'ctx', 0, 0)]
    all_to_all x1, starting transfers between devices: 3.45 us -> 6.88 us  [body(): lax.all_to_all(jnp.broadcast_to(late, (ctx_size,) + late.shape), 'ctx', 0...]
    unnamed x85 -> x67, local copies, waits for them, and re-layouts: 7.69 us -> 6 us
    ppermute x46 -> x48, starting transfers between devices: 50.1 us -> 48.9 us  [swap(): return lax.ppermute(values, axis, [(i, i ^ mask) for i in range(size)])]
  transfers between devices with their start and end apart: 50 -> 52, of which waited for: 20 -> 22; matrix products, arithmetic and copies ran while one was open for 5% -> 5% of each run, Pallas kernels for 26% -> 29%
where the time goes in v4:
time: 305 us
  waiting for transfers between devices  105 us (34%)
  Pallas kernels  92.8 us (30%)
  starting transfers between devices  75.5 us (25%)
  other arithmetic  16.7 us (5%)
  local copies, waits for them, and re-layouts  13.3 us (4%)
    ppermute x48, waiting for transfers between devices, swap(): return lax.ppermute(values, axis, [(i, i ^ mask) for i in range(size)])  96.1 us
    ppermute x48, starting transfers between devices, swap(): return lax.ppermute(values, axis, [(i, i ^ mask) for i in range(size)])  48.9 us
    pallas_call x2, Pallas kernels, feed_stage(): pl.pallas_call(functools.partial(feed_kernel, pieces=pieces, part=part, f...  43.9 us
    pallas_call x2, Pallas kernels, attend_back(): pl.pallas_call(functools.partial(attend_back_kernel, seq=seq, blocks=bloc...  13.1 us
    pallas_call x1, Pallas kernels, attend(): pl.pallas_call(functools.partial(attend_kernel, blocks=blocks, tile_rows=...  9.45 us
    all_to_all x1, waiting for transfers between devices, body(): late = lax.all_to_all(late, 'ctx', 0, 0)  8.95 us
    all_to_all x1, starting transfers between devices, body(): lax.all_to_all(arriving, 'ctx', 0, 0, axis_index_groups=[list(range(x, ct...  7.97 us
    all_to_all x1, starting transfers between devices, body(): lax.all_to_all(jnp.broadcast_to(late, (ctx_size,) + late.shape), 'ctx', 0...  6.88 us
  transfers between devices with their start and end apart: 52, of which 22 were waited for; matrix products, arithmetic and copies ran while one was open for 5% of the time, Pallas kernels for 29%

profile of v4, /device:TPU:0, one launch (start us, length us, event | category | flops | bytes accessed | tf_op | source)
XLA Modules:
  0.0 304.5 jit_solution(11190290312839194271)
XLA Ops:
  2.1 3.0 collective-permute-start.1
  9.4 4.3 %first_norm.1 = (bf16[512,768]{1,0:T(8,128)(2,1)}, bf16[8,544,128]{2,1,0:T(8,128)(2,1)}) custom-call(s32[1]{0:T(128)} %bitcast.spot_ref, bf16[512,768]{1,0:T(8,128)(2,1)} %bitcast.89, f32[1,768]{1,0:T(1,128)} %reshape_squeeze.6.gain, bf16[2,2,128]{2,1,0:T(2,128)(2,1)} %reshape.175.documents, bf16[208,128]{1,0:T(8,128)(2,1)} %copy-done.25, ...), custom_call_target="tpu_custom_call" | custom-call | flops 1 | bytes 1 | tf_op jit(solution)/shard_map/first_norm/pallas_call | solution.py:150
  14.8 5.8 %all-to-all-start = ((bf16[8,544,128]{2,1,0:T(8,128)(2,1)}), bf16[8,544,128]{2,1,0:T(8,128)(2,1)S(1)}, u32[]{:S(2)}, u32[]{:S(2)}) async-start(bf16[8,544,128]{2,1,0:T(8,128)(2,1)} %get-tuple-element.218), calls=%async_computation | async-start | bytes 2228224 | tf_op jit(solution)/shard_map/all_to_all | solution.py:1136
  20.6 3.2 %pack.1 = (bf16[1536,256]{1,0:T(8,128)(2,1)}, bf16[1536,256]{1,0:T(8,128)(2,1)}, bf16[1536,256]{1,0:T(8,128)(2,1)}) custom-call(bf16[192,3072]{1,0:T(8,128)(2,1)} %up, bf16[768,768]{1,0:T(8,128)(2,1)} %down), custom_call_target="tpu_custom_call" | custom-call | flops 1 | bytes 1 | tf_op jit(solution)/shard_map/pack/pallas_call | solution.py:95
  27.6 3.3 %project.1 = bf16[512,768]{1,0:T(8,128)(2,1)} custom-call(s32[1]{0:T(128)} %bitcast.spot_ref, bf16[512,768]{1,0:T(8,128)(2,1)} %get-tuple-element.223.operand.scaled, bf16[192,768]{1,0:T(8,128)(2,1)} %rest_2_.1, bf16[192,768]{1,0:T(8,128)(2,1)} %copy-done.14, bf16[192,768]{1,0:T(8,128)(2,1)} %copy-done.13, bf16[192,768]{1,0:T(8,128)(2,1)} %copy-done.15), custom_call_target="tpu_custom_call" | custom-call | flops 1 | bytes 1 | tf_op jit(solution)/shard_map/project/pallas_call | solution.py:179
  30.9 18.3 %collective-permute-done.5.refs_11_.refs_7_ = bf16[192,768]{1,0:T(8,128)(2,1)S(1)} collective-permute-done((bf16[192,768]{1,0:T(8,128)(2,1)S(1)}, bf16[192,768]{1,0:T(8,128)(2,1)S(1)}, u32[]{:S(2)}, u32[]{:S(2)}) %collective-permute-start.5) | collective-permute-done | bytes 294944 | tf_op jit(solution)/shard_map/ppermute | solution.py:974
  50.2 1.5 collective-permute-start.8
  52.8 9.4 %attend.1 = (s32[2,256,128]{2,1,0:T(8,128)}, f32[2,256,768]{2,1,0:T(8,128)}, bf16[2,256,768]{2,1,0:T(8,128)(2,1)}, f32[2,256,768]{2,1,0:T(8,128)}) custom-call(s32[1]{0:T(128)} %bitcast.1.place_ref, bf16[2,256,768]{2,1,0:T(8,128)(2,1)} %bitcast.86, f32[2,256,128]{2,1,0:T(8,128)} %broadcast_in_dim.4.marks, bf16[8,2,272,128]{3,2,1,0:T(8,128)(2,1)} %bitcast.83), custom_call_target="tpu_custom_call" | custom-call | flops 1 | bytes 1 | tf_op jit(solution)/shard_map/attend/pallas_call | solution.py:444
  62.2 6.6 %collective-permute-done.8.refs_7_ = bf16[1536,256]{1,0:T(8,128)(2,1)} collective-permute-done((bf16[1536,256]{1,0:T(8,128)(2,1)}, bf16[1536,256]{1,0:T(8,128)(2,1)}, u32[]{:S(2)}, u32[]{:S(2)}) %collective-permute-start.8) | collective-permute-done | bytes 786464 | tf_op jit(solution)/shard_map/ppermute | solution.py:974
  68.8 1.8 collective-permute-start.15
  73.2 23.8 %feed0.1 = (bf16[2,1536,256]{2,1,0:T(8,128)(2,1)}, bf16[2,1536,256]{2,1,0:T(8,128)(2,1)}, bf16[2,2,768,256]{3,2,1,0:T(8,128)(2,1)}, bf16[2,2,768,256]{3,2,1,0:T(...) custom-call(s32[1]{0:T(128)} %bitcast.spot_ref, ...), custom_call_target="tpu_custom_call" | custom-call | flops 1 | bytes 1 | tf_op jit(solution)/shard_map/feed0/pallas_call | solution.py:770
  99.0 2.6 collective-permute-done.16
  101.6 2.6 fusion
  104.2 1.9 collective-permute-done.17
  106.4 1.5 collective-permute-start.21
  109.0 20.1 %feed2.1 = (bf16[2,2176,256]{2,1,0:T(8,128)(2,1)}, bf16[2,2176,256]{2,1,0:T(8,128)(2,1)}, bf16[512,768]{1,0:T(8,128)(2,1)}, f32[512,768]{1,0:T(8,128)}, bf16[512,768]{1,0:T(8,128)(2,1)}) custom-call(s32[1]{0:T(128)} %bitcast.spot_ref, bf16[512,768]{1,0:T(8,128)(2,1)} %bitcast.93, bf16[1536,256]{1,0:T(8,128)(2,1)} %get-tuple-element.245.refs_1_, ...), custom_call_target="tpu_custom_call" | custom-call | flops 1 | bytes 1 | tf_op jit(solution)/shard_map/feed2/pallas_call | solution.py:770
  131.6 2.1 collective-permute-done.22
  138.4 6.6 %attend_back.2 = (bf16[1,256,768]{2,1,0:T(8,128)(2,1)}, bf16[4,256,128]{2,1,0:T(8,128)(2,1)}, bf16[4,256,128]{2,1,0:T(8,128)(2,1)}) custom-call(s32[1]{0:T(128)} %bitcast.1.place_ref, bf16[2,256,768]{2,1,0:T(8,128)(2,1)} %bitcast.87, s32[2,256,128]{2,1,0:T(8,128)} %get-tuple-element.286.starts, f32[2,256,768]{2,1,0:T(8,128)} %get-tuple-element.287.exact, ...), custom_call_target="tpu_custom_call" | custom-call | flops 1 | bytes 1 | tf_op jit(solution)/shard_map/attend_back/pallas_call | solution.py:488
  145.2 2.8 collective-permute-done.23
  148.0 9.1 %collective-permute-done.24 = bf16[4,192,256]{2,1,0:T(8,128)(2,1)} collective-permute-done((bf16[4,192,256]{2,1,0:T(8,128)(2,1)}, bf16[4,192,256]{2,1,0:T(8,128)(2,1)}, u32[]{:S(2)}, u32[]{:S(2)}) %collective-permute-start.24) | collective-permute-done | bytes 393248 | tf_op jit(solution)/shard_map/ppermute | solution.py:974
  161.2 1.4 collective-permute-start.26
  162.6 4.7 %collective-permute-start.27 = (bf16[2,192,256]{2,1,0:T(8,128)(2,1)S(1)}, bf16[2,192,256]{2,1,0:T(8,128)(2,1)S(1)}, u32[]{:S(2)}, u32[]{:S(2)}) collective-permute-start(bf16[2,192,256]{2,1,0:T(8,128)(2,1)S(1)} %pad_maximum_fusion.6), channel_id=1, source_target_pairs={{0,16},{4,20},{8,24},{12,28},{16,0},{20,4},{24,8},{28,12},{1,17},{... | collective-permute-start | bytes 589832 | tf_op jit(solution)/shard_map/ppermute | solution.py:974
  167.3 6.5 %attend_back.3 = (bf16[1,256,768]{2,1,0:T(8,128)(2,1)}, bf16[4,256,128]{2,1,0:T(8,128)(2,1)}, bf16[4,256,128]{2,1,0:T(8,128)(2,1)}) custom-call(s32[1]{0:T(128)} %bitcast.1.place_ref, bf16[2,256,768]{2,1,0:T(8,128)(2,1)} %bitcast.88, s32[2,256,128]{2,1,0:T(8,128)} %get-tuple-element.286.starts, f32[2,256,768]{2,1,0:T(8,128)} %get-tuple-element.287.exact, ...), custom_call_target="tpu_custom_call" | custom-call | flops 1 | bytes 1 | tf_op jit(solution)/shard_map/attend_back/pallas_call | solution.py:488
  174.9 6.6 %collective-permute-done.27 = bf16[2,192,256]{2,1,0:T(8,128)(2,1)S(1)} collective-permute-done((bf16[2,192,256]{2,1,0:T(8,128)(2,1)S(1)}, bf16[2,192,256]{2,1,0:T(8,128)(2,1)S(1)}, u32[]{:S(2)}, u32[]{:S(2)}) %collective-permute-start.27) | collective-permute-done | bytes 196640 | tf_op jit(solution)/shard_map/ppermute | solution.py:974
  181.5 1.9 collective-permute-start.31
  184.6 4.7 %query_grad.1 = (f32[512,768]{1,0:T(8,128)}, bf16[2,576,256]{2,1,0:T(8,128)(2,1)}, bf16[2,576,256]{2,1,0:T(8,128)(2,1)}) custom-call(s32[1]{0:T(128)} %bitcast.spot_ref, bf16[512,768]{1,0:T(8,128)(2,1)} %get-tuple-element.223.operand.scaled, bf16[256,768]{1,0:T(8,128)(2,1)} %bitcast.107, bf16[256,768]{1,0:T(8,128)(2,1)} %bitcast.108, ...), custom_call_target="tpu_custom_call" | custom-call | flops 1 | bytes 1 | tf_op jit(solution)/shard_map/query_grad/pallas_call | solution.py:815
  190.4 8.0 %all-to-all-start.1 = ((bf16[4,2,256,128]{3,2,1,0:T(8,128)(2,1)}), bf16[4,2,256,128]{3,2,1,0:T(8,128)(2,1)S(1)}, u32[]{:S(2)}, u32[]{:S(2)}) async-start(bf16[4,2,256,128]{3,2,1,0:T(8,128)(2,1)} %pad_maximum_fusion.2), calls=%async_computation.1 | async-start | bytes 1048576 | tf_op jit(solution)/shard_map/all_to_all | solution.py:1211
  198.3 1.3 collective-permute-start.33
  199.7 1.9 fusion.5
  201.6 1.6 collective-permute-start.37
  203.2 10.1 %collective-permute-done.33 = bf16[4,272,256]{2,1,0:T(8,128)(2,1)S(1)} collective-permute-done((bf16[4,272,256]{2,1,0:T(8,128)(2,1)}, bf16[4,272,256]{2,1,0:T(8,128)(2,1)S(1)}, u32[]{:S(2)}, u32[]{:S(2)}) %collective-permute-start.33) | collective-permute-done | bytes 557088 | tf_op jit(solution)/shard_map/ppermute | solution.py:974
  214.2 1.7 collective-permute-start.34
  215.9 2.4 collective-permute-start.35
  219.4 5.9 %last.1 = (f32[512,768]{1,0:T(8,128)}, bf16[2,192,256]{2,1,0:T(8,128)(2,1)}, bf16[2,192,256]{2,1,0:T(8,128)(2,1)}) custom-call(s32[1]{0:T(128)} %bitcast.spot_ref, bf16[512,768]{1,0:T(8,128)(2,1)} %bitcast.91, f32[1,768]{1,0:T(1,128)} %reshape_squeeze.6.gain, bf16[512,768]{1,0:T(8,128)(2,1)} %get-tuple-element.223.operand.scaled, ...), custom_call_target="tpu_custom_call" | custom-call | flops 1 | bytes 1 | tf_op jit(solution)/shard_map/last/pallas_call | solution.py:872
  225.3 3.3 %collective-permute-start.39 = (bf16[2,192,256]{2,1,0:T(8,128)(2,1)S(1)}, bf16[2,192,256]{2,1,0:T(8,128)(2,1)S(1)}, u32[]{:S(2)}, u32[]{:S(2)}) collective-permute-start(bf16[2,192,256]{2,1,0:T(8,128)(2,1)S(1)} %add_convert_fusion.11), channel_id=1, source_target_pairs={{0,16},{4,20},{8,24},{12,28},{16,0},{20,4},{24,8},{28,12},{1,17},{... | collective-permute-start | bytes 589832 | tf_op jit(solution)/shard_map/ppermute | solution.py:974
  230.2 14.3 %collective-permute-done.39 = bf16[2,192,256]{2,1,0:T(8,128)(2,1)S(1)} collective-permute-done((bf16[2,192,256]{2,1,0:T(8,128)(2,1)S(1)}, bf16[2,192,256]{2,1,0:T(8,128)(2,1)S(1)}, u32[]{:S(2)}, u32[]{:S(2)}) %collective-permute-start.39) | collective-permute-done | bytes 196640 | tf_op jit(solution)/shard_map/ppermute | solution.py:974
  244.7 2.3 collective-permute-start.42
  247.0 2.6 collective-permute-done.42
  250.5 5.9 %all-to-all-start.2 = ((bf16[8,96,256]{2,1,0:T(8,128)(2,1)}), bf16[8,96,256]{2,1,0:T(8,128)(2,1)S(1)}, u32[]{:S(2)}, u32[]{:S(2)}) async-start(bf16[8,96,256]{2,1,0:T(8,128)(2,1)} %pad_maximum_fusion.4), calls=%async_computation.2 | async-start | bytes 786432 | tf_op jit(solution)/shard_map/all_to_all | solution.py:1237
  256.4 2.0 collective-permute-start.43
  258.5 2.4 collective-permute-start.44
  260.9 2.0 collective-permute-start.46
  262.8 8.9 %all-to-all-done.2 = bf16[8,96,256]{2,1,0:T(8,128)(2,1)S(1)} async-done(((bf16[8,96,256]{2,1,0:T(8,128)(2,1)}), bf16[8,96,256]{2,1,0:T(8,128)(2,1)S(1)}, u32[]{:S(2)}, u32[]{:S(2)}) %all-to-all-start.2) | async-done | bytes 393248 | tf_op jit(solution)/shard_map/all_to_all | solution.py:1237
  272.6 6.9 %all-to-all-start.3 = ((bf16[8,96,256]{2,1,0:T(8,128)(2,1)}), bf16[8,96,256]{2,1,0:T(8,128)(2,1)S(1)}, u32[]{:S(2)}, u32[]{:S(2)}) async-start(bf16[8,96,256]{2,1,0:T(8,128)(2,1)} %broadcast_in_dim.10), calls=%async_computation.3 | async-start | bytes 786432 | tf_op jit(solution)/shard_map/all_to_all | solution.py:1241
  279.6 2.1 collective-permute-start.47
  281.7 1.7 collective-permute-done.46.early_other
  283.4 11.9 %collective-permute-done.47.last_other = bf16[4,1,272,256]{3,2,1,0:T(8,128)(2,1)S(1)} collective-permute-done((bf16[4,1,272,256]{3,2,1,0:T(8,128)(2,1)S(1)}, bf16[4,1,272,256]{3,2,1,0:T(8,128)(2,1)S(1)}, u32[]{:S(2)}, u32[]{:S(2)}) %collective-permute-start.47) | collective-permute-done | bytes 557088 | tf_op jit(solution)/shard_map/ppermute | solution.py:974
  296.9 5.0 %final.1 = (f32[768,768]{1,0:T(8,128)}, f32[192,3072]{1,0:T(8,128)}, f32[192,768]{1,0:T(8,128)}, f32[192,768]{1,0:T(8,128)}, f32[192,128]{1,0:T(8,128)}, /*index=5*/f32[8,128]{1,0:T(8,128)}, f32[8,128]{1,0:T(8,128)}) custom-call(s32[1]{0:T(128)} %bitcast.1.place_ref, bf16[4,2,192,256]{3,2,1,0:T(8,128)(2,1)} %copy-done.4, ...), custom_call_target="tpu_custom_call" | custom-call | flops 1 | bytes 1 | tf_op jit(solution)/shard_map/final/pallas_call | solution.py:947
  (190 shorter events, 42.9 us)
Async XLA Ops:
  2.1 5.2 %collective-permute-start.1 = (bf16[208,128]{1,0:T(8,128)(2,1)S(1)}, bf16[208,128]{1,0:T(8,128)(2,1)S(1)}, u32[]{:S(2)}, u32[]{:S(2)}) collective-permute-start(bf16[208,128]{1,0:T(8,128)(2,1)S(1)} %fusion.13.rest_0_), channel_id=1, source_target_pairs={{0,2},{1,3},{2,0},{3,1},{4,6},{5,7},{6,4},{7,5},{8,10},{9,11},{10,... | collective-permute-start | bytes 159752 | tf_op jit(solution)/shard_map/ppermute | solution.py:974
  5.2 2.8 collective-permute-start
  5.2 9.6 %collective-permute-start.3 = (bf16[192,768]{1,0:T(8,128)(2,1)}, bf16[192,768]{1,0:T(8,128)(2,1)S(1)}, u32[]{:S(2)}, u32[]{:S(2)}) collective-permute-start(bf16[192,768]{1,0:T(8,128)(2,1)} %rest_2_.1), channel_id=1, source_target_pairs={{0,2},{1,3},{2,0},{3,1},{4,6},{5,7},{6,4},{7,5},{8,10},{9,11},{10,... | collective-permute-start | bytes 884744 | tf_op jit(solution)/shard_map/ppermute | solution.py:974
  14.8 34.4 %all-to-all-start = ((bf16[8,544,128]{2,1,0:T(8,128)(2,1)}), bf16[8,544,128]{2,1,0:T(8,128)(2,1)S(1)}, u32[]{:S(2)}, u32[]{:S(2)}) async-start(bf16[8,544,128]{2,1,0:T(8,128)(2,1)} %get-tuple-element.218), calls=%async_computation | async-start | bytes 2228224 | tf_op jit(solution)/shard_map/all_to_all | solution.py:1136
  23.8 25.4 %collective-permute-start.4 = (bf16[1536,256]{1,0:T(8,128)(2,1)}, bf16[1536,256]{1,0:T(8,128)(2,1)}, u32[]{:S(2)}, u32[]{:S(2)}) collective-permute-start(bf16[1536,256]{1,0:T(8,128)(2,1)} %get-tuple-element.221.refs_1_), channel_id=1, source_target_pairs={{0,2},{1,3},{2,0},{3,1},{4,6},{5,7},{6,4},{7,5},{8,10},{9,11},{10,... | collective-permute-start | bytes 2359304 | tf_op jit(solution)/shard_map/ppermute | solution.py:974
  25.4 23.8 %collective-permute-start.5 = (bf16[192,768]{1,0:T(8,128)(2,1)S(1)}, bf16[192,768]{1,0:T(8,128)(2,1)S(1)}, u32[]{:S(2)}, u32[]{:S(2)}) collective-permute-start(bf16[192,768]{1,0:T(8,128)(2,1)S(1)} %copy-done.11), channel_id=1, source_target_pairs={{0,2},{1,3},{2,0},{3,1},{4,6},{5,7},{6,4},{7,5},{8,10},{9,11},{10,... | collective-permute-start | bytes 884744 | tf_op jit(solution)/shard_map/ppermute | solution.py:974
  50.2 18.6 %collective-permute-start.8 = (bf16[1536,256]{1,0:T(8,128)(2,1)}, bf16[1536,256]{1,0:T(8,128)(2,1)}, u32[]{:S(2)}, u32[]{:S(2)}) collective-permute-start(bf16[1536,256]{1,0:T(8,128)(2,1)} %get-tuple-element.231.refs_5_), channel_id=1, source_target_pairs={{0,2},{1,3},{2,0},{3,1},{4,6},{5,7},{6,4},{7,5},{8,10},{9,11},{10,... | collective-permute-start | bytes 2359304 | tf_op jit(solution)/shard_map/ppermute | solution.py:974
  51.8 18.9 %collective-permute-start.9 = (bf16[1536,256]{1,0:T(8,128)(2,1)}, bf16[1536,256]{1,0:T(8,128)(2,1)}, u32[]{:S(2)}, u32[]{:S(2)}) collective-permute-start(bf16[1536,256]{1,0:T(8,128)(2,1)} %get-tuple-element.221.refs_1_), channel_id=1, source_target_pairs={{0,1},{1,0},{2,3},{3,2},{4,5},{5,4},{6,7},{7,6},{8,9},{9,8},{10,11... | collective-permute-start | bytes 2359304 | tf_op jit(solution)/shard_map/ppermute | solution.py:974
  51.8 17.0 %collective-permute-start.13 = (bf16[192,768]{1,0:T(8,128)(2,1)S(1)}, bf16[192,768]{1,0:T(8,128)(2,1)S(1)}, u32[]{:S(2)}, u32[]{:S(2)}) collective-permute-start(bf16[192,768]{1,0:T(8,128)(2,1)S(1)} %copy-done.11), channel_id=1, source_target_pairs={{0,1},{1,0},{2,3},{3,2},{4,5},{5,4},{6,7},{7,6},{8,9},{9,8},{10,11... | collective-permute-start | bytes 884744 | tf_op jit(solution)/shard_map/ppermute | solution.py:974
  52.3 19.9 %collective-permute-start.11 = (bf16[1536,256]{1,0:T(8,128)(2,1)}, bf16[1536,256]{1,0:T(8,128)(2,1)}, u32[]{:S(2)}, u32[]{:S(2)}) collective-permute-start(bf16[1536,256]{1,0:T(8,128)(2,1)} %get-tuple-element.231.refs_5_), channel_id=1, source_target_pairs={{0,1},{1,0},{2,3},{3,2},{4,5},{5,4},{6,7},{7,6},{8,9},{9,8},{10,11... | collective-permute-start | bytes 2359304 | tf_op jit(solution)/shard_map/ppermute | solution.py:974
  52.3 19.9 %collective-permute-start.10 = (bf16[1536,256]{1,0:T(8,128)(2,1)}, bf16[1536,256]{1,0:T(8,128)(2,1)}, u32[]{:S(2)}, u32[]{:S(2)}) collective-permute-start(bf16[1536,256]{1,0:T(8,128)(2,1)} %collective-permute-done.4.refs_3_), channel_id=1, source_target_pairs={{0,1},{1,0},{2,3},{3,2},{4,5},{5,4},{6,7},{7,6},{8,9},{9,8},{10,11... | collective-permute-start | bytes 2359304 | tf_op jit(solution)/shard_map/ppermute | solution.py:974
  68.8 3.4 %collective-permute-start.12 = (bf16[1536,256]{1,0:T(8,128)(2,1)}, bf16[1536,256]{1,0:T(8,128)(2,1)S(1)}, u32[]{:S(2)}, u32[]{:S(2)}) collective-permute-start(bf16[1536,256]{1,0:T(8,128)(2,1)} %collective-permute-done.8.refs_7_), channel_id=1, source_target_pairs={{0,1},{1,0},{2,3},{3,2},{4,5},{5,4},{6,7},{7,6},{8,9},{9,8},{10,11... | collective-permute-start | bytes 2359304 | tf_op jit(solution)/shard_map/ppermute | solution.py:974
  68.8 28.2 %collective-permute-start.15 = (bf16[1536,256]{1,0:T(8,128)(2,1)S(1)}, bf16[1536,256]{1,0:T(8,128)(2,1)S(1)}, u32[]{:S(2)}, u32[]{:S(2)}) collective-permute-start(bf16[1536,256]{1,0:T(8,128)(2,1)S(1)} %copy-done.19), channel_id=1, source_target_pairs={{0,2},{1,3},{2,0},{3,1},{4,6},{5,7},{6,4},{7,5},{8,10},{9,11},{10,... | collective-permute-start | bytes 2359304 | tf_op jit(solution)/shard_map/ppermute | solution.py:974
  97.9 3.6 %collective-permute-start.16 = (bf16[2,2,4,192,256]{4,3,2,1,0:T(8,128)(2,1)}, bf16[2,2,4,192,256]{4,3,2,1,0:T(8,128)(2,1)S(1)}, u32[]{:S(2)}, u32[]{:S(2)}) collective-permute-start(bf16[2,2,4,192,256]{4,3,2,1,0:T(8,128)(2,1)} %bitcast.121), channel_id=1, source_target_pairs={{0,1},{1,0},{2,3},{3,2},{4,5},{5,4},{6,7},{7,6},{8,9},{9,8},{10,11... | collective-permute-start | bytes 4718600 | tf_op jit(solution)/shard_map/ppermute | solution.py:974
  98.2 7.9 %collective-permute-start.17 = (bf16[2,2,4,192,256]{4,3,2,1,0:T(8,128)(2,1)}, bf16[2,2,4,192,256]{4,3,2,1,0:T(8,128)(2,1)S(1)}, u32[]{:S(2)}, u32[]{:S(2)}) collective-permute-start(bf16[2,2,4,192,256]{4,3,2,1,0:T(8,128)(2,1)} %bitcast.120), channel_id=1, source_target_pairs={{0,1},{1,0},{2,3},{3,2},{4,5},{5,4},{6,7},{7,6},{8,9},{9,8},{10,11... | collective-permute-start | bytes 4718600 | tf_op jit(solution)/shard_map/ppermute | solution.py:974
  98.5 10.5 %collective-permute-start.18 = (bf16[1536,256]{1,0:T(8,128)(2,1)}, bf16[1536,256]{1,0:T(8,128)(2,1)}, u32[]{:S(2)}, u32[]{:S(2)}) collective-permute-start(bf16[1536,256]{1,0:T(8,128)(2,1)} %get-tuple-element.245.refs_1_), channel_id=1, source_target_pairs={{0,1},{1,0},{2,3},{3,2},{4,5},{5,4},{6,7},{7,6},{8,9},{9,8},{10,11... | collective-permute-start | bytes 2359304 | tf_op jit(solution)/shard_map/ppermute | solution.py:974
  98.7 10.3 %collective-permute-start.19 = (bf16[1536,256]{1,0:T(8,128)(2,1)}, bf16[1536,256]{1,0:T(8,128)(2,1)}, u32[]{:S(2)}, u32[]{:S(2)}) collective-permute-start(bf16[1536,256]{1,0:T(8,128)(2,1)} %copy-done.20), channel_id=1, source_target_pairs={{0,1},{1,0},{2,3},{3,2},{4,5},{5,4},{6,7},{7,6},{8,9},{9,8},{10,11... | collective-permute-start | bytes 2359304 | tf_op jit(solution)/shard_map/ppermute | solution.py:974
  106.4 22.6 %collective-permute-start.21 = (bf16[2,4,192,256]{3,2,1,0:T(8,128)(2,1)S(1)}, bf16[2,4,192,256]{3,2,1,0:T(8,128)(2,1)S(1)}, u32[]{:S(2)}, u32[]{:S(2)}) collective-permute-start(bf16[2,4,192,256]{3,2,1,0:T(8,128)(2,1)S(1)} %get-tuple-element.295), channel_id=1, source_target_pairs={{0,4},{4,0},{8,12},{12,8},{16,20},{20,16},{24,28},{28,24},{1,5},{5... | collective-permute-start | bytes 2359304 | tf_op jit(solution)/shard_map/ppermute | solution.py:974
  107.9 21.2 %collective-permute-start.20 = (bf16[2,4,192,256]{3,2,1,0:T(8,128)(2,1)}, bf16[2,4,192,256]{3,2,1,0:T(8,128)(2,1)S(1)}, u32[]{:S(2)}, u32[]{:S(2)}) collective-permute-start(bf16[2,4,192,256]{3,2,1,0:T(8,128)(2,1)} %get-tuple-element.294), channel_id=1, source_target_pairs={{0,2},{1,3},{2,0},{3,1},{4,6},{5,7},{6,4},{7,5},{8,10},{9,11},{10,... | collective-permute-start | bytes 2359304 | tf_op jit(solution)/shard_map/ppermute | solution.py:974
  129.1 4.6 %collective-permute-start.22 = (bf16[2,2,4,272,256]{4,3,2,1,0:T(8,128)(2,1)}, bf16[2,2,4,272,256]{4,3,2,1,0:T(8,128)(2,1)S(1)}, u32[]{:S(2)}, u32[]{:S(2)}) collective-permute-start(bf16[2,2,4,272,256]{4,3,2,1,0:T(8,128)(2,1)} %bitcast.118), channel_id=1, source_target_pairs={{0,1},{1,0},{2,3},{3,2},{4,5},{5,4},{6,7},{7,6},{8,9},{9,8},{10,11... | collective-permute-start | bytes 6684680 | tf_op jit(solution)/shard_map/ppermute | solution.py:974
  135.8 21.3 %collective-permute-start.25 = (bf16[2,4,112,256]{3,2,1,0:T(8,128)(2,1)}, bf16[2,4,112,256]{3,2,1,0:T(8,128)(2,1)}, u32[]{:S(2)}, u32[]{:S(2)}) collective-permute-start(bf16[2,4,112,256]{3,2,1,0:T(8,128)(2,1)} %add_convert_fusion.4), channel_id=1, source_target_pairs={{0,2},{1,3},{2,0},{3,1},{4,6},{5,7},{6,4},{7,5},{8,10},{9,11},{10,... | collective-permute-start | bytes 1376264 | tf_op jit(solution)/shard_map/ppermute | solution.py:974
  136.8 11.2 %collective-permute-start.23 = (bf16[4,192,256]{2,1,0:T(8,128)(2,1)}, bf16[4,192,256]{2,1,0:T(8,128)(2,1)}, u32[]{:S(2)}, u32[]{:S(2)}) collective-permute-start(bf16[4,192,256]{2,1,0:T(8,128)(2,1)} %get-tuple-element.315), channel_id=1, source_target_pairs={{0,4},{4,0},{8,12},{12,8},{16,20},{20,16},{24,28},{28,24},{1,5},{5... | collective-permute-start | bytes 1179656 | tf_op jit(solution)/shard_map/ppermute | solution.py:974
  137.4 19.7 %collective-permute-start.24 = (bf16[4,192,256]{2,1,0:T(8,128)(2,1)}, bf16[4,192,256]{2,1,0:T(8,128)(2,1)}, u32[]{:S(2)}, u32[]{:S(2)}) collective-permute-start(bf16[4,192,256]{2,1,0:T(8,128)(2,1)} %get-tuple-element.316), channel_id=1, source_target_pairs={{0,2},{1,3},{2,0},{3,1},{4,6},{5,7},{6,4},{7,5},{8,10},{9,11},{10,... | collective-permute-start | bytes 1179656 | tf_op jit(solution)/shard_map/ppermute | solution.py:974
  159.5 22.0 %collective-permute-start.29 = (bf16[2,4,160,256]{3,2,1,0:T(8,128)(2,1)S(1)}, bf16[2,4,160,256]{3,2,1,0:T(8,128)(2,1)S(1)}, u32[]{:S(2)}, u32[]{:S(2)}) collective-permute-start(bf16[2,4,160,256]{3,2,1,0:T(8,128)(2,1)S(1)} %add_convert_fusion.2), channel_id=1, source_target_pairs={{0,2},{1,3},{2,0},{3,1},{4,6},{5,7},{6,4},{7,5},{8,10},{9,11},{10,... | collective-permute-start | bytes 1966088 | tf_op jit(solution)/shard_map/ppermute | solution.py:974
  160.6 20.9 %collective-permute-start.30 = (bf16[4,256,128]{2,1,0:T(8,128)(2,1)S(1)}, bf16[4,256,128]{2,1,0:T(8,128)(2,1)S(1)}, u32[]{:S(2)}, u32[]{:S(2)}) collective-permute-start(bf16[4,256,128]{2,1,0:T(8,128)(2,1)S(1)} %copy-done.32), channel_id=1, source_target_pairs={{0,4},{4,0},{8,12},{12,8},{16,20},{20,16},{24,28},{28,24},{1,5},{5... | collective-permute-start | bytes 786440 | tf_op jit(solution)/shard_map/ppermute | solution.py:974
  161.2 13.7 %collective-permute-start.26 = (bf16[2,192,256]{2,1,0:T(8,128)(2,1)S(1)}, bf16[2,192,256]{2,1,0:T(8,128)(2,1)S(1)}, u32[]{:S(2)}, u32[]{:S(2)}) collective-permute-start(bf16[2,192,256]{2,1,0:T(8,128)(2,1)S(1)} %pad_maximum_fusion.5), channel_id=1, source_target_pairs={{0,8},{4,12},{8,0},{12,4},{16,24},{20,28},{24,16},{28,20},{1,9},{5... | collective-permute-start | bytes 589832 | tf_op jit(solution)/shard_map/ppermute | solution.py:974
  162.6 18.9 %collective-permute-start.27 = (bf16[2,192,256]{2,1,0:T(8,128)(2,1)S(1)}, bf16[2,192,256]{2,1,0:T(8,128)(2,1)S(1)}, u32[]{:S(2)}, u32[]{:S(2)}) collective-permute-start(bf16[2,192,256]{2,1,0:T(8,128)(2,1)S(1)} %pad_maximum_fusion.6), channel_id=1, source_target_pairs={{0,16},{4,20},{8,24},{12,28},{16,0},{20,4},{24,8},{28,12},{1,17},{... | collective-permute-start | bytes 589832 | tf_op jit(solution)/shard_map/ppermute | solution.py:974
  167.3 14.2 %collective-permute-start.28 = (bf16[2,192,256]{2,1,0:T(8,128)(2,1)S(1)}, bf16[2,192,256]{2,1,0:T(8,128)(2,1)S(1)}, u32[]{:S(2)}, u32[]{:S(2)}) collective-permute-start(bf16[2,192,256]{2,1,0:T(8,128)(2,1)S(1)} %pad_maximum_fusion.7), channel_id=1, source_target_pairs={{0,24},{4,28},{8,16},{12,20},{16,8},{20,12},{24,0},{28,4},{1,25},{... | collective-permute-start | bytes 589832 | tf_op jit(solution)/shard_map/ppermute | solution.py:974
  181.5 7.8 %collective-permute-start.31 = (bf16[4,256,128]{2,1,0:T(8,128)(2,1)}, bf16[4,256,128]{2,1,0:T(8,128)(2,1)S(1)}, u32[]{:S(2)}, u32[]{:S(2)}) collective-permute-start(bf16[4,256,128]{2,1,0:T(8,128)(2,1)} %get-tuple-element.353), channel_id=1, source_target_pairs={{0,4},{4,0},{8,12},{12,8},{16,20},{20,16},{24,28},{28,24},{1,5},{5... | collective-permute-start | bytes 786440 | tf_op jit(solution)/shard_map/ppermute | solution.py:974
  189.3 10.4 %collective-permute-start.32 = (bf16[2,2,4,72,256]{4,3,2,1,0:T(8,128)(2,1)}, bf16[2,2,4,72,256]{4,3,2,1,0:T(8,128)(2,1)}, u32[]{:S(2)}, u32[]{:S(2)}) collective-permute-start(bf16[2,2,4,72,256]{4,3,2,1,0:T(8,128)(2,1)} %bitcast.123), channel_id=1, source_target_pairs={{0,1},{1,0},{2,3},{3,2},{4,5},{5,4},{6,7},{7,6},{8,9},{9,8},{10,11... | collective-permute-start | bytes 1769480 | tf_op jit(solution)/shard_map/ppermute | solution.py:974
  190.4 23.8 %all-to-all-start.1 = ((bf16[4,2,256,128]{3,2,1,0:T(8,128)(2,1)}), bf16[4,2,256,128]{3,2,1,0:T(8,128)(2,1)S(1)}, u32[]{:S(2)}, u32[]{:S(2)}) async-start(bf16[4,2,256,128]{3,2,1,0:T(8,128)(2,1)} %pad_maximum_fusion.2), calls=%async_computation.1 | async-start | bytes 1048576 | tf_op jit(solution)/shard_map/all_to_all | solution.py:1211
  198.3 15.0 %collective-permute-start.33 = (bf16[4,272,256]{2,1,0:T(8,128)(2,1)}, bf16[4,272,256]{2,1,0:T(8,128)(2,1)S(1)}, u32[]{:S(2)}, u32[]{:S(2)}) collective-permute-start(bf16[4,272,256]{2,1,0:T(8,128)(2,1)} %get-tuple-element.365), channel_id=1, source_target_pairs={{0,4},{4,0},{8,12},{12,8},{16,20},{20,16},{24,28},{28,24},{1,5},{5... | collective-permute-start | bytes 1671176 | tf_op jit(solution)/shard_map/ppermute | solution.py:974
  201.6 23.7 %collective-permute-start.37 = (bf16[2,4,72,256]{3,2,1,0:T(8,128)(2,1)}, bf16[2,4,72,256]{3,2,1,0:T(8,128)(2,1)S(1)}, u32[]{:S(2)}, u32[]{:S(2)}) collective-permute-start(bf16[2,4,72,256]{3,2,1,0:T(8,128)(2,1)} %get-tuple-element.382), channel_id=1, source_target_pairs={{0,2},{1,3},{2,0},{3,1},{4,6},{5,7},{6,4},{7,5},{8,10},{9,11},{10,... | collective-permute-start | bytes 884744 | tf_op jit(solution)/shard_map/ppermute | solution.py:974
  214.2 14.5 %collective-permute-start.34 = (bf16[1,272,256]{2,1,0:T(8,128)(2,1)}, bf16[1,272,256]{2,1,0:T(8,128)(2,1)S(1)}, u32[]{:S(2)}, u32[]{:S(2)}) collective-permute-start(bf16[1,272,256]{2,1,0:T(8,128)(2,1)} %get-tuple-element.379), channel_id=1, source_target_pairs={{0,8},{4,12},{8,0},{12,4},{16,24},{20,28},{24,16},{28,20},{1,9},{5... | collective-permute-start | bytes 417800 | tf_op jit(solution)/shard_map/ppermute | solution.py:974
  215.9 13.0 %collective-permute-start.35 = (bf16[1,272,256]{2,1,0:T(8,128)(2,1)}, bf16[1,272,256]{2,1,0:T(8,128)(2,1)S(1)}, u32[]{:S(2)}, u32[]{:S(2)}) collective-permute-start(bf16[1,272,256]{2,1,0:T(8,128)(2,1)} %get-tuple-element.380), channel_id=1, source_target_pairs={{0,16},{4,20},{8,24},{12,28},{16,0},{20,4},{24,8},{28,12},{1,17},{... | collective-permute-start | bytes 417800 | tf_op jit(solution)/shard_map/ppermute | solution.py:974
  218.3 10.8 %collective-permute-start.36 = (bf16[1,272,256]{2,1,0:T(8,128)(2,1)S(1)}, bf16[1,272,256]{2,1,0:T(8,128)(2,1)S(1)}, u32[]{:S(2)}, u32[]{:S(2)}) collective-permute-start(bf16[1,272,256]{2,1,0:T(8,128)(2,1)S(1)} %get-tuple-element.381), channel_id=1, source_target_pairs={{0,24},{4,28},{8,16},{12,20},{16,8},{20,12},{24,0},{28,4},{1,25},{... | collective-permute-start | bytes 417800 | tf_op jit(solution)/shard_map/ppermute | solution.py:974
  218.6 11.7 %collective-permute-start.38 = (bf16[2,192,256]{2,1,0:T(8,128)(2,1)S(1)}, bf16[2,192,256]{2,1,0:T(8,128)(2,1)S(1)}, u32[]{:S(2)}, u32[]{:S(2)}) collective-permute-start(bf16[2,192,256]{2,1,0:T(8,128)(2,1)S(1)} %add_convert_fusion.11), channel_id=1, source_target_pairs={{0,8},{4,12},{8,0},{12,4},{16,24},{20,28},{24,16},{28,20},{1,9},{5... | collective-permute-start | bytes 589832 | tf_op jit(solution)/shard_map/ppermute | solution.py:974
  225.3 19.2 %collective-permute-start.39 = (bf16[2,192,256]{2,1,0:T(8,128)(2,1)S(1)}, bf16[2,192,256]{2,1,0:T(8,128)(2,1)S(1)}, u32[]{:S(2)}, u32[]{:S(2)}) collective-permute-start(bf16[2,192,256]{2,1,0:T(8,128)(2,1)S(1)} %add_convert_fusion.11), channel_id=1, source_target_pairs={{0,16},{4,20},{8,24},{12,28},{16,0},{20,4},{24,8},{28,12},{1,17},{... | collective-permute-start | bytes 589832 | tf_op jit(solution)/shard_map/ppermute | solution.py:974
  228.6 15.9 %collective-permute-start.40 = (bf16[2,192,256]{2,1,0:T(8,128)(2,1)S(1)}, bf16[2,192,256]{2,1,0:T(8,128)(2,1)S(1)}, u32[]{:S(2)}, u32[]{:S(2)}) collective-permute-start(bf16[2,192,256]{2,1,0:T(8,128)(2,1)S(1)} %add_convert_fusion.11), channel_id=1, source_target_pairs={{0,24},{4,28},{8,16},{12,20},{16,8},{20,12},{24,0},{28,4},{1,25},{... | collective-permute-start | bytes 589832 | tf_op jit(solution)/shard_map/ppermute | solution.py:974
  229.0 15.6 %collective-permute-start.41 = (bf16[2,2,4,24,256]{4,3,2,1,0:T(8,128)(2,1)}, bf16[2,2,4,24,256]{4,3,2,1,0:T(8,128)(2,1)S(1)}, u32[]{:S(2)}, u32[]{:S(2)}) collective-permute-start(bf16[2,2,4,24,256]{4,3,2,1,0:T(8,128)(2,1)} %bitcast.124), channel_id=1, source_target_pairs={{0,1},{1,0},{2,3},{3,2},{4,5},{5,4},{6,7},{7,6},{8,9},{9,8},{10,11... | collective-permute-start | bytes 589832 | tf_op jit(solution)/shard_map/ppermute | solution.py:974
  244.7 4.9 %collective-permute-start.42 = (bf16[2,4,24,256]{3,2,1,0:T(8,128)(2,1)S(1)}, bf16[2,4,24,256]{3,2,1,0:T(8,128)(2,1)S(1)}, u32[]{:S(2)}, u32[]{:S(2)}) collective-permute-start(bf16[2,4,24,256]{3,2,1,0:T(8,128)(2,1)S(1)} %get-tuple-element.403), channel_id=1, source_target_pairs={{0,2},{1,3},{2,0},{3,1},{4,6},{5,7},{6,4},{7,5},{8,10},{9,11},{10,... | collective-permute-start | bytes 294920 | tf_op jit(solution)/shard_map/ppermute | solution.py:974
  250.5 21.3 %all-to-all-start.2 = ((bf16[8,96,256]{2,1,0:T(8,128)(2,1)}), bf16[8,96,256]{2,1,0:T(8,128)(2,1)S(1)}, u32[]{:S(2)}, u32[]{:S(2)}) async-start(bf16[8,96,256]{2,1,0:T(8,128)(2,1)} %pad_maximum_fusion.4), calls=%async_computation.2 | async-start | bytes 786432 | tf_op jit(solution)/shard_map/all_to_all | solution.py:1237
  256.4 23.1 %collective-permute-start.43 = (bf16[1,272,256]{2,1,0:T(8,128)(2,1)S(1)}, bf16[1,272,256]{2,1,0:T(8,128)(2,1)S(1)}, u32[]{:S(2)}, u32[]{:S(2)}) collective-permute-start(bf16[1,272,256]{2,1,0:T(8,128)(2,1)S(1)} %add_convert_fusion.12), channel_id=1, source_target_pairs={{0,8},{4,12},{8,0},{12,4},{16,24},{20,28},{24,16},{28,20},{1,9},{5... | collective-permute-start | bytes 417800 | tf_op jit(solution)/shard_map/ppermute | solution.py:974
  258.5 21.1 %collective-permute-start.44 = (bf16[1,272,256]{2,1,0:T(8,128)(2,1)S(1)}, bf16[1,272,256]{2,1,0:T(8,128)(2,1)S(1)}, u32[]{:S(2)}, u32[]{:S(2)}) collective-permute-start(bf16[1,272,256]{2,1,0:T(8,128)(2,1)S(1)} %add_convert_fusion.12), channel_id=1, source_target_pairs={{0,16},{4,20},{8,24},{12,28},{16,0},{20,4},{24,8},{28,12},{1,17},{... | collective-permute-start | bytes 417800 | tf_op jit(solution)/shard_map/ppermute | solution.py:974
  260.8 18.7 %collective-permute-start.45 = (bf16[1,272,256]{2,1,0:T(8,128)(2,1)S(1)}, bf16[1,272,256]{2,1,0:T(8,128)(2,1)S(1)}, u32[]{:S(2)}, u32[]{:S(2)}) collective-permute-start(bf16[1,272,256]{2,1,0:T(8,128)(2,1)S(1)} %add_convert_fusion.12), channel_id=1, source_target_pairs={{0,24},{4,28},{8,16},{12,20},{16,8},{20,12},{24,0},{28,4},{1,25},{... | collective-permute-start | bytes 417800 | tf_op jit(solution)/shard_map/ppermute | solution.py:974
  260.9 22.6 %collective-permute-start.46 = (bf16[4,2,192,256]{3,2,1,0:T(8,128)(2,1)S(1)}, bf16[4,2,192,256]{3,2,1,0:T(8,128)(2,1)S(1)}, u32[]{:S(2)}, u32[]{:S(2)}) collective-permute-start(bf16[4,2,192,256]{3,2,1,0:T(8,128)(2,1)S(1)} %pad_maximum_fusion.early_own), channel_id=1, source_target_pairs={{0,4},{4,0},{8,12},{12,8},{16,20},{20,16},{24,28},{28,24},{1,5},{5... | collective-permute-start | bytes 2359304 | tf_op jit(solution)/shard_map/ppermute | solution.py:974
  272.6 22.7 %all-to-all-start.3 = ((bf16[8,96,256]{2,1,0:T(8,128)(2,1)}), bf16[8,96,256]{2,1,0:T(8,128)(2,1)S(1)}, u32[]{:S(2)}, u32[]{:S(2)}) async-start(bf16[8,96,256]{2,1,0:T(8,128)(2,1)} %broadcast_in_dim.10), calls=%async_computation.3 | async-start | bytes 786432 | tf_op jit(solution)/shard_map/all_to_all | solution.py:1241
  279.6 15.7 %collective-permute-start.47 = (bf16[4,1,272,256]{3,2,1,0:T(8,128)(2,1)S(1)}, bf16[4,1,272,256]{3,2,1,0:T(8,128)(2,1)S(1)}, u32[]{:S(2)}, u32[]{:S(2)}) collective-permute-start(bf16[4,1,272,256]{3,2,1,0:T(8,128)(2,1)S(1)} %pad_maximum_fusion.1.last_own), channel_id=1, source_target_pairs={{0,4},{4,0},{8,12},{12,8},{16,20},{20,16},{24,28},{28,24},{1,5},{5... | collective-permute-start | bytes 1671176 | tf_op jit(solution)/shard_map/ppermute | solution.py:974
  (37 other events, 243.8 us)

commit v5 on v4

--- a/solution.py
+++ b/solution.py
@@ -221,7 +221,7 @@
 
 
 def attend_kernel(
-    place_ref, queries, marks, keyvals, starts_out, exact_out, rounded_out, logs_out, *rest,
+    place_ref, queries, keyvals, starts_out, exact_out, rounded_out, logs_out, *rest,
     blocks, tile_rows, tile_keys
 ):
     key_even, key_odd, value_even, value_odd, score_scratch, most, total = rest
@@ -242,12 +242,22 @@
             value_odd[place, 0:LANES] = jnp.where(low, 0.0, whole).astype(BF16)
             value_odd[place, LANES:] = jnp.where(low, 0.0, 1.0).astype(BF16)
 
+    own = keyvals[place_ref[0], 0, rows:, :].astype(F32)
+    lines = rows // LANES
+    marks = [jnp.broadcast_to(own[h : h + 1, :], (LANES, LANES)).T for h in range(lines)]
+    marks = jnp.concatenate(marks, axis=0)
+    if tile_rows != rows:
+        marks = sum(
+            jnp.where(tile == t, marks[t * tile_rows : (t + 1) * tile_rows, :], 0.0)
+            for t in range(rows // tile_rows)
+        )
+
     def smaller(j, count):
         lines = keyvals[block_at(place_ref, j, blocks), 0, rows:, :].astype(F32)
         missing = place_ref[0] - (blocks - 1) + j < 0
         for h in range(rows // LANES):
             line = jnp.where(missing, -1.0, lines[h : h + 1, :])
-            count = count + jnp.where(line < marks[0], 1.0, 0.0)
+            count = count + jnp.where(line < marks, 1.0, 0.0)
         return count
 
     count = lax.fori_loop(0, blocks, smaller, jnp.zeros((tile_rows, LANES), F32))
@@ -426,17 +436,19 @@
         lax.fori_loop(missing, blocks, block_terms, 0)
 
 
-def attention_sizes(rows, blocks):
-    tile_rows = 128 if rows % 128 == 0 else rows
+def attention_sizes(rows, blocks, kept):
     tile_keys = 256 if rows % 256 == 0 else 128
+    tile_rows = 128
+    if kept and rows % 256 == 0 and blocks * rows * 256 * HEADS * 4 < 24 * 1024 * 1024:
+        tile_rows = 256
     return tile_rows, tile_keys, blocks * rows // tile_keys
 
 
-def attend(place, queries, marks, keyvals, blocks):
+def attend(place, queries, keyvals, blocks):
     unused, seqs, tall, unused = keyvals.shape
     rows = tall - DOC_ROWS
     width = queries.shape[2]
-    tile_rows, tile_keys, key_tiles = attention_sizes(rows, blocks)
+    tile_rows, tile_keys, key_tiles = attention_sizes(rows, blocks, True)
     stack = PAIRS * tile_rows
     keys = blocks * rows
     row_spec = lambda lanes: pl.BlockSpec((1, tile_rows, lanes), lambda s, t, *_: (s, t, 0))
@@ -450,7 +462,6 @@
             grid=(seqs, rows // tile_rows),
             in_specs=[
                 row_spec(width),
-                row_spec(LANES),
                 pl.BlockSpec((keyvals.shape[0], 1, tall, LANES), lambda s, t, *_: (0, s, 0, 0)),
             ],
             out_specs=[row_spec(LANES)] + [row_spec(width)] * 3,
@@ -473,7 +484,7 @@
         compiler_params=params("arbitrary", "arbitrary"),
         cost_estimate=weight(),
         name="attend",
-    )(place, queries, marks, keyvals)
+    )(place, queries, keyvals)
 
 
 def attend_back(
@@ -481,7 +492,7 @@
 ):
     seqs, rows, width = queries.shape
     ctx_size = keyvals.shape[0]
-    tile_rows, tile_keys, key_tiles = attention_sizes(rows, blocks)
+    tile_rows, tile_keys, key_tiles = attention_sizes(rows, blocks, False)
     stack = PAIRS * tile_rows
     keys = blocks * rows
     row_spec = lambda lanes: pl.BlockSpec((1, tile_rows, lanes), lambda t, *_: (seq, t, 0))
@@ -554,7 +565,7 @@
             out[at, first_row:, LANES:] = jnp.zeros((height, lanes - LANES), BF16)
 
 
-def feed_kernel(spot_ref, *refs, pieces, part, first, last, names):
+def feed_kernel(spot_ref, *refs, pieces, part, first, last, names, early, late):
     use = dict(zip(names, refs))
     spot = spot_ref[0]
     step = pl.program_id(0)
@@ -593,11 +604,19 @@
                     down_sems.at[n, h, g],
                 )
 
+    def beside(kind, names):
+        for name in names:
+            pair = use[f"{name}_far"], use[name]
+            source, target = pair if kind == "in" else pair[::-1]
+            yield pltpu.make_async_copy(source, target, use[f"{name}_sem"])
+
     @pl.when(step == 0)
     def _():
         for n in range(steps):
             for one in copies(n):
                 one.start()
+        for one in beside("in", late):
+            one.start()
         if first:
 
             def begin(here):
@@ -609,6 +628,20 @@
 
             place_rows(spot, [use[f"mixing{r}"] for r in range(pieces)], use["mixing_all"])
             over_rows(rows, begin)
+            for one in beside("out", ("hidden", "scaled")):
+                one.start()
+
+    if first:
+
+        @pl.when(step == pieces // 2)
+        def _():
+            for one in beside("out", ("keep0", "send0")):
+                one.start()
+
+        @pl.when(step == steps - 1)
+        def _():
+            for one in beside("out", early):
+                one.wait()
 
     for n in range(steps):
 
@@ -634,12 +667,8 @@
 
     @pl.when(step == 0)
     def _():
-        if first:
-            reduced[...] = reduced_here
-            grads[...] = grads_here
-        else:
-            reduced[...] = use["reduced_in"][...] + reduced_here
-            grads[...] = use["grads_in"][...] + grads_here
+        reduced[...] = reduced_here
+        grads[...] = grads_here
 
     @pl.when(step > 0)
     def _():
@@ -682,14 +711,17 @@
         @pl.when(step == steps - 1)
         def _():
             sums, grad_mixed, term = use["sums"], use["grad_mixed"], use["term"]
+            for one in beside("in", late):
+                one.wait()
             sums[...] = jnp.zeros_like(sums)
             place_rows(spot, [use[f"mixing{r}"] for r in range(pieces)], use["mixing_all"])
 
             def end(here):
                 values = hidden[here, :]
-                use["layer_out"][here, :] = (values + reduced[here, :]).astype(BF16)
+                total = use["reduced_in"][here, :] + reduced[here, :]
+                use["layer_out"][here, :] = (values + total).astype(BF16)
                 normed, inverse = normalize(values)
-                grad = grads[here, :]
+                grad = use["grads_in"][here, :] + grads[here, :]
                 sums[...] += jnp.sum((grad * normed).reshape(STEP // 8, 8, width), axis=0)
                 grad_hidden = cotangent[here, :].astype(F32) + norm_back(
                     grad * use["gain"][...], normed, inverse
@@ -735,14 +767,18 @@
     for r in range(pieces):
         inputs[f"mixing{r}"] = mixing_pieces[r]
     scratch["mixing_all"] = pltpu.VMEM((width, width), BF16)
+    early, late = (), ()
     if first:
         for name in ("attended", "tokens", "gain"):
             inputs[name] = arrays[name]
         outputs.update(hidden=wide, scaled=narrow, reduced=wide, grads=wide)
+        early = ("hidden", "scaled", "keep0", "send0")
     if last:
-        for name in ("attended", "gain", "scaled", "hidden"):
+        for name in ("gain", "scaled"):
             inputs[name] = arrays[name]
-        inputs["reduced_in"], inputs["grads_in"] = arrays["reduced"], arrays["grads"]
+        late = ("attended", "hidden", "reduced_in", "grads_in")
+        for name in late:
+            inputs[f"{name}_far"] = arrays[name.removesuffix("_in")]
         outputs.update(layer_out=narrow, grad_hidden=wide, grad_attended=narrow)
         scratch.update(
             reduced=pltpu.VMEM((rows, width), F32),
@@ -751,6 +787,13 @@
             grad_mixed=pltpu.VMEM((rows, width), BF16),
             term=pltpu.VMEM((width, width), F32),
         )
+    for name in early:
+        scratch[name] = pltpu.VMEM(outputs[name].shape, outputs[name].dtype)
+    for name in late:
+        scratch[name] = pltpu.VMEM(inputs[f"{name}_far"].shape, inputs[f"{name}_far"].dtype)
+    for name in early + late:
+        scratch[f"{name}_sem"] = pltpu.SemaphoreType.DMA
+    outputs = {f"{name}_far" if name in early else name: one for name, one in outputs.items()}
     steps = len(part) * (pieces // 2)
     scratch.update(
         up_tile=pltpu.VMEM((steps, width, 2 * TILE), BF16),
@@ -761,7 +804,7 @@
     )
 
     def spec(name, array):
-        if name[:7] == "message":
+        if name[:7] == "message" or name[-4:] == "_far":
             return pl.BlockSpec(memory_space=pl.ANY)
         once = pl.Buffered(1)
         rank = len(array.shape)
@@ -775,6 +818,8 @@
             first=first,
             last=last,
             names=(*inputs, *outputs, *scratch),
+            early=early,
+            late=late,
         ),
         grid_spec=pltpu.PrefetchScalarGridSpec(
             num_scalar_prefetch=1,
@@ -788,7 +833,7 @@
         cost_estimate=weight(),
         name=f"feed{part[0]}",
     )(spot, *inputs.values())
-    return {**arrays, **dict(zip(outputs, results))}
+    return {**arrays, **dict(zip((name.removesuffix("_far") for name in outputs), results))}
 
 
 def query_kernel(spot_ref, scaled, *rest, pieces, seqs):
@@ -892,7 +937,7 @@
 
 def final_kernel(
     place_ref, early_own, early_other, last_own, last_other, late,
-    down_out, up_out, mixing_out, query_out, shared_out, first_out, second_out, whole,
+    down_out, up_out, mixing_out, query_out, shared_out, gains_out, whole,
     *, chunks, pieces, width, query_rows,
 ):
     height = width // pieces
@@ -930,18 +975,19 @@
     put_chunk(chunks - 1)
     columns(mixing_out, 2 * width, height, 0, groups)
     row = 2 * width + groups * height
-    second_out[...] = whole[row : row + second_out.shape[0], 0:LANES]
+    for i in range(width // LANES):
+        gains_out[1:2, i * LANES : (i + 1) * LANES] = whole[row + i : row + i + 1, 0:LANES]
     load(late, 0, query_rows)
     columns(query_out, 0, height, 0, groups)
     load(late, query_rows, late.shape[1] - query_rows)
     shared_out[...] = whole[0:height, 0:LANES]
-    first_out[...] = whole[0 : first_out.shape[0], LANES:]
+    for i in range(width // LANES):
+        gains_out[0:1, i * LANES : (i + 1) * LANES] = whole[i : i + 1, LANES:]
 
 
 def final_stage(place, halves, late, query_rows, chunks, pieces, width):
     height = width // pieces
     shape = lambda *dims: jax.ShapeDtypeStruct(dims, F32)
-    vector = round_up(width // LANES, 8)
     tallest = max(2 * one.shape[0] * one.shape[2] for one in halves)
     tallest = max(tallest, late.shape[0] * late.shape[1])
     return pl.pallas_call(
@@ -952,7 +998,7 @@
             num_scalar_prefetch=1,
             grid=(),
             in_specs=[pl.BlockSpec(memory_space=pltpu.VMEM)] * 5,
-            out_specs=[pl.BlockSpec(memory_space=pltpu.VMEM)] * 7,
+            out_specs=[pl.BlockSpec(memory_space=pltpu.VMEM)] * 6,
             scratch_shapes=[pltpu.VMEM((tallest, TILE), F32)],
         ),
         out_shape=[
@@ -961,8 +1007,7 @@
             shape(height, width),
             shape(height, width),
             shape(height, LANES),
-            shape(vector, LANES),
-            shape(vector, LANES),
+            shape(2, width),
         ],
         compiler_params=params(),
         cost_estimate=weight(),
@@ -1137,20 +1182,17 @@
     packed = list(pack_stage(*packed, chunks, wt_size))
     gathers = [Gather(packed[0], wt_size)]
     mixing_gather = Gather(mixing_weight, wt_size)
-    marks = jnp.broadcast_to(documents.astype(F32)[:, :, None], (seqs, rows, LANES))
     query_pieces = query_gather.finish()
     place_one = place.astype(jnp.int32).reshape(1)
 
     queries = project(spot, scaled_one, query_pieces).reshape(seqs, rows, width)
-    keyvals, gathers[0].far, mixing_gather.far, queries, marks, packed[1:] = (
-        lax.optimization_barrier(
-            (keyvals, gathers[0].far, mixing_gather.far, queries, marks, packed[1:])
-        )
+    keyvals, gathers[0].far, mixing_gather.far, queries, packed[1:] = lax.optimization_barrier(
+        (keyvals, gathers[0].far, mixing_gather.far, queries, packed[1:])
     )
     gathered = [gathers[0].finish()]
     mixing_pieces = mixing_gather.finish()
     gathers.append(Gather(packed[1], wt_size))
-    starts, exact, attended, logs = attend(place_one, queries, marks, keyvals, blocks)
+    starts, exact, attended, logs = attend(place_one, queries, keyvals, blocks)
     attended, gathers[1].far, packed[2:] = lax.optimization_barrier(
         (attended, gathers[1].far, packed[2:])
     )
@@ -1239,7 +1281,7 @@
     input_grad = tie(input_grad, two)
     late = jnp.sum(late.astype(F32), axis=0).astype(BF16)
     late = lax.all_to_all(jnp.broadcast_to(late, (ctx_size,) + late.shape), "ctx", 0, 0)
-    down_grad, up_grad, mixing_grad, query_grad, shared_grad, first_grad, second_grad = final_stage(
+    down_grad, up_grad, mixing_grad, query_grad, shared_grad, gain_grads = final_stage(
         place_one,
         [zero.held, zero.coming[0], two.held, two.coming[0]],
         late,
@@ -1249,18 +1291,15 @@
         width,
     )
 
-    def own_gain(lines):
-        vector = lines[: width // LANES].reshape(width)
-        return lax.dynamic_slice_in_dim(vector, spot_index * height, height, 0)
-
+    gain_grads = lax.dynamic_slice_in_dim(gain_grads, spot_index * height, height, 1)
     return (
         arrays["layer_out"].reshape(seqs, rows, width),
         input_grad.reshape(seqs, rows, width),
-        own_gain(first_grad),
+        gain_grads[0],
         query_grad,
         shared_grad,
         mixing_grad,
-        own_gain(second_grad),
+        gain_grads[1],
         up_grad,
         down_grad,
     )

time: 305 us -> 298 us (0.977); the launches traced: 305 us -> 294 us
  starting transfers between devices: 75.5 us -> 68.3 us
  Pallas kernels: 92.8 us -> 88.2 us
    ppermute x48, starting transfers between devices: 48.9 us -> 45 us  [swap(): return lax.ppermute(values, axis, [(i, i ^ mask) for i in range(size)])]
    pallas_call x2, Pallas kernels: 43.9 us -> 40.3 us  [feed_stage(): pl.pallas_call(functools.partial(feed_kernel, pieces=pieces, part=part, f...]
    all_to_all x1, starting transfers between devices: 7.97 us -> 4.74 us  [body(): lax.all_to_all(arriving, 'ctx', 0, 0, axis_index_groups=[list(range(x, ct...]
    ppermute x48, waiting for transfers between devices: 96.1 us -> 99.3 us  [swap(): return lax.ppermute(values, axis, [(i, i ^ mask) for i in range(size)])]
  transfers between devices with their start and end apart: 52 -> 52, of which waited for: 22 -> 22; matrix products, arithmetic and copies ran while one was open for 5% -> 5% of each run, Pallas kernels for 29% -> 28%
where the time goes in v5:
time: 298 us; the launch traced here: 294 us
  waiting for transfers between devices  108 us (36%)
  Pallas kernels  88.2 us (30%)
  starting transfers between devices  68.3 us (23%)
  other arithmetic  16.6 us (6%)
  local copies, waits for them, and re-layouts  11 us (4%)
    ppermute x48, waiting for transfers between devices, swap(): return lax.ppermute(values, axis, [(i, i ^ mask) for i in range(size)])  99.3 us
    ppermute x48, starting transfers between devices, swap(): return lax.ppermute(values, axis, [(i, i ^ mask) for i in range(size)])  45 us
    pallas_call x2, Pallas kernels, feed_stage(): pl.pallas_call(functools.partial(feed_kernel, pieces=pieces, part=part, f...  40.3 us
    pallas_call x2, Pallas kernels, attend_back(): pl.pallas_call(functools.partial(attend_back_kernel, seq=seq, blocks=bloc...  13.2 us
    all_to_all x1, waiting for transfers between devices, body(): late = lax.all_to_all(late, 'ctx', 0, 0)  8.96 us
    pallas_call x1, Pallas kernels, attend(): pl.pallas_call(functools.partial(attend_kernel, blocks=blocks, tile_rows=...  8.37 us
    all_to_all x1, starting transfers between devices, body(): lax.all_to_all(jnp.broadcast_to(late, (ctx_size,) + late.shape), 'ctx', 0...  6.87 us
    convert_element_type x6, other arithmetic, y(): self.add(lambda v: v[1][..., begin:end, :]).astype(BF16)  6.78 us
  transfers between devices with their start and end apart: 52, of which 22 were waited for; matrix products, arithmetic and copies ran while one was open for 5% of the time, Pallas kernels for 28%

profile of v5, /device:TPU:0, one launch (start us, length us, event | category | flops | bytes accessed | tf_op | source)
XLA Modules:
  0.0 293.7 jit_solution(12658881866961377601)
XLA Ops:
  2.1 3.0 %collective-permute-start.1 = (bf16[208,128]{1,0:T(8,128)(2,1)S(1)}, bf16[208,128]{1,0:T(8,128)(2,1)S(1)}, u32[]{:S(2)}, u32[]{:S(2)}) collective-permute-start(bf16[208,128]{1,0:T(8,128)(2,1)S(1)} %fusion.13.rest_0_), channel_id=1, source_target_pairs={{0,2},{1,3},{2,0},{3,1},{4,6},{5,7},{6,4},{7,5},{8,10},{9,11},{10,... | collective-permute-start | bytes 159752 | tf_op jit(solution)/shard_map/ppermute | solution.py:1019
  5.3 2.0 collective-permute-done.1.rest_2_
  9.5 4.3 %first_norm.1 = (bf16[512,768]{1,0:T(8,128)(2,1)}, bf16[8,544,128]{2,1,0:T(8,128)(2,1)}) custom-call(s32[1]{0:T(128)} %bitcast.spot_ref, bf16[512,768]{1,0:T(8,128)(2,1)} %bitcast.87, f32[1,768]{1,0:T(1,128)} %reshape_squeeze.6.gain, bf16[2,2,128]{2,1,0:T(2,128)(2,1)} %reshape.168.documents, bf16[208,128]{1,0:T(8,128)(2,1)} %copy-done.25, ...), custom_call_target="tpu_custom_call" | custom-call | flops 1 | bytes 1 | tf_op jit(solution)/shard_map/first_norm/pallas_call | solution.py:150
  14.8 5.8 %all-to-all-start = ((bf16[8,544,128]{2,1,0:T(8,128)(2,1)}), bf16[8,544,128]{2,1,0:T(8,128)(2,1)S(1)}, u32[]{:S(2)}, u32[]{:S(2)}) async-start(bf16[8,544,128]{2,1,0:T(8,128)(2,1)} %get-tuple-element.216), calls=%async_computation | async-start | bytes 2228224 | tf_op jit(solution)/shard_map/all_to_all | solution.py:1181
  20.6 3.2 %pack.1 = (bf16[1536,256]{1,0:T(8,128)(2,1)}, bf16[1536,256]{1,0:T(8,128)(2,1)}, bf16[1536,256]{1,0:T(8,128)(2,1)}) custom-call(bf16[192,3072]{1,0:T(8,128)(2,1)} %up, bf16[768,768]{1,0:T(8,128)(2,1)} %down), custom_call_target="tpu_custom_call" | custom-call | flops 1 | bytes 1 | tf_op jit(solution)/shard_map/pack/pallas_call | solution.py:95
  27.8 3.3 %project.1 = bf16[512,768]{1,0:T(8,128)(2,1)} custom-call(s32[1]{0:T(128)} %bitcast.spot_ref, bf16[512,768]{1,0:T(8,128)(2,1)} %get-tuple-element.221.operand.scaled, bf16[192,768]{1,0:T(8,128)(2,1)} %rest_2_.1, bf16[192,768]{1,0:T(8,128)(2,1)} %copy-done.14, bf16[192,768]{1,0:T(8,128)(2,1)} %copy-done.13, bf16[192,768]{1,0:T(8,128)(2,1)} %copy-done.15), custom_call_target="tpu_custom_call" | custom-call | flops 1 | bytes 1 | tf_op jit(solution)/shard_map/project/pallas_call | solution.py:179
  31.1 18.4 %collective-permute-done.5.refs_11_.refs_7_ = bf16[192,768]{1,0:T(8,128)(2,1)S(1)} collective-permute-done((bf16[192,768]{1,0:T(8,128)(2,1)S(1)}, bf16[192,768]{1,0:T(8,128)(2,1)S(1)}, u32[]{:S(2)}, u32[]{:S(2)}) %collective-permute-start.5) | collective-permute-done | bytes 294944 | tf_op jit(solution)/shard_map/ppermute | solution.py:1019
  49.5 1.8 collective-permute-start.8
  52.3 8.4 %attend.1 = (s32[2,256,128]{2,1,0:T(8,128)}, f32[2,256,768]{2,1,0:T(8,128)}, bf16[2,256,768]{2,1,0:T(8,128)(2,1)}, f32[2,256,768]{2,1,0:T(8,128)}) custom-call(s32[1]{0:T(128)} %bitcast.1.place_ref, bf16[2,256,768]{2,1,0:T(8,128)(2,1)} %bitcast.84, bf16[8,2,272,128]{3,2,1,0:T(8,128)(2,1)} %bitcast.81), custom_call_target="tpu_custom_call" | custom-call | flops 1 | bytes 1 | tf_op jit(solution)/shard_map/attend/pallas_call | solution.py:456
  60.7 8.0 %collective-permute-done.8.refs_7_ = bf16[1536,256]{1,0:T(8,128)(2,1)} collective-permute-done((bf16[1536,256]{1,0:T(8,128)(2,1)}, bf16[1536,256]{1,0:T(8,128)(2,1)}, u32[]{:S(2)}, u32[]{:S(2)}) %collective-permute-start.8) | collective-permute-done | bytes 786464 | tf_op jit(solution)/shard_map/ppermute | solution.py:1019
  68.8 1.8 collective-permute-start.15
  73.1 22.1 %feed0.1 = (bf16[2,1536,256]{2,1,0:T(8,128)(2,1)}, bf16[2,1536,256]{2,1,0:T(8,128)(2,1)}, bf16[2,2,768,256]{3,2,1,0:T(8,128)(2,1)}, bf16[2,2,768,256]{3,2,1,0:T(...) custom-call(s32[1]{0:T(128)} %bitcast.spot_ref, ...), custom_call_target="tpu_custom_call" | custom-call | flops 1 | bytes 1 | tf_op jit(solution)/shard_map/feed0/pallas_call | solution.py:813
  97.2 2.6 collective-permute-done.16
  99.8 2.6 fusion
  102.4 1.9 collective-permute-done.17
  104.6 1.5 collective-permute-start.21
  107.2 18.2 %feed2.1 = (bf16[2,2176,256]{2,1,0:T(8,128)(2,1)}, bf16[2,2176,256]{2,1,0:T(8,128)(2,1)}, bf16[512,768]{1,0:T(8,128)(2,1)}, f32[512,768]{1,0:T(8,128)}, bf16[512,768]{1,0:T(8,128)(2,1)}) custom-call(s32[1]{0:T(128)} %bitcast.spot_ref, bf16[512,768]{1,0:T(8,128)(2,1)} %bitcast.91, bf16[1536,256]{1,0:T(8,128)(2,1)} %get-tuple-element.242.refs_1_, ...), custom_call_target="tpu_custom_call" | custom-call | flops 1 | bytes 1 | tf_op jit(solution)/shard_map/feed2/pallas_call | solution.py:813
  128.1 2.2 collective-permute-done.22
  135.0 6.6 %attend_back.2 = (bf16[1,256,768]{2,1,0:T(8,128)(2,1)}, bf16[4,256,128]{2,1,0:T(8,128)(2,1)}, bf16[4,256,128]{2,1,0:T(8,128)(2,1)}) custom-call(s32[1]{0:T(128)} %bitcast.1.place_ref, bf16[2,256,768]{2,1,0:T(8,128)(2,1)} %bitcast.85, s32[2,256,128]{2,1,0:T(8,128)} %get-tuple-element.283.starts, f32[2,256,768]{2,1,0:T(8,128)} %get-tuple-element.284.exact, ...), custom_call_target="tpu_custom_call" | custom-call | flops 1 | bytes 1 | tf_op jit(solution)/shard_map/attend_back/pallas_call | solution.py:499
  141.7 2.7 collective-permute-done.23
  144.5 9.2 %collective-permute-done.24 = bf16[4,192,256]{2,1,0:T(8,128)(2,1)} collective-permute-done((bf16[4,192,256]{2,1,0:T(8,128)(2,1)}, bf16[4,192,256]{2,1,0:T(8,128)(2,1)}, u32[]{:S(2)}, u32[]{:S(2)}) %collective-permute-start.24) | collective-permute-done | bytes 393248 | tf_op jit(solution)/shard_map/ppermute | solution.py:1019
  157.7 1.4 collective-permute-start.26
  159.1 2.9 collective-permute-start.27
  162.1 6.7 %attend_back.3 = (bf16[1,256,768]{2,1,0:T(8,128)(2,1)}, bf16[4,256,128]{2,1,0:T(8,128)(2,1)}, bf16[4,256,128]{2,1,0:T(8,128)(2,1)}) custom-call(s32[1]{0:T(128)} %bitcast.1.place_ref, bf16[2,256,768]{2,1,0:T(8,128)(2,1)} %bitcast.86, s32[2,256,128]{2,1,0:T(8,128)} %get-tuple-element.283.starts, f32[2,256,768]{2,1,0:T(8,128)} %get-tuple-element.284.exact, ...), custom_call_target="tpu_custom_call" | custom-call | flops 1 | bytes 1 | tf_op jit(solution)/shard_map/attend_back/pallas_call | solution.py:499
  169.8 6.3 %collective-permute-done.27 = bf16[2,192,256]{2,1,0:T(8,128)(2,1)S(1)} collective-permute-done((bf16[2,192,256]{2,1,0:T(8,128)(2,1)S(1)}, bf16[2,192,256]{2,1,0:T(8,128)(2,1)S(1)}, u32[]{:S(2)}, u32[]{:S(2)}) %collective-permute-start.27) | collective-permute-done | bytes 196640 | tf_op jit(solution)/shard_map/ppermute | solution.py:1019
  176.1 1.3 collective-permute-start.31
  178.6 4.7 %query_grad.1 = (f32[512,768]{1,0:T(8,128)}, bf16[2,576,256]{2,1,0:T(8,128)(2,1)}, bf16[2,576,256]{2,1,0:T(8,128)(2,1)}) custom-call(s32[1]{0:T(128)} %bitcast.spot_ref, bf16[512,768]{1,0:T(8,128)(2,1)} %get-tuple-element.221.operand.scaled, bf16[256,768]{1,0:T(8,128)(2,1)} %bitcast.105, bf16[256,768]{1,0:T(8,128)(2,1)} %bitcast.106, ...), custom_call_target="tpu_custom_call" | custom-call | flops 1 | bytes 1 | tf_op jit(solution)/shard_map/query_grad/pallas_call | solution.py:860
  184.3 4.7 %all-to-all-start.1 = ((bf16[4,2,256,128]{3,2,1,0:T(8,128)(2,1)}), bf16[4,2,256,128]{3,2,1,0:T(8,128)(2,1)S(1)}, u32[]{:S(2)}, u32[]{:S(2)}) async-start(bf16[4,2,256,128]{3,2,1,0:T(8,128)(2,1)} %pad_maximum_fusion.2), calls=%async_computation.1 | async-start | bytes 1048576 | tf_op jit(solution)/shard_map/all_to_all | solution.py:1253
  190.0 1.9 fusion.5
  193.1 10.9 %collective-permute-done.33 = bf16[4,272,256]{2,1,0:T(8,128)(2,1)S(1)} collective-permute-done((bf16[4,272,256]{2,1,0:T(8,128)(2,1)}, bf16[4,272,256]{2,1,0:T(8,128)(2,1)S(1)}, u32[]{:S(2)}, u32[]{:S(2)}) %collective-permute-start.33) | collective-permute-done | bytes 557088 | tf_op jit(solution)/shard_map/ppermute | solution.py:1019
  204.9 1.7 collective-permute-start.34
  206.6 2.4 collective-permute-start.35
  210.1 5.9 %last.1 = (f32[512,768]{1,0:T(8,128)}, bf16[2,192,256]{2,1,0:T(8,128)(2,1)}, bf16[2,192,256]{2,1,0:T(8,128)(2,1)}) custom-call(s32[1]{0:T(128)} %bitcast.spot_ref, bf16[512,768]{1,0:T(8,128)(2,1)} %bitcast.89, f32[1,768]{1,0:T(1,128)} %reshape_squeeze.6.gain, bf16[512,768]{1,0:T(8,128)(2,1)} %get-tuple-element.221.operand.scaled, ...), custom_call_target="tpu_custom_call" | custom-call | flops 1 | bytes 1 | tf_op jit(solution)/shard_map/last/pallas_call | solution.py:917
  216.0 3.3 %collective-permute-start.39 = (bf16[2,192,256]{2,1,0:T(8,128)(2,1)S(1)}, bf16[2,192,256]{2,1,0:T(8,128)(2,1)S(1)}, u32[]{:S(2)}, u32[]{:S(2)}) collective-permute-start(bf16[2,192,256]{2,1,0:T(8,128)(2,1)S(1)} %add_convert_fusion.11), channel_id=1, source_target_pairs={{0,16},{4,20},{8,24},{12,28},{16,0},{20,4},{24,8},{28,12},{1,17},{... | collective-permute-start | bytes 589832 | tf_op jit(solution)/shard_map/ppermute | solution.py:1019
  221.0 14.3 %collective-permute-done.39 = bf16[2,192,256]{2,1,0:T(8,128)(2,1)S(1)} collective-permute-done((bf16[2,192,256]{2,1,0:T(8,128)(2,1)S(1)}, bf16[2,192,256]{2,1,0:T(8,128)(2,1)S(1)}, u32[]{:S(2)}, u32[]{:S(2)}) %collective-permute-start.39) | collective-permute-done | bytes 196640 | tf_op jit(solution)/shard_map/ppermute | solution.py:1019
  235.4 1.5 collective-permute-start.42
  236.9 3.2 %collective-permute-done.42 = bf16[2,4,24,256]{3,2,1,0:T(8,128)(2,1)S(1)} collective-permute-done((bf16[2,4,24,256]{3,2,1,0:T(8,128)(2,1)S(1)}, bf16[2,4,24,256]{3,2,1,0:T(8,128)(2,1)S(1)}, u32[]{:S(2)}, u32[]{:S(2)}) %collective-permute-start.42) | collective-permute-done | bytes 98336 | tf_op jit(solution)/shard_map/ppermute | solution.py:1019
  241.0 5.8 %all-to-all-start.2 = ((bf16[8,96,256]{2,1,0:T(8,128)(2,1)}), bf16[8,96,256]{2,1,0:T(8,128)(2,1)S(1)}, u32[]{:S(2)}, u32[]{:S(2)}) async-start(bf16[8,96,256]{2,1,0:T(8,128)(2,1)} %pad_maximum_fusion.4), calls=%async_computation.2 | async-start | bytes 786432 | tf_op jit(solution)/shard_map/all_to_all | solution.py:1279
  246.8 2.0 collective-permute-start.43
  248.8 2.4 collective-permute-start.44
  251.2 2.0 collective-permute-start.46
  253.2 9.0 %all-to-all-done.2 = bf16[8,96,256]{2,1,0:T(8,128)(2,1)S(1)} async-done(((bf16[8,96,256]{2,1,0:T(8,128)(2,1)}), bf16[8,96,256]{2,1,0:T(8,128)(2,1)S(1)}, u32[]{:S(2)}, u32[]{:S(2)}) %all-to-all-start.2) | async-done | bytes 393248 | tf_op jit(solution)/shard_map/all_to_all | solution.py:1279
  263.0 6.9 %all-to-all-start.3 = ((bf16[8,96,256]{2,1,0:T(8,128)(2,1)}), bf16[8,96,256]{2,1,0:T(8,128)(2,1)S(1)}, u32[]{:S(2)}, u32[]{:S(2)}) async-start(bf16[8,96,256]{2,1,0:T(8,128)(2,1)} %broadcast_in_dim.3), calls=%async_computation.3 | async-start | bytes 786432 | tf_op jit(solution)/shard_map/all_to_all | solution.py:1283
  270.0 2.1 collective-permute-start.47
  272.1 1.7 collective-permute-done.46.early_other
  273.8 11.9 %collective-permute-done.47.last_other = bf16[4,1,272,256]{3,2,1,0:T(8,128)(2,1)S(1)} collective-permute-done((bf16[4,1,272,256]{3,2,1,0:T(8,128)(2,1)S(1)}, bf16[4,1,272,256]{3,2,1,0:T(8,128)(2,1)S(1)}, u32[]{:S(2)}, u32[]{:S(2)}) %collective-permute-start.47) | collective-permute-done | bytes 557088 | tf_op jit(solution)/shard_map/ppermute | solution.py:1019
  287.3 5.0 %final.1 = (f32[768,768]{1,0:T(8,128)}, f32[192,3072]{1,0:T(8,128)}, f32[192,768]{1,0:T(8,128)}, f32[192,768]{1,0:T(8,128)}, f32[192,128]{1,0:T(8,128)}, /*index=5*/f32[2,768]{1,0:T(2,128)}) custom-call(s32[1]{0:T(128)} %bitcast.1.place_ref, bf16[4,2,192,256]{3,2,1,0:T(8,128)(2,1)} %copy-done.4, bf16[4,2,192,256]{3,2,1,0:T(8,128)(2,1)} %copy-done.22, ...), custom_call_target="tpu_custom_call" | custom-call | flops 1 | bytes 1 | tf_op jit(solution)/shard_map/final/pallas_call | solution.py:993
  292.3 1.4 fusion.15
  (186 shorter events, 39.7 us)
Async XLA Ops:
  2.1 5.2 %collective-permute-start.1 = (bf16[208,128]{1,0:T(8,128)(2,1)S(1)}, bf16[208,128]{1,0:T(8,128)(2,1)S(1)}, u32[]{:S(2)}, u32[]{:S(2)}) collective-permute-start(bf16[208,128]{1,0:T(8,128)(2,1)S(1)} %fusion.13.rest_0_), channel_id=1, source_target_pairs={{0,2},{1,3},{2,0},{3,1},{4,6},{5,7},{6,4},{7,5},{8,10},{9,11},{10,... | collective-permute-start | bytes 159752 | tf_op jit(solution)/shard_map/ppermute | solution.py:1019
  5.2 3.5 %collective-permute-start = (bf16[208,128]{1,0:T(8,128)(2,1)S(1)}, bf16[208,128]{1,0:T(8,128)(2,1)S(1)}, u32[]{:S(2)}, u32[]{:S(2)}) collective-permute-start(bf16[208,128]{1,0:T(8,128)(2,1)S(1)} %fusion.13.rest_0_), channel_id=1, source_target_pairs={{0,1},{1,0},{2,3},{3,2},{4,5},{5,4},{6,7},{7,6},{8,9},{9,8},{10,11... | collective-permute-start | bytes 159752 | tf_op jit(solution)/shard_map/ppermute | solution.py:1019
  5.2 9.6 %collective-permute-start.3 = (bf16[192,768]{1,0:T(8,128)(2,1)}, bf16[192,768]{1,0:T(8,128)(2,1)S(1)}, u32[]{:S(2)}, u32[]{:S(2)}) collective-permute-start(bf16[192,768]{1,0:T(8,128)(2,1)} %rest_2_.1), channel_id=1, source_target_pairs={{0,2},{1,3},{2,0},{3,1},{4,6},{5,7},{6,4},{7,5},{8,10},{9,11},{10,... | collective-permute-start | bytes 884744 | tf_op jit(solution)/shard_map/ppermute | solution.py:1019
  14.8 34.7 %all-to-all-start = ((bf16[8,544,128]{2,1,0:T(8,128)(2,1)}), bf16[8,544,128]{2,1,0:T(8,128)(2,1)S(1)}, u32[]{:S(2)}, u32[]{:S(2)}) async-start(bf16[8,544,128]{2,1,0:T(8,128)(2,1)} %get-tuple-element.216), calls=%async_computation | async-start | bytes 2228224 | tf_op jit(solution)/shard_map/all_to_all | solution.py:1181
  23.8 25.7 %collective-permute-start.4 = (bf16[1536,256]{1,0:T(8,128)(2,1)}, bf16[1536,256]{1,0:T(8,128)(2,1)}, u32[]{:S(2)}, u32[]{:S(2)}) collective-permute-start(bf16[1536,256]{1,0:T(8,128)(2,1)} %get-tuple-element.219.refs_1_), channel_id=1, source_target_pairs={{0,2},{1,3},{2,0},{3,1},{4,6},{5,7},{6,4},{7,5},{8,10},{9,11},{10,... | collective-permute-start | bytes 2359304 | tf_op jit(solution)/shard_map/ppermute | solution.py:1019
  25.6 23.9 %collective-permute-start.5 = (bf16[192,768]{1,0:T(8,128)(2,1)S(1)}, bf16[192,768]{1,0:T(8,128)(2,1)S(1)}, u32[]{:S(2)}, u32[]{:S(2)}) collective-permute-start(bf16[192,768]{1,0:T(8,128)(2,1)S(1)} %copy-done.11), channel_id=1, source_target_pairs={{0,2},{1,3},{2,0},{3,1},{4,6},{5,7},{6,4},{7,5},{8,10},{9,11},{10,... | collective-permute-start | bytes 884744 | tf_op jit(solution)/shard_map/ppermute | solution.py:1019
  49.5 19.2 %collective-permute-start.8 = (bf16[1536,256]{1,0:T(8,128)(2,1)}, bf16[1536,256]{1,0:T(8,128)(2,1)}, u32[]{:S(2)}, u32[]{:S(2)}) collective-permute-start(bf16[1536,256]{1,0:T(8,128)(2,1)} %get-tuple-element.228.refs_5_), channel_id=1, source_target_pairs={{0,2},{1,3},{2,0},{3,1},{4,6},{5,7},{6,4},{7,5},{8,10},{9,11},{10,... | collective-permute-start | bytes 2359304 | tf_op jit(solution)/shard_map/ppermute | solution.py:1019
  51.3 19.3 %collective-permute-start.9 = (bf16[1536,256]{1,0:T(8,128)(2,1)}, bf16[1536,256]{1,0:T(8,128)(2,1)}, u32[]{:S(2)}, u32[]{:S(2)}) collective-permute-start(bf16[1536,256]{1,0:T(8,128)(2,1)} %get-tuple-element.219.refs_1_), channel_id=1, source_target_pairs={{0,1},{1,0},{2,3},{3,2},{4,5},{5,4},{6,7},{7,6},{8,9},{9,8},{10,11... | collective-permute-start | bytes 2359304 | tf_op jit(solution)/shard_map/ppermute | solution.py:1019
  51.3 17.4 %collective-permute-start.13 = (bf16[192,768]{1,0:T(8,128)(2,1)S(1)}, bf16[192,768]{1,0:T(8,128)(2,1)S(1)}, u32[]{:S(2)}, u32[]{:S(2)}) collective-permute-start(bf16[192,768]{1,0:T(8,128)(2,1)S(1)} %copy-done.11), channel_id=1, source_target_pairs={{0,1},{1,0},{2,3},{3,2},{4,5},{5,4},{6,7},{7,6},{8,9},{9,8},{10,11... | collective-permute-start | bytes 884744 | tf_op jit(solution)/shard_map/ppermute | solution.py:1019
  51.8 20.3 %collective-permute-start.11 = (bf16[1536,256]{1,0:T(8,128)(2,1)}, bf16[1536,256]{1,0:T(8,128)(2,1)}, u32[]{:S(2)}, u32[]{:S(2)}) collective-permute-start(bf16[1536,256]{1,0:T(8,128)(2,1)} %get-tuple-element.228.refs_5_), channel_id=1, source_target_pairs={{0,1},{1,0},{2,3},{3,2},{4,5},{5,4},{6,7},{7,6},{8,9},{9,8},{10,11... | collective-permute-start | bytes 2359304 | tf_op jit(solution)/shard_map/ppermute | solution.py:1019
  51.8 20.3 %collective-permute-start.10 = (bf16[1536,256]{1,0:T(8,128)(2,1)}, bf16[1536,256]{1,0:T(8,128)(2,1)}, u32[]{:S(2)}, u32[]{:S(2)}) collective-permute-start(bf16[1536,256]{1,0:T(8,128)(2,1)} %collective-permute-done.4.refs_3_), channel_id=1, source_target_pairs={{0,1},{1,0},{2,3},{3,2},{4,5},{5,4},{6,7},{7,6},{8,9},{9,8},{10,11... | collective-permute-start | bytes 2359304 | tf_op jit(solution)/shard_map/ppermute | solution.py:1019
  68.7 3.4 %collective-permute-start.12 = (bf16[1536,256]{1,0:T(8,128)(2,1)}, bf16[1536,256]{1,0:T(8,128)(2,1)S(1)}, u32[]{:S(2)}, u32[]{:S(2)}) collective-permute-start(bf16[1536,256]{1,0:T(8,128)(2,1)} %collective-permute-done.8.refs_7_), channel_id=1, source_target_pairs={{0,1},{1,0},{2,3},{3,2},{4,5},{5,4},{6,7},{7,6},{8,9},{9,8},{10,11... | collective-permute-start | bytes 2359304 | tf_op jit(solution)/shard_map/ppermute | solution.py:1019
  68.8 26.5 %collective-permute-start.15 = (bf16[1536,256]{1,0:T(8,128)(2,1)S(1)}, bf16[1536,256]{1,0:T(8,128)(2,1)S(1)}, u32[]{:S(2)}, u32[]{:S(2)}) collective-permute-start(bf16[1536,256]{1,0:T(8,128)(2,1)S(1)} %copy-done.19), channel_id=1, source_target_pairs={{0,2},{1,3},{2,0},{3,1},{4,6},{5,7},{6,4},{7,5},{8,10},{9,11},{10,... | collective-permute-start | bytes 2359304 | tf_op jit(solution)/shard_map/ppermute | solution.py:1019
  96.1 3.6 %collective-permute-start.16 = (bf16[2,2,4,192,256]{4,3,2,1,0:T(8,128)(2,1)}, bf16[2,2,4,192,256]{4,3,2,1,0:T(8,128)(2,1)S(1)}, u32[]{:S(2)}, u32[]{:S(2)}) collective-permute-start(bf16[2,2,4,192,256]{4,3,2,1,0:T(8,128)(2,1)} %bitcast.121), channel_id=1, source_target_pairs={{0,1},{1,0},{2,3},{3,2},{4,5},{5,4},{6,7},{7,6},{8,9},{9,8},{10,11... | collective-permute-start | bytes 4718600 | tf_op jit(solution)/shard_map/ppermute | solution.py:1019
  96.4 7.9 %collective-permute-start.17 = (bf16[2,2,4,192,256]{4,3,2,1,0:T(8,128)(2,1)}, bf16[2,2,4,192,256]{4,3,2,1,0:T(8,128)(2,1)S(1)}, u32[]{:S(2)}, u32[]{:S(2)}) collective-permute-start(bf16[2,2,4,192,256]{4,3,2,1,0:T(8,128)(2,1)} %bitcast.120), channel_id=1, source_target_pairs={{0,1},{1,0},{2,3},{3,2},{4,5},{5,4},{6,7},{7,6},{8,9},{9,8},{10,11... | collective-permute-start | bytes 4718600 | tf_op jit(solution)/shard_map/ppermute | solution.py:1019
  96.7 10.5 %collective-permute-start.18 = (bf16[1536,256]{1,0:T(8,128)(2,1)}, bf16[1536,256]{1,0:T(8,128)(2,1)}, u32[]{:S(2)}, u32[]{:S(2)}) collective-permute-start(bf16[1536,256]{1,0:T(8,128)(2,1)} %get-tuple-element.242.refs_1_), channel_id=1, source_target_pairs={{0,1},{1,0},{2,3},{3,2},{4,5},{5,4},{6,7},{7,6},{8,9},{9,8},{10,11... | collective-permute-start | bytes 2359304 | tf_op jit(solution)/shard_map/ppermute | solution.py:1019
  96.9 10.3 %collective-permute-start.19 = (bf16[1536,256]{1,0:T(8,128)(2,1)}, bf16[1536,256]{1,0:T(8,128)(2,1)}, u32[]{:S(2)}, u32[]{:S(2)}) collective-permute-start(bf16[1536,256]{1,0:T(8,128)(2,1)} %copy-done.20), channel_id=1, source_target_pairs={{0,1},{1,0},{2,3},{3,2},{4,5},{5,4},{6,7},{7,6},{8,9},{9,8},{10,11... | collective-permute-start | bytes 2359304 | tf_op jit(solution)/shard_map/ppermute | solution.py:1019
  104.6 20.7 %collective-permute-start.21 = (bf16[2,4,192,256]{3,2,1,0:T(8,128)(2,1)S(1)}, bf16[2,4,192,256]{3,2,1,0:T(8,128)(2,1)S(1)}, u32[]{:S(2)}, u32[]{:S(2)}) collective-permute-start(bf16[2,4,192,256]{3,2,1,0:T(8,128)(2,1)S(1)} %get-tuple-element.292), channel_id=1, source_target_pairs={{0,4},{4,0},{8,12},{12,8},{16,20},{20,16},{24,28},{28,24},{1,5},{5... | collective-permute-start | bytes 2359304 | tf_op jit(solution)/shard_map/ppermute | solution.py:1019
  106.1 19.6 %collective-permute-start.20 = (bf16[2,4,192,256]{3,2,1,0:T(8,128)(2,1)}, bf16[2,4,192,256]{3,2,1,0:T(8,128)(2,1)S(1)}, u32[]{:S(2)}, u32[]{:S(2)}) collective-permute-start(bf16[2,4,192,256]{3,2,1,0:T(8,128)(2,1)} %get-tuple-element.291), channel_id=1, source_target_pairs={{0,2},{1,3},{2,0},{3,1},{4,6},{5,7},{6,4},{7,5},{8,10},{9,11},{10,... | collective-permute-start | bytes 2359304 | tf_op jit(solution)/shard_map/ppermute | solution.py:1019
  125.7 4.6 %collective-permute-start.22 = (bf16[2,2,4,272,256]{4,3,2,1,0:T(8,128)(2,1)}, bf16[2,2,4,272,256]{4,3,2,1,0:T(8,128)(2,1)S(1)}, u32[]{:S(2)}, u32[]{:S(2)}) collective-permute-start(bf16[2,2,4,272,256]{4,3,2,1,0:T(8,128)(2,1)} %bitcast.118), channel_id=1, source_target_pairs={{0,1},{1,0},{2,3},{3,2},{4,5},{5,4},{6,7},{7,6},{8,9},{9,8},{10,11... | collective-permute-start | bytes 6684680 | tf_op jit(solution)/shard_map/ppermute | solution.py:1019
  132.3 21.3 %collective-permute-start.25 = (bf16[2,4,112,256]{3,2,1,0:T(8,128)(2,1)}, bf16[2,4,112,256]{3,2,1,0:T(8,128)(2,1)}, u32[]{:S(2)}, u32[]{:S(2)}) collective-permute-start(bf16[2,4,112,256]{3,2,1,0:T(8,128)(2,1)} %add_convert_fusion.4), channel_id=1, source_target_pairs={{0,2},{1,3},{2,0},{3,1},{4,6},{5,7},{6,4},{7,5},{8,10},{9,11},{10,... | collective-permute-start | bytes 1376264 | tf_op jit(solution)/shard_map/ppermute | solution.py:1019
  133.3 11.2 %collective-permute-start.23 = (bf16[4,192,256]{2,1,0:T(8,128)(2,1)}, bf16[4,192,256]{2,1,0:T(8,128)(2,1)}, u32[]{:S(2)}, u32[]{:S(2)}) collective-permute-start(bf16[4,192,256]{2,1,0:T(8,128)(2,1)} %get-tuple-element.312), channel_id=1, source_target_pairs={{0,4},{4,0},{8,12},{12,8},{16,20},{20,16},{24,28},{28,24},{1,5},{5... | collective-permute-start | bytes 1179656 | tf_op jit(solution)/shard_map/ppermute | solution.py:1019
  133.9 19.7 %collective-permute-start.24 = (bf16[4,192,256]{2,1,0:T(8,128)(2,1)}, bf16[4,192,256]{2,1,0:T(8,128)(2,1)}, u32[]{:S(2)}, u32[]{:S(2)}) collective-permute-start(bf16[4,192,256]{2,1,0:T(8,128)(2,1)} %get-tuple-element.313), channel_id=1, source_target_pairs={{0,2},{1,3},{2,0},{3,1},{4,6},{5,7},{6,4},{7,5},{8,10},{9,11},{10,... | collective-permute-start | bytes 1179656 | tf_op jit(solution)/shard_map/ppermute | solution.py:1019
  156.1 20.1 %collective-permute-start.29 = (bf16[2,4,160,256]{3,2,1,0:T(8,128)(2,1)S(1)}, bf16[2,4,160,256]{3,2,1,0:T(8,128)(2,1)S(1)}, u32[]{:S(2)}, u32[]{:S(2)}) collective-permute-start(bf16[2,4,160,256]{3,2,1,0:T(8,128)(2,1)S(1)} %add_convert_fusion.2), channel_id=1, source_target_pairs={{0,2},{1,3},{2,0},{3,1},{4,6},{5,7},{6,4},{7,5},{8,10},{9,11},{10,... | collective-permute-start | bytes 1966088 | tf_op jit(solution)/shard_map/ppermute | solution.py:1019
  157.1 19.0 %collective-permute-start.30 = (bf16[4,256,128]{2,1,0:T(8,128)(2,1)S(1)}, bf16[4,256,128]{2,1,0:T(8,128)(2,1)S(1)}, u32[]{:S(2)}, u32[]{:S(2)}) collective-permute-start(bf16[4,256,128]{2,1,0:T(8,128)(2,1)S(1)} %copy-done.32), channel_id=1, source_target_pairs={{0,4},{4,0},{8,12},{12,8},{16,20},{20,16},{24,28},{28,24},{1,5},{5... | collective-permute-start | bytes 786440 | tf_op jit(solution)/shard_map/ppermute | solution.py:1019
  157.7 12.1 %collective-permute-start.26 = (bf16[2,192,256]{2,1,0:T(8,128)(2,1)S(1)}, bf16[2,192,256]{2,1,0:T(8,128)(2,1)S(1)}, u32[]{:S(2)}, u32[]{:S(2)}) collective-permute-start(bf16[2,192,256]{2,1,0:T(8,128)(2,1)S(1)} %pad_maximum_fusion.5), channel_id=1, source_target_pairs={{0,8},{4,12},{8,0},{12,4},{16,24},{20,28},{24,16},{28,20},{1,9},{5... | collective-permute-start | bytes 589832 | tf_op jit(solution)/shard_map/ppermute | solution.py:1019
  159.1 17.0 %collective-permute-start.27 = (bf16[2,192,256]{2,1,0:T(8,128)(2,1)S(1)}, bf16[2,192,256]{2,1,0:T(8,128)(2,1)S(1)}, u32[]{:S(2)}, u32[]{:S(2)}) collective-permute-start(bf16[2,192,256]{2,1,0:T(8,128)(2,1)S(1)} %pad_maximum_fusion.6), channel_id=1, source_target_pairs={{0,16},{4,20},{8,24},{12,28},{16,0},{20,4},{24,8},{28,12},{1,17},{... | collective-permute-start | bytes 589832 | tf_op jit(solution)/shard_map/ppermute | solution.py:1019
  162.0 14.1 %collective-permute-start.28 = (bf16[2,192,256]{2,1,0:T(8,128)(2,1)S(1)}, bf16[2,192,256]{2,1,0:T(8,128)(2,1)S(1)}, u32[]{:S(2)}, u32[]{:S(2)}) collective-permute-start(bf16[2,192,256]{2,1,0:T(8,128)(2,1)S(1)} %pad_maximum_fusion.7), channel_id=1, source_target_pairs={{0,24},{4,28},{8,16},{12,20},{16,8},{20,12},{24,0},{28,4},{1,25},{... | collective-permute-start | bytes 589832 | tf_op jit(solution)/shard_map/ppermute | solution.py:1019
  176.1 7.2 %collective-permute-start.31 = (bf16[4,256,128]{2,1,0:T(8,128)(2,1)}, bf16[4,256,128]{2,1,0:T(8,128)(2,1)S(1)}, u32[]{:S(2)}, u32[]{:S(2)}) collective-permute-start(bf16[4,256,128]{2,1,0:T(8,128)(2,1)} %get-tuple-element.350), channel_id=1, source_target_pairs={{0,4},{4,0},{8,12},{12,8},{16,20},{20,16},{24,28},{28,24},{1,5},{5... | collective-permute-start | bytes 786440 | tf_op jit(solution)/shard_map/ppermute | solution.py:1019
  183.3 6.7 %collective-permute-start.32 = (bf16[2,2,4,72,256]{4,3,2,1,0:T(8,128)(2,1)}, bf16[2,2,4,72,256]{4,3,2,1,0:T(8,128)(2,1)}, u32[]{:S(2)}, u32[]{:S(2)}) collective-permute-start(bf16[2,2,4,72,256]{4,3,2,1,0:T(8,128)(2,1)} %bitcast.123), channel_id=1, source_target_pairs={{0,1},{1,0},{2,3},{3,2},{4,5},{5,4},{6,7},{7,6},{8,9},{9,8},{10,11... | collective-permute-start | bytes 1769480 | tf_op jit(solution)/shard_map/ppermute | solution.py:1019
  184.3 20.5 %all-to-all-start.1 = ((bf16[4,2,256,128]{3,2,1,0:T(8,128)(2,1)}), bf16[4,2,256,128]{3,2,1,0:T(8,128)(2,1)S(1)}, u32[]{:S(2)}, u32[]{:S(2)}) async-start(bf16[4,2,256,128]{3,2,1,0:T(8,128)(2,1)} %pad_maximum_fusion.2), calls=%async_computation.1 | async-start | bytes 1048576 | tf_op jit(solution)/shard_map/all_to_all | solution.py:1253
  189.1 14.9 %collective-permute-start.33 = (bf16[4,272,256]{2,1,0:T(8,128)(2,1)}, bf16[4,272,256]{2,1,0:T(8,128)(2,1)S(1)}, u32[]{:S(2)}, u32[]{:S(2)}) collective-permute-start(bf16[4,272,256]{2,1,0:T(8,128)(2,1)} %get-tuple-element.362), channel_id=1, source_target_pairs={{0,4},{4,0},{8,12},{12,8},{16,20},{20,16},{24,28},{28,24},{1,5},{5... | collective-permute-start | bytes 1671176 | tf_op jit(solution)/shard_map/ppermute | solution.py:1019
  191.9 24.1 %collective-permute-start.37 = (bf16[2,4,72,256]{3,2,1,0:T(8,128)(2,1)}, bf16[2,4,72,256]{3,2,1,0:T(8,128)(2,1)S(1)}, u32[]{:S(2)}, u32[]{:S(2)}) collective-permute-start(bf16[2,4,72,256]{3,2,1,0:T(8,128)(2,1)} %get-tuple-element.379), channel_id=1, source_target_pairs={{0,2},{1,3},{2,0},{3,1},{4,6},{5,7},{6,4},{7,5},{8,10},{9,11},{10,... | collective-permute-start | bytes 884744 | tf_op jit(solution)/shard_map/ppermute | solution.py:1019
  204.9 14.5 %collective-permute-start.34 = (bf16[1,272,256]{2,1,0:T(8,128)(2,1)}, bf16[1,272,256]{2,1,0:T(8,128)(2,1)S(1)}, u32[]{:S(2)}, u32[]{:S(2)}) collective-permute-start(bf16[1,272,256]{2,1,0:T(8,128)(2,1)} %get-tuple-element.376), channel_id=1, source_target_pairs={{0,8},{4,12},{8,0},{12,4},{16,24},{20,28},{24,16},{28,20},{1,9},{5... | collective-permute-start | bytes 417800 | tf_op jit(solution)/shard_map/ppermute | solution.py:1019
  206.6 13.0 %collective-permute-start.35 = (bf16[1,272,256]{2,1,0:T(8,128)(2,1)}, bf16[1,272,256]{2,1,0:T(8,128)(2,1)S(1)}, u32[]{:S(2)}, u32[]{:S(2)}) collective-permute-start(bf16[1,272,256]{2,1,0:T(8,128)(2,1)} %get-tuple-element.377), channel_id=1, source_target_pairs={{0,16},{4,20},{8,24},{12,28},{16,0},{20,4},{24,8},{28,12},{1,17},{... | collective-permute-start | bytes 417800 | tf_op jit(solution)/shard_map/ppermute | solution.py:1019
  209.0 10.8 %collective-permute-start.36 = (bf16[1,272,256]{2,1,0:T(8,128)(2,1)S(1)}, bf16[1,272,256]{2,1,0:T(8,128)(2,1)S(1)}, u32[]{:S(2)}, u32[]{:S(2)}) collective-permute-start(bf16[1,272,256]{2,1,0:T(8,128)(2,1)S(1)} %get-tuple-element.378), channel_id=1, source_target_pairs={{0,24},{4,28},{8,16},{12,20},{16,8},{20,12},{24,0},{28,4},{1,25},{... | collective-permute-start | bytes 417800 | tf_op jit(solution)/shard_map/ppermute | solution.py:1019
  209.3 11.7 %collective-permute-start.38 = (bf16[2,192,256]{2,1,0:T(8,128)(2,1)S(1)}, bf16[2,192,256]{2,1,0:T(8,128)(2,1)S(1)}, u32[]{:S(2)}, u32[]{:S(2)}) collective-permute-start(bf16[2,192,256]{2,1,0:T(8,128)(2,1)S(1)} %add_convert_fusion.11), channel_id=1, source_target_pairs={{0,8},{4,12},{8,0},{12,4},{16,24},{20,28},{24,16},{28,20},{1,9},{5... | collective-permute-start | bytes 589832 | tf_op jit(solution)/shard_map/ppermute | solution.py:1019
  216.0 19.2 %collective-permute-start.39 = (bf16[2,192,256]{2,1,0:T(8,128)(2,1)S(1)}, bf16[2,192,256]{2,1,0:T(8,128)(2,1)S(1)}, u32[]{:S(2)}, u32[]{:S(2)}) collective-permute-start(bf16[2,192,256]{2,1,0:T(8,128)(2,1)S(1)} %add_convert_fusion.11), channel_id=1, source_target_pairs={{0,16},{4,20},{8,24},{12,28},{16,0},{20,4},{24,8},{28,12},{1,17},{... | collective-permute-start | bytes 589832 | tf_op jit(solution)/shard_map/ppermute | solution.py:1019
  219.4 15.9 %collective-permute-start.40 = (bf16[2,192,256]{2,1,0:T(8,128)(2,1)S(1)}, bf16[2,192,256]{2,1,0:T(8,128)(2,1)S(1)}, u32[]{:S(2)}, u32[]{:S(2)}) collective-permute-start(bf16[2,192,256]{2,1,0:T(8,128)(2,1)S(1)} %add_convert_fusion.11), channel_id=1, source_target_pairs={{0,24},{4,28},{8,16},{12,20},{16,8},{20,12},{24,0},{28,4},{1,25},{... | collective-permute-start | bytes 589832 | tf_op jit(solution)/shard_map/ppermute | solution.py:1019
  219.8 15.6 %collective-permute-start.41 = (bf16[2,2,4,24,256]{4,3,2,1,0:T(8,128)(2,1)}, bf16[2,2,4,24,256]{4,3,2,1,0:T(8,128)(2,1)S(1)}, u32[]{:S(2)}, u32[]{:S(2)}) collective-permute-start(bf16[2,2,4,24,256]{4,3,2,1,0:T(8,128)(2,1)} %bitcast.124), channel_id=1, source_target_pairs={{0,1},{1,0},{2,3},{3,2},{4,5},{5,4},{6,7},{7,6},{8,9},{9,8},{10,11... | collective-permute-start | bytes 589832 | tf_op jit(solution)/shard_map/ppermute | solution.py:1019
  235.4 4.7 %collective-permute-start.42 = (bf16[2,4,24,256]{3,2,1,0:T(8,128)(2,1)S(1)}, bf16[2,4,24,256]{3,2,1,0:T(8,128)(2,1)S(1)}, u32[]{:S(2)}, u32[]{:S(2)}) collective-permute-start(bf16[2,4,24,256]{3,2,1,0:T(8,128)(2,1)S(1)} %get-tuple-element.400), channel_id=1, source_target_pairs={{0,2},{1,3},{2,0},{3,1},{4,6},{5,7},{6,4},{7,5},{8,10},{9,11},{10,... | collective-permute-start | bytes 294920 | tf_op jit(solution)/shard_map/ppermute | solution.py:1019
  241.0 21.2 %all-to-all-start.2 = ((bf16[8,96,256]{2,1,0:T(8,128)(2,1)}), bf16[8,96,256]{2,1,0:T(8,128)(2,1)S(1)}, u32[]{:S(2)}, u32[]{:S(2)}) async-start(bf16[8,96,256]{2,1,0:T(8,128)(2,1)} %pad_maximum_fusion.4), calls=%async_computation.2 | async-start | bytes 786432 | tf_op jit(solution)/shard_map/all_to_all | solution.py:1279
  246.8 23.1 %collective-permute-start.43 = (bf16[1,272,256]{2,1,0:T(8,128)(2,1)S(1)}, bf16[1,272,256]{2,1,0:T(8,128)(2,1)S(1)}, u32[]{:S(2)}, u32[]{:S(2)}) collective-permute-start(bf16[1,272,256]{2,1,0:T(8,128)(2,1)S(1)} %add_convert_fusion.12), channel_id=1, source_target_pairs={{0,8},{4,12},{8,0},{12,4},{16,24},{20,28},{24,16},{28,20},{1,9},{5... | collective-permute-start | bytes 417800 | tf_op jit(solution)/shard_map/ppermute | solution.py:1019
  248.8 21.1 %collective-permute-start.44 = (bf16[1,272,256]{2,1,0:T(8,128)(2,1)S(1)}, bf16[1,272,256]{2,1,0:T(8,128)(2,1)S(1)}, u32[]{:S(2)}, u32[]{:S(2)}) collective-permute-start(bf16[1,272,256]{2,1,0:T(8,128)(2,1)S(1)} %add_convert_fusion.12), channel_id=1, source_target_pairs={{0,16},{4,20},{8,24},{12,28},{16,0},{20,4},{24,8},{28,12},{1,17},{... | collective-permute-start | bytes 417800 | tf_op jit(solution)/shard_map/ppermute | solution.py:1019
  251.2 18.7 %collective-permute-start.45 = (bf16[1,272,256]{2,1,0:T(8,128)(2,1)S(1)}, bf16[1,272,256]{2,1,0:T(8,128)(2,1)S(1)}, u32[]{:S(2)}, u32[]{:S(2)}) collective-permute-start(bf16[1,272,256]{2,1,0:T(8,128)(2,1)S(1)} %add_convert_fusion.12), channel_id=1, source_target_pairs={{0,24},{4,28},{8,16},{12,20},{16,8},{20,12},{24,0},{28,4},{1,25},{... | collective-permute-start | bytes 417800 | tf_op jit(solution)/shard_map/ppermute | solution.py:1019
  251.2 22.6 %collective-permute-start.46 = (bf16[4,2,192,256]{3,2,1,0:T(8,128)(2,1)S(1)}, bf16[4,2,192,256]{3,2,1,0:T(8,128)(2,1)S(1)}, u32[]{:S(2)}, u32[]{:S(2)}) collective-permute-start(bf16[4,2,192,256]{3,2,1,0:T(8,128)(2,1)S(1)} %pad_maximum_fusion.early_own), channel_id=1, source_target_pairs={{0,4},{4,0},{8,12},{12,8},{16,20},{20,16},{24,28},{28,24},{1,5},{5... | collective-permute-start | bytes 2359304 | tf_op jit(solution)/shard_map/ppermute | solution.py:1019
  263.0 22.7 %all-to-all-start.3 = ((bf16[8,96,256]{2,1,0:T(8,128)(2,1)}), bf16[8,96,256]{2,1,0:T(8,128)(2,1)S(1)}, u32[]{:S(2)}, u32[]{:S(2)}) async-start(bf16[8,96,256]{2,1,0:T(8,128)(2,1)} %broadcast_in_dim.3), calls=%async_computation.3 | async-start | bytes 786432 | tf_op jit(solution)/shard_map/all_to_all | solution.py:1283
  270.0 15.7 %collective-permute-start.47 = (bf16[4,1,272,256]{3,2,1,0:T(8,128)(2,1)S(1)}, bf16[4,1,272,256]{3,2,1,0:T(8,128)(2,1)S(1)}, u32[]{:S(2)}, u32[]{:S(2)}) collective-permute-start(bf16[4,1,272,256]{3,2,1,0:T(8,128)(2,1)S(1)} %pad_maximum_fusion.1.last_own), channel_id=1, source_target_pairs={{0,4},{4,0},{8,12},{12,8},{16,20},{20,16},{24,28},{28,24},{1,5},{5... | collective-permute-start | bytes 1671176 | tf_op jit(solution)/shard_map/ppermute | solution.py:1019
  (37 other events, 238.9 us)

commit v6 on v5

--- a/solution.py
+++ b/solution.py
@@ -118,24 +118,18 @@
 
     def run(index, carried):
         here = pl.ds(pl.multiple_of(index * STEP, STEP), STEP)
-        seq = index // per_seq
-        there = pl.multiple_of(seq * tall + (index - seq * per_seq) * STEP, DOC_ROWS)
         normed, unused = normalize(tokens[here, :].astype(F32))
-        scaled = (normed * gain[...]).astype(BF16)
-        scaled_out[here, :] = scaled
-        shared = dot_nn(scaled, weight[...]).astype(BF16)
-
-        def put(c, carried):
-            shared_out[c, pl.ds(there, STEP), :] = shared
-            return carried
-
-        return lax.fori_loop(0, places, put, carried)
+        scaled_out[here, :] = (normed * gain[...]).astype(BF16)
+        return carried
 
     lax.fori_loop(0, seqs * per_seq, run, 0)
+    shared = dot_nn(scaled_out[...], weight[...]).astype(BF16)
 
     def put(c, carried):
         for seq in range(seqs):
-            begin = seq * tall + rows
+            begin = seq * tall
+            shared_out[c, begin : begin + rows, :] = shared[seq * rows : (seq + 1) * rows, :]
+            begin = begin + rows
             shared_out[c, begin : begin + DOC_ROWS, :] = jnp.zeros((DOC_ROWS, LANES), BF16)
             shared_out[c, begin : begin + doc_lines, :] = documents[seq]
         return carried
@@ -620,13 +614,13 @@
         if first:
 
             def begin(here):
-                mixed = dot_nn(use["attended"][here, :], use["mixing_all"][...])
-                values = use["tokens"][here, :].astype(F32) + mixed
+                values = use["tokens"][here, :].astype(F32) + hidden[here, :]
                 hidden[here, :] = values
                 normed, unused = normalize(values)
                 scaled[here, :] = (normed * use["gain"][...]).astype(BF16)
 
             place_rows(spot, [use[f"mixing{r}"] for r in range(pieces)], use["mixing_all"])
+            hidden[...] = dot_nn(use["attended"][...], use["mixing_all"][...])
             over_rows(rows, begin)
             for one in beside("out", ("hidden", "scaled")):
                 one.start()
@@ -727,13 +721,10 @@
                     grad * use["gain"][...], normed, inverse
                 )
                 use["grad_hidden"][here, :] = grad_hidden
-                rounded = grad_hidden.astype(BF16)
-                grad_mixed[here, :] = rounded
-                use["grad_attended"][here, :] = dot_nt(rounded, use["mixing_all"][...]).astype(
-                    BF16
-                )
+                grad_mixed[here, :] = grad_hidden.astype(BF16)
 
             over_rows(rows, end)
+            use["grad_attended"][...] = dot_nt(grad_mixed[...], use["mixing_all"][...]).astype(BF16)
             term[...] = dot_tn(use["attended"][...], grad_mixed[...])
             tall = 2 * width
             messages = messages_of(part[-1])
@@ -935,84 +926,131 @@
     )(spot, tokens, gain, scaled, arrived, grad_scaled, grad_hidden, *weights)
 
 
+def put_halves(whole, own, other, at, place, first):
+    deep, unused, rows, unused = own.shape
+    low = place & 1
+    for half, x in ((own, low), (other, 1 - low)):
+        for k in range(deep):
+            begin = pl.multiple_of((x * deep + (first ^ k)) * rows, 8)
+            whole[pl.ds(begin, rows), :] = half[k, at].astype(F32)
+
+
+def early_kernel(place_ref, own, other, down_out, up_out, whole, *, chunks, pieces):
+    width = down_out.shape[1]
+    height = width // pieces
+    place = place_ref[0]
+    for chunk in range(own.shape[1]):
+        put_halves(whole, own, other, chunk, place, place >> 1)
+        for g in range(width // TILE):
+            down_out[chunk * TILE : (chunk + 1) * TILE, g * TILE : (g + 1) * TILE] = whole[
+                g * TILE : (g + 1) * TILE, :
+            ]
+        for j in range(pieces):
+            row, column = width + j * height, (j * chunks + chunk) * TILE
+            up_out[:, column : column + TILE] = whole[row : row + height, :]
+
+
+def early_stage(place, own, other, chunks, pieces, width):
+    shape = lambda *dims: jax.ShapeDtypeStruct(dims, F32)
+    vmem = pl.BlockSpec(memory_space=pltpu.VMEM)
+    return pl.pallas_call(
+        functools.partial(early_kernel, chunks=chunks, pieces=pieces),
+        grid_spec=pltpu.PrefetchScalarGridSpec(
+            num_scalar_prefetch=1,
+            grid=(),
+            in_specs=[vmem] * 2,
+            out_specs=[vmem] * 2,
+            scratch_shapes=[pltpu.VMEM((2 * width, TILE), F32)],
+        ),
+        out_shape=[shape(chunks * TILE, width), shape(width // pieces, pieces * chunks * TILE)],
+        compiler_params=params(),
+        cost_estimate=weight(),
+        name="early_sums",
+    )(place, own, other)
+
+
 def final_kernel(
-    place_ref, early_own, early_other, last_own, last_other, late,
-    down_out, up_out, mixing_out, query_out, shared_out, gains_out, whole,
-    *, chunks, pieces, width, query_rows,
+    place_ref, own, other, late, down_in, up_in,
+    down_out, up_out, mixing_out, query_out, shared_out, gains_out,
+    whole, down_part, up_part, sems,
+    *, chunks, pieces, query_rows,
 ):
-    height = width // pieces
+    height, width = mixing_out.shape
     groups = width // TILE
-    places, deep = late.shape[0], last_own.shape[0]
-    low, high = place_ref[0] & 1, place_ref[0] >> 1
-
-    def columns(out, first_row, rows, out_row, across):
-        for g in range(across):
+    place = place_ref[0]
+
+    def columns(out, first_row, rows):
+        for g in range(groups):
             row = first_row + g * rows
-            out[out_row : out_row + rows, g * TILE : (g + 1) * TILE] = whole[row : row + rows, :]
-
-    def put_chunk(chunk):
-        columns(down_out, 0, TILE, chunk * TILE, groups)
-        for j in range(pieces):
-            row = width + j * height
-            column = (j * chunks + chunk) * TILE
-            up_out[:, column : column + TILE] = whole[row : row + height, :]
-
-    def load(source, begin, rows):
-        for c in range(places):
-            whole[c * rows : (c + 1) * rows, :] = source[c, begin : begin + rows, :].astype(F32)
-
-    def load_halves(own, other, at):
-        rows = own.shape[2]
-        for half, x in ((own, low), (other, 1 - low)):
-            for k in range(deep):
-                begin = pl.multiple_of((x * deep + (high ^ k)) * rows, 8)
-                whole[pl.ds(begin, rows), :] = half[k, at].astype(F32)
-
-    for chunk in range(chunks - 1):
-        load_halves(early_own, early_other, chunk)
-        put_chunk(chunk)
-    load_halves(last_own, last_other, 0)
-    put_chunk(chunks - 1)
-    columns(mixing_out, 2 * width, height, 0, groups)
+            out[:, g * TILE : (g + 1) * TILE] = whole[row : row + rows, :]
+
+    def load(begin, rows):
+        for c in range(late.shape[0]):
+            whole[c * rows : (c + 1) * rows, :] = late[c, begin : begin + rows, :].astype(F32)
+
+    put_halves(whole, own, other, 0, place, place >> 1)
+    columns(down_part, 0, TILE)
+    copies = [
+        pltpu.make_async_copy(
+            down_part, down_out.at[pl.ds((chunks - 1) * TILE, TILE), :], sems.at[pieces]
+        )
+    ]
+    for j in range(pieces):
+        up_part[j] = whole[width + j * height : width + (j + 1) * height, :]
+        column = (j * chunks + chunks - 1) * TILE
+        copies.append(
+            pltpu.make_async_copy(up_part.at[j], up_out.at[:, pl.ds(column, TILE)], sems.at[j])
+        )
+    for one in copies:
+        one.start()
+    columns(mixing_out, 2 * width, height)
     row = 2 * width + groups * height
     for i in range(width // LANES):
         gains_out[1:2, i * LANES : (i + 1) * LANES] = whole[row + i : row + i + 1, 0:LANES]
-    load(late, 0, query_rows)
-    columns(query_out, 0, height, 0, groups)
-    load(late, query_rows, late.shape[1] - query_rows)
+    load(0, query_rows)
+    columns(query_out, 0, height)
+    load(query_rows, late.shape[1] - query_rows)
     shared_out[...] = whole[0:height, 0:LANES]
     for i in range(width // LANES):
         gains_out[0:1, i * LANES : (i + 1) * LANES] = whole[i : i + 1, LANES:]
-
-
-def final_stage(place, halves, late, query_rows, chunks, pieces, width):
+    for one in copies:
+        one.wait()
+
+
+def final_stage(place, own, other, late, down, up, query_rows, chunks, pieces, width):
     height = width // pieces
     shape = lambda *dims: jax.ShapeDtypeStruct(dims, F32)
-    tallest = max(2 * one.shape[0] * one.shape[2] for one in halves)
-    tallest = max(tallest, late.shape[0] * late.shape[1])
+    tallest = max(2 * own.shape[0] * own.shape[2], late.shape[0] * late.shape[1])
+    vmem, anywhere = pl.BlockSpec(memory_space=pltpu.VMEM), pl.BlockSpec(memory_space=pl.ANY)
     return pl.pallas_call(
         functools.partial(
-            final_kernel, chunks=chunks, pieces=pieces, width=width, query_rows=query_rows
+            final_kernel, chunks=chunks, pieces=pieces, query_rows=query_rows
         ),
         grid_spec=pltpu.PrefetchScalarGridSpec(
             num_scalar_prefetch=1,
             grid=(),
-            in_specs=[pl.BlockSpec(memory_space=pltpu.VMEM)] * 5,
-            out_specs=[pl.BlockSpec(memory_space=pltpu.VMEM)] * 6,
-            scratch_shapes=[pltpu.VMEM((tallest, TILE), F32)],
+            in_specs=[vmem] * 3 + [anywhere] * 2,
+            out_specs=[anywhere] * 2 + [vmem] * 4,
+            scratch_shapes=[
+                pltpu.VMEM((tallest, TILE), F32),
+                pltpu.VMEM((TILE, width), F32),
+                pltpu.VMEM((pieces, height, TILE), F32),
+                pltpu.SemaphoreType.DMA((pieces + 1,)),
+            ],
         ),
         out_shape=[
-            shape(chunks * TILE, width),
-            shape(height, pieces * chunks * TILE),
+            shape(*down.shape),
+            shape(*up.shape),
             shape(height, width),
             shape(height, width),
             shape(height, LANES),
             shape(2, width),
         ],
+        input_output_aliases={4: 0, 5: 1},
         compiler_params=params(),
         cost_estimate=weight(),
         name="final",
-    )(place, *halves, late)
+    )(place, own, other, late, down, up)
 
 
 def swap(values, axis, size, mask):
@@ -1071,7 +1109,7 @@
             self.add(lambda v: v[1][..., begin:end, :]).astype(BF16)
             for begin, end in zip(edges, edges[1:])
         ]
-        self.held = self.add(lambda v: v[0])
+        self.held = self.add(lambda v: v[0]).astype(BF16)
         self.sent = [self.later.pop(0)]
         self.routes = [("wt", self.wt_size, 2)]
 
@@ -1082,8 +1120,8 @@
         self.coming = [jnp.concatenate(self.before + self.coming, axis=-2)]
 
     def x(self):
-        half = lambda x: self.add(lambda v: lax.dynamic_index_in_dim(v, x, 0, False))
-        self.held, self.sent = half(self.low), [half(1 - self.low).astype(BF16)]
+        half = lambda x: self.add(lambda v: lax.dynamic_index_in_dim(v, x, 0, False)).astype(BF16)
+        self.held, self.sent = half(self.low), [half(1 - self.low)]
         self.routes = [("ctx", self.ctx_size, 1)]
 
     def far(self):
@@ -1092,9 +1130,9 @@
     def z(self, *others):
         def part(k):
             pick = lambda v: lax.dynamic_index_in_dim(v, self.high ^ k, 0, False)
-            return jnp.stack([one.add(pick) for one in (self, *others)])
-
-        self.sent = [part(k).astype(BF16) for k in range(1, self.groups)]
+            return jnp.stack([one.add(pick) for one in (self, *others)]).astype(BF16)
+
+        self.sent = [part(k) for k in range(1, self.groups)]
         self.held = part(0)
         self.routes = self.far()
 
@@ -1269,11 +1307,11 @@
     input_grad = tie(input_grad, zero, two, shared, query, came=[two, query])
     two.z_back()
     input_grad = tie(input_grad, two)
-    zero.x_back()
-    input_grad = tie(input_grad, zero)
     input_grad = tie(input_grad, shared, query, came=[shared])
     shared.y()
     input_grad = tie(input_grad, shared)
+    zero.x_back()
+    input_grad = tie(input_grad, zero)
     input_grad = tie(input_grad, shared, query, came=[shared])
     late = jnp.concatenate([query.everywhere(), shared.everywhere()], axis=1)
     late = lax.all_to_all(late, "ctx", 0, 0)
@@ -1281,16 +1319,23 @@
     input_grad = tie(input_grad, two)
     late = jnp.sum(late.astype(F32), axis=0).astype(BF16)
     late = lax.all_to_all(jnp.broadcast_to(late, (ctx_size,) + late.shape), "ctx", 0, 0)
+    two.launch()
+    down_grad, up_grad = early_stage(
+        place_one, zero.held, zero.coming[0], chunks, wt_size, width
+    )
+    down_grad, up_grad, two.coming = lax.optimization_barrier((down_grad, up_grad, two.coming))
     down_grad, up_grad, mixing_grad, query_grad, shared_grad, gain_grads = final_stage(
         place_one,
-        [zero.held, zero.coming[0], two.held, two.coming[0]],
+        two.held,
+        two.coming[0],
         late,
+        down_grad,
+        up_grad,
         query.rows // ctx_size,
         chunks,
         wt_size,
         width,
     )
-
     gain_grads = lax.dynamic_slice_in_dim(gain_grads, spot_index * height, height, 1)
     return (
         arrays["layer_out"].reshape(seqs, rows, width),

time: 298 us -> 292 us (0.980)
  waiting for transfers between devices: 108 us -> 103 us
    ppermute x48, waiting for transfers between devices: 99.3 us -> 94.7 us  [swap(): return lax.ppermute(values, axis, [(i, i ^ mask) for i in range(size)])]
    all_to_all x1, starting transfers between devices: 4.74 us -> 9.22 us  [body(): lax.all_to_all(arriving, 'ctx', 0, 0, axis_index_groups=[list(range(x, ct...]
    pallas_call x0 -> x1, Pallas kernels: none -> 3.91 us  [early_stage(): pl.pallas_call(functools.partial(early_kernel, chunks=chunks, pieces=piec...]
    unnamed x67 -> x65, local copies, waits for them, and re-layouts: 6 us -> 7.94 us
  transfers between devices with their start and end apart: 52 -> 52, of which waited for: 22 -> 18; matrix products, arithmetic and copies ran while one was open for 5% -> 5% of each run, Pallas kernels for 28% -> 29%
where the time goes in v6:
time: 292 us; the launch traced here: 290 us
  waiting for transfers between devices  103 us (35%)
  Pallas kernels  88.6 us (30%)
  starting transfers between devices  69.3 us (24%)
  other arithmetic  15.5 us (5%)
  local copies, waits for them, and re-layouts  13 us (4%)
    ppermute x48, waiting for transfers between devices, swap(): return lax.ppermute(values, axis, [(i, i ^ mask) for i in range(size)])  94.7 us
    ppermute x48, starting transfers between devices, swap(): return lax.ppermute(values, axis, [(i, i ^ mask) for i in range(size)])  42.3 us
    pallas_call x2, Pallas kernels, feed_stage(): pl.pallas_call(functools.partial(feed_kernel, pieces=pieces, part=part, f...  38.5 us
    pallas_call x2, Pallas kernels, attend_back(): pl.pallas_call(functools.partial(attend_back_kernel, seq=seq, blocks=bloc...  13.2 us
    all_to_all x1, starting transfers between devices, body(): lax.all_to_all(arriving, 'ctx', 0, 0, axis_index_groups=[list(range(x, ct...  9.22 us
    pallas_call x1, Pallas kernels, attend(): pl.pallas_call(functools.partial(attend_kernel, blocks=blocks, tile_rows=...  8.37 us
    all_to_all x1, waiting for transfers between devices, body(): late = lax.all_to_all(late, 'ctx', 0, 0)  8.2 us
    unnamed x65, local copies, waits for them, and re-layouts  7.94 us
  transfers between devices with their start and end apart: 52, of which 18 were waited for; matrix products, arithmetic and copies ran while one was open for 5% of the time, Pallas kernels for 29%

profile of v6, /device:TPU:0, one launch (start us, length us, event | category | flops | bytes accessed | tf_op | source)
XLA Modules:
  0.0 290.4 jit_solution(7247031040499713794)
XLA Ops:
  2.1 3.0 %collective-permute-start.1 = (bf16[208,128]{1,0:T(8,128)(2,1)S(1)}, bf16[208,128]{1,0:T(8,128)(2,1)S(1)}, u32[]{:S(2)}, u32[]{:S(2)}) collective-permute-start(bf16[208,128]{1,0:T(8,128)(2,1)S(1)} %fusion.21.rest_0_), channel_id=1, source_target_pairs={{0,2},{1,3},{2,0},{3,1},{4,6},{5,7},{6,4},{7,5},{8,10},{9,11},{10,... | collective-permute-start | bytes 159752 | tf_op jit(solution)/shard_map/ppermute | solution.py:1057
  5.3 2.0 collective-permute-done.1.rest_2_
  9.5 3.9 %first_norm.1 = (bf16[512,768]{1,0:T(8,128)(2,1)}, bf16[8,544,128]{2,1,0:T(8,128)(2,1)}) custom-call(s32[1]{0:T(128)} %bitcast.spot_ref, bf16[512,768]{1,0:T(8,128)(2,1)} %bitcast.87, f32[1,768]{1,0:T(1,128)} %reshape_squeeze.6.gain, bf16[2,2,128]{2,1,0:T(2,128)(2,1)} %reshape.183.documents, bf16[208,128]{1,0:T(8,128)(2,1)} %copy-done.25, ...), custom_call_target="tpu_custom_call" | custom-call | flops 1 | bytes 1 | tf_op jit(solution)/shard_map/first_norm/pallas_call | solution.py:144
  13.4 1.4 collective-permute-done.3.rest_2_.rest_4_
  14.8 5.8 %all-to-all-start = ((bf16[8,544,128]{2,1,0:T(8,128)(2,1)}), bf16[8,544,128]{2,1,0:T(8,128)(2,1)S(1)}, u32[]{:S(2)}, u32[]{:S(2)}) async-start(bf16[8,544,128]{2,1,0:T(8,128)(2,1)} %get-tuple-element.221), calls=%async_computation | async-start | bytes 2228224 | tf_op jit(solution)/shard_map/all_to_all | solution.py:1219
  20.6 3.2 %pack.1 = (bf16[1536,256]{1,0:T(8,128)(2,1)}, bf16[1536,256]{1,0:T(8,128)(2,1)}, bf16[1536,256]{1,0:T(8,128)(2,1)}) custom-call(bf16[192,3072]{1,0:T(8,128)(2,1)} %up, bf16[768,768]{1,0:T(8,128)(2,1)} %down), custom_call_target="tpu_custom_call" | custom-call | flops 1 | bytes 1 | tf_op jit(solution)/shard_map/pack/pallas_call | solution.py:95
  27.4 3.3 %project.1 = bf16[512,768]{1,0:T(8,128)(2,1)} custom-call(s32[1]{0:T(128)} %bitcast.spot_ref, bf16[512,768]{1,0:T(8,128)(2,1)} %get-tuple-element.226.operand.scaled, bf16[192,768]{1,0:T(8,128)(2,1)} %rest_2_.1, bf16[192,768]{1,0:T(8,128)(2,1)} %copy-done.12, bf16[192,768]{1,0:T(8,128)(2,1)} %copy-done.11, bf16[192,768]{1,0:T(8,128)(2,1)} %copy-done.13), custom_call_target="tpu_custom_call" | custom-call | flops 1 | bytes 1 | tf_op jit(solution)/shard_map/project/pallas_call | solution.py:173
  30.7 18.5 %collective-permute-done.5.refs_11_.refs_7_ = bf16[192,768]{1,0:T(8,128)(2,1)S(1)} collective-permute-done((bf16[192,768]{1,0:T(8,128)(2,1)S(1)}, bf16[192,768]{1,0:T(8,128)(2,1)S(1)}, u32[]{:S(2)}, u32[]{:S(2)}) %collective-permute-start.5) | collective-permute-done | bytes 294944 | tf_op jit(solution)/shard_map/ppermute | solution.py:1057
  49.2 1.7 collective-permute-start.8
  51.9 8.4 %attend.1 = (s32[2,256,128]{2,1,0:T(8,128)}, f32[2,256,768]{2,1,0:T(8,128)}, bf16[2,256,768]{2,1,0:T(8,128)(2,1)}, f32[2,256,768]{2,1,0:T(8,128)}) custom-call(s32[1]{0:T(128)} %bitcast.1.place_ref, bf16[2,256,768]{2,1,0:T(8,128)(2,1)} %bitcast.84, bf16[8,2,272,128]{3,2,1,0:T(8,128)(2,1)} %bitcast.81), custom_call_target="tpu_custom_call" | custom-call | flops 1 | bytes 1 | tf_op jit(solution)/shard_map/attend/pallas_call | solution.py:450
  60.3 8.0 %collective-permute-done.8.refs_7_ = bf16[1536,256]{1,0:T(8,128)(2,1)} collective-permute-done((bf16[1536,256]{1,0:T(8,128)(2,1)}, bf16[1536,256]{1,0:T(8,128)(2,1)}, u32[]{:S(2)}, u32[]{:S(2)}) %collective-permute-start.8) | collective-permute-done | bytes 786464 | tf_op jit(solution)/shard_map/ppermute | solution.py:1057
  68.4 1.8 collective-permute-start.15
  72.7 21.6 %feed0.1 = (bf16[2,1536,256]{2,1,0:T(8,128)(2,1)}, bf16[2,1536,256]{2,1,0:T(8,128)(2,1)}, bf16[2,2,768,256]{3,2,1,0:T(8,128)(2,1)}, bf16[2,2,768,256]{3,2,1,0:T(...) custom-call(s32[1]{0:T(128)} %bitcast.spot_ref, ...), custom_call_target="tpu_custom_call" | custom-call | flops 1 | bytes 1 | tf_op jit(solution)/shard_map/feed0/pallas_call | solution.py:804
  96.3 2.6 collective-permute-done.16
  98.9 2.7 fusion.2
  102.1 1.5 collective-permute-start.21
  106.4 16.9 %feed2.1 = (bf16[2,2176,256]{2,1,0:T(8,128)(2,1)}, bf16[2,2176,256]{2,1,0:T(8,128)(2,1)}, bf16[512,768]{1,0:T(8,128)(2,1)}, f32[512,768]{1,0:T(8,128)}, bf16[512,768]{1,0:T(8,128)(2,1)}) custom-call(s32[1]{0:T(128)} %bitcast.spot_ref, bf16[512,768]{1,0:T(8,128)(2,1)} %bitcast.91, bf16[1536,256]{1,0:T(8,128)(2,1)} %get-tuple-element.247.refs_1_, ...), custom_call_target="tpu_custom_call" | custom-call | flops 1 | bytes 1 | tf_op jit(solution)/shard_map/feed2/pallas_call | solution.py:804
  125.6 2.4 collective-permute-done.22
  132.0 6.5 %attend_back.2 = (bf16[1,256,768]{2,1,0:T(8,128)(2,1)}, bf16[4,256,128]{2,1,0:T(8,128)(2,1)}, bf16[4,256,128]{2,1,0:T(8,128)(2,1)}) custom-call(s32[1]{0:T(128)} %bitcast.1.place_ref, bf16[2,256,768]{2,1,0:T(8,128)(2,1)} %bitcast.85, s32[2,256,128]{2,1,0:T(8,128)} %get-tuple-element.288.starts, f32[2,256,768]{2,1,0:T(8,128)} %get-tuple-element.289.exact, ...), custom_call_target="tpu_custom_call" | custom-call | flops 1 | bytes 1 | tf_op jit(solution)/shard_map/attend_back/pallas_call | solution.py:493
  138.7 2.9 collective-permute-done.23
  141.6 9.1 %collective-permute-done.24 = bf16[4,192,256]{2,1,0:T(8,128)(2,1)} collective-permute-done((bf16[4,192,256]{2,1,0:T(8,128)(2,1)}, bf16[4,192,256]{2,1,0:T(8,128)(2,1)}, u32[]{:S(2)}, u32[]{:S(2)}) %collective-permute-start.24) | collective-permute-done | bytes 393248 | tf_op jit(solution)/shard_map/ppermute | solution.py:1057
  151.8 1.2 add_convert_fusion.27
  154.8 1.4 collective-permute-start.26
  156.2 3.5 %collective-permute-start.27 = (bf16[2,192,256]{2,1,0:T(8,128)(2,1)S(1)}, bf16[2,192,256]{2,1,0:T(8,128)(2,1)S(1)}, u32[]{:S(2)}, u32[]{:S(2)}) collective-permute-start(bf16[2,192,256]{2,1,0:T(8,128)(2,1)S(1)} %pad_maximum_fusion.6), channel_id=1, source_target_pairs={{0,16},{4,20},{8,24},{12,28},{16,0},{20,4},{24,8},{28,12},{1,17},{... | collective-permute-start | bytes 589832 | tf_op jit(solution)/shard_map/ppermute | solution.py:1057
  159.7 6.7 %attend_back.3 = (bf16[1,256,768]{2,1,0:T(8,128)(2,1)}, bf16[4,256,128]{2,1,0:T(8,128)(2,1)}, bf16[4,256,128]{2,1,0:T(8,128)(2,1)}) custom-call(s32[1]{0:T(128)} %bitcast.1.place_ref, bf16[2,256,768]{2,1,0:T(8,128)(2,1)} %bitcast.86, s32[2,256,128]{2,1,0:T(8,128)} %get-tuple-element.288.starts, f32[2,256,768]{2,1,0:T(8,128)} %get-tuple-element.289.exact, ...), custom_call_target="tpu_custom_call" | custom-call | flops 1 | bytes 1 | tf_op jit(solution)/shard_map/attend_back/pallas_call | solution.py:493
  167.5 6.3 %collective-permute-done.27 = bf16[2,192,256]{2,1,0:T(8,128)(2,1)S(1)} collective-permute-done((bf16[2,192,256]{2,1,0:T(8,128)(2,1)S(1)}, bf16[2,192,256]{2,1,0:T(8,128)(2,1)S(1)}, u32[]{:S(2)}, u32[]{:S(2)}) %collective-permute-start.27) | collective-permute-done | bytes 196640 | tf_op jit(solution)/shard_map/ppermute | solution.py:1057
  176.1 4.7 %query_grad.1 = (f32[512,768]{1,0:T(8,128)}, bf16[2,576,256]{2,1,0:T(8,128)(2,1)}, bf16[2,576,256]{2,1,0:T(8,128)(2,1)}) custom-call(s32[1]{0:T(128)} %bitcast.spot_ref, bf16[512,768]{1,0:T(8,128)(2,1)} %get-tuple-element.226.operand.scaled, bf16[256,768]{1,0:T(8,128)(2,1)} %bitcast.105, bf16[256,768]{1,0:T(8,128)(2,1)} %bitcast.106, ...), custom_call_target="tpu_custom_call" | custom-call | flops 1 | bytes 1 | tf_op jit(solution)/shard_map/query_grad/pallas_call | solution.py:851
  181.8 9.2 %all-to-all-start.1 = ((bf16[4,2,256,128]{3,2,1,0:T(8,128)(2,1)}), bf16[4,2,256,128]{3,2,1,0:T(8,128)(2,1)S(1)}, u32[]{:S(2)}, u32[]{:S(2)}) async-start(bf16[4,2,256,128]{3,2,1,0:T(8,128)(2,1)} %pad_maximum_fusion.2), calls=%async_computation.1 | async-start | bytes 1048576 | tf_op jit(solution)/shard_map/all_to_all | solution.py:1291
  192.6 13.4 %collective-permute-done.33 = bf16[4,272,256]{2,1,0:T(8,128)(2,1)S(1)} collective-permute-done((bf16[4,272,256]{2,1,0:T(8,128)(2,1)}, bf16[4,272,256]{2,1,0:T(8,128)(2,1)S(1)}, u32[]{:S(2)}, u32[]{:S(2)}) %collective-permute-start.33) | collective-permute-done | bytes 557088 | tf_op jit(solution)/shard_map/ppermute | solution.py:1057
  206.2 1.8 collective-permute-start.34
  208.0 2.4 collective-permute-start.35
  211.5 5.9 %last.1 = (f32[512,768]{1,0:T(8,128)}, bf16[2,192,256]{2,1,0:T(8,128)(2,1)}, bf16[2,192,256]{2,1,0:T(8,128)(2,1)}) custom-call(s32[1]{0:T(128)} %bitcast.spot_ref, bf16[512,768]{1,0:T(8,128)(2,1)} %bitcast.89, f32[1,768]{1,0:T(1,128)} %reshape_squeeze.6.gain, bf16[512,768]{1,0:T(8,128)(2,1)} %get-tuple-element.226.operand.scaled, ...), custom_call_target="tpu_custom_call" | custom-call | flops 1 | bytes 1 | tf_op jit(solution)/shard_map/last/pallas_call | solution.py:908
  217.4 3.3 %collective-permute-start.40 = (bf16[2,192,256]{2,1,0:T(8,128)(2,1)S(1)}, bf16[2,192,256]{2,1,0:T(8,128)(2,1)S(1)}, u32[]{:S(2)}, u32[]{:S(2)}) collective-permute-start(bf16[2,192,256]{2,1,0:T(8,128)(2,1)S(1)} %add_convert_fusion.18), channel_id=1, source_target_pairs={{0,16},{4,20},{8,24},{12,28},{16,0},{20,4},{24,8},{28,12},{1,17},{... | collective-permute-start | bytes 589832 | tf_op jit(solution)/shard_map/ppermute | solution.py:1057
  221.0 1.6 collective-permute-done.38
  223.7 12.7 %collective-permute-done.40 = bf16[2,192,256]{2,1,0:T(8,128)(2,1)S(1)} collective-permute-done((bf16[2,192,256]{2,1,0:T(8,128)(2,1)S(1)}, bf16[2,192,256]{2,1,0:T(8,128)(2,1)S(1)}, u32[]{:S(2)}, u32[]{:S(2)}) %collective-permute-start.40) | collective-permute-done | bytes 196640 | tf_op jit(solution)/shard_map/ppermute | solution.py:1057
  237.5 6.0 %all-to-all-start.2 = ((bf16[8,96,256]{2,1,0:T(8,128)(2,1)}), bf16[8,96,256]{2,1,0:T(8,128)(2,1)S(1)}, u32[]{:S(2)}, u32[]{:S(2)}) async-start(bf16[8,96,256]{2,1,0:T(8,128)(2,1)} %pad_maximum_fusion.3), calls=%async_computation.2 | async-start | bytes 786432 | tf_op jit(solution)/shard_map/all_to_all | solution.py:1317
  243.4 2.0 collective-permute-start.43
  245.5 2.4 collective-permute-start.44
  247.9 2.0 collective-permute-start.46
  249.9 8.2 %all-to-all-done.2 = bf16[8,96,256]{2,1,0:T(8,128)(2,1)S(1)} async-done(((bf16[8,96,256]{2,1,0:T(8,128)(2,1)}), bf16[8,96,256]{2,1,0:T(8,128)(2,1)S(1)}, u32[]{:S(2)}, u32[]{:S(2)}) %all-to-all-start.2) | async-done | bytes 393248 | tf_op jit(solution)/shard_map/all_to_all | solution.py:1317
  258.9 6.0 %all-to-all-start.3 = ((bf16[8,96,256]{2,1,0:T(8,128)(2,1)}), bf16[8,96,256]{2,1,0:T(8,128)(2,1)S(1)}, u32[]{:S(2)}, u32[]{:S(2)}) async-start(bf16[8,96,256]{2,1,0:T(8,128)(2,1)} %broadcast_in_dim.3), calls=%async_computation.3 | async-start | bytes 786432 | tf_op jit(solution)/shard_map/all_to_all | solution.py:1321
  264.9 2.5 collective-permute-done.44
  267.4 1.4 collective-permute-start.47
  268.8 2.8 collective-permute-done.46.other
  272.5 3.9 %early_sums.1 = (f32[768,768]{1,0:T(8,128)}, f32[192,3072]{1,0:T(8,128)}) custom-call(s32[1]{0:T(128)} %bitcast.1.place_ref, bf16[4,2,192,256]{3,2,1,0:T(8,128)(2,1)} %copy-done.1, bf16[4,2,192,256]{3,2,1,0:T(8,128)(2,1)} %copy-done.22), custom_call_target="tpu_custom_call" | custom-call | flops 1 | bytes 1 | tf_op jit(solution)/shard_map/early_sums/pallas_call | solution.py:956
  276.4 7.4 %collective-permute-done.47.other = bf16[4,1,272,256]{3,2,1,0:T(8,128)(2,1)S(1)} collective-permute-done((bf16[4,1,272,256]{3,2,1,0:T(8,128)(2,1)S(1)}, bf16[4,1,272,256]{3,2,1,0:T(8,128)(2,1)S(1)}, u32[]{:S(2)}, u32[]{:S(2)}) %collective-permute-start.47) | collective-permute-done | bytes 557088 | tf_op jit(solution)/shard_map/ppermute | solution.py:1057
  285.3 3.7 %final.1 = (f32[768,768]{1,0:T(8,128)}, f32[192,3072]{1,0:T(8,128)}, f32[192,768]{1,0:T(8,128)}, f32[192,768]{1,0:T(8,128)}, f32[192,128]{1,0:T(8,128)}, /*index=5*/f32[2,768]{1,0:T(2,128)}) custom-call(s32[1]{0:T(128)} %bitcast.1.place_ref, bf16[4,1,272,256]{3,2,1,0:T(8,128)(2,1)} %copy-done.2, ...), custom_call_target="tpu_custom_call", output_to_operand_aliasing={{0}: (4, {}), {1}: (5, {})} | custom-call | flops 1 | bytes 1 | tf_op jit(solution)/shard_map/final/pallas_call | solution.py:1025
  289.0 1.4 fusion.23
  (185 shorter events, 38.5 us)
Async XLA Ops:
  2.1 5.2 %collective-permute-start.1 = (bf16[208,128]{1,0:T(8,128)(2,1)S(1)}, bf16[208,128]{1,0:T(8,128)(2,1)S(1)}, u32[]{:S(2)}, u32[]{:S(2)}) collective-permute-start(bf16[208,128]{1,0:T(8,128)(2,1)S(1)} %fusion.21.rest_0_), channel_id=1, source_target_pairs={{0,2},{1,3},{2,0},{3,1},{4,6},{5,7},{6,4},{7,5},{8,10},{9,11},{10,... | collective-permute-start | bytes 159752 | tf_op jit(solution)/shard_map/ppermute | solution.py:1057
  5.2 3.5 %collective-permute-start = (bf16[208,128]{1,0:T(8,128)(2,1)S(1)}, bf16[208,128]{1,0:T(8,128)(2,1)S(1)}, u32[]{:S(2)}, u32[]{:S(2)}) collective-permute-start(bf16[208,128]{1,0:T(8,128)(2,1)S(1)} %fusion.21.rest_0_), channel_id=1, source_target_pairs={{0,1},{1,0},{2,3},{3,2},{4,5},{5,4},{6,7},{7,6},{8,9},{9,8},{10,11... | collective-permute-start | bytes 159752 | tf_op jit(solution)/shard_map/ppermute | solution.py:1057
  5.2 9.6 %collective-permute-start.3 = (bf16[192,768]{1,0:T(8,128)(2,1)}, bf16[192,768]{1,0:T(8,128)(2,1)S(1)}, u32[]{:S(2)}, u32[]{:S(2)}) collective-permute-start(bf16[192,768]{1,0:T(8,128)(2,1)} %rest_2_.1), channel_id=1, source_target_pairs={{0,2},{1,3},{2,0},{3,1},{4,6},{5,7},{6,4},{7,5},{8,10},{9,11},{10,... | collective-permute-start | bytes 884744 | tf_op jit(solution)/shard_map/ppermute | solution.py:1057
  14.8 34.4 %all-to-all-start = ((bf16[8,544,128]{2,1,0:T(8,128)(2,1)}), bf16[8,544,128]{2,1,0:T(8,128)(2,1)S(1)}, u32[]{:S(2)}, u32[]{:S(2)}) async-start(bf16[8,544,128]{2,1,0:T(8,128)(2,1)} %get-tuple-element.221), calls=%async_computation | async-start | bytes 2228224 | tf_op jit(solution)/shard_map/all_to_all | solution.py:1219
  23.8 25.4 %collective-permute-start.4 = (bf16[1536,256]{1,0:T(8,128)(2,1)}, bf16[1536,256]{1,0:T(8,128)(2,1)}, u32[]{:S(2)}, u32[]{:S(2)}) collective-permute-start(bf16[1536,256]{1,0:T(8,128)(2,1)} %get-tuple-element.224.refs_1_), channel_id=1, source_target_pairs={{0,2},{1,3},{2,0},{3,1},{4,6},{5,7},{6,4},{7,5},{8,10},{9,11},{10,... | collective-permute-start | bytes 2359304 | tf_op jit(solution)/shard_map/ppermute | solution.py:1057
  24.6 2.0 collective-permute-start.7
  25.1 24.1 %collective-permute-start.5 = (bf16[192,768]{1,0:T(8,128)(2,1)S(1)}, bf16[192,768]{1,0:T(8,128)(2,1)S(1)}, u32[]{:S(2)}, u32[]{:S(2)}) collective-permute-start(bf16[192,768]{1,0:T(8,128)(2,1)S(1)} %copy-done.9), channel_id=1, source_target_pairs={{0,2},{1,3},{2,0},{3,1},{4,6},{5,7},{6,4},{7,5},{8,10},{9,11},{10,... | collective-permute-start | bytes 884744 | tf_op jit(solution)/shard_map/ppermute | solution.py:1057
  49.2 19.1 %collective-permute-start.8 = (bf16[1536,256]{1,0:T(8,128)(2,1)}, bf16[1536,256]{1,0:T(8,128)(2,1)}, u32[]{:S(2)}, u32[]{:S(2)}) collective-permute-start(bf16[1536,256]{1,0:T(8,128)(2,1)} %get-tuple-element.233.refs_5_), channel_id=1, source_target_pairs={{0,2},{1,3},{2,0},{3,1},{4,6},{5,7},{6,4},{7,5},{8,10},{9,11},{10,... | collective-permute-start | bytes 2359304 | tf_op jit(solution)/shard_map/ppermute | solution.py:1057
  50.9 19.3 %collective-permute-start.9 = (bf16[1536,256]{1,0:T(8,128)(2,1)}, bf16[1536,256]{1,0:T(8,128)(2,1)}, u32[]{:S(2)}, u32[]{:S(2)}) collective-permute-start(bf16[1536,256]{1,0:T(8,128)(2,1)} %get-tuple-element.224.refs_1_), channel_id=1, source_target_pairs={{0,1},{1,0},{2,3},{3,2},{4,5},{5,4},{6,7},{7,6},{8,9},{9,8},{10,11... | collective-permute-start | bytes 2359304 | tf_op jit(solution)/shard_map/ppermute | solution.py:1057
  50.9 17.4 %collective-permute-start.13 = (bf16[192,768]{1,0:T(8,128)(2,1)S(1)}, bf16[192,768]{1,0:T(8,128)(2,1)S(1)}, u32[]{:S(2)}, u32[]{:S(2)}) collective-permute-start(bf16[192,768]{1,0:T(8,128)(2,1)S(1)} %copy-done.9), channel_id=1, source_target_pairs={{0,1},{1,0},{2,3},{3,2},{4,5},{5,4},{6,7},{7,6},{8,9},{9,8},{10,11... | collective-permute-start | bytes 884744 | tf_op jit(solution)/shard_map/ppermute | solution.py:1057
  51.4 20.3 %collective-permute-start.11 = (bf16[1536,256]{1,0:T(8,128)(2,1)}, bf16[1536,256]{1,0:T(8,128)(2,1)}, u32[]{:S(2)}, u32[]{:S(2)}) collective-permute-start(bf16[1536,256]{1,0:T(8,128)(2,1)} %get-tuple-element.233.refs_5_), channel_id=1, source_target_pairs={{0,1},{1,0},{2,3},{3,2},{4,5},{5,4},{6,7},{7,6},{8,9},{9,8},{10,11... | collective-permute-start | bytes 2359304 | tf_op jit(solution)/shard_map/ppermute | solution.py:1057
  51.4 20.3 %collective-permute-start.10 = (bf16[1536,256]{1,0:T(8,128)(2,1)}, bf16[1536,256]{1,0:T(8,128)(2,1)}, u32[]{:S(2)}, u32[]{:S(2)}) collective-permute-start(bf16[1536,256]{1,0:T(8,128)(2,1)} %collective-permute-done.4.refs_3_), channel_id=1, source_target_pairs={{0,1},{1,0},{2,3},{3,2},{4,5},{5,4},{6,7},{7,6},{8,9},{9,8},{10,11... | collective-permute-start | bytes 2359304 | tf_op jit(solution)/shard_map/ppermute | solution.py:1057
  68.3 3.4 %collective-permute-start.12 = (bf16[1536,256]{1,0:T(8,128)(2,1)}, bf16[1536,256]{1,0:T(8,128)(2,1)S(1)}, u32[]{:S(2)}, u32[]{:S(2)}) collective-permute-start(bf16[1536,256]{1,0:T(8,128)(2,1)} %collective-permute-done.8.refs_7_), channel_id=1, source_target_pairs={{0,1},{1,0},{2,3},{3,2},{4,5},{5,4},{6,7},{7,6},{8,9},{9,8},{10,11... | collective-permute-start | bytes 2359304 | tf_op jit(solution)/shard_map/ppermute | solution.py:1057
  68.4 26.0 %collective-permute-start.15 = (bf16[1536,256]{1,0:T(8,128)(2,1)S(1)}, bf16[1536,256]{1,0:T(8,128)(2,1)S(1)}, u32[]{:S(2)}, u32[]{:S(2)}) collective-permute-start(bf16[1536,256]{1,0:T(8,128)(2,1)S(1)} %copy-done.17), channel_id=1, source_target_pairs={{0,2},{1,3},{2,0},{3,1},{4,6},{5,7},{6,4},{7,5},{8,10},{9,11},{10,... | collective-permute-start | bytes 2359304 | tf_op jit(solution)/shard_map/ppermute | solution.py:1057
  95.2 3.6 %collective-permute-start.16 = (bf16[2,2,4,192,256]{4,3,2,1,0:T(8,128)(2,1)}, bf16[2,2,4,192,256]{4,3,2,1,0:T(8,128)(2,1)S(1)}, u32[]{:S(2)}, u32[]{:S(2)}) collective-permute-start(bf16[2,2,4,192,256]{4,3,2,1,0:T(8,128)(2,1)} %bitcast.121), channel_id=1, source_target_pairs={{0,1},{1,0},{2,3},{3,2},{4,5},{5,4},{6,7},{7,6},{8,9},{9,8},{10,11... | collective-permute-start | bytes 4718600 | tf_op jit(solution)/shard_map/ppermute | solution.py:1057
  95.5 6.1 %collective-permute-start.17 = (bf16[2,2,4,192,256]{4,3,2,1,0:T(8,128)(2,1)}, bf16[2,2,4,192,256]{4,3,2,1,0:T(8,128)(2,1)S(1)}, u32[]{:S(2)}, u32[]{:S(2)}) collective-permute-start(bf16[2,2,4,192,256]{4,3,2,1,0:T(8,128)(2,1)} %bitcast.120), channel_id=1, source_target_pairs={{0,1},{1,0},{2,3},{3,2},{4,5},{5,4},{6,7},{7,6},{8,9},{9,8},{10,11... | collective-permute-start | bytes 4718600 | tf_op jit(solution)/shard_map/ppermute | solution.py:1057
  95.8 8.9 %collective-permute-start.18 = (bf16[1536,256]{1,0:T(8,128)(2,1)}, bf16[1536,256]{1,0:T(8,128)(2,1)S(1)}, u32[]{:S(2)}, u32[]{:S(2)}) collective-permute-start(bf16[1536,256]{1,0:T(8,128)(2,1)} %get-tuple-element.247.refs_1_), channel_id=1, source_target_pairs={{0,1},{1,0},{2,3},{3,2},{4,5},{5,4},{6,7},{7,6},{8,9},{9,8},{10,11... | collective-permute-start | bytes 2359304 | tf_op jit(solution)/shard_map/ppermute | solution.py:1057
  96.0 8.6 %collective-permute-start.19 = (bf16[1536,256]{1,0:T(8,128)(2,1)}, bf16[1536,256]{1,0:T(8,128)(2,1)S(1)}, u32[]{:S(2)}, u32[]{:S(2)}) collective-permute-start(bf16[1536,256]{1,0:T(8,128)(2,1)} %copy-done.18), channel_id=1, source_target_pairs={{0,1},{1,0},{2,3},{3,2},{4,5},{5,4},{6,7},{7,6},{8,9},{9,8},{10,11... | collective-permute-start | bytes 2359304 | tf_op jit(solution)/shard_map/ppermute | solution.py:1057
  102.1 21.3 %collective-permute-start.21 = (bf16[2,4,192,256]{3,2,1,0:T(8,128)(2,1)S(1)}, bf16[2,4,192,256]{3,2,1,0:T(8,128)(2,1)S(1)}, u32[]{:S(2)}, u32[]{:S(2)}) collective-permute-start(bf16[2,4,192,256]{3,2,1,0:T(8,128)(2,1)S(1)} %get-tuple-element.297), channel_id=1, source_target_pairs={{0,4},{4,0},{8,12},{12,8},{16,20},{20,16},{24,28},{28,24},{1,5},{5... | collective-permute-start | bytes 2359304 | tf_op jit(solution)/shard_map/ppermute | solution.py:1057
  103.6 19.8 %collective-permute-start.20 = (bf16[2,4,192,256]{3,2,1,0:T(8,128)(2,1)}, bf16[2,4,192,256]{3,2,1,0:T(8,128)(2,1)S(1)}, u32[]{:S(2)}, u32[]{:S(2)}) collective-permute-start(bf16[2,4,192,256]{3,2,1,0:T(8,128)(2,1)} %get-tuple-element.296), channel_id=1, source_target_pairs={{0,2},{1,3},{2,0},{3,1},{4,6},{5,7},{6,4},{7,5},{8,10},{9,11},{10,... | collective-permute-start | bytes 2359304 | tf_op jit(solution)/shard_map/ppermute | solution.py:1057
  123.4 4.6 %collective-permute-start.22 = (bf16[2,2,4,272,256]{4,3,2,1,0:T(8,128)(2,1)}, bf16[2,2,4,272,256]{4,3,2,1,0:T(8,128)(2,1)S(1)}, u32[]{:S(2)}, u32[]{:S(2)}) collective-permute-start(bf16[2,2,4,272,256]{4,3,2,1,0:T(8,128)(2,1)} %bitcast.118), channel_id=1, source_target_pairs={{0,1},{1,0},{2,3},{3,2},{4,5},{5,4},{6,7},{7,6},{8,9},{9,8},{10,11... | collective-permute-start | bytes 6684680 | tf_op jit(solution)/shard_map/ppermute | solution.py:1057
  129.4 21.3 %collective-permute-start.25 = (bf16[2,4,112,256]{3,2,1,0:T(8,128)(2,1)}, bf16[2,4,112,256]{3,2,1,0:T(8,128)(2,1)}, u32[]{:S(2)}, u32[]{:S(2)}) collective-permute-start(bf16[2,4,112,256]{3,2,1,0:T(8,128)(2,1)} %add_convert_fusion.8), channel_id=1, source_target_pairs={{0,2},{1,3},{2,0},{3,1},{4,6},{5,7},{6,4},{7,5},{8,10},{9,11},{10,... | collective-permute-start | bytes 1376264 | tf_op jit(solution)/shard_map/ppermute | solution.py:1057
  130.4 11.2 %collective-permute-start.23 = (bf16[4,192,256]{2,1,0:T(8,128)(2,1)}, bf16[4,192,256]{2,1,0:T(8,128)(2,1)}, u32[]{:S(2)}, u32[]{:S(2)}) collective-permute-start(bf16[4,192,256]{2,1,0:T(8,128)(2,1)} %get-tuple-element.317), channel_id=1, source_target_pairs={{0,4},{4,0},{8,12},{12,8},{16,20},{20,16},{24,28},{28,24},{1,5},{5... | collective-permute-start | bytes 1179656 | tf_op jit(solution)/shard_map/ppermute | solution.py:1057
  131.0 19.7 %collective-permute-start.24 = (bf16[4,192,256]{2,1,0:T(8,128)(2,1)}, bf16[4,192,256]{2,1,0:T(8,128)(2,1)}, u32[]{:S(2)}, u32[]{:S(2)}) collective-permute-start(bf16[4,192,256]{2,1,0:T(8,128)(2,1)} %get-tuple-element.318), channel_id=1, source_target_pairs={{0,2},{1,3},{2,0},{3,1},{4,6},{5,7},{6,4},{7,5},{8,10},{9,11},{10,... | collective-permute-start | bytes 1179656 | tf_op jit(solution)/shard_map/ppermute | solution.py:1057
  153.1 20.7 %collective-permute-start.29 = (bf16[2,4,160,256]{3,2,1,0:T(8,128)(2,1)S(1)}, bf16[2,4,160,256]{3,2,1,0:T(8,128)(2,1)S(1)}, u32[]{:S(2)}, u32[]{:S(2)}) collective-permute-start(bf16[2,4,160,256]{3,2,1,0:T(8,128)(2,1)S(1)} %add_convert_fusion.5), channel_id=1, source_target_pairs={{0,2},{1,3},{2,0},{3,1},{4,6},{5,7},{6,4},{7,5},{8,10},{9,11},{10,... | collective-permute-start | bytes 1966088 | tf_op jit(solution)/shard_map/ppermute | solution.py:1057
  154.2 19.6 %collective-permute-start.30 = (bf16[4,256,128]{2,1,0:T(8,128)(2,1)S(1)}, bf16[4,256,128]{2,1,0:T(8,128)(2,1)S(1)}, u32[]{:S(2)}, u32[]{:S(2)}) collective-permute-start(bf16[4,256,128]{2,1,0:T(8,128)(2,1)S(1)} %copy-done.31), channel_id=1, source_target_pairs={{0,4},{4,0},{8,12},{12,8},{16,20},{20,16},{24,28},{28,24},{1,5},{5... | collective-permute-start | bytes 786440 | tf_op jit(solution)/shard_map/ppermute | solution.py:1057
  154.8 12.7 %collective-permute-start.26 = (bf16[2,192,256]{2,1,0:T(8,128)(2,1)S(1)}, bf16[2,192,256]{2,1,0:T(8,128)(2,1)S(1)}, u32[]{:S(2)}, u32[]{:S(2)}) collective-permute-start(bf16[2,192,256]{2,1,0:T(8,128)(2,1)S(1)} %pad_maximum_fusion.5), channel_id=1, source_target_pairs={{0,8},{4,12},{8,0},{12,4},{16,24},{20,28},{24,16},{28,20},{1,9},{5... | collective-permute-start | bytes 589832 | tf_op jit(solution)/shard_map/ppermute | solution.py:1057
  156.2 17.6 %collective-permute-start.27 = (bf16[2,192,256]{2,1,0:T(8,128)(2,1)S(1)}, bf16[2,192,256]{2,1,0:T(8,128)(2,1)S(1)}, u32[]{:S(2)}, u32[]{:S(2)}) collective-permute-start(bf16[2,192,256]{2,1,0:T(8,128)(2,1)S(1)} %pad_maximum_fusion.6), channel_id=1, source_target_pairs={{0,16},{4,20},{8,24},{12,28},{16,0},{20,4},{24,8},{28,12},{1,17},{... | collective-permute-start | bytes 589832 | tf_op jit(solution)/shard_map/ppermute | solution.py:1057
  159.7 14.1 %collective-permute-start.28 = (bf16[2,192,256]{2,1,0:T(8,128)(2,1)S(1)}, bf16[2,192,256]{2,1,0:T(8,128)(2,1)S(1)}, u32[]{:S(2)}, u32[]{:S(2)}) collective-permute-start(bf16[2,192,256]{2,1,0:T(8,128)(2,1)S(1)} %pad_maximum_fusion.7), channel_id=1, source_target_pairs={{0,24},{4,28},{8,16},{12,20},{16,8},{20,12},{24,0},{28,4},{1,25},{... | collective-permute-start | bytes 589832 | tf_op jit(solution)/shard_map/ppermute | solution.py:1057
  173.8 7.0 %collective-permute-start.31 = (bf16[4,256,128]{2,1,0:T(8,128)(2,1)}, bf16[4,256,128]{2,1,0:T(8,128)(2,1)S(1)}, u32[]{:S(2)}, u32[]{:S(2)}) collective-permute-start(bf16[4,256,128]{2,1,0:T(8,128)(2,1)} %get-tuple-element.355), channel_id=1, source_target_pairs={{0,4},{4,0},{8,12},{12,8},{16,20},{20,16},{24,28},{28,24},{1,5},{5... | collective-permute-start | bytes 786440 | tf_op jit(solution)/shard_map/ppermute | solution.py:1057
  180.8 10.8 %collective-permute-start.32 = (bf16[2,2,4,72,256]{4,3,2,1,0:T(8,128)(2,1)}, bf16[2,2,4,72,256]{4,3,2,1,0:T(8,128)(2,1)S(1)}, u32[]{:S(2)}, u32[]{:S(2)}) collective-permute-start(bf16[2,2,4,72,256]{4,3,2,1,0:T(8,128)(2,1)} %bitcast.123), channel_id=1, source_target_pairs={{0,1},{1,0},{2,3},{3,2},{4,5},{5,4},{6,7},{7,6},{8,9},{9,8},{10,11... | collective-permute-start | bytes 1769480 | tf_op jit(solution)/shard_map/ppermute | solution.py:1057
  181.8 24.4 %all-to-all-start.1 = ((bf16[4,2,256,128]{3,2,1,0:T(8,128)(2,1)}), bf16[4,2,256,128]{3,2,1,0:T(8,128)(2,1)S(1)}, u32[]{:S(2)}, u32[]{:S(2)}) async-start(bf16[4,2,256,128]{3,2,1,0:T(8,128)(2,1)} %pad_maximum_fusion.2), calls=%async_computation.1 | async-start | bytes 1048576 | tf_op jit(solution)/shard_map/all_to_all | solution.py:1291
  191.0 15.0 %collective-permute-start.33 = (bf16[4,272,256]{2,1,0:T(8,128)(2,1)}, bf16[4,272,256]{2,1,0:T(8,128)(2,1)S(1)}, u32[]{:S(2)}, u32[]{:S(2)}) collective-permute-start(bf16[4,272,256]{2,1,0:T(8,128)(2,1)} %get-tuple-element.367), channel_id=1, source_target_pairs={{0,4},{4,0},{8,12},{12,8},{16,20},{20,16},{24,28},{28,24},{1,5},{5... | collective-permute-start | bytes 1671176 | tf_op jit(solution)/shard_map/ppermute | solution.py:1057
  191.8 25.6 %collective-permute-start.37 = (bf16[2,4,72,256]{3,2,1,0:T(8,128)(2,1)S(1)}, bf16[2,4,72,256]{3,2,1,0:T(8,128)(2,1)S(1)}, u32[]{:S(2)}, u32[]{:S(2)}) collective-permute-start(bf16[2,4,72,256]{3,2,1,0:T(8,128)(2,1)S(1)} %get-tuple-element.384), channel_id=1, source_target_pairs={{0,2},{1,3},{2,0},{3,1},{4,6},{5,7},{6,4},{7,5},{8,10},{9,11},{10,... | collective-permute-start | bytes 884744 | tf_op jit(solution)/shard_map/ppermute | solution.py:1057
  206.2 14.5 %collective-permute-start.34 = (bf16[1,272,256]{2,1,0:T(8,128)(2,1)S(1)}, bf16[1,272,256]{2,1,0:T(8,128)(2,1)S(1)}, u32[]{:S(2)}, u32[]{:S(2)}) collective-permute-start(bf16[1,272,256]{2,1,0:T(8,128)(2,1)S(1)} %get-tuple-element.381), channel_id=1, source_target_pairs={{0,8},{4,12},{8,0},{12,4},{16,24},{20,28},{24,16},{28,20},{1,9},{5... | collective-permute-start | bytes 417800 | tf_op jit(solution)/shard_map/ppermute | solution.py:1057
  208.0 12.9 %collective-permute-start.35 = (bf16[1,272,256]{2,1,0:T(8,128)(2,1)S(1)}, bf16[1,272,256]{2,1,0:T(8,128)(2,1)S(1)}, u32[]{:S(2)}, u32[]{:S(2)}) collective-permute-start(bf16[1,272,256]{2,1,0:T(8,128)(2,1)S(1)} %get-tuple-element.382), channel_id=1, source_target_pairs={{0,16},{4,20},{8,24},{12,28},{16,0},{20,4},{24,8},{28,12},{1,17},{... | collective-permute-start | bytes 417800 | tf_op jit(solution)/shard_map/ppermute | solution.py:1057
  210.3 10.6 %collective-permute-start.36 = (bf16[1,272,256]{2,1,0:T(8,128)(2,1)S(1)}, bf16[1,272,256]{2,1,0:T(8,128)(2,1)S(1)}, u32[]{:S(2)}, u32[]{:S(2)}) collective-permute-start(bf16[1,272,256]{2,1,0:T(8,128)(2,1)S(1)} %get-tuple-element.383), channel_id=1, source_target_pairs={{0,24},{4,28},{8,16},{12,20},{16,8},{20,12},{24,0},{28,4},{1,25},{... | collective-permute-start | bytes 417800 | tf_op jit(solution)/shard_map/ppermute | solution.py:1057
  210.6 13.0 %collective-permute-start.39 = (bf16[2,192,256]{2,1,0:T(8,128)(2,1)S(1)}, bf16[2,192,256]{2,1,0:T(8,128)(2,1)S(1)}, u32[]{:S(2)}, u32[]{:S(2)}) collective-permute-start(bf16[2,192,256]{2,1,0:T(8,128)(2,1)S(1)} %add_convert_fusion.18), channel_id=1, source_target_pairs={{0,8},{4,12},{8,0},{12,4},{16,24},{20,28},{24,16},{28,20},{1,9},{5... | collective-permute-start | bytes 589832 | tf_op jit(solution)/shard_map/ppermute | solution.py:1057
  217.4 19.0 %collective-permute-start.40 = (bf16[2,192,256]{2,1,0:T(8,128)(2,1)S(1)}, bf16[2,192,256]{2,1,0:T(8,128)(2,1)S(1)}, u32[]{:S(2)}, u32[]{:S(2)}) collective-permute-start(bf16[2,192,256]{2,1,0:T(8,128)(2,1)S(1)} %add_convert_fusion.18), channel_id=1, source_target_pairs={{0,16},{4,20},{8,24},{12,28},{16,0},{20,4},{24,8},{28,12},{1,17},{... | collective-permute-start | bytes 589832 | tf_op jit(solution)/shard_map/ppermute | solution.py:1057
  220.6 15.7 %collective-permute-start.41 = (bf16[2,192,256]{2,1,0:T(8,128)(2,1)S(1)}, bf16[2,192,256]{2,1,0:T(8,128)(2,1)S(1)}, u32[]{:S(2)}, u32[]{:S(2)}) collective-permute-start(bf16[2,192,256]{2,1,0:T(8,128)(2,1)S(1)} %add_convert_fusion.18), channel_id=1, source_target_pairs={{0,24},{4,28},{8,16},{12,20},{16,8},{20,12},{24,0},{28,4},{1,25},{... | collective-permute-start | bytes 589832 | tf_op jit(solution)/shard_map/ppermute | solution.py:1057
  223.6 12.9 %collective-permute-start.42 = (bf16[2,4,24,256]{3,2,1,0:T(8,128)(2,1)S(1)}, bf16[2,4,24,256]{3,2,1,0:T(8,128)(2,1)S(1)}, u32[]{:S(2)}, u32[]{:S(2)}) collective-permute-start(bf16[2,4,24,256]{3,2,1,0:T(8,128)(2,1)S(1)} %get-tuple-element.405), channel_id=1, source_target_pairs={{0,2},{1,3},{2,0},{3,1},{4,6},{5,7},{6,4},{7,5},{8,10},{9,11},{10,... | collective-permute-start | bytes 294920 | tf_op jit(solution)/shard_map/ppermute | solution.py:1057
  237.5 20.6 %all-to-all-start.2 = ((bf16[8,96,256]{2,1,0:T(8,128)(2,1)}), bf16[8,96,256]{2,1,0:T(8,128)(2,1)S(1)}, u32[]{:S(2)}, u32[]{:S(2)}) async-start(bf16[8,96,256]{2,1,0:T(8,128)(2,1)} %pad_maximum_fusion.3), calls=%async_computation.2 | async-start | bytes 786432 | tf_op jit(solution)/shard_map/all_to_all | solution.py:1317
  243.4 21.4 %collective-permute-start.43 = (bf16[1,272,256]{2,1,0:T(8,128)(2,1)S(1)}, bf16[1,272,256]{2,1,0:T(8,128)(2,1)S(1)}, u32[]{:S(2)}, u32[]{:S(2)}) collective-permute-start(bf16[1,272,256]{2,1,0:T(8,128)(2,1)S(1)} %add_convert_fusion.19), channel_id=1, source_target_pairs={{0,8},{4,12},{8,0},{12,4},{16,24},{20,28},{24,16},{28,20},{1,9},{5... | collective-permute-start | bytes 417800 | tf_op jit(solution)/shard_map/ppermute | solution.py:1057
  245.5 21.9 %collective-permute-start.44 = (bf16[1,272,256]{2,1,0:T(8,128)(2,1)S(1)}, bf16[1,272,256]{2,1,0:T(8,128)(2,1)S(1)}, u32[]{:S(2)}, u32[]{:S(2)}) collective-permute-start(bf16[1,272,256]{2,1,0:T(8,128)(2,1)S(1)} %add_convert_fusion.19), channel_id=1, source_target_pairs={{0,16},{4,20},{8,24},{12,28},{16,0},{20,4},{24,8},{28,12},{1,17},{... | collective-permute-start | bytes 417800 | tf_op jit(solution)/shard_map/ppermute | solution.py:1057
  247.8 19.5 %collective-permute-start.45 = (bf16[1,272,256]{2,1,0:T(8,128)(2,1)S(1)}, bf16[1,272,256]{2,1,0:T(8,128)(2,1)S(1)}, u32[]{:S(2)}, u32[]{:S(2)}) collective-permute-start(bf16[1,272,256]{2,1,0:T(8,128)(2,1)S(1)} %add_convert_fusion.19), channel_id=1, source_target_pairs={{0,24},{4,28},{8,16},{12,20},{16,8},{20,12},{24,0},{28,4},{1,25},{... | collective-permute-start | bytes 417800 | tf_op jit(solution)/shard_map/ppermute | solution.py:1057
  247.9 23.7 %collective-permute-start.46 = (bf16[4,2,192,256]{3,2,1,0:T(8,128)(2,1)S(1)}, bf16[4,2,192,256]{3,2,1,0:T(8,128)(2,1)S(1)}, u32[]{:S(2)}, u32[]{:S(2)}) collective-permute-start(bf16[4,2,192,256]{3,2,1,0:T(8,128)(2,1)S(1)} %pad_maximum_fusion.own), channel_id=1, source_target_pairs={{0,4},{4,0},{8,12},{12,8},{16,20},{20,16},{24,28},{28,24},{1,5},{5... | collective-permute-start | bytes 2359304 | tf_op jit(solution)/shard_map/ppermute | solution.py:1057
  258.9 24.9 %all-to-all-start.3 = ((bf16[8,96,256]{2,1,0:T(8,128)(2,1)}), bf16[8,96,256]{2,1,0:T(8,128)(2,1)S(1)}, u32[]{:S(2)}, u32[]{:S(2)}) async-start(bf16[8,96,256]{2,1,0:T(8,128)(2,1)} %broadcast_in_dim.3), calls=%async_computation.3 | async-start | bytes 786432 | tf_op jit(solution)/shard_map/all_to_all | solution.py:1321
  267.4 16.3 %collective-permute-start.47 = (bf16[4,1,272,256]{3,2,1,0:T(8,128)(2,1)S(1)}, bf16[4,1,272,256]{3,2,1,0:T(8,128)(2,1)S(1)}, u32[]{:S(2)}, u32[]{:S(2)}) collective-permute-start(bf16[4,1,272,256]{3,2,1,0:T(8,128)(2,1)S(1)} %pad_maximum_fusion.1.own), channel_id=1, source_target_pairs={{0,4},{4,0},{8,12},{12,8},{16,20},{20,16},{24,28},{28,24},{1,5},{5... | collective-permute-start | bytes 1671176 | tf_op jit(solution)/shard_map/ppermute | solution.py:1057
  (36 other events, 210.3 us)

commit v7 on v6

--- a/solution.py
+++ b/solution.py
@@ -63,7 +63,7 @@
         scratch[pl.ds(begin, height), :] = piece[0:height, :]
 
 
-STEP = 128
+STEP = 256
 
 
 def over_rows(rows, run):
@@ -1263,7 +1263,7 @@
     zero.x()
     one.y()
     grad_attended = tie(grad_attended, zero, one, two, came=[two])
-    two.y([round_up(two.rows // ctx_size * 2 // 5, 8)])
+    two.y([round_up(two.rows // ctx_size // 3, 8)])
     grad_attended = tie(grad_attended, zero, one, two).reshape(seqs, rows, width)
     grad_queries, terms = [], []
     for seq in range(seqs):

time: 292 us -> 288 us (0.986)
  transfers between devices with their start and end apart: 52 -> 52, of which waited for: 18 -> 19; matrix products, arithmetic and copies ran while one was open for 5% -> 5% of each run, Pallas kernels for 29% -> 29%
where the time goes in v7:
time: 288 us
  waiting for transfers between devices  101 us (35%)
  Pallas kernels  87.8 us (30%)
  starting transfers between devices  70.3 us (24%)
  other arithmetic  15.5 us (5%)
  local copies, waits for them, and re-layouts  13 us (5%)
    ppermute x48, waiting for transfers between devices, swap(): return lax.ppermute(values, axis, [(i, i ^ mask) for i in range(size)])  92.3 us
    ppermute x48, starting transfers between devices, swap(): return lax.ppermute(values, axis, [(i, i ^ mask) for i in range(size)])  44.8 us
    pallas_call x2, Pallas kernels, feed_stage(): pl.pallas_call(functools.partial(feed_kernel, pieces=pieces, part=part, f...  38.3 us
    pallas_call x2, Pallas kernels, attend_back(): pl.pallas_call(functools.partial(attend_back_kernel, seq=seq, blocks=bloc...  13.2 us
    pallas_call x1, Pallas kernels, attend(): pl.pallas_call(functools.partial(attend_kernel, blocks=blocks, tile_rows=...  8.36 us
    all_to_all x1, waiting for transfers between devices, body(): late = lax.all_to_all(late, 'ctx', 0, 0)  8.2 us
    unnamed x65, local copies, waits for them, and re-layouts  7.91 us
    all_to_all x1, starting transfers between devices, body(): lax.all_to_all(arriving, 'ctx', 0, 0, axis_index_groups=[list(range(x, ct...  7.78 us
  transfers between devices with their start and end apart: 52, of which 19 were waited for; matrix products, arithmetic and copies ran while one was open for 5% of the time, Pallas kernels for 29%

profile of v7, /device:TPU:0, one launch (start us, length us, event | category | flops | bytes accessed | tf_op | source)
XLA Modules:
  0.0 288.3 jit_solution(9417342460863124432)
XLA Ops:
  2.1 3.0 %collective-permute-start.1 = (bf16[208,128]{1,0:T(8,128)(2,1)S(1)}, bf16[208,128]{1,0:T(8,128)(2,1)S(1)}, u32[]{:S(2)}, u32[]{:S(2)}) collective-permute-start(bf16[208,128]{1,0:T(8,128)(2,1)S(1)} %fusion.21.rest_0_), channel_id=1, source_target_pairs={{0,2},{1,3},{2,0},{3,1},{4,6},{5,7},{6,4},{7,5},{8,10},{9,11},{10,... | collective-permute-start | bytes 159752 | tf_op jit(solution)/shard_map/ppermute | solution.py:1057
  5.3 2.0 collective-permute-done.1.rest_2_
  9.5 3.5 %first_norm.1 = (bf16[512,768]{1,0:T(8,128)(2,1)}, bf16[8,544,128]{2,1,0:T(8,128)(2,1)}) custom-call(s32[1]{0:T(128)} %bitcast.spot_ref, bf16[512,768]{1,0:T(8,128)(2,1)} %bitcast.87, f32[1,768]{1,0:T(1,128)} %reshape_squeeze.6.gain, bf16[2,2,128]{2,1,0:T(2,128)(2,1)} %reshape.183.documents, bf16[208,128]{1,0:T(8,128)(2,1)} %copy-done.25, ...), custom_call_target="tpu_custom_call" | custom-call | flops 1 | bytes 1 | tf_op jit(solution)/shard_map/first_norm/pallas_call | solution.py:144
  13.1 1.7 collective-permute-done.3.rest_2_.rest_4_
  14.8 5.8 %all-to-all-start = ((bf16[8,544,128]{2,1,0:T(8,128)(2,1)}), bf16[8,544,128]{2,1,0:T(8,128)(2,1)S(1)}, u32[]{:S(2)}, u32[]{:S(2)}) async-start(bf16[8,544,128]{2,1,0:T(8,128)(2,1)} %get-tuple-element.221), calls=%async_computation | async-start | bytes 2228224 | tf_op jit(solution)/shard_map/all_to_all | solution.py:1219
  20.6 3.2 %pack.1 = (bf16[1536,256]{1,0:T(8,128)(2,1)}, bf16[1536,256]{1,0:T(8,128)(2,1)}, bf16[1536,256]{1,0:T(8,128)(2,1)}) custom-call(bf16[192,3072]{1,0:T(8,128)(2,1)} %up, bf16[768,768]{1,0:T(8,128)(2,1)} %down), custom_call_target="tpu_custom_call" | custom-call | flops 1 | bytes 1 | tf_op jit(solution)/shard_map/pack/pallas_call | solution.py:95
  27.3 3.3 %project.1 = bf16[512,768]{1,0:T(8,128)(2,1)} custom-call(s32[1]{0:T(128)} %bitcast.spot_ref, bf16[512,768]{1,0:T(8,128)(2,1)} %get-tuple-element.226.operand.scaled, bf16[192,768]{1,0:T(8,128)(2,1)} %rest_2_.1, bf16[192,768]{1,0:T(8,128)(2,1)} %copy-done.12, bf16[192,768]{1,0:T(8,128)(2,1)} %copy-done.11, bf16[192,768]{1,0:T(8,128)(2,1)} %copy-done.13), custom_call_target="tpu_custom_call" | custom-call | flops 1 | bytes 1 | tf_op jit(solution)/shard_map/project/pallas_call | solution.py:173
  30.6 18.6 %collective-permute-done.5.refs_11_.refs_7_ = bf16[192,768]{1,0:T(8,128)(2,1)S(1)} collective-permute-done((bf16[192,768]{1,0:T(8,128)(2,1)S(1)}, bf16[192,768]{1,0:T(8,128)(2,1)S(1)}, u32[]{:S(2)}, u32[]{:S(2)}) %collective-permute-start.5) | collective-permute-done | bytes 294944 | tf_op jit(solution)/shard_map/ppermute | solution.py:1057
  51.6 8.4 %attend.1 = (s32[2,256,128]{2,1,0:T(8,128)}, f32[2,256,768]{2,1,0:T(8,128)}, bf16[2,256,768]{2,1,0:T(8,128)(2,1)}, f32[2,256,768]{2,1,0:T(8,128)}) custom-call(s32[1]{0:T(128)} %bitcast.1.place_ref, bf16[2,256,768]{2,1,0:T(8,128)(2,1)} %bitcast.84, bf16[8,2,272,128]{3,2,1,0:T(8,128)(2,1)} %bitcast.81), custom_call_target="tpu_custom_call" | custom-call | flops 1 | bytes 1 | tf_op jit(solution)/shard_map/attend/pallas_call | solution.py:450
  60.0 7.7 %collective-permute-done.8.refs_7_ = bf16[1536,256]{1,0:T(8,128)(2,1)} collective-permute-done((bf16[1536,256]{1,0:T(8,128)(2,1)}, bf16[1536,256]{1,0:T(8,128)(2,1)}, u32[]{:S(2)}, u32[]{:S(2)}) %collective-permute-start.8) | collective-permute-done | bytes 786464 | tf_op jit(solution)/shard_map/ppermute | solution.py:1057
  67.7 1.8 collective-permute-start.15
  72.1 21.5 %feed0.1 = (bf16[2,1536,256]{2,1,0:T(8,128)(2,1)}, bf16[2,1536,256]{2,1,0:T(8,128)(2,1)}, bf16[2,2,768,256]{3,2,1,0:T(8,128)(2,1)}, bf16[2,2,768,256]{3,2,1,0:T(...) custom-call(s32[1]{0:T(128)} %bitcast.spot_ref, ...), custom_call_target="tpu_custom_call" | custom-call | flops 1 | bytes 1 | tf_op jit(solution)/shard_map/feed0/pallas_call | solution.py:804
  95.5 2.6 collective-permute-done.16
  98.1 2.7 fusion.2
  101.3 1.5 collective-permute-start.21
  105.6 16.8 %feed2.1 = (bf16[2,2176,256]{2,1,0:T(8,128)(2,1)}, bf16[2,2176,256]{2,1,0:T(8,128)(2,1)}, bf16[512,768]{1,0:T(8,128)(2,1)}, f32[512,768]{1,0:T(8,128)}, bf16[512,768]{1,0:T(8,128)(2,1)}) custom-call(s32[1]{0:T(128)} %bitcast.spot_ref, bf16[512,768]{1,0:T(8,128)(2,1)} %bitcast.91, bf16[1536,256]{1,0:T(8,128)(2,1)} %get-tuple-element.247.refs_1_, ...), custom_call_target="tpu_custom_call" | custom-call | flops 1 | bytes 1 | tf_op jit(solution)/shard_map/feed2/pallas_call | solution.py:804
  124.8 2.3 collective-permute-done.22
  131.1 6.5 %attend_back.2 = (bf16[1,256,768]{2,1,0:T(8,128)(2,1)}, bf16[4,256,128]{2,1,0:T(8,128)(2,1)}, bf16[4,256,128]{2,1,0:T(8,128)(2,1)}) custom-call(s32[1]{0:T(128)} %bitcast.1.place_ref, bf16[2,256,768]{2,1,0:T(8,128)(2,1)} %bitcast.85, s32[2,256,128]{2,1,0:T(8,128)} %get-tuple-element.288.starts, f32[2,256,768]{2,1,0:T(8,128)} %get-tuple-element.289.exact, ...), custom_call_target="tpu_custom_call" | custom-call | flops 1 | bytes 1 | tf_op jit(solution)/shard_map/attend_back/pallas_call | solution.py:493
  137.8 3.0 %collective-permute-done.25 = bf16[2,4,96,256]{3,2,1,0:T(8,128)(2,1)} collective-permute-done((bf16[2,4,96,256]{3,2,1,0:T(8,128)(2,1)}, bf16[2,4,96,256]{3,2,1,0:T(8,128)(2,1)}, u32[]{:S(2)}, u32[]{:S(2)}) %collective-permute-start.25) | collective-permute-done | bytes 393248 | tf_op jit(solution)/shard_map/ppermute | solution.py:1057
  140.7 7.6 %collective-permute-done.24 = bf16[4,192,256]{2,1,0:T(8,128)(2,1)} collective-permute-done((bf16[4,192,256]{2,1,0:T(8,128)(2,1)}, bf16[4,192,256]{2,1,0:T(8,128)(2,1)}, u32[]{:S(2)}, u32[]{:S(2)}) %collective-permute-start.24) | collective-permute-done | bytes 393248 | tf_op jit(solution)/shard_map/ppermute | solution.py:1057
  152.5 1.4 collective-permute-start.26
  153.9 4.0 %collective-permute-start.27 = (bf16[2,192,256]{2,1,0:T(8,128)(2,1)S(1)}, bf16[2,192,256]{2,1,0:T(8,128)(2,1)S(1)}, u32[]{:S(2)}, u32[]{:S(2)}) collective-permute-start(bf16[2,192,256]{2,1,0:T(8,128)(2,1)S(1)} %pad_maximum_fusion.6), channel_id=1, source_target_pairs={{0,16},{4,20},{8,24},{12,28},{16,0},{20,4},{24,8},{28,12},{1,17},{... | collective-permute-start | bytes 589832 | tf_op jit(solution)/shard_map/ppermute | solution.py:1057
  157.9 6.7 %attend_back.3 = (bf16[1,256,768]{2,1,0:T(8,128)(2,1)}, bf16[4,256,128]{2,1,0:T(8,128)(2,1)}, bf16[4,256,128]{2,1,0:T(8,128)(2,1)}) custom-call(s32[1]{0:T(128)} %bitcast.1.place_ref, bf16[2,256,768]{2,1,0:T(8,128)(2,1)} %bitcast.86, s32[2,256,128]{2,1,0:T(8,128)} %get-tuple-element.288.starts, f32[2,256,768]{2,1,0:T(8,128)} %get-tuple-element.289.exact, ...), custom_call_target="tpu_custom_call" | custom-call | flops 1 | bytes 1 | tf_op jit(solution)/shard_map/attend_back/pallas_call | solution.py:493
  165.7 6.5 %collective-permute-done.27 = bf16[2,192,256]{2,1,0:T(8,128)(2,1)S(1)} collective-permute-done((bf16[2,192,256]{2,1,0:T(8,128)(2,1)S(1)}, bf16[2,192,256]{2,1,0:T(8,128)(2,1)S(1)}, u32[]{:S(2)}, u32[]{:S(2)}) %collective-permute-start.27) | collective-permute-done | bytes 196640 | tf_op jit(solution)/shard_map/ppermute | solution.py:1057
  172.2 1.9 collective-permute-start.31
  175.4 4.7 %query_grad.1 = (f32[512,768]{1,0:T(8,128)}, bf16[2,576,256]{2,1,0:T(8,128)(2,1)}, bf16[2,576,256]{2,1,0:T(8,128)(2,1)}) custom-call(s32[1]{0:T(128)} %bitcast.spot_ref, bf16[512,768]{1,0:T(8,128)(2,1)} %get-tuple-element.226.operand.scaled, bf16[256,768]{1,0:T(8,128)(2,1)} %bitcast.105, bf16[256,768]{1,0:T(8,128)(2,1)} %bitcast.106, ...), custom_call_target="tpu_custom_call" | custom-call | flops 1 | bytes 1 | tf_op jit(solution)/shard_map/query_grad/pallas_call | solution.py:851
  181.1 7.8 %all-to-all-start.1 = ((bf16[4,2,256,128]{3,2,1,0:T(8,128)(2,1)}), bf16[4,2,256,128]{3,2,1,0:T(8,128)(2,1)S(1)}, u32[]{:S(2)}, u32[]{:S(2)}) async-start(bf16[4,2,256,128]{3,2,1,0:T(8,128)(2,1)} %pad_maximum_fusion.2), calls=%async_computation.1 | async-start | bytes 1048576 | tf_op jit(solution)/shard_map/all_to_all | solution.py:1291
  189.3 1.5 collective-permute-start.37
  190.8 13.0 %collective-permute-done.33 = bf16[4,272,256]{2,1,0:T(8,128)(2,1)S(1)} collective-permute-done((bf16[4,272,256]{2,1,0:T(8,128)(2,1)}, bf16[4,272,256]{2,1,0:T(8,128)(2,1)S(1)}, u32[]{:S(2)}, u32[]{:S(2)}) %collective-permute-start.33) | collective-permute-done | bytes 557088 | tf_op jit(solution)/shard_map/ppermute | solution.py:1057
  204.0 1.8 collective-permute-start.34
  205.8 2.4 collective-permute-start.35
  209.3 5.7 %last.1 = (f32[512,768]{1,0:T(8,128)}, bf16[2,192,256]{2,1,0:T(8,128)(2,1)}, bf16[2,192,256]{2,1,0:T(8,128)(2,1)}) custom-call(s32[1]{0:T(128)} %bitcast.spot_ref, bf16[512,768]{1,0:T(8,128)(2,1)} %bitcast.89, f32[1,768]{1,0:T(1,128)} %reshape_squeeze.6.gain, bf16[512,768]{1,0:T(8,128)(2,1)} %get-tuple-element.226.operand.scaled, ...), custom_call_target="tpu_custom_call" | custom-call | flops 1 | bytes 1 | tf_op jit(solution)/shard_map/last/pallas_call | solution.py:908
  215.0 3.3 %collective-permute-start.40 = (bf16[2,192,256]{2,1,0:T(8,128)(2,1)S(1)}, bf16[2,192,256]{2,1,0:T(8,128)(2,1)S(1)}, u32[]{:S(2)}, u32[]{:S(2)}) collective-permute-start(bf16[2,192,256]{2,1,0:T(8,128)(2,1)S(1)} %add_convert_fusion.18), channel_id=1, source_target_pairs={{0,16},{4,20},{8,24},{12,28},{16,0},{20,4},{24,8},{28,12},{1,17},{... | collective-permute-start | bytes 589832 | tf_op jit(solution)/shard_map/ppermute | solution.py:1057
  218.8 1.6 collective-permute-done.38
  222.4 11.8 %collective-permute-done.40 = bf16[2,192,256]{2,1,0:T(8,128)(2,1)S(1)} collective-permute-done((bf16[2,192,256]{2,1,0:T(8,128)(2,1)S(1)}, bf16[2,192,256]{2,1,0:T(8,128)(2,1)S(1)}, u32[]{:S(2)}, u32[]{:S(2)}) %collective-permute-start.40) | collective-permute-done | bytes 196640 | tf_op jit(solution)/shard_map/ppermute | solution.py:1057
  235.3 5.9 %all-to-all-start.2 = ((bf16[8,96,256]{2,1,0:T(8,128)(2,1)}), bf16[8,96,256]{2,1,0:T(8,128)(2,1)S(1)}, u32[]{:S(2)}, u32[]{:S(2)}) async-start(bf16[8,96,256]{2,1,0:T(8,128)(2,1)} %pad_maximum_fusion.3), calls=%async_computation.2 | async-start | bytes 786432 | tf_op jit(solution)/shard_map/all_to_all | solution.py:1317
  241.2 2.0 collective-permute-start.43
  243.3 2.4 collective-permute-start.44
  245.7 2.0 collective-permute-start.46
  247.7 8.2 %all-to-all-done.2 = bf16[8,96,256]{2,1,0:T(8,128)(2,1)S(1)} async-done(((bf16[8,96,256]{2,1,0:T(8,128)(2,1)}), bf16[8,96,256]{2,1,0:T(8,128)(2,1)S(1)}, u32[]{:S(2)}, u32[]{:S(2)}) %all-to-all-start.2) | async-done | bytes 393248 | tf_op jit(solution)/shard_map/all_to_all | solution.py:1317
  256.7 6.0 %all-to-all-start.3 = ((bf16[8,96,256]{2,1,0:T(8,128)(2,1)}), bf16[8,96,256]{2,1,0:T(8,128)(2,1)S(1)}, u32[]{:S(2)}, u32[]{:S(2)}) async-start(bf16[8,96,256]{2,1,0:T(8,128)(2,1)} %broadcast_in_dim.3), calls=%async_computation.3 | async-start | bytes 786432 | tf_op jit(solution)/shard_map/all_to_all | solution.py:1321
  262.7 2.5 collective-permute-done.44
  265.2 1.4 collective-permute-start.47
  266.6 2.8 collective-permute-done.46.other
  270.3 3.9 %early_sums.1 = (f32[768,768]{1,0:T(8,128)}, f32[192,3072]{1,0:T(8,128)}) custom-call(s32[1]{0:T(128)} %bitcast.1.place_ref, bf16[4,2,192,256]{3,2,1,0:T(8,128)(2,1)} %copy-done.1, bf16[4,2,192,256]{3,2,1,0:T(8,128)(2,1)} %copy-done.22), custom_call_target="tpu_custom_call" | custom-call | flops 1 | bytes 1 | tf_op jit(solution)/shard_map/early_sums/pallas_call | solution.py:956
  274.2 7.4 %collective-permute-done.47.other = bf16[4,1,272,256]{3,2,1,0:T(8,128)(2,1)S(1)} collective-permute-done((bf16[4,1,272,256]{3,2,1,0:T(8,128)(2,1)S(1)}, bf16[4,1,272,256]{3,2,1,0:T(8,128)(2,1)S(1)}, u32[]{:S(2)}, u32[]{:S(2)}) %collective-permute-start.47) | collective-permute-done | bytes 557088 | tf_op jit(solution)/shard_map/ppermute | solution.py:1057
  283.1 3.7 %final.1 = (f32[768,768]{1,0:T(8,128)}, f32[192,3072]{1,0:T(8,128)}, f32[192,768]{1,0:T(8,128)}, f32[192,768]{1,0:T(8,128)}, f32[192,128]{1,0:T(8,128)}, /*index=5*/f32[2,768]{1,0:T(2,128)}) custom-call(s32[1]{0:T(128)} %bitcast.1.place_ref, bf16[4,1,272,256]{3,2,1,0:T(8,128)(2,1)} %copy-done.2, ...), custom_call_target="tpu_custom_call", output_to_operand_aliasing={{0}: (4, {}), {1}: (5, {})} | custom-call | flops 1 | bytes 1 | tf_op jit(solution)/shard_map/final/pallas_call | solution.py:1025
  286.8 1.4 fusion.23
  (185 shorter events, 40.1 us)
Async XLA Ops:
  2.1 5.2 %collective-permute-start.1 = (bf16[208,128]{1,0:T(8,128)(2,1)S(1)}, bf16[208,128]{1,0:T(8,128)(2,1)S(1)}, u32[]{:S(2)}, u32[]{:S(2)}) collective-permute-start(bf16[208,128]{1,0:T(8,128)(2,1)S(1)} %fusion.21.rest_0_), channel_id=1, source_target_pairs={{0,2},{1,3},{2,0},{3,1},{4,6},{5,7},{6,4},{7,5},{8,10},{9,11},{10,... | collective-permute-start | bytes 159752 | tf_op jit(solution)/shard_map/ppermute | solution.py:1057
  5.2 3.5 %collective-permute-start = (bf16[208,128]{1,0:T(8,128)(2,1)S(1)}, bf16[208,128]{1,0:T(8,128)(2,1)S(1)}, u32[]{:S(2)}, u32[]{:S(2)}) collective-permute-start(bf16[208,128]{1,0:T(8,128)(2,1)S(1)} %fusion.21.rest_0_), channel_id=1, source_target_pairs={{0,1},{1,0},{2,3},{3,2},{4,5},{5,4},{6,7},{7,6},{8,9},{9,8},{10,11... | collective-permute-start | bytes 159752 | tf_op jit(solution)/shard_map/ppermute | solution.py:1057
  5.2 9.6 %collective-permute-start.3 = (bf16[192,768]{1,0:T(8,128)(2,1)}, bf16[192,768]{1,0:T(8,128)(2,1)S(1)}, u32[]{:S(2)}, u32[]{:S(2)}) collective-permute-start(bf16[192,768]{1,0:T(8,128)(2,1)} %rest_2_.1), channel_id=1, source_target_pairs={{0,2},{1,3},{2,0},{3,1},{4,6},{5,7},{6,4},{7,5},{8,10},{9,11},{10,... | collective-permute-start | bytes 884744 | tf_op jit(solution)/shard_map/ppermute | solution.py:1057
  14.8 34.4 %all-to-all-start = ((bf16[8,544,128]{2,1,0:T(8,128)(2,1)}), bf16[8,544,128]{2,1,0:T(8,128)(2,1)S(1)}, u32[]{:S(2)}, u32[]{:S(2)}) async-start(bf16[8,544,128]{2,1,0:T(8,128)(2,1)} %get-tuple-element.221), calls=%async_computation | async-start | bytes 2228224 | tf_op jit(solution)/shard_map/all_to_all | solution.py:1219
  23.8 25.4 %collective-permute-start.4 = (bf16[1536,256]{1,0:T(8,128)(2,1)}, bf16[1536,256]{1,0:T(8,128)(2,1)}, u32[]{:S(2)}, u32[]{:S(2)}) collective-permute-start(bf16[1536,256]{1,0:T(8,128)(2,1)} %get-tuple-element.224.refs_1_), channel_id=1, source_target_pairs={{0,2},{1,3},{2,0},{3,1},{4,6},{5,7},{6,4},{7,5},{8,10},{9,11},{10,... | collective-permute-start | bytes 2359304 | tf_op jit(solution)/shard_map/ppermute | solution.py:1057
  24.6 2.0 collective-permute-start.7
  25.1 24.1 %collective-permute-start.5 = (bf16[192,768]{1,0:T(8,128)(2,1)S(1)}, bf16[192,768]{1,0:T(8,128)(2,1)S(1)}, u32[]{:S(2)}, u32[]{:S(2)}) collective-permute-start(bf16[192,768]{1,0:T(8,128)(2,1)S(1)} %copy-done.9), channel_id=1, source_target_pairs={{0,2},{1,3},{2,0},{3,1},{4,6},{5,7},{6,4},{7,5},{8,10},{9,11},{10,... | collective-permute-start | bytes 884744 | tf_op jit(solution)/shard_map/ppermute | solution.py:1057
  49.2 18.4 %collective-permute-start.8 = (bf16[1536,256]{1,0:T(8,128)(2,1)}, bf16[1536,256]{1,0:T(8,128)(2,1)}, u32[]{:S(2)}, u32[]{:S(2)}) collective-permute-start(bf16[1536,256]{1,0:T(8,128)(2,1)} %get-tuple-element.233.refs_5_), channel_id=1, source_target_pairs={{0,2},{1,3},{2,0},{3,1},{4,6},{5,7},{6,4},{7,5},{8,10},{9,11},{10,... | collective-permute-start | bytes 2359304 | tf_op jit(solution)/shard_map/ppermute | solution.py:1057
  50.6 18.9 %collective-permute-start.9 = (bf16[1536,256]{1,0:T(8,128)(2,1)}, bf16[1536,256]{1,0:T(8,128)(2,1)}, u32[]{:S(2)}, u32[]{:S(2)}) collective-permute-start(bf16[1536,256]{1,0:T(8,128)(2,1)} %get-tuple-element.224.refs_1_), channel_id=1, source_target_pairs={{0,1},{1,0},{2,3},{3,2},{4,5},{5,4},{6,7},{7,6},{8,9},{9,8},{10,11... | collective-permute-start | bytes 2359304 | tf_op jit(solution)/shard_map/ppermute | solution.py:1057
  50.6 17.1 %collective-permute-start.13 = (bf16[192,768]{1,0:T(8,128)(2,1)S(1)}, bf16[192,768]{1,0:T(8,128)(2,1)S(1)}, u32[]{:S(2)}, u32[]{:S(2)}) collective-permute-start(bf16[192,768]{1,0:T(8,128)(2,1)S(1)} %copy-done.9), channel_id=1, source_target_pairs={{0,1},{1,0},{2,3},{3,2},{4,5},{5,4},{6,7},{7,6},{8,9},{9,8},{10,11... | collective-permute-start | bytes 884744 | tf_op jit(solution)/shard_map/ppermute | solution.py:1057
  51.1 20.0 %collective-permute-start.11 = (bf16[1536,256]{1,0:T(8,128)(2,1)}, bf16[1536,256]{1,0:T(8,128)(2,1)}, u32[]{:S(2)}, u32[]{:S(2)}) collective-permute-start(bf16[1536,256]{1,0:T(8,128)(2,1)} %get-tuple-element.233.refs_5_), channel_id=1, source_target_pairs={{0,1},{1,0},{2,3},{3,2},{4,5},{5,4},{6,7},{7,6},{8,9},{9,8},{10,11... | collective-permute-start | bytes 2359304 | tf_op jit(solution)/shard_map/ppermute | solution.py:1057
  51.1 20.0 %collective-permute-start.10 = (bf16[1536,256]{1,0:T(8,128)(2,1)}, bf16[1536,256]{1,0:T(8,128)(2,1)}, u32[]{:S(2)}, u32[]{:S(2)}) collective-permute-start(bf16[1536,256]{1,0:T(8,128)(2,1)} %collective-permute-done.4.refs_3_), channel_id=1, source_target_pairs={{0,1},{1,0},{2,3},{3,2},{4,5},{5,4},{6,7},{7,6},{8,9},{9,8},{10,11... | collective-permute-start | bytes 2359304 | tf_op jit(solution)/shard_map/ppermute | solution.py:1057
  67.7 3.4 %collective-permute-start.12 = (bf16[1536,256]{1,0:T(8,128)(2,1)}, bf16[1536,256]{1,0:T(8,128)(2,1)S(1)}, u32[]{:S(2)}, u32[]{:S(2)}) collective-permute-start(bf16[1536,256]{1,0:T(8,128)(2,1)} %collective-permute-done.8.refs_7_), channel_id=1, source_target_pairs={{0,1},{1,0},{2,3},{3,2},{4,5},{5,4},{6,7},{7,6},{8,9},{9,8},{10,11... | collective-permute-start | bytes 2359304 | tf_op jit(solution)/shard_map/ppermute | solution.py:1057
  67.7 25.8 %collective-permute-start.15 = (bf16[1536,256]{1,0:T(8,128)(2,1)S(1)}, bf16[1536,256]{1,0:T(8,128)(2,1)S(1)}, u32[]{:S(2)}, u32[]{:S(2)}) collective-permute-start(bf16[1536,256]{1,0:T(8,128)(2,1)S(1)} %copy-done.17), channel_id=1, source_target_pairs={{0,2},{1,3},{2,0},{3,1},{4,6},{5,7},{6,4},{7,5},{8,10},{9,11},{10,... | collective-permute-start | bytes 2359304 | tf_op jit(solution)/shard_map/ppermute | solution.py:1057
  94.4 3.6 %collective-permute-start.16 = (bf16[2,2,4,192,256]{4,3,2,1,0:T(8,128)(2,1)}, bf16[2,2,4,192,256]{4,3,2,1,0:T(8,128)(2,1)S(1)}, u32[]{:S(2)}, u32[]{:S(2)}) collective-permute-start(bf16[2,2,4,192,256]{4,3,2,1,0:T(8,128)(2,1)} %bitcast.121), channel_id=1, source_target_pairs={{0,1},{1,0},{2,3},{3,2},{4,5},{5,4},{6,7},{7,6},{8,9},{9,8},{10,11... | collective-permute-start | bytes 4718600 | tf_op jit(solution)/shard_map/ppermute | solution.py:1057
  94.7 6.1 %collective-permute-start.17 = (bf16[2,2,4,192,256]{4,3,2,1,0:T(8,128)(2,1)}, bf16[2,2,4,192,256]{4,3,2,1,0:T(8,128)(2,1)S(1)}, u32[]{:S(2)}, u32[]{:S(2)}) collective-permute-start(bf16[2,2,4,192,256]{4,3,2,1,0:T(8,128)(2,1)} %bitcast.120), channel_id=1, source_target_pairs={{0,1},{1,0},{2,3},{3,2},{4,5},{5,4},{6,7},{7,6},{8,9},{9,8},{10,11... | collective-permute-start | bytes 4718600 | tf_op jit(solution)/shard_map/ppermute | solution.py:1057
  95.0 8.9 %collective-permute-start.18 = (bf16[1536,256]{1,0:T(8,128)(2,1)}, bf16[1536,256]{1,0:T(8,128)(2,1)S(1)}, u32[]{:S(2)}, u32[]{:S(2)}) collective-permute-start(bf16[1536,256]{1,0:T(8,128)(2,1)} %get-tuple-element.247.refs_1_), channel_id=1, source_target_pairs={{0,1},{1,0},{2,3},{3,2},{4,5},{5,4},{6,7},{7,6},{8,9},{9,8},{10,11... | collective-permute-start | bytes 2359304 | tf_op jit(solution)/shard_map/ppermute | solution.py:1057
  95.2 8.6 %collective-permute-start.19 = (bf16[1536,256]{1,0:T(8,128)(2,1)}, bf16[1536,256]{1,0:T(8,128)(2,1)S(1)}, u32[]{:S(2)}, u32[]{:S(2)}) collective-permute-start(bf16[1536,256]{1,0:T(8,128)(2,1)} %copy-done.18), channel_id=1, source_target_pairs={{0,1},{1,0},{2,3},{3,2},{4,5},{5,4},{6,7},{7,6},{8,9},{9,8},{10,11... | collective-permute-start | bytes 2359304 | tf_op jit(solution)/shard_map/ppermute | solution.py:1057
  101.3 21.2 %collective-permute-start.21 = (bf16[2,4,192,256]{3,2,1,0:T(8,128)(2,1)S(1)}, bf16[2,4,192,256]{3,2,1,0:T(8,128)(2,1)S(1)}, u32[]{:S(2)}, u32[]{:S(2)}) collective-permute-start(bf16[2,4,192,256]{3,2,1,0:T(8,128)(2,1)S(1)} %get-tuple-element.297), channel_id=1, source_target_pairs={{0,4},{4,0},{8,12},{12,8},{16,20},{20,16},{24,28},{28,24},{1,5},{5... | collective-permute-start | bytes 2359304 | tf_op jit(solution)/shard_map/ppermute | solution.py:1057
  102.8 19.7 %collective-permute-start.20 = (bf16[2,4,192,256]{3,2,1,0:T(8,128)(2,1)}, bf16[2,4,192,256]{3,2,1,0:T(8,128)(2,1)S(1)}, u32[]{:S(2)}, u32[]{:S(2)}) collective-permute-start(bf16[2,4,192,256]{3,2,1,0:T(8,128)(2,1)} %get-tuple-element.296), channel_id=1, source_target_pairs={{0,2},{1,3},{2,0},{3,1},{4,6},{5,7},{6,4},{7,5},{8,10},{9,11},{10,... | collective-permute-start | bytes 2359304 | tf_op jit(solution)/shard_map/ppermute | solution.py:1057
  122.5 4.6 %collective-permute-start.22 = (bf16[2,2,4,272,256]{4,3,2,1,0:T(8,128)(2,1)}, bf16[2,2,4,272,256]{4,3,2,1,0:T(8,128)(2,1)S(1)}, u32[]{:S(2)}, u32[]{:S(2)}) collective-permute-start(bf16[2,2,4,272,256]{4,3,2,1,0:T(8,128)(2,1)} %bitcast.118), channel_id=1, source_target_pairs={{0,1},{1,0},{2,3},{3,2},{4,5},{5,4},{6,7},{7,6},{8,9},{9,8},{10,11... | collective-permute-start | bytes 6684680 | tf_op jit(solution)/shard_map/ppermute | solution.py:1057
  128.5 12.3 %collective-permute-start.25 = (bf16[2,4,96,256]{3,2,1,0:T(8,128)(2,1)}, bf16[2,4,96,256]{3,2,1,0:T(8,128)(2,1)}, u32[]{:S(2)}, u32[]{:S(2)}) collective-permute-start(bf16[2,4,96,256]{3,2,1,0:T(8,128)(2,1)} %add_convert_fusion.8), channel_id=1, source_target_pairs={{0,2},{1,3},{2,0},{3,1},{4,6},{5,7},{6,4},{7,5},{8,10},{9,11},{10,... | collective-permute-start | bytes 1179656 | tf_op jit(solution)/shard_map/ppermute | solution.py:1057
  129.5 11.3 %collective-permute-start.23 = (bf16[4,192,256]{2,1,0:T(8,128)(2,1)}, bf16[4,192,256]{2,1,0:T(8,128)(2,1)}, u32[]{:S(2)}, u32[]{:S(2)}) collective-permute-start(bf16[4,192,256]{2,1,0:T(8,128)(2,1)} %get-tuple-element.317), channel_id=1, source_target_pairs={{0,4},{4,0},{8,12},{12,8},{16,20},{20,16},{24,28},{28,24},{1,5},{5... | collective-permute-start | bytes 1179656 | tf_op jit(solution)/shard_map/ppermute | solution.py:1057
  130.0 18.3 %collective-permute-start.24 = (bf16[4,192,256]{2,1,0:T(8,128)(2,1)}, bf16[4,192,256]{2,1,0:T(8,128)(2,1)}, u32[]{:S(2)}, u32[]{:S(2)}) collective-permute-start(bf16[4,192,256]{2,1,0:T(8,128)(2,1)} %get-tuple-element.318), channel_id=1, source_target_pairs={{0,2},{1,3},{2,0},{3,1},{4,6},{5,7},{6,4},{7,5},{8,10},{9,11},{10,... | collective-permute-start | bytes 1179656 | tf_op jit(solution)/shard_map/ppermute | solution.py:1057
  150.8 21.4 %collective-permute-start.29 = (bf16[2,4,176,256]{3,2,1,0:T(8,128)(2,1)S(1)}, bf16[2,4,176,256]{3,2,1,0:T(8,128)(2,1)S(1)}, u32[]{:S(2)}, u32[]{:S(2)}) collective-permute-start(bf16[2,4,176,256]{3,2,1,0:T(8,128)(2,1)S(1)} %add_convert_fusion.5), channel_id=1, source_target_pairs={{0,2},{1,3},{2,0},{3,1},{4,6},{5,7},{6,4},{7,5},{8,10},{9,11},{10,... | collective-permute-start | bytes 2162696 | tf_op jit(solution)/shard_map/ppermute | solution.py:1057
  151.9 20.3 %collective-permute-start.30 = (bf16[4,256,128]{2,1,0:T(8,128)(2,1)S(1)}, bf16[4,256,128]{2,1,0:T(8,128)(2,1)S(1)}, u32[]{:S(2)}, u32[]{:S(2)}) collective-permute-start(bf16[4,256,128]{2,1,0:T(8,128)(2,1)S(1)} %copy-done.31), channel_id=1, source_target_pairs={{0,4},{4,0},{8,12},{12,8},{16,20},{20,16},{24,28},{28,24},{1,5},{5... | collective-permute-start | bytes 786440 | tf_op jit(solution)/shard_map/ppermute | solution.py:1057
  152.5 13.2 %collective-permute-start.26 = (bf16[2,192,256]{2,1,0:T(8,128)(2,1)S(1)}, bf16[2,192,256]{2,1,0:T(8,128)(2,1)S(1)}, u32[]{:S(2)}, u32[]{:S(2)}) collective-permute-start(bf16[2,192,256]{2,1,0:T(8,128)(2,1)S(1)} %pad_maximum_fusion.5), channel_id=1, source_target_pairs={{0,8},{4,12},{8,0},{12,4},{16,24},{20,28},{24,16},{28,20},{1,9},{5... | collective-permute-start | bytes 589832 | tf_op jit(solution)/shard_map/ppermute | solution.py:1057
  153.9 18.3 %collective-permute-start.27 = (bf16[2,192,256]{2,1,0:T(8,128)(2,1)S(1)}, bf16[2,192,256]{2,1,0:T(8,128)(2,1)S(1)}, u32[]{:S(2)}, u32[]{:S(2)}) collective-permute-start(bf16[2,192,256]{2,1,0:T(8,128)(2,1)S(1)} %pad_maximum_fusion.6), channel_id=1, source_target_pairs={{0,16},{4,20},{8,24},{12,28},{16,0},{20,4},{24,8},{28,12},{1,17},{... | collective-permute-start | bytes 589832 | tf_op jit(solution)/shard_map/ppermute | solution.py:1057
  157.9 14.2 %collective-permute-start.28 = (bf16[2,192,256]{2,1,0:T(8,128)(2,1)S(1)}, bf16[2,192,256]{2,1,0:T(8,128)(2,1)S(1)}, u32[]{:S(2)}, u32[]{:S(2)}) collective-permute-start(bf16[2,192,256]{2,1,0:T(8,128)(2,1)S(1)} %pad_maximum_fusion.7), channel_id=1, source_target_pairs={{0,24},{4,28},{8,16},{12,20},{16,8},{20,12},{24,0},{28,4},{1,25},{... | collective-permute-start | bytes 589832 | tf_op jit(solution)/shard_map/ppermute | solution.py:1057
  172.2 7.8 %collective-permute-start.31 = (bf16[4,256,128]{2,1,0:T(8,128)(2,1)}, bf16[4,256,128]{2,1,0:T(8,128)(2,1)S(1)}, u32[]{:S(2)}, u32[]{:S(2)}) collective-permute-start(bf16[4,256,128]{2,1,0:T(8,128)(2,1)} %get-tuple-element.355), channel_id=1, source_target_pairs={{0,4},{4,0},{8,12},{12,8},{16,20},{20,16},{24,28},{28,24},{1,5},{5... | collective-permute-start | bytes 786440 | tf_op jit(solution)/shard_map/ppermute | solution.py:1057
  180.0 9.1 %collective-permute-start.32 = (bf16[2,2,4,72,256]{4,3,2,1,0:T(8,128)(2,1)}, bf16[2,2,4,72,256]{4,3,2,1,0:T(8,128)(2,1)S(1)}, u32[]{:S(2)}, u32[]{:S(2)}) collective-permute-start(bf16[2,2,4,72,256]{4,3,2,1,0:T(8,128)(2,1)} %bitcast.123), channel_id=1, source_target_pairs={{0,1},{1,0},{2,3},{3,2},{4,5},{5,4},{6,7},{7,6},{8,9},{9,8},{10,11... | collective-permute-start | bytes 1769480 | tf_op jit(solution)/shard_map/ppermute | solution.py:1057
  181.1 22.9 %all-to-all-start.1 = ((bf16[4,2,256,128]{3,2,1,0:T(8,128)(2,1)}), bf16[4,2,256,128]{3,2,1,0:T(8,128)(2,1)S(1)}, u32[]{:S(2)}, u32[]{:S(2)}) async-start(bf16[4,2,256,128]{3,2,1,0:T(8,128)(2,1)} %pad_maximum_fusion.2), calls=%async_computation.1 | async-start | bytes 1048576 | tf_op jit(solution)/shard_map/all_to_all | solution.py:1291
  188.9 15.0 %collective-permute-start.33 = (bf16[4,272,256]{2,1,0:T(8,128)(2,1)}, bf16[4,272,256]{2,1,0:T(8,128)(2,1)S(1)}, u32[]{:S(2)}, u32[]{:S(2)}) collective-permute-start(bf16[4,272,256]{2,1,0:T(8,128)(2,1)} %get-tuple-element.367), channel_id=1, source_target_pairs={{0,4},{4,0},{8,12},{12,8},{16,20},{20,16},{24,28},{28,24},{1,5},{5... | collective-permute-start | bytes 1671176 | tf_op jit(solution)/shard_map/ppermute | solution.py:1057
  189.3 25.7 %collective-permute-start.37 = (bf16[2,4,72,256]{3,2,1,0:T(8,128)(2,1)S(1)}, bf16[2,4,72,256]{3,2,1,0:T(8,128)(2,1)S(1)}, u32[]{:S(2)}, u32[]{:S(2)}) collective-permute-start(bf16[2,4,72,256]{3,2,1,0:T(8,128)(2,1)S(1)} %get-tuple-element.384), channel_id=1, source_target_pairs={{0,2},{1,3},{2,0},{3,1},{4,6},{5,7},{6,4},{7,5},{8,10},{9,11},{10,... | collective-permute-start | bytes 884744 | tf_op jit(solution)/shard_map/ppermute | solution.py:1057
  204.0 14.2 %collective-permute-start.34 = (bf16[1,272,256]{2,1,0:T(8,128)(2,1)S(1)}, bf16[1,272,256]{2,1,0:T(8,128)(2,1)S(1)}, u32[]{:S(2)}, u32[]{:S(2)}) collective-permute-start(bf16[1,272,256]{2,1,0:T(8,128)(2,1)S(1)} %get-tuple-element.381), channel_id=1, source_target_pairs={{0,8},{4,12},{8,0},{12,4},{16,24},{20,28},{24,16},{28,20},{1,9},{5... | collective-permute-start | bytes 417800 | tf_op jit(solution)/shard_map/ppermute | solution.py:1057
  205.8 12.7 %collective-permute-start.35 = (bf16[1,272,256]{2,1,0:T(8,128)(2,1)S(1)}, bf16[1,272,256]{2,1,0:T(8,128)(2,1)S(1)}, u32[]{:S(2)}, u32[]{:S(2)}) collective-permute-start(bf16[1,272,256]{2,1,0:T(8,128)(2,1)S(1)} %get-tuple-element.382), channel_id=1, source_target_pairs={{0,16},{4,20},{8,24},{12,28},{16,0},{20,4},{24,8},{28,12},{1,17},{... | collective-permute-start | bytes 417800 | tf_op jit(solution)/shard_map/ppermute | solution.py:1057
  208.2 10.6 %collective-permute-start.36 = (bf16[1,272,256]{2,1,0:T(8,128)(2,1)S(1)}, bf16[1,272,256]{2,1,0:T(8,128)(2,1)S(1)}, u32[]{:S(2)}, u32[]{:S(2)}) collective-permute-start(bf16[1,272,256]{2,1,0:T(8,128)(2,1)S(1)} %get-tuple-element.383), channel_id=1, source_target_pairs={{0,24},{4,28},{8,16},{12,20},{16,8},{20,12},{24,0},{28,4},{1,25},{... | collective-permute-start | bytes 417800 | tf_op jit(solution)/shard_map/ppermute | solution.py:1057
  208.5 14.0 %collective-permute-start.39 = (bf16[2,192,256]{2,1,0:T(8,128)(2,1)S(1)}, bf16[2,192,256]{2,1,0:T(8,128)(2,1)S(1)}, u32[]{:S(2)}, u32[]{:S(2)}) collective-permute-start(bf16[2,192,256]{2,1,0:T(8,128)(2,1)S(1)} %add_convert_fusion.18), channel_id=1, source_target_pairs={{0,8},{4,12},{8,0},{12,4},{16,24},{20,28},{24,16},{28,20},{1,9},{5... | collective-permute-start | bytes 589832 | tf_op jit(solution)/shard_map/ppermute | solution.py:1057
  215.0 19.2 %collective-permute-start.40 = (bf16[2,192,256]{2,1,0:T(8,128)(2,1)S(1)}, bf16[2,192,256]{2,1,0:T(8,128)(2,1)S(1)}, u32[]{:S(2)}, u32[]{:S(2)}) collective-permute-start(bf16[2,192,256]{2,1,0:T(8,128)(2,1)S(1)} %add_convert_fusion.18), channel_id=1, source_target_pairs={{0,16},{4,20},{8,24},{12,28},{16,0},{20,4},{24,8},{28,12},{1,17},{... | collective-permute-start | bytes 589832 | tf_op jit(solution)/shard_map/ppermute | solution.py:1057
  218.3 16.0 %collective-permute-start.41 = (bf16[2,192,256]{2,1,0:T(8,128)(2,1)S(1)}, bf16[2,192,256]{2,1,0:T(8,128)(2,1)S(1)}, u32[]{:S(2)}, u32[]{:S(2)}) collective-permute-start(bf16[2,192,256]{2,1,0:T(8,128)(2,1)S(1)} %add_convert_fusion.18), channel_id=1, source_target_pairs={{0,24},{4,28},{8,16},{12,20},{16,8},{20,12},{24,0},{28,4},{1,25},{... | collective-permute-start | bytes 589832 | tf_op jit(solution)/shard_map/ppermute | solution.py:1057
  221.4 13.0 %collective-permute-start.42 = (bf16[2,4,24,256]{3,2,1,0:T(8,128)(2,1)S(1)}, bf16[2,4,24,256]{3,2,1,0:T(8,128)(2,1)S(1)}, u32[]{:S(2)}, u32[]{:S(2)}) collective-permute-start(bf16[2,4,24,256]{3,2,1,0:T(8,128)(2,1)S(1)} %get-tuple-element.405), channel_id=1, source_target_pairs={{0,2},{1,3},{2,0},{3,1},{4,6},{5,7},{6,4},{7,5},{8,10},{9,11},{10,... | collective-permute-start | bytes 294920 | tf_op jit(solution)/shard_map/ppermute | solution.py:1057
  235.3 20.5 %all-to-all-start.2 = ((bf16[8,96,256]{2,1,0:T(8,128)(2,1)}), bf16[8,96,256]{2,1,0:T(8,128)(2,1)S(1)}, u32[]{:S(2)}, u32[]{:S(2)}) async-start(bf16[8,96,256]{2,1,0:T(8,128)(2,1)} %pad_maximum_fusion.3), calls=%async_computation.2 | async-start | bytes 786432 | tf_op jit(solution)/shard_map/all_to_all | solution.py:1317
  241.2 21.4 %collective-permute-start.43 = (bf16[1,272,256]{2,1,0:T(8,128)(2,1)S(1)}, bf16[1,272,256]{2,1,0:T(8,128)(2,1)S(1)}, u32[]{:S(2)}, u32[]{:S(2)}) collective-permute-start(bf16[1,272,256]{2,1,0:T(8,128)(2,1)S(1)} %add_convert_fusion.19), channel_id=1, source_target_pairs={{0,8},{4,12},{8,0},{12,4},{16,24},{20,28},{24,16},{28,20},{1,9},{5... | collective-permute-start | bytes 417800 | tf_op jit(solution)/shard_map/ppermute | solution.py:1057
  243.3 21.9 %collective-permute-start.44 = (bf16[1,272,256]{2,1,0:T(8,128)(2,1)S(1)}, bf16[1,272,256]{2,1,0:T(8,128)(2,1)S(1)}, u32[]{:S(2)}, u32[]{:S(2)}) collective-permute-start(bf16[1,272,256]{2,1,0:T(8,128)(2,1)S(1)} %add_convert_fusion.19), channel_id=1, source_target_pairs={{0,16},{4,20},{8,24},{12,28},{16,0},{20,4},{24,8},{28,12},{1,17},{... | collective-permute-start | bytes 417800 | tf_op jit(solution)/shard_map/ppermute | solution.py:1057
  245.6 19.5 %collective-permute-start.45 = (bf16[1,272,256]{2,1,0:T(8,128)(2,1)S(1)}, bf16[1,272,256]{2,1,0:T(8,128)(2,1)S(1)}, u32[]{:S(2)}, u32[]{:S(2)}) collective-permute-start(bf16[1,272,256]{2,1,0:T(8,128)(2,1)S(1)} %add_convert_fusion.19), channel_id=1, source_target_pairs={{0,24},{4,28},{8,16},{12,20},{16,8},{20,12},{24,0},{28,4},{1,25},{... | collective-permute-start | bytes 417800 | tf_op jit(solution)/shard_map/ppermute | solution.py:1057
  245.7 23.7 %collective-permute-start.46 = (bf16[4,2,192,256]{3,2,1,0:T(8,128)(2,1)S(1)}, bf16[4,2,192,256]{3,2,1,0:T(8,128)(2,1)S(1)}, u32[]{:S(2)}, u32[]{:S(2)}) collective-permute-start(bf16[4,2,192,256]{3,2,1,0:T(8,128)(2,1)S(1)} %pad_maximum_fusion.own), channel_id=1, source_target_pairs={{0,4},{4,0},{8,12},{12,8},{16,20},{20,16},{24,28},{28,24},{1,5},{5... | collective-permute-start | bytes 2359304 | tf_op jit(solution)/shard_map/ppermute | solution.py:1057
  256.7 24.9 %all-to-all-start.3 = ((bf16[8,96,256]{2,1,0:T(8,128)(2,1)}), bf16[8,96,256]{2,1,0:T(8,128)(2,1)S(1)}, u32[]{:S(2)}, u32[]{:S(2)}) async-start(bf16[8,96,256]{2,1,0:T(8,128)(2,1)} %broadcast_in_dim.3), calls=%async_computation.3 | async-start | bytes 786432 | tf_op jit(solution)/shard_map/all_to_all | solution.py:1321
  265.2 16.3 %collective-permute-start.47 = (bf16[4,1,272,256]{3,2,1,0:T(8,128)(2,1)S(1)}, bf16[4,1,272,256]{3,2,1,0:T(8,128)(2,1)S(1)}, u32[]{:S(2)}, u32[]{:S(2)}) collective-permute-start(bf16[4,1,272,256]{3,2,1,0:T(8,128)(2,1)S(1)} %pad_maximum_fusion.1.own), channel_id=1, source_target_pairs={{0,4},{4,0},{8,12},{12,8},{16,20},{20,16},{24,28},{28,24},{1,5},{5... | collective-permute-start | bytes 1671176 | tf_op jit(solution)/shard_map/ppermute | solution.py:1057
  (36 other events, 204.0 us)

commit v8 on v7

--- a/solution.py
+++ b/solution.py
@@ -970,8 +970,8 @@
 
 
 def final_kernel(
-    place_ref, own, other, late, down_in, up_in,
-    down_out, up_out, mixing_out, query_out, shared_out, gains_out,
+    place_ref, spot_ref, own, other, late, down_in, up_in,
+    down_out, up_out, mixing_out, query_out, shared_out, first_out, second_out,
     whole, down_part, up_part, sems,
     *, chunks, pieces, query_rows,
 ):
@@ -987,6 +987,17 @@
     def load(begin, rows):
         for c in range(late.shape[0]):
             whole[c * rows : (c + 1) * rows, :] = late[c, begin : begin + rows, :].astype(F32)
+
+    def own_gain(out, row, begin):
+        lines = [
+            whole[row + i : row + i + 1, begin : begin + LANES] for i in range(width // LANES)
+        ]
+        vector = jnp.concatenate(lines, axis=1)
+        total = jnp.zeros((1, height), F32)
+        for o in range(pieces):
+            mine = vector[:, o * height : (o + 1) * height]
+            total = jnp.where(spot_ref[0] == o, mine, total)
+        out[...] = total
 
     put_halves(whole, own, other, 0, place, place >> 1)
     columns(down_part, 0, TILE)
@@ -1005,19 +1016,17 @@
         one.start()
     columns(mixing_out, 2 * width, height)
     row = 2 * width + groups * height
-    for i in range(width // LANES):
-        gains_out[1:2, i * LANES : (i + 1) * LANES] = whole[row + i : row + i + 1, 0:LANES]
+    own_gain(second_out, row, 0)
     load(0, query_rows)
     columns(query_out, 0, height)
     load(query_rows, late.shape[1] - query_rows)
     shared_out[...] = whole[0:height, 0:LANES]
-    for i in range(width // LANES):
-        gains_out[0:1, i * LANES : (i + 1) * LANES] = whole[i : i + 1, LANES:]
+    own_gain(first_out, 0, LANES)
     for one in copies:
         one.wait()
 
 
-def final_stage(place, own, other, late, down, up, query_rows, chunks, pieces, width):
+def final_stage(place, spot, own, other, late, down, up, query_rows, chunks, pieces, width):
     height = width // pieces
     shape = lambda *dims: jax.ShapeDtypeStruct(dims, F32)
     tallest = max(2 * own.shape[0] * own.shape[2], late.shape[0] * late.shape[1])
@@ -1027,10 +1036,10 @@
             final_kernel, chunks=chunks, pieces=pieces, query_rows=query_rows
         ),
         grid_spec=pltpu.PrefetchScalarGridSpec(
-            num_scalar_prefetch=1,
+            num_scalar_prefetch=2,
             grid=(),
             in_specs=[vmem] * 3 + [anywhere] * 2,
-            out_specs=[anywhere] * 2 + [vmem] * 4,
+            out_specs=[anywhere] * 2 + [vmem] * 5,
             scratch_shapes=[
                 pltpu.VMEM((tallest, TILE), F32),
                 pltpu.VMEM((TILE, width), F32),
@@ -1044,13 +1053,14 @@
             shape(height, width),
             shape(height, width),
             shape(height, LANES),
-            shape(2, width),
+            shape(1, height),
+            shape(1, height),
         ],
-        input_output_aliases={4: 0, 5: 1},
+        input_output_aliases={5: 0, 6: 1},
         compiler_params=params(),
         cost_estimate=weight(),
         name="final",
-    )(place, own, other, late, down, up)
+    )(place, spot, own, other, late, down, up)
 
 
 def swap(values, axis, size, mask):
@@ -1324,8 +1334,9 @@
         place_one, zero.held, zero.coming[0], chunks, wt_size, width
     )
     down_grad, up_grad, two.coming = lax.optimization_barrier((down_grad, up_grad, two.coming))
-    down_grad, up_grad, mixing_grad, query_grad, shared_grad, gain_grads = final_stage(
+    down_grad, up_grad, mixing_grad, query_grad, shared_grad, first_grad, second_grad = final_stage(
         place_one,
+        spot,
         two.held,
         two.coming[0],
         late,
@@ -1336,15 +1347,14 @@
         wt_size,
         width,
     )
-    gain_grads = lax.dynamic_slice_in_dim(gain_grads, spot_index * height, height, 1)
     return (
         arrays["layer_out"].reshape(seqs, rows, width),
         input_grad.reshape(seqs, rows, width),
-        gain_grads[0],
+        first_grad.reshape(height),
         query_grad,
         shared_grad,
         mixing_grad,
-        gain_grads[1],
+        second_grad.reshape(height),
         up_grad,
         down_grad,
     )

time: 288 us -> 289 us (level)
  transfers between devices with their start and end apart: 52 -> 52, of which waited for: 19 -> 20; matrix products, arithmetic and copies ran while one was open for 5% -> 5% of each run, Pallas kernels for 29% -> 29%
where the time goes in v8:
time: 289 us
  waiting for transfers between devices  100 us (35%)
  Pallas kernels  87.8 us (30%)
  starting transfers between devices  72.5 us (25%)
  other arithmetic  15.5 us (5%)
  local copies, waits for them, and re-layouts  11.6 us (4%)
    ppermute x48, waiting for transfers between devices, swap(): return lax.ppermute(values, axis, [(i, i ^ mask) for i in range(size)])  92 us
    ppermute x48, starting transfers between devices, swap(): return lax.ppermute(values, axis, [(i, i ^ mask) for i in range(size)])  46.1 us
    pallas_call x2, Pallas kernels, feed_stage(): pl.pallas_call(functools.partial(feed_kernel, pieces=pieces, part=part, f...  38.3 us
    pallas_call x2, Pallas kernels, attend_back(): pl.pallas_call(functools.partial(attend_back_kernel, seq=seq, blocks=bloc...  13 us
    all_to_all x1, starting transfers between devices, body(): lax.all_to_all(arriving, 'ctx', 0, 0, axis_index_groups=[list(range(x, ct...  8.67 us
    pallas_call x1, Pallas kernels, attend(): pl.pallas_call(functools.partial(attend_kernel, blocks=blocks, tile_rows=...  8.37 us
    all_to_all x1, waiting for transfers between devices, body(): late = lax.all_to_all(late, 'ctx', 0, 0)  8.2 us
    unnamed x65, local copies, waits for them, and re-layouts  7.93 us
  transfers between devices with their start and end apart: 52, of which 20 were waited for; matrix products, arithmetic and copies ran while one was open for 5% of the time, Pallas kernels for 29%

profile of v8, /device:TPU:0, one launch (start us, length us, event | category | flops | bytes accessed | tf_op | source)
XLA Modules:
  0.0 289.0 jit_solution(11176616579364121179)
XLA Ops:
  2.1 3.0 %collective-permute-start.1 = (bf16[208,128]{1,0:T(8,128)(2,1)S(1)}, bf16[208,128]{1,0:T(8,128)(2,1)S(1)}, u32[]{:S(2)}, u32[]{:S(2)}) collective-permute-start(bf16[208,128]{1,0:T(8,128)(2,1)S(1)} %fusion.21.rest_0_), channel_id=1, source_target_pairs={{0,2},{1,3},{2,0},{3,1},{4,6},{5,7},{6,4},{7,5},{8,10},{9,11},{10,... | collective-permute-start | bytes 159752 | tf_op jit(solution)/shard_map/ppermute | solution.py:1067
  5.3 2.0 collective-permute-done.1.rest_2_
  9.5 3.5 %first_norm.1 = (bf16[512,768]{1,0:T(8,128)(2,1)}, bf16[8,544,128]{2,1,0:T(8,128)(2,1)}) custom-call(s32[1]{0:T(128)} %bitcast.spot_ref, bf16[512,768]{1,0:T(8,128)(2,1)} %bitcast.87, f32[1,768]{1,0:T(1,128)} %reshape_squeeze.6.gain, bf16[2,2,128]{2,1,0:T(2,128)(2,1)} %reshape.189.documents, bf16[208,128]{1,0:T(8,128)(2,1)} %copy-done.25, ...), custom_call_target="tpu_custom_call" | custom-call | flops 1 | bytes 1 | tf_op jit(solution)/shard_map/first_norm/pallas_call | solution.py:144
  13.1 1.7 collective-permute-done.3.rest_2_.rest_4_
  14.8 5.8 %all-to-all-start = ((bf16[8,544,128]{2,1,0:T(8,128)(2,1)}), bf16[8,544,128]{2,1,0:T(8,128)(2,1)S(1)}, u32[]{:S(2)}, u32[]{:S(2)}) async-start(bf16[8,544,128]{2,1,0:T(8,128)(2,1)} %get-tuple-element.222), calls=%async_computation | async-start | bytes 2228224 | tf_op jit(solution)/shard_map/all_to_all | solution.py:1229
  20.6 3.1 %pack.1 = (bf16[1536,256]{1,0:T(8,128)(2,1)}, bf16[1536,256]{1,0:T(8,128)(2,1)}, bf16[1536,256]{1,0:T(8,128)(2,1)}) custom-call(bf16[192,3072]{1,0:T(8,128)(2,1)} %up, bf16[768,768]{1,0:T(8,128)(2,1)} %down), custom_call_target="tpu_custom_call" | custom-call | flops 1 | bytes 1 | tf_op jit(solution)/shard_map/pack/pallas_call | solution.py:95
  25.1 1.2 collective-permute-start.5
  27.3 3.3 %project.1 = bf16[512,768]{1,0:T(8,128)(2,1)} custom-call(s32[1]{0:T(128)} %bitcast.spot_ref, bf16[512,768]{1,0:T(8,128)(2,1)} %get-tuple-element.227.operand.scaled, bf16[192,768]{1,0:T(8,128)(2,1)} %rest_2_.1, bf16[192,768]{1,0:T(8,128)(2,1)} %copy-done.12, bf16[192,768]{1,0:T(8,128)(2,1)} %copy-done.11, bf16[192,768]{1,0:T(8,128)(2,1)} %copy-done.13), custom_call_target="tpu_custom_call" | custom-call | flops 1 | bytes 1 | tf_op jit(solution)/shard_map/project/pallas_call | solution.py:173
  30.6 18.6 %collective-permute-done.5.refs_11_.refs_7_ = bf16[192,768]{1,0:T(8,128)(2,1)S(1)} collective-permute-done((bf16[192,768]{1,0:T(8,128)(2,1)S(1)}, bf16[192,768]{1,0:T(8,128)(2,1)S(1)}, u32[]{:S(2)}, u32[]{:S(2)}) %collective-permute-start.5) | collective-permute-done | bytes 294944 | tf_op jit(solution)/shard_map/ppermute | solution.py:1067
  49.2 1.4 collective-permute-start.8
  51.6 8.4 %attend.1 = (s32[2,256,128]{2,1,0:T(8,128)}, f32[2,256,768]{2,1,0:T(8,128)}, bf16[2,256,768]{2,1,0:T(8,128)(2,1)}, f32[2,256,768]{2,1,0:T(8,128)}) custom-call(s32[1]{0:T(128)} %bitcast.1.place_ref, bf16[2,256,768]{2,1,0:T(8,128)(2,1)} %bitcast.84, bf16[8,2,272,128]{3,2,1,0:T(8,128)(2,1)} %bitcast.81), custom_call_target="tpu_custom_call" | custom-call | flops 1 | bytes 1 | tf_op jit(solution)/shard_map/attend/pallas_call | solution.py:450
  60.0 7.7 %collective-permute-done.8.refs_7_ = bf16[1536,256]{1,0:T(8,128)(2,1)} collective-permute-done((bf16[1536,256]{1,0:T(8,128)(2,1)}, bf16[1536,256]{1,0:T(8,128)(2,1)}, u32[]{:S(2)}, u32[]{:S(2)}) %collective-permute-start.8) | collective-permute-done | bytes 786464 | tf_op jit(solution)/shard_map/ppermute | solution.py:1067
  67.7 1.8 collective-permute-start.15
  72.1 21.5 %feed0.1 = (bf16[2,1536,256]{2,1,0:T(8,128)(2,1)}, bf16[2,1536,256]{2,1,0:T(8,128)(2,1)}, bf16[2,2,768,256]{3,2,1,0:T(8,128)(2,1)}, bf16[2,2,768,256]{3,2,1,0:T(...) custom-call(s32[1]{0:T(128)} %bitcast.spot_ref, ...), custom_call_target="tpu_custom_call" | custom-call | flops 1 | bytes 1 | tf_op jit(solution)/shard_map/feed0/pallas_call | solution.py:804
  95.5 2.6 collective-permute-done.16
  98.1 2.8 fusion.2
  101.3 1.5 collective-permute-start.21
  105.7 16.8 %feed2.1 = (bf16[2,2176,256]{2,1,0:T(8,128)(2,1)}, bf16[2,2176,256]{2,1,0:T(8,128)(2,1)}, bf16[512,768]{1,0:T(8,128)(2,1)}, f32[512,768]{1,0:T(8,128)}, bf16[512,768]{1,0:T(8,128)(2,1)}) custom-call(s32[1]{0:T(128)} %bitcast.spot_ref, bf16[512,768]{1,0:T(8,128)(2,1)} %bitcast.91, bf16[1536,256]{1,0:T(8,128)(2,1)} %get-tuple-element.248.refs_1_, ...), custom_call_target="tpu_custom_call" | custom-call | flops 1 | bytes 1 | tf_op jit(solution)/shard_map/feed2/pallas_call | solution.py:804
  124.8 2.3 collective-permute-done.22
  131.1 6.5 %attend_back.2 = (bf16[1,256,768]{2,1,0:T(8,128)(2,1)}, bf16[4,256,128]{2,1,0:T(8,128)(2,1)}, bf16[4,256,128]{2,1,0:T(8,128)(2,1)}) custom-call(s32[1]{0:T(128)} %bitcast.1.place_ref, bf16[2,256,768]{2,1,0:T(8,128)(2,1)} %bitcast.85, s32[2,256,128]{2,1,0:T(8,128)} %get-tuple-element.289.starts, f32[2,256,768]{2,1,0:T(8,128)} %get-tuple-element.290.exact, ...), custom_call_target="tpu_custom_call" | custom-call | flops 1 | bytes 1 | tf_op jit(solution)/shard_map/attend_back/pallas_call | solution.py:493
  137.8 2.9 %collective-permute-done.25 = bf16[2,4,96,256]{3,2,1,0:T(8,128)(2,1)} collective-permute-done((bf16[2,4,96,256]{3,2,1,0:T(8,128)(2,1)}, bf16[2,4,96,256]{3,2,1,0:T(8,128)(2,1)}, u32[]{:S(2)}, u32[]{:S(2)}) %collective-permute-start.25) | collective-permute-done | bytes 393248 | tf_op jit(solution)/shard_map/ppermute | solution.py:1067
  140.8 7.6 %collective-permute-done.24 = bf16[4,192,256]{2,1,0:T(8,128)(2,1)} collective-permute-done((bf16[4,192,256]{2,1,0:T(8,128)(2,1)}, bf16[4,192,256]{2,1,0:T(8,128)(2,1)}, u32[]{:S(2)}, u32[]{:S(2)}) %collective-permute-start.24) | collective-permute-done | bytes 393248 | tf_op jit(solution)/shard_map/ppermute | solution.py:1067
  152.5 1.4 collective-permute-start.26
  153.9 4.3 %collective-permute-start.27 = (bf16[2,192,256]{2,1,0:T(8,128)(2,1)S(1)}, bf16[2,192,256]{2,1,0:T(8,128)(2,1)S(1)}, u32[]{:S(2)}, u32[]{:S(2)}) collective-permute-start(bf16[2,192,256]{2,1,0:T(8,128)(2,1)S(1)} %pad_maximum_fusion.6), channel_id=1, source_target_pairs={{0,16},{4,20},{8,24},{12,28},{16,0},{20,4},{24,8},{28,12},{1,17},{... | collective-permute-start | bytes 589832 | tf_op jit(solution)/shard_map/ppermute | solution.py:1067
  159.2 6.5 %attend_back.3 = (bf16[1,256,768]{2,1,0:T(8,128)(2,1)}, bf16[4,256,128]{2,1,0:T(8,128)(2,1)}, bf16[4,256,128]{2,1,0:T(8,128)(2,1)}) custom-call(s32[1]{0:T(128)} %bitcast.1.place_ref, bf16[2,256,768]{2,1,0:T(8,128)(2,1)} %bitcast.86, s32[2,256,128]{2,1,0:T(8,128)} %get-tuple-element.289.starts, f32[2,256,768]{2,1,0:T(8,128)} %get-tuple-element.290.exact, ...), custom_call_target="tpu_custom_call" | custom-call | flops 1 | bytes 1 | tf_op jit(solution)/shard_map/attend_back/pallas_call | solution.py:493
  166.7 5.8 %collective-permute-done.27 = bf16[2,192,256]{2,1,0:T(8,128)(2,1)S(1)} collective-permute-done((bf16[2,192,256]{2,1,0:T(8,128)(2,1)S(1)}, bf16[2,192,256]{2,1,0:T(8,128)(2,1)S(1)}, u32[]{:S(2)}, u32[]{:S(2)}) %collective-permute-start.27) | collective-permute-done | bytes 196640 | tf_op jit(solution)/shard_map/ppermute | solution.py:1067
  172.5 2.0 collective-permute-start.31
  175.8 4.7 %query_grad.1 = (f32[512,768]{1,0:T(8,128)}, bf16[2,576,256]{2,1,0:T(8,128)(2,1)}, bf16[2,576,256]{2,1,0:T(8,128)(2,1)}) custom-call(s32[1]{0:T(128)} %bitcast.spot_ref, bf16[512,768]{1,0:T(8,128)(2,1)} %get-tuple-element.227.operand.scaled, bf16[256,768]{1,0:T(8,128)(2,1)} %bitcast.105, bf16[256,768]{1,0:T(8,128)(2,1)} %bitcast.106, ...), custom_call_target="tpu_custom_call" | custom-call | flops 1 | bytes 1 | tf_op jit(solution)/shard_map/query_grad/pallas_call | solution.py:851
  181.9 8.7 %all-to-all-start.1 = ((bf16[4,2,256,128]{3,2,1,0:T(8,128)(2,1)}), bf16[4,2,256,128]{3,2,1,0:T(8,128)(2,1)S(1)}, u32[]{:S(2)}, u32[]{:S(2)}) async-start(bf16[4,2,256,128]{3,2,1,0:T(8,128)(2,1)} %pad_maximum_fusion.2), calls=%async_computation.1 | async-start | bytes 1048576 | tf_op jit(solution)/shard_map/all_to_all | solution.py:1301
  192.4 13.1 %collective-permute-done.33 = bf16[4,272,256]{2,1,0:T(8,128)(2,1)S(1)} collective-permute-done((bf16[4,272,256]{2,1,0:T(8,128)(2,1)}, bf16[4,272,256]{2,1,0:T(8,128)(2,1)S(1)}, u32[]{:S(2)}, u32[]{:S(2)}) %collective-permute-start.33) | collective-permute-done | bytes 557088 | tf_op jit(solution)/shard_map/ppermute | solution.py:1067
  205.7 1.8 collective-permute-start.34
  207.5 2.4 collective-permute-start.35
  211.0 5.7 %last.1 = (f32[512,768]{1,0:T(8,128)}, bf16[2,192,256]{2,1,0:T(8,128)(2,1)}, bf16[2,192,256]{2,1,0:T(8,128)(2,1)}) custom-call(s32[1]{0:T(128)} %bitcast.spot_ref, bf16[512,768]{1,0:T(8,128)(2,1)} %bitcast.89, f32[1,768]{1,0:T(1,128)} %reshape_squeeze.6.gain, bf16[512,768]{1,0:T(8,128)(2,1)} %get-tuple-element.227.operand.scaled, ...), custom_call_target="tpu_custom_call" | custom-call | flops 1 | bytes 1 | tf_op jit(solution)/shard_map/last/pallas_call | solution.py:908
  216.7 3.3 %collective-permute-start.40 = (bf16[2,192,256]{2,1,0:T(8,128)(2,1)S(1)}, bf16[2,192,256]{2,1,0:T(8,128)(2,1)S(1)}, u32[]{:S(2)}, u32[]{:S(2)}) collective-permute-start(bf16[2,192,256]{2,1,0:T(8,128)(2,1)S(1)} %add_convert_fusion.18), channel_id=1, source_target_pairs={{0,16},{4,20},{8,24},{12,28},{16,0},{20,4},{24,8},{28,12},{1,17},{... | collective-permute-start | bytes 589832 | tf_op jit(solution)/shard_map/ppermute | solution.py:1067
  220.5 1.6 collective-permute-done.38
  224.2 11.7 %collective-permute-done.40 = bf16[2,192,256]{2,1,0:T(8,128)(2,1)S(1)} collective-permute-done((bf16[2,192,256]{2,1,0:T(8,128)(2,1)S(1)}, bf16[2,192,256]{2,1,0:T(8,128)(2,1)S(1)}, u32[]{:S(2)}, u32[]{:S(2)}) %collective-permute-start.40) | collective-permute-done | bytes 196640 | tf_op jit(solution)/shard_map/ppermute | solution.py:1067
  237.0 6.0 %all-to-all-start.2 = ((bf16[8,96,256]{2,1,0:T(8,128)(2,1)}), bf16[8,96,256]{2,1,0:T(8,128)(2,1)S(1)}, u32[]{:S(2)}, u32[]{:S(2)}) async-start(bf16[8,96,256]{2,1,0:T(8,128)(2,1)} %pad_maximum_fusion.3), calls=%async_computation.2 | async-start | bytes 786432 | tf_op jit(solution)/shard_map/all_to_all | solution.py:1327
  243.0 2.0 collective-permute-start.43
  245.0 2.4 collective-permute-start.44
  247.4 2.0 collective-permute-start.46
  249.4 8.2 %all-to-all-done.2 = bf16[8,96,256]{2,1,0:T(8,128)(2,1)S(1)} async-done(((bf16[8,96,256]{2,1,0:T(8,128)(2,1)}), bf16[8,96,256]{2,1,0:T(8,128)(2,1)S(1)}, u32[]{:S(2)}, u32[]{:S(2)}) %all-to-all-start.2) | async-done | bytes 393248 | tf_op jit(solution)/shard_map/all_to_all | solution.py:1327
  258.4 6.0 %all-to-all-start.3 = ((bf16[8,96,256]{2,1,0:T(8,128)(2,1)}), bf16[8,96,256]{2,1,0:T(8,128)(2,1)S(1)}, u32[]{:S(2)}, u32[]{:S(2)}) async-start(bf16[8,96,256]{2,1,0:T(8,128)(2,1)} %broadcast_in_dim.3), calls=%async_computation.3 | async-start | bytes 786432 | tf_op jit(solution)/shard_map/all_to_all | solution.py:1331
  264.4 2.5 collective-permute-done.44
  267.0 1.4 collective-permute-start.47
  268.3 2.8 collective-permute-done.46.other
  272.0 3.9 %early_sums.1 = (f32[768,768]{1,0:T(8,128)}, f32[192,3072]{1,0:T(8,128)}) custom-call(s32[1]{0:T(128)} %bitcast.1.place_ref, bf16[4,2,192,256]{3,2,1,0:T(8,128)(2,1)} %copy-done.1, bf16[4,2,192,256]{3,2,1,0:T(8,128)(2,1)} %copy-done.22), custom_call_target="tpu_custom_call" | custom-call | flops 1 | bytes 1 | tf_op jit(solution)/shard_map/early_sums/pallas_call | solution.py:956
  275.9 7.4 %collective-permute-done.47.other = bf16[4,1,272,256]{3,2,1,0:T(8,128)(2,1)S(1)} collective-permute-done((bf16[4,1,272,256]{3,2,1,0:T(8,128)(2,1)S(1)}, bf16[4,1,272,256]{3,2,1,0:T(8,128)(2,1)S(1)}, u32[]{:S(2)}, u32[]{:S(2)}) %collective-permute-start.47) | collective-permute-done | bytes 557088 | tf_op jit(solution)/shard_map/ppermute | solution.py:1067
  284.9 3.9 %final.1 = (f32[768,768]{1,0:T(8,128)}, f32[192,3072]{1,0:T(8,128)}, f32[192,768]{1,0:T(8,128)}, f32[192,768]{1,0:T(8,128)}, f32[192,128]{1,0:T(8,128)}, /*index=5*/f32[1,192]{1,0:T(1,128)}, f32[1,192]{1,0:T(1,128)}) custom-call(s32[1]{0:T(128)} %bitcast.1.place_ref, s32[1]{0:T(128)} %bitcast.spot_ref, ...), custom_call_target="tpu_custom_call", output_to_operand_aliasing={{0}: (5, {}), {1}: (6, {})} | custom-call | flops 1 | bytes 1 | tf_op jit(solution)/shard_map/final/pallas_call | solution.py:1034
  (184 shorter events, 40.3 us)
Async XLA Ops:
  2.1 5.2 %collective-permute-start.1 = (bf16[208,128]{1,0:T(8,128)(2,1)S(1)}, bf16[208,128]{1,0:T(8,128)(2,1)S(1)}, u32[]{:S(2)}, u32[]{:S(2)}) collective-permute-start(bf16[208,128]{1,0:T(8,128)(2,1)S(1)} %fusion.21.rest_0_), channel_id=1, source_target_pairs={{0,2},{1,3},{2,0},{3,1},{4,6},{5,7},{6,4},{7,5},{8,10},{9,11},{10,... | collective-permute-start | bytes 159752 | tf_op jit(solution)/shard_map/ppermute | solution.py:1067
  5.2 3.5 %collective-permute-start = (bf16[208,128]{1,0:T(8,128)(2,1)S(1)}, bf16[208,128]{1,0:T(8,128)(2,1)S(1)}, u32[]{:S(2)}, u32[]{:S(2)}) collective-permute-start(bf16[208,128]{1,0:T(8,128)(2,1)S(1)} %fusion.21.rest_0_), channel_id=1, source_target_pairs={{0,1},{1,0},{2,3},{3,2},{4,5},{5,4},{6,7},{7,6},{8,9},{9,8},{10,11... | collective-permute-start | bytes 159752 | tf_op jit(solution)/shard_map/ppermute | solution.py:1067
  5.2 9.6 %collective-permute-start.3 = (bf16[192,768]{1,0:T(8,128)(2,1)}, bf16[192,768]{1,0:T(8,128)(2,1)S(1)}, u32[]{:S(2)}, u32[]{:S(2)}) collective-permute-start(bf16[192,768]{1,0:T(8,128)(2,1)} %rest_2_.1), channel_id=1, source_target_pairs={{0,2},{1,3},{2,0},{3,1},{4,6},{5,7},{6,4},{7,5},{8,10},{9,11},{10,... | collective-permute-start | bytes 884744 | tf_op jit(solution)/shard_map/ppermute | solution.py:1067
  14.8 34.4 %all-to-all-start = ((bf16[8,544,128]{2,1,0:T(8,128)(2,1)}), bf16[8,544,128]{2,1,0:T(8,128)(2,1)S(1)}, u32[]{:S(2)}, u32[]{:S(2)}) async-start(bf16[8,544,128]{2,1,0:T(8,128)(2,1)} %get-tuple-element.222), calls=%async_computation | async-start | bytes 2228224 | tf_op jit(solution)/shard_map/all_to_all | solution.py:1229
  23.8 25.4 %collective-permute-start.4 = (bf16[1536,256]{1,0:T(8,128)(2,1)}, bf16[1536,256]{1,0:T(8,128)(2,1)}, u32[]{:S(2)}, u32[]{:S(2)}) collective-permute-start(bf16[1536,256]{1,0:T(8,128)(2,1)} %get-tuple-element.225.refs_1_), channel_id=1, source_target_pairs={{0,2},{1,3},{2,0},{3,1},{4,6},{5,7},{6,4},{7,5},{8,10},{9,11},{10,... | collective-permute-start | bytes 2359304 | tf_op jit(solution)/shard_map/ppermute | solution.py:1067
  24.6 2.0 collective-permute-start.7
  25.1 24.1 %collective-permute-start.5 = (bf16[192,768]{1,0:T(8,128)(2,1)S(1)}, bf16[192,768]{1,0:T(8,128)(2,1)S(1)}, u32[]{:S(2)}, u32[]{:S(2)}) collective-permute-start(bf16[192,768]{1,0:T(8,128)(2,1)S(1)} %copy-done.9), channel_id=1, source_target_pairs={{0,2},{1,3},{2,0},{3,1},{4,6},{5,7},{6,4},{7,5},{8,10},{9,11},{10,... | collective-permute-start | bytes 884744 | tf_op jit(solution)/shard_map/ppermute | solution.py:1067
  49.2 18.5 %collective-permute-start.8 = (bf16[1536,256]{1,0:T(8,128)(2,1)}, bf16[1536,256]{1,0:T(8,128)(2,1)}, u32[]{:S(2)}, u32[]{:S(2)}) collective-permute-start(bf16[1536,256]{1,0:T(8,128)(2,1)} %get-tuple-element.234.refs_5_), channel_id=1, source_target_pairs={{0,2},{1,3},{2,0},{3,1},{4,6},{5,7},{6,4},{7,5},{8,10},{9,11},{10,... | collective-permute-start | bytes 2359304 | tf_op jit(solution)/shard_map/ppermute | solution.py:1067
  50.6 18.9 %collective-permute-start.9 = (bf16[1536,256]{1,0:T(8,128)(2,1)}, bf16[1536,256]{1,0:T(8,128)(2,1)}, u32[]{:S(2)}, u32[]{:S(2)}) collective-permute-start(bf16[1536,256]{1,0:T(8,128)(2,1)} %get-tuple-element.225.refs_1_), channel_id=1, source_target_pairs={{0,1},{1,0},{2,3},{3,2},{4,5},{5,4},{6,7},{7,6},{8,9},{9,8},{10,11... | collective-permute-start | bytes 2359304 | tf_op jit(solution)/shard_map/ppermute | solution.py:1067
  50.6 17.1 %collective-permute-start.13 = (bf16[192,768]{1,0:T(8,128)(2,1)S(1)}, bf16[192,768]{1,0:T(8,128)(2,1)S(1)}, u32[]{:S(2)}, u32[]{:S(2)}) collective-permute-start(bf16[192,768]{1,0:T(8,128)(2,1)S(1)} %copy-done.9), channel_id=1, source_target_pairs={{0,1},{1,0},{2,3},{3,2},{4,5},{5,4},{6,7},{7,6},{8,9},{9,8},{10,11... | collective-permute-start | bytes 884744 | tf_op jit(solution)/shard_map/ppermute | solution.py:1067
  51.1 20.0 %collective-permute-start.11 = (bf16[1536,256]{1,0:T(8,128)(2,1)}, bf16[1536,256]{1,0:T(8,128)(2,1)}, u32[]{:S(2)}, u32[]{:S(2)}) collective-permute-start(bf16[1536,256]{1,0:T(8,128)(2,1)} %get-tuple-element.234.refs_5_), channel_id=1, source_target_pairs={{0,1},{1,0},{2,3},{3,2},{4,5},{5,4},{6,7},{7,6},{8,9},{9,8},{10,11... | collective-permute-start | bytes 2359304 | tf_op jit(solution)/shard_map/ppermute | solution.py:1067
  51.1 20.0 %collective-permute-start.10 = (bf16[1536,256]{1,0:T(8,128)(2,1)}, bf16[1536,256]{1,0:T(8,128)(2,1)}, u32[]{:S(2)}, u32[]{:S(2)}) collective-permute-start(bf16[1536,256]{1,0:T(8,128)(2,1)} %collective-permute-done.4.refs_3_), channel_id=1, source_target_pairs={{0,1},{1,0},{2,3},{3,2},{4,5},{5,4},{6,7},{7,6},{8,9},{9,8},{10,11... | collective-permute-start | bytes 2359304 | tf_op jit(solution)/shard_map/ppermute | solution.py:1067
  67.7 3.4 %collective-permute-start.12 = (bf16[1536,256]{1,0:T(8,128)(2,1)}, bf16[1536,256]{1,0:T(8,128)(2,1)S(1)}, u32[]{:S(2)}, u32[]{:S(2)}) collective-permute-start(bf16[1536,256]{1,0:T(8,128)(2,1)} %collective-permute-done.8.refs_7_), channel_id=1, source_target_pairs={{0,1},{1,0},{2,3},{3,2},{4,5},{5,4},{6,7},{7,6},{8,9},{9,8},{10,11... | collective-permute-start | bytes 2359304 | tf_op jit(solution)/shard_map/ppermute | solution.py:1067
  67.7 25.9 %collective-permute-start.15 = (bf16[1536,256]{1,0:T(8,128)(2,1)S(1)}, bf16[1536,256]{1,0:T(8,128)(2,1)S(1)}, u32[]{:S(2)}, u32[]{:S(2)}) collective-permute-start(bf16[1536,256]{1,0:T(8,128)(2,1)S(1)} %copy-done.17), channel_id=1, source_target_pairs={{0,2},{1,3},{2,0},{3,1},{4,6},{5,7},{6,4},{7,5},{8,10},{9,11},{10,... | collective-permute-start | bytes 2359304 | tf_op jit(solution)/shard_map/ppermute | solution.py:1067
  94.5 3.6 %collective-permute-start.16 = (bf16[2,2,4,192,256]{4,3,2,1,0:T(8,128)(2,1)}, bf16[2,2,4,192,256]{4,3,2,1,0:T(8,128)(2,1)S(1)}, u32[]{:S(2)}, u32[]{:S(2)}) collective-permute-start(bf16[2,2,4,192,256]{4,3,2,1,0:T(8,128)(2,1)} %bitcast.119), channel_id=1, source_target_pairs={{0,1},{1,0},{2,3},{3,2},{4,5},{5,4},{6,7},{7,6},{8,9},{9,8},{10,11... | collective-permute-start | bytes 4718600 | tf_op jit(solution)/shard_map/ppermute | solution.py:1067
  94.7 6.2 %collective-permute-start.17 = (bf16[2,2,4,192,256]{4,3,2,1,0:T(8,128)(2,1)}, bf16[2,2,4,192,256]{4,3,2,1,0:T(8,128)(2,1)S(1)}, u32[]{:S(2)}, u32[]{:S(2)}) collective-permute-start(bf16[2,2,4,192,256]{4,3,2,1,0:T(8,128)(2,1)} %bitcast.118), channel_id=1, source_target_pairs={{0,1},{1,0},{2,3},{3,2},{4,5},{5,4},{6,7},{7,6},{8,9},{9,8},{10,11... | collective-permute-start | bytes 4718600 | tf_op jit(solution)/shard_map/ppermute | solution.py:1067
  95.0 8.8 %collective-permute-start.18 = (bf16[1536,256]{1,0:T(8,128)(2,1)}, bf16[1536,256]{1,0:T(8,128)(2,1)S(1)}, u32[]{:S(2)}, u32[]{:S(2)}) collective-permute-start(bf16[1536,256]{1,0:T(8,128)(2,1)} %get-tuple-element.248.refs_1_), channel_id=1, source_target_pairs={{0,1},{1,0},{2,3},{3,2},{4,5},{5,4},{6,7},{7,6},{8,9},{9,8},{10,11... | collective-permute-start | bytes 2359304 | tf_op jit(solution)/shard_map/ppermute | solution.py:1067
  95.2 8.7 %collective-permute-start.19 = (bf16[1536,256]{1,0:T(8,128)(2,1)}, bf16[1536,256]{1,0:T(8,128)(2,1)S(1)}, u32[]{:S(2)}, u32[]{:S(2)}) collective-permute-start(bf16[1536,256]{1,0:T(8,128)(2,1)} %copy-done.18), channel_id=1, source_target_pairs={{0,1},{1,0},{2,3},{3,2},{4,5},{5,4},{6,7},{7,6},{8,9},{9,8},{10,11... | collective-permute-start | bytes 2359304 | tf_op jit(solution)/shard_map/ppermute | solution.py:1067
  101.3 21.2 %collective-permute-start.21 = (bf16[2,4,192,256]{3,2,1,0:T(8,128)(2,1)S(1)}, bf16[2,4,192,256]{3,2,1,0:T(8,128)(2,1)S(1)}, u32[]{:S(2)}, u32[]{:S(2)}) collective-permute-start(bf16[2,4,192,256]{3,2,1,0:T(8,128)(2,1)S(1)} %get-tuple-element.298), channel_id=1, source_target_pairs={{0,4},{4,0},{8,12},{12,8},{16,20},{20,16},{24,28},{28,24},{1,5},{5... | collective-permute-start | bytes 2359304 | tf_op jit(solution)/shard_map/ppermute | solution.py:1067
  102.8 19.7 %collective-permute-start.20 = (bf16[2,4,192,256]{3,2,1,0:T(8,128)(2,1)}, bf16[2,4,192,256]{3,2,1,0:T(8,128)(2,1)S(1)}, u32[]{:S(2)}, u32[]{:S(2)}) collective-permute-start(bf16[2,4,192,256]{3,2,1,0:T(8,128)(2,1)} %get-tuple-element.297), channel_id=1, source_target_pairs={{0,2},{1,3},{2,0},{3,1},{4,6},{5,7},{6,4},{7,5},{8,10},{9,11},{10,... | collective-permute-start | bytes 2359304 | tf_op jit(solution)/shard_map/ppermute | solution.py:1067
  122.5 4.6 %collective-permute-start.22 = (bf16[2,2,4,272,256]{4,3,2,1,0:T(8,128)(2,1)}, bf16[2,2,4,272,256]{4,3,2,1,0:T(8,128)(2,1)S(1)}, u32[]{:S(2)}, u32[]{:S(2)}) collective-permute-start(bf16[2,2,4,272,256]{4,3,2,1,0:T(8,128)(2,1)} %bitcast.116), channel_id=1, source_target_pairs={{0,1},{1,0},{2,3},{3,2},{4,5},{5,4},{6,7},{7,6},{8,9},{9,8},{10,11... | collective-permute-start | bytes 6684680 | tf_op jit(solution)/shard_map/ppermute | solution.py:1067
  128.5 12.3 %collective-permute-start.25 = (bf16[2,4,96,256]{3,2,1,0:T(8,128)(2,1)}, bf16[2,4,96,256]{3,2,1,0:T(8,128)(2,1)}, u32[]{:S(2)}, u32[]{:S(2)}) collective-permute-start(bf16[2,4,96,256]{3,2,1,0:T(8,128)(2,1)} %add_convert_fusion.8), channel_id=1, source_target_pairs={{0,2},{1,3},{2,0},{3,1},{4,6},{5,7},{6,4},{7,5},{8,10},{9,11},{10,... | collective-permute-start | bytes 1179656 | tf_op jit(solution)/shard_map/ppermute | solution.py:1067
  129.5 11.3 %collective-permute-start.23 = (bf16[4,192,256]{2,1,0:T(8,128)(2,1)}, bf16[4,192,256]{2,1,0:T(8,128)(2,1)}, u32[]{:S(2)}, u32[]{:S(2)}) collective-permute-start(bf16[4,192,256]{2,1,0:T(8,128)(2,1)} %get-tuple-element.318), channel_id=1, source_target_pairs={{0,4},{4,0},{8,12},{12,8},{16,20},{20,16},{24,28},{28,24},{1,5},{5... | collective-permute-start | bytes 1179656 | tf_op jit(solution)/shard_map/ppermute | solution.py:1067
  130.1 18.3 %collective-permute-start.24 = (bf16[4,192,256]{2,1,0:T(8,128)(2,1)}, bf16[4,192,256]{2,1,0:T(8,128)(2,1)}, u32[]{:S(2)}, u32[]{:S(2)}) collective-permute-start(bf16[4,192,256]{2,1,0:T(8,128)(2,1)} %get-tuple-element.319), channel_id=1, source_target_pairs={{0,2},{1,3},{2,0},{3,1},{4,6},{5,7},{6,4},{7,5},{8,10},{9,11},{10,... | collective-permute-start | bytes 1179656 | tf_op jit(solution)/shard_map/ppermute | solution.py:1067
  150.8 21.6 %collective-permute-start.29 = (bf16[2,4,176,256]{3,2,1,0:T(8,128)(2,1)S(1)}, bf16[2,4,176,256]{3,2,1,0:T(8,128)(2,1)S(1)}, u32[]{:S(2)}, u32[]{:S(2)}) collective-permute-start(bf16[2,4,176,256]{3,2,1,0:T(8,128)(2,1)S(1)} %add_convert_fusion.5), channel_id=1, source_target_pairs={{0,2},{1,3},{2,0},{3,1},{4,6},{5,7},{6,4},{7,5},{8,10},{9,11},{10,... | collective-permute-start | bytes 2162696 | tf_op jit(solution)/shard_map/ppermute | solution.py:1067
  151.9 20.5 %collective-permute-start.30 = (bf16[4,256,128]{2,1,0:T(8,128)(2,1)S(1)}, bf16[4,256,128]{2,1,0:T(8,128)(2,1)S(1)}, u32[]{:S(2)}, u32[]{:S(2)}) collective-permute-start(bf16[4,256,128]{2,1,0:T(8,128)(2,1)S(1)} %copy-done.31), channel_id=1, source_target_pairs={{0,4},{4,0},{8,12},{12,8},{16,20},{20,16},{24,28},{28,24},{1,5},{5... | collective-permute-start | bytes 786440 | tf_op jit(solution)/shard_map/ppermute | solution.py:1067
  152.5 14.2 %collective-permute-start.26 = (bf16[2,192,256]{2,1,0:T(8,128)(2,1)S(1)}, bf16[2,192,256]{2,1,0:T(8,128)(2,1)S(1)}, u32[]{:S(2)}, u32[]{:S(2)}) collective-permute-start(bf16[2,192,256]{2,1,0:T(8,128)(2,1)S(1)} %pad_maximum_fusion.5), channel_id=1, source_target_pairs={{0,8},{4,12},{8,0},{12,4},{16,24},{20,28},{24,16},{28,20},{1,9},{5... | collective-permute-start | bytes 589832 | tf_op jit(solution)/shard_map/ppermute | solution.py:1067
  153.9 18.5 %collective-permute-start.27 = (bf16[2,192,256]{2,1,0:T(8,128)(2,1)S(1)}, bf16[2,192,256]{2,1,0:T(8,128)(2,1)S(1)}, u32[]{:S(2)}, u32[]{:S(2)}) collective-permute-start(bf16[2,192,256]{2,1,0:T(8,128)(2,1)S(1)} %pad_maximum_fusion.6), channel_id=1, source_target_pairs={{0,16},{4,20},{8,24},{12,28},{16,0},{20,4},{24,8},{28,12},{1,17},{... | collective-permute-start | bytes 589832 | tf_op jit(solution)/shard_map/ppermute | solution.py:1067
  158.3 14.2 %collective-permute-start.28 = (bf16[2,192,256]{2,1,0:T(8,128)(2,1)S(1)}, bf16[2,192,256]{2,1,0:T(8,128)(2,1)S(1)}, u32[]{:S(2)}, u32[]{:S(2)}) collective-permute-start(bf16[2,192,256]{2,1,0:T(8,128)(2,1)S(1)} %pad_maximum_fusion.7), channel_id=1, source_target_pairs={{0,24},{4,28},{8,16},{12,20},{16,8},{20,12},{24,0},{28,4},{1,25},{... | collective-permute-start | bytes 589832 | tf_op jit(solution)/shard_map/ppermute | solution.py:1067
  172.5 8.4 %collective-permute-start.31 = (bf16[4,256,128]{2,1,0:T(8,128)(2,1)}, bf16[4,256,128]{2,1,0:T(8,128)(2,1)S(1)}, u32[]{:S(2)}, u32[]{:S(2)}) collective-permute-start(bf16[4,256,128]{2,1,0:T(8,128)(2,1)} %get-tuple-element.356), channel_id=1, source_target_pairs={{0,4},{4,0},{8,12},{12,8},{16,20},{20,16},{24,28},{28,24},{1,5},{5... | collective-permute-start | bytes 786440 | tf_op jit(solution)/shard_map/ppermute | solution.py:1067
  180.9 10.3 %collective-permute-start.32 = (bf16[2,2,4,72,256]{4,3,2,1,0:T(8,128)(2,1)}, bf16[2,2,4,72,256]{4,3,2,1,0:T(8,128)(2,1)S(1)}, u32[]{:S(2)}, u32[]{:S(2)}) collective-permute-start(bf16[2,2,4,72,256]{4,3,2,1,0:T(8,128)(2,1)} %bitcast.121), channel_id=1, source_target_pairs={{0,1},{1,0},{2,3},{3,2},{4,5},{5,4},{6,7},{7,6},{8,9},{9,8},{10,11... | collective-permute-start | bytes 1769480 | tf_op jit(solution)/shard_map/ppermute | solution.py:1067
  181.9 23.8 %all-to-all-start.1 = ((bf16[4,2,256,128]{3,2,1,0:T(8,128)(2,1)}), bf16[4,2,256,128]{3,2,1,0:T(8,128)(2,1)S(1)}, u32[]{:S(2)}, u32[]{:S(2)}) async-start(bf16[4,2,256,128]{3,2,1,0:T(8,128)(2,1)} %pad_maximum_fusion.2), calls=%async_computation.1 | async-start | bytes 1048576 | tf_op jit(solution)/shard_map/all_to_all | solution.py:1301
  190.6 15.0 %collective-permute-start.33 = (bf16[4,272,256]{2,1,0:T(8,128)(2,1)}, bf16[4,272,256]{2,1,0:T(8,128)(2,1)S(1)}, u32[]{:S(2)}, u32[]{:S(2)}) collective-permute-start(bf16[4,272,256]{2,1,0:T(8,128)(2,1)} %get-tuple-element.368), channel_id=1, source_target_pairs={{0,4},{4,0},{8,12},{12,8},{16,20},{20,16},{24,28},{28,24},{1,5},{5... | collective-permute-start | bytes 1671176 | tf_op jit(solution)/shard_map/ppermute | solution.py:1067
  191.3 25.4 %collective-permute-start.37 = (bf16[2,4,72,256]{3,2,1,0:T(8,128)(2,1)S(1)}, bf16[2,4,72,256]{3,2,1,0:T(8,128)(2,1)S(1)}, u32[]{:S(2)}, u32[]{:S(2)}) collective-permute-start(bf16[2,4,72,256]{3,2,1,0:T(8,128)(2,1)S(1)} %get-tuple-element.385), channel_id=1, source_target_pairs={{0,2},{1,3},{2,0},{3,1},{4,6},{5,7},{6,4},{7,5},{8,10},{9,11},{10,... | collective-permute-start | bytes 884744 | tf_op jit(solution)/shard_map/ppermute | solution.py:1067
  205.7 14.2 %collective-permute-start.34 = (bf16[1,272,256]{2,1,0:T(8,128)(2,1)S(1)}, bf16[1,272,256]{2,1,0:T(8,128)(2,1)S(1)}, u32[]{:S(2)}, u32[]{:S(2)}) collective-permute-start(bf16[1,272,256]{2,1,0:T(8,128)(2,1)S(1)} %get-tuple-element.382), channel_id=1, source_target_pairs={{0,8},{4,12},{8,0},{12,4},{16,24},{20,28},{24,16},{28,20},{1,9},{5... | collective-permute-start | bytes 417800 | tf_op jit(solution)/shard_map/ppermute | solution.py:1067
  207.5 12.7 %collective-permute-start.35 = (bf16[1,272,256]{2,1,0:T(8,128)(2,1)S(1)}, bf16[1,272,256]{2,1,0:T(8,128)(2,1)S(1)}, u32[]{:S(2)}, u32[]{:S(2)}) collective-permute-start(bf16[1,272,256]{2,1,0:T(8,128)(2,1)S(1)} %get-tuple-element.383), channel_id=1, source_target_pairs={{0,16},{4,20},{8,24},{12,28},{16,0},{20,4},{24,8},{28,12},{1,17},{... | collective-permute-start | bytes 417800 | tf_op jit(solution)/shard_map/ppermute | solution.py:1067
  209.9 10.6 %collective-permute-start.36 = (bf16[1,272,256]{2,1,0:T(8,128)(2,1)S(1)}, bf16[1,272,256]{2,1,0:T(8,128)(2,1)S(1)}, u32[]{:S(2)}, u32[]{:S(2)}) collective-permute-start(bf16[1,272,256]{2,1,0:T(8,128)(2,1)S(1)} %get-tuple-element.384), channel_id=1, source_target_pairs={{0,24},{4,28},{8,16},{12,20},{16,8},{20,12},{24,0},{28,4},{1,25},{... | collective-permute-start | bytes 417800 | tf_op jit(solution)/shard_map/ppermute | solution.py:1067
  210.2 14.0 %collective-permute-start.39 = (bf16[2,192,256]{2,1,0:T(8,128)(2,1)S(1)}, bf16[2,192,256]{2,1,0:T(8,128)(2,1)S(1)}, u32[]{:S(2)}, u32[]{:S(2)}) collective-permute-start(bf16[2,192,256]{2,1,0:T(8,128)(2,1)S(1)} %add_convert_fusion.18), channel_id=1, source_target_pairs={{0,8},{4,12},{8,0},{12,4},{16,24},{20,28},{24,16},{28,20},{1,9},{5... | collective-permute-start | bytes 589832 | tf_op jit(solution)/shard_map/ppermute | solution.py:1067
  216.7 19.2 %collective-permute-start.40 = (bf16[2,192,256]{2,1,0:T(8,128)(2,1)S(1)}, bf16[2,192,256]{2,1,0:T(8,128)(2,1)S(1)}, u32[]{:S(2)}, u32[]{:S(2)}) collective-permute-start(bf16[2,192,256]{2,1,0:T(8,128)(2,1)S(1)} %add_convert_fusion.18), channel_id=1, source_target_pairs={{0,16},{4,20},{8,24},{12,28},{16,0},{20,4},{24,8},{28,12},{1,17},{... | collective-permute-start | bytes 589832 | tf_op jit(solution)/shard_map/ppermute | solution.py:1067
  220.0 15.9 %collective-permute-start.41 = (bf16[2,192,256]{2,1,0:T(8,128)(2,1)S(1)}, bf16[2,192,256]{2,1,0:T(8,128)(2,1)S(1)}, u32[]{:S(2)}, u32[]{:S(2)}) collective-permute-start(bf16[2,192,256]{2,1,0:T(8,128)(2,1)S(1)} %add_convert_fusion.18), channel_id=1, source_target_pairs={{0,24},{4,28},{8,16},{12,20},{16,8},{20,12},{24,0},{28,4},{1,25},{... | collective-permute-start | bytes 589832 | tf_op jit(solution)/shard_map/ppermute | solution.py:1067
  223.1 12.9 %collective-permute-start.42 = (bf16[2,4,24,256]{3,2,1,0:T(8,128)(2,1)S(1)}, bf16[2,4,24,256]{3,2,1,0:T(8,128)(2,1)S(1)}, u32[]{:S(2)}, u32[]{:S(2)}) collective-permute-start(bf16[2,4,24,256]{3,2,1,0:T(8,128)(2,1)S(1)} %get-tuple-element.406), channel_id=1, source_target_pairs={{0,2},{1,3},{2,0},{3,1},{4,6},{5,7},{6,4},{7,5},{8,10},{9,11},{10,... | collective-permute-start | bytes 294920 | tf_op jit(solution)/shard_map/ppermute | solution.py:1067
  237.0 20.6 %all-to-all-start.2 = ((bf16[8,96,256]{2,1,0:T(8,128)(2,1)}), bf16[8,96,256]{2,1,0:T(8,128)(2,1)S(1)}, u32[]{:S(2)}, u32[]{:S(2)}) async-start(bf16[8,96,256]{2,1,0:T(8,128)(2,1)} %pad_maximum_fusion.3), calls=%async_computation.2 | async-start | bytes 786432 | tf_op jit(solution)/shard_map/all_to_all | solution.py:1327
  243.0 21.4 %collective-permute-start.43 = (bf16[1,272,256]{2,1,0:T(8,128)(2,1)S(1)}, bf16[1,272,256]{2,1,0:T(8,128)(2,1)S(1)}, u32[]{:S(2)}, u32[]{:S(2)}) collective-permute-start(bf16[1,272,256]{2,1,0:T(8,128)(2,1)S(1)} %add_convert_fusion.19), channel_id=1, source_target_pairs={{0,8},{4,12},{8,0},{12,4},{16,24},{20,28},{24,16},{28,20},{1,9},{5... | collective-permute-start | bytes 417800 | tf_op jit(solution)/shard_map/ppermute | solution.py:1067
  245.0 21.9 %collective-permute-start.44 = (bf16[1,272,256]{2,1,0:T(8,128)(2,1)S(1)}, bf16[1,272,256]{2,1,0:T(8,128)(2,1)S(1)}, u32[]{:S(2)}, u32[]{:S(2)}) collective-permute-start(bf16[1,272,256]{2,1,0:T(8,128)(2,1)S(1)} %add_convert_fusion.19), channel_id=1, source_target_pairs={{0,16},{4,20},{8,24},{12,28},{16,0},{20,4},{24,8},{28,12},{1,17},{... | collective-permute-start | bytes 417800 | tf_op jit(solution)/shard_map/ppermute | solution.py:1067
  247.4 19.5 %collective-permute-start.45 = (bf16[1,272,256]{2,1,0:T(8,128)(2,1)S(1)}, bf16[1,272,256]{2,1,0:T(8,128)(2,1)S(1)}, u32[]{:S(2)}, u32[]{:S(2)}) collective-permute-start(bf16[1,272,256]{2,1,0:T(8,128)(2,1)S(1)} %add_convert_fusion.19), channel_id=1, source_target_pairs={{0,24},{4,28},{8,16},{12,20},{16,8},{20,12},{24,0},{28,4},{1,25},{... | collective-permute-start | bytes 417800 | tf_op jit(solution)/shard_map/ppermute | solution.py:1067
  247.4 23.7 %collective-permute-start.46 = (bf16[4,2,192,256]{3,2,1,0:T(8,128)(2,1)S(1)}, bf16[4,2,192,256]{3,2,1,0:T(8,128)(2,1)S(1)}, u32[]{:S(2)}, u32[]{:S(2)}) collective-permute-start(bf16[4,2,192,256]{3,2,1,0:T(8,128)(2,1)S(1)} %pad_maximum_fusion.own), channel_id=1, source_target_pairs={{0,4},{4,0},{8,12},{12,8},{16,20},{20,16},{24,28},{28,24},{1,5},{5... | collective-permute-start | bytes 2359304 | tf_op jit(solution)/shard_map/ppermute | solution.py:1067
  258.4 24.9 %all-to-all-start.3 = ((bf16[8,96,256]{2,1,0:T(8,128)(2,1)}), bf16[8,96,256]{2,1,0:T(8,128)(2,1)S(1)}, u32[]{:S(2)}, u32[]{:S(2)}) async-start(bf16[8,96,256]{2,1,0:T(8,128)(2,1)} %broadcast_in_dim.3), calls=%async_computation.3 | async-start | bytes 786432 | tf_op jit(solution)/shard_map/all_to_all | solution.py:1331
  267.0 16.3 %collective-permute-start.47 = (bf16[4,1,272,256]{3,2,1,0:T(8,128)(2,1)S(1)}, bf16[4,1,272,256]{3,2,1,0:T(8,128)(2,1)S(1)}, u32[]{:S(2)}, u32[]{:S(2)}) collective-permute-start(bf16[4,1,272,256]{3,2,1,0:T(8,128)(2,1)S(1)} %pad_maximum_fusion.1.own), channel_id=1, source_target_pairs={{0,4},{4,0},{8,12},{12,8},{16,20},{20,16},{24,28},{28,24},{1,5},{5... | collective-permute-start | bytes 1671176 | tf_op jit(solution)/shard_map/ppermute | solution.py:1067
  (36 other events, 206.1 us)
